TPU v7x, 512 devices: a whole 4x8x8 slice. The times are simulated.
512 devices in a mesh: blk: 128 (over z, y, core), rhs: 4 (over x).
Axes of the slice: x: 4, y: 8, z: 8, core: 2. Of those that a mesh axis runs over, the one named last changes fastest.
Arguments:
- thermal_solution: float32 [16, 1024, 1024], P('rhs', 'blk'), may hold values from -6 to 6
- heat_forcing: float32 [16, 1024, 1024], P('rhs', 'blk'), may hold values from -6 to 6
- extinction_factor: float32 [1024, 1024], P('blk'), may hold values from 0.01 to 1
- cluster_label: int32 [1024, 1024], P('blk'), may hold values from 0 to 511, as said below
Outputs:
- corrected: float32 [16, 1024, 1024], P('rhs', 'blk')
- residual_ratio: float32 [16], replicated
Inputs may be any that keep to these rules, and one draw needn't show every extreme that they name: `cluster_label`: each aggregate number of a slab is held by 4 or more of that slab's cells, and the cells of one aggregate lie within 8 rows and 8 columns of one another.
All inputs are finite; a program needn't handle non-finite values.
Results may differ from a plain program's by a relative error of at most 0.0003.
Values sent between devices are 32-bit elements; how exact they have to be, the bound alone decides.
No kernel may reach another device: no remote copies, remote signals or barrier semaphores. Data moves between devices by JAX's collectives and lax.ppermute only.
A program may use at most 64 MiB of HBM per device.

v0:
```python
import jax
import jax.numpy as jnp
from jax import lax
from jax.sharding import PartitionSpec as P

damping_fine = 0.8
damping_coarse = 0.5


def with_halo(shard, sides, width):
    for axis, dim in sides:
        size, length = (lax.axis_size(axis), shard.shape[dim])
        up = [(i, (i + 1) % size) for i in range(size - 1)]
        down = [(j, i) for i, j in up]
        last = lax.slice_in_dim(shard, length - width, length, axis=dim)
        initial = lax.slice_in_dim(shard, 0, width, axis=dim)
        before = lax.ppermute(last, axis, up)
        after = lax.ppermute(initial, axis, down)
        shard = jnp.concatenate([before, shard, after], axis=dim)
    return shard


def stencil_rows(center, above, below, extinction_factor):
    sideways = jnp.pad(center, ((0, 0), (0, 0), (1, 1)))
    neighbours = above + below + sideways[:, :, :-2] + sideways[:, :, 2:]
    return (4.0 + extinction_factor) * center - neighbours


def local(thermal_solution, heat_forcing, extinction_factor, cluster_label):
    forcing_total, strip_lines_here, mesh_width = thermal_solution.shape
    blk_devices = lax.axis_size("blk")
    dev_index = lax.axis_index("blk")
    groups = strip_lines_here * mesh_width // 16
    slab_count = float(blk_devices)
    flat_ids = cluster_label.reshape(-1)
    diagonal0 = 4.0 + extinction_factor

    def fine_apply(field):
        padded = with_halo(field, (("blk", 1),), 1)
        return stencil_rows(field, padded[:, :-2], padded[:, 2:], extinction_factor)

    def top_level_smoother(iterate):
        return iterate + damping_fine * (heat_forcing - fine_apply(iterate)) / diagonal0

    def smoother_pairing(iterate):
        return top_level_smoother(top_level_smoother(iterate))

    def restrict(field):
        return jax.vmap(
            lambda plane: jax.ops.segment_sum(plane.reshape(-1), flat_ids, num_segments=groups)
        )(field)

    def prolong(coarse):
        return jnp.take(coarse, flat_ids, axis=1).reshape(
            forcing_total, strip_lines_here, mesh_width
        )

    def apply_coarse(coarse):
        return restrict(fine_apply(prolong(coarse)))

    idpad = jnp.pad(cluster_label, 1, constant_values=-1)
    same = (
        (idpad[:-2, 1:-1] == cluster_label).astype(jnp.float32)
        + (idpad[2:, 1:-1] == cluster_label).astype(jnp.float32)
        + (idpad[1:-1, :-2] == cluster_label).astype(jnp.float32)
        + (idpad[1:-1, 2:] == cluster_label).astype(jnp.float32)
    )
    diagonal1 = jax.ops.segment_sum(
        (4.0 + extinction_factor - same).reshape(-1), flat_ids, num_segments=groups
    )
    smoothed_iterate = smoother_pairing(thermal_solution)
    coarse_rhs = restrict(heat_forcing - fine_apply(smoothed_iterate))
    level_one = damping_coarse * coarse_rhs / diagonal1
    level_one = level_one + damping_coarse * (coarse_rhs - apply_coarse(level_one)) / diagonal1
    coarse_res = coarse_rhs - apply_coarse(level_one)
    slab_rhs = jnp.sum(coarse_res, axis=1) / (groups * slab_count)
    slab_diag = 2.0 + jnp.mean(extinction_factor) / (slab_count * slab_count)
    every_diag, every_rhs = (
        lax.all_gather(slab_diag[None], "blk", axis=0, tiled=True),
        lax.all_gather(slab_rhs[None], "blk", axis=0, tiled=True),
    )
    offdiag = jnp.full((blk_devices,), -1.0, jnp.float32)
    lower_band = offdiag.at[0].set(0.0)
    upper_band = offdiag.at[blk_devices - 1].set(0.0)
    solved = lax.linalg.tridiagonal_solve(lower_band, every_diag, upper_band, every_rhs)
    slab_corr = lax.dynamic_index_in_dim(solved, dev_index, 0, keepdims=False)
    level_one = level_one + slab_corr[:, None]
    for sweep_number in range(2):
        level_one = level_one + damping_coarse * (coarse_rhs - apply_coarse(level_one)) / diagonal1
    corrected = smoother_pairing(smoothed_iterate + prolong(level_one))
    final_res = heat_forcing - fine_apply(corrected)
    res_total, load_total = lax.psum(
        (
            jnp.sum(final_res * final_res, axis=(1, 2)),
            jnp.sum(heat_forcing * heat_forcing, axis=(1, 2)),
        ),
        "blk",
    )
    ratios = jnp.sqrt(res_total / load_total)
    every_ratio = lax.all_gather(ratios, "rhs", axis=0, tiled=True)
    return (corrected, every_ratio)


def solution(mesh):
    in_specs = (P("rhs", "blk", None), P("rhs", "blk", None), P("blk", None), P("blk", None))
    out_specs = (P("rhs", "blk", None), P())
    return jax.shard_map(local, mesh=mesh, in_specs=in_specs, out_specs=out_specs, check_vma=False)
```

profile of v0, /device:TPU:256, one launch (start us, length us, event | category | flops | bytes accessed | tf_op | source)
XLA Modules:
  0.0 1339.1 jit_solution(6194506778977129185)
XLA Ops:
  1.6 1.9 collective-permute-start
  3.6 7.0 collective-permute-start.1
  13.8 1.9 collective-permute-start.2
  15.7 7.0 collective-permute-start.3
  25.2 1.9 collective-permute-start.4
  27.1 7.0 collective-permute-start.5
  35.6 57.0 %scatter_custom_fusion.1 = f32[512]{0:T(512)S(1)} fusion(s32[8192]{0:T(1024)S(1)} %bitcast.1186, f32[8192]{0:T(1024)S(1)} %bitcast.1192, f32[]{:T(128)} %constant.278.clone.1), kind=kCustom, calls=%fused_computation.406 | custom fusion | flops 8192 | bytes 2052 | tf_op jit(solution)/shard_map/scatter-add | solution.py:68
  93.7 2.7 copy.566
  96.4 47.3 %scatter_custom_fusion = f32[4,512]{0,1:T(8,128)S(1)} fusion(s32[8192]{0:T(1024)S(1)} %bitcast.1187, f32[8192,4]{1,0:T(8,128)} %bitcast.1110, f32[]{:T(128)} %constant.278.clone.1), kind=kCustom, calls=%fused_computation.352 | custom fusion | flops 32768 | bytes 8704 | tf_op jit(solution)/shard_map/vmap()/scatter-add | solution.py:50
  144.0 27.7 %gather_fusion = f32[8192,4]{1,0:T(8,128)} fusion(f32[4,512]{0,1:T(8,128)S(1)} %copy.460, s32[8192]{0:T(1024)S(1)} %fusion.234), kind=kCustom, calls=%fused_computation.clone | custom fusion | bytes 294912 | tf_op jit(solution)/shard_map/jit(_take)/gather | solution.py:54
  171.7 7.5 broadcast_select_fusion.4
  179.1 2.9 copy.461
  182.0 1.9 collective-permute-start.6
  183.9 7.0 collective-permute-start.7
  192.5 2.7 copy.567
  195.2 47.3 %scatter_custom_fusion.2 = f32[4,512]{0,1:T(8,128)S(1)} fusion(s32[8192]{0:T(1024)S(1)} %bitcast.1188, f32[8192,4]{1,0:T(8,128)} %bitcast.1111, f32[]{:T(128)} %constant.278.clone.1), kind=kCustom, calls=%fused_computation.350 | custom fusion | flops 32768 | bytes 8704 | tf_op jit(solution)/shard_map/vmap()/scatter-add | solution.py:50
  242.7 27.7 %gather_fusion.1 = f32[8192,4]{1,0:T(8,128)} fusion(f32[4,512]{0,1:T(8,128)S(1)} %copy.470, s32[8192]{0:T(1024)S(1)} %fusion.234), kind=kCustom, calls=%fused_computation.1.clone | custom fusion | bytes 294912 | tf_op jit(solution)/shard_map/jit(_take)/gather | solution.py:54
  270.4 7.5 broadcast_select_fusion.3
  277.9 2.9 copy.471
  280.8 1.9 collective-permute-start.8
  282.7 7.0 collective-permute-start.9
  293.5 2.7 copy.568
  296.2 47.3 %scatter_custom_fusion.3 = f32[4,512]{0,1:T(8,128)S(1)} fusion(s32[8192]{0:T(1024)S(1)} %bitcast.1189, f32[8192,4]{1,0:T(8,128)} %bitcast.1112, f32[]{:T(128)} %constant.278.clone.1), kind=kCustom, calls=%fused_computation.348 | custom fusion | flops 32768 | bytes 8704 | tf_op jit(solution)/shard_map/vmap()/scatter-add | solution.py:50
  343.7 249.6 %all-reduce.15 = (f32[128]{0:T(128)S(1)}, f32[512]{0:T(512)S(1)}) all-reduce(f32[128]{0:T(128)S(1)} %dynamic-update-slice.4, f32[512]{0:T(512)S(1)} %multiply_dynamic-update-slice_fusion), channel_id=1, replica_groups=mesh['blk'=128,'rhs'=4] {'blk'}, use_global_device_ids=true, to_apply=%add.11 | all-reduce | flops 640 | bytes 5120
  596.5 79.1 %while.36 = (s32[]{:T(128)}, f32[]{:T(128)}, f32[4]{0:T(128)S(1)}, f32[3,32]{1,0:T(4,128)S(1)}, f32[3,32,4]{1,0,2:T(4,128)S(1)}, /*index=5*/f32[3,32]{1,0:T(4,12...) while((s32[]{:T(128)}, f32[]{:T(128)}, f32[4]{0:T(128)S(1)}, ...), condition=%wide.region_7.9_spmd, body=%wide.region_6.8_spmd.sunk | while | flops 513 | bytes 7277 | solution.py:85
  702.3 74.6 %while.37 = (s32[]{:T(128)}, f32[4]{0:T(128)S(1)}, f32[3,32,4]{1,0,2:T(4,128)S(1)}, f32[3,32,4]{2,1,0:T(8,128)S(1)}, f32[3,32]{1,0:T(4,128)S(1)}, /*index=5*/s32...) while((s32[]{:T(128)}, f32[4]{0:T(128)S(1)}, ...), condition=%wide.region_9.11_spmd, body=%wide.region_8.10_spmd.sunk | while | flops 290 | bytes 5637 | solution.py:85
  703.8 20.3 %fusion.405 = (f32[4]{0:T(128)S(1)}, f32[4]{0:T(128)S(1)}, f32[4]{0:T(128)S(1)}, f32[4]{0:T(128)S(1)}, f32[4]{0:T(128)S(1)}, /*index=5*/f32[4]{0:T(128)S(1)}, f3...) fusion(f32[3,32,4]{2,1,0:T(8,128)S(1)} %get-tuple-element.1117,, ...), kind=kLoop, calls=%fused_computation.176.clone.1 | loop fusion | flops 256 | bytes 1296 | tf_op jit(solution)/shard_map/while/body/eval_jaxpr/sub | solution.py:85
  728.7 20.3 %fusion.405 = (f32[4]{0:T(128)S(1)}, f32[4]{0:T(128)S(1)}, f32[4]{0:T(128)S(1)}, f32[4]{0:T(128)S(1)}, f32[4]{0:T(128)S(1)}, /*index=5*/f32[4]{0:T(128)S(1)}, f3...) fusion(f32[3,32,4]{2,1,0:T(8,128)S(1)} %get-tuple-element.1117,, ...), kind=kLoop, calls=%fused_computation.176.clone.1 | loop fusion | flops 256 | bytes 1296 | tf_op jit(solution)/shard_map/while/body/eval_jaxpr/sub | solution.py:85
  753.5 20.3 %fusion.405 = (f32[4]{0:T(128)S(1)}, f32[4]{0:T(128)S(1)}, f32[4]{0:T(128)S(1)}, f32[4]{0:T(128)S(1)}, f32[4]{0:T(128)S(1)}, /*index=5*/f32[4]{0:T(128)S(1)}, f3...) fusion(f32[3,32,4]{2,1,0:T(8,128)S(1)} %get-tuple-element.1117,, ...), kind=kLoop, calls=%fused_computation.176.clone.1 | loop fusion | flops 256 | bytes 1296 | tf_op jit(solution)/shard_map/while/body/eval_jaxpr/sub | solution.py:85
  776.9 1.9 fusion.269
  780.6 1.9 fusion.271
  782.5 1.9 fusion.272
  784.4 1.9 fusion.273
  788.2 1.9 fusion.275
  790.1 1.9 fusion.276
  793.8 1.9 fusion.278
  799.3 1.9 fusion.281
  801.3 1.9 fusion.282
  803.2 1.9 subtract_bitcast_fusion.1
  808.7 27.7 %gather_fusion.2 = f32[8192,4]{1,0:T(8,128)} fusion(f32[4,512]{0,1:T(8,128)S(1)} %copy.544, s32[8192]{0:T(1024)S(1)} %fusion.234), kind=kCustom, calls=%fused_computation.2.clone | custom fusion | bytes 294912 | tf_op jit(solution)/shard_map/jit(_take)/gather | solution.py:54
  836.4 7.5 broadcast_select_fusion.2
  843.9 2.9 copy.545
  846.8 1.9 collective-permute-start.10
  848.7 7.0 collective-permute-start.11
  857.2 2.7 copy.570
  859.9 47.5 %scatter_custom_fusion.4 = f32[4,512]{0,1:T(8,128)S(1)} fusion(s32[8192]{0:T(1024)S(1)} %bitcast.1190, f32[8192,4]{1,0:T(8,128)} %bitcast.1113, f32[]{:T(128)} %constant.278.clone.1), kind=kCustom, calls=%fused_computation.346 | custom fusion | flops 32768 | bytes 8704 | tf_op jit(solution)/shard_map/vmap()/scatter-add | solution.py:50
  907.8 27.7 %gather_fusion.3 = f32[8192,4]{1,0:T(8,128)} fusion(f32[4,512]{0,1:T(8,128)S(1)} %copy.554, s32[8192]{0:T(1024)S(1)} %fusion.234), kind=kCustom, calls=%fused_computation.3.clone | custom fusion | bytes 294912 | tf_op jit(solution)/shard_map/jit(_take)/gather | solution.py:54
  935.5 7.5 broadcast_select_fusion.1
  942.9 2.9 copy.555
  945.8 1.9 collective-permute-start.12
  947.8 7.0 collective-permute-start.13
  956.3 2.7 copy.571
  959.0 47.3 %scatter_custom_fusion.5 = f32[4,512]{0,1:T(8,128)S(1)} fusion(s32[8192]{0:T(1024)S(1)} %bitcast.1191, f32[8192,4]{1,0:T(8,128)} %bitcast.1109, f32[]{:T(128)} %constant.278.clone.1), kind=kCustom, calls=%fused_computation.344 | custom fusion | flops 32768 | bytes 8704 | tf_op jit(solution)/shard_map/vmap()/scatter-add | solution.py:50
  1006.6 27.7 %gather_fusion.4 = f32[8192,4]{1,0:T(8,128)} fusion(f32[4,512]{0,1:T(8,128)S(1)} %copy.564, s32[8192]{0:T(1024)S(1)} %fusion.234), kind=kCustom, calls=%fused_computation.4.clone | custom fusion | bytes 294912 | tf_op jit(solution)/shard_map/jit(_take)/gather | solution.py:54
  1034.3 7.5 broadcast_select_fusion
  1041.7 2.9 copy.565
  1044.7 1.9 collective-permute-start.14
  1046.6 7.0 collective-permute-start.15
  1055.2 1.9 collective-permute-start.16
  1057.1 7.0 collective-permute-start.17
  1065.7 1.9 collective-permute-start.18
  1067.6 7.0 collective-permute-start.19
  1076.8 251.3 %all-reduce.14 = (f32[4]{0:T(128)S(1)}, f32[4]{0:T(128)S(1)}) all-reduce(f32[4]{0:T(128)S(1)} %get-tuple-element.247, f32[4]{0:T(128)S(1)} %get-tuple-element.246), channel_id=1, replica_groups=mesh['blk'=128,'rhs'=4] {'blk'}, use_global_device_ids=true, to_apply=%region_13.15 | all-reduce | flops 8 | bytes 64 | tf_op jit(solution)/shard_map/psum | solution.py:92
  1328.2 11.0 all-reduce.13
  (401 shorter events, 72.8 us)
Async XLA Ops:
  1.6 10.5 collective-permute-start
  3.6 8.6 collective-permute-start.1
  13.8 9.7 collective-permute-start.2
  15.7 8.4 collective-permute-start.3
  25.2 67.5 %collective-permute-start.4 = (f32[4,1,1024]{2,1,0:T(1,128)S(1)}, f32[4,1,1024]{2,1,0:T(1,128)S(1)}, u32[]{:S(2)}, u32[]{:S(2)}) collective-permute-start(f32[4,1,1024]{2,1,0:T(1,128)S(1)} %get-tuple-element.510), channel_id=1, source_target_pairs={{0,4},{4,8},{8,12},{12,16},{16,20},{20,24},{24,28},{28,32},{32,36}... | collective-permute-start | bytes 49160 | tf_op jit(solution)/shard_map/ppermute | solution.py:17
  27.1 65.5 %collective-permute-start.5 = (f32[4,1,1024]{2,1,0:T(1,128)S(1)}, f32[4,1,1024]{2,1,0:T(1,128)S(1)}, u32[]{:S(2)}, u32[]{:S(2)}) collective-permute-start(f32[4,1,1024]{2,1,0:T(1,128)S(1)} %get-tuple-element.511), channel_id=1, source_target_pairs={{4,0},{8,4},{12,8},{16,12},{20,16},{24,20},{28,24},{32,28},{36,32}... | collective-permute-start | bytes 49160 | tf_op jit(solution)/shard_map/ppermute | solution.py:18
  182.0 8.9 collective-permute-start.6
  183.9 8.4 collective-permute-start.7
  280.8 12.5 collective-permute-start.8
  282.7 10.6 collective-permute-start.9
  846.8 8.9 collective-permute-start.10
  848.7 8.4 collective-permute-start.11
  945.8 8.9 collective-permute-start.12
  947.8 8.4 collective-permute-start.13
  1041.7 13.3 copy-start
  1044.7 8.9 collective-permute-start.14
  1046.6 8.4 collective-permute-start.15
  1055.2 8.9 collective-permute-start.16
  1057.1 8.4 collective-permute-start.17
  1065.7 273.5 %copy-start.1 = (f32[4,8,1024]{2,1,0:T(8,128)}, f32[4,8,1024]{2,1,0:T(8,128)S(1)}, u32[]{:S(2)}) copy-start(f32[4,8,1024]{2,1,0:T(8,128)S(1)} %fusion.203) | copy-start | bytes 393220
  1065.7 10.8 collective-permute-start.18
  1067.6 8.9 collective-permute-start.19
where the time goes:
time: 1340 us
  blocking collectives  512 us (38%)
  other arithmetic  430 us (32%)
  local copies, waits for them, and re-layouts  212 us (16%)
  starting transfers between devices  88.8 us (7%)
  loops' own time  64 us (5%)
  between operations  24.8 us (2%)
    unnamed x2, blocking collectives  261 us
    psum x1, blocking collectives, local(): lax.psum((jnp.sum(final_res * final_res, axis=(1, 2)), jnp.sum(heat_forci...  251 us
    scatter-add x5, other arithmetic, restrict(): jax.ops.segment_sum(plane.reshape(-1), flat_ids, num_segments=groups)  237 us
    gather x5, local copies, waits for them, and re-layouts, prolong(): jnp.take(coarse, flat_ids, axis=1)  138 us
    ppermute x10, starting transfers between devices, with_halo(): after = lax.ppermute(initial, axis, down)  69.6 us
    another operation x2, loops' own time, local(): lax.linalg.tridiagonal_solve(lower_band, every_diag, upper_band, every_rhs)  64 us
    sub x3, other arithmetic, local(): lax.linalg.tridiagonal_solve(lower_band, every_diag, upper_band, every_rhs)  60.8 us
    scatter-add x1, other arithmetic, local(): jax.ops.segment_sum((4.0 + extinction_factor - same).reshape(-1), flat_id...  57 us
  transfers between devices with their start and end apart: 20, of which 6 were waited for; matrix products, arithmetic and copies ran while one was open for 5% of the time, Pallas kernels for 0%

commit v1 on v0

v1 whole, which is shorter than its diff:
```python
import functools

import jax
import jax.numpy as jnp
from jax import lax
from jax.experimental import pallas as pl
from jax.experimental.pallas import tpu as pltpu
from jax.sharding import PartitionSpec as P

damping_fine = 0.8
damping_coarse = 0.5
REACH = 7
F32 = jnp.float32


def vmem_call(body, outs, scratch=(), smem_args=(), n_in=0):
    in_specs = [
        pl.BlockSpec(memory_space=pltpu.SMEM if k in smem_args else pltpu.VMEM)
        for k in range(n_in)
    ]
    return pl.pallas_call(
        body,
        out_shape=[jax.ShapeDtypeStruct(s, F32) for s in outs],
        in_specs=in_specs,
        out_specs=[pl.BlockSpec(memory_space=pltpu.VMEM)] * len(outs),
        scratch_shapes=list(scratch),
        compiler_params=pltpu.CompilerParams(vmem_limit_bytes=48 << 20),
    )


def iotas(shape):
    return (
        lax.broadcasted_iota(jnp.int32, shape, 0),
        lax.broadcasted_iota(jnp.int32, shape, 1),
    )


def sideways(x):
    rows, width = x.shape
    col = lax.broadcasted_iota(jnp.int32, x.shape, 1)
    left = jnp.where(col == 0, 0.0, pltpu.roll(x, 1, 1))
    right = jnp.where(col == width - 1, 0.0, pltpu.roll(x, width - 1, 1))
    return left + right


def neighbours(x, above, below):
    rows = x.shape[0]
    row = lax.broadcasted_iota(jnp.int32, x.shape, 0)
    up = jnp.where(row == 0, above, pltpu.roll(x, 1, 0))
    down = jnp.where(row == rows - 1, below, pltpu.roll(x, rows - 1, 0))
    return up + down + sideways(x)


def seg_sum(lab, fields, lab_ref, lab_shift, field_shift, out_ref):
    rows, width = lab.shape
    n = len(fields)
    shifts = list(range(-REACH, REACH + 1))
    for d, dx in enumerate(shifts):
        amount = (-dx) % width
        lab_shift[d] = pltpu.roll(lab, amount, 1) if amount else lab
        for f in range(n):
            field_shift[d, f] = pltpu.roll(fields[f], amount, 1) if amount else fields[f]
    chunk = 256

    def step(j, carry):
        at = pl.ds(pl.multiple_of(j * chunk, chunk), chunk)
        own = lab_ref[:, at]
        sums = [jnp.zeros((rows, chunk), F32) for _ in range(n)]
        for d in range(len(shifts)):
            for r in range(rows):
                there = jnp.broadcast_to(lab_shift[d, pl.ds(r, 1), at], (rows, chunk))
                same = there == own
                for f in range(n):
                    w = jnp.broadcast_to(field_shift[d, f, pl.ds(r, 1), at], (rows, chunk))
                    sums[f] = sums[f] + jnp.where(same, w, 0.0)
        for f in range(n):
            out_ref[f, :, at] = sums[f]
        return carry

    lax.fori_loop(0, width // chunk, step, 0)


def seg_scratch(n, rows, width):
    d = 2 * REACH + 1
    return [
        pltpu.VMEM((d, rows, width), jnp.int32),
        pltpu.VMEM((d, n, rows, width), F32),
        pltpu.VMEM((n, rows, width), F32),
    ]


def pack_kernel(u, f, ext, first, last):
    cases, rows, width = u.shape
    ones = jnp.ones((cases, width), F32)
    for out, order in ((first, (0, 1, 2)), (last, (rows - 1, rows - 2, rows - 3))):
        for k in range(3):
            out[k] = u[:, order[k], :]
        for k in range(2):
            out[3 + k] = f[:, order[k], :]
            out[5 + k] = jnp.broadcast_to(ext[pl.ds(order[k], 1), :], (cases, width))
        out[7] = ones


def both(before, after, k):
    return jnp.concatenate([before[k], after[k]], axis=0)


def two_sweeps(u, u_halo, f, f_halo, diag, diag_halo, valid):
    cases = len(u)
    rows = u[0].shape[0]
    gain = damping_fine / diag
    gain_halo = [damping_fine / d for d in diag_halo]
    keep = 1.0 - damping_fine

    def edge(x):
        return jnp.concatenate(
            [v[0:1] for v in x] + [v[rows - 1 : rows] for v in x], axis=0
        )

    def sweep(x, halo, depth):
        new = [
            keep * x[c]
            + gain * (f[c] + neighbours(x[c], halo[0][c : c + 1], halo[0][cases + c : cases + c + 1]))
            for c in range(cases)
        ]
        inner = [edge(x)] + halo
        new_halo = []
        for k in range(depth):
            v = keep * halo[k] + gain_halo[k] * (
                f_halo[k] + inner[k] + inner[k + 2] + sideways(halo[k])
            )
            new_halo.append(v * valid)
        return new, new_halo

    x, h = sweep(u, u_halo, 2)
    x, h = sweep(x, h, 1)
    res = [
        f[c] - diag * x[c] + neighbours(x[c], h[0][c : c + 1], h[0][cases + c : cases + c + 1])
        for c in range(cases)
    ]
    return x, res


def total(x):
    rows, width = x.shape
    part = x[:, 0:128]
    for k in range(1, width // 128):
        part = part + x[:, k * 128 : (k + 1) * 128]
    return jnp.sum(jnp.sum(part, axis=1, keepdims=True), axis=0, keepdims=True)


def lane_row(values):
    lane = lax.broadcasted_iota(jnp.int32, (1, 128), 1)
    row = jnp.zeros((1, 128), F32)
    for k, v in values:
        row = jnp.where(lane == k, v, row)
    return row


def pre_kernel(u, f, ext, lab, before, after, smooth, b, h, x0, first, last, rsum, ls, fs, ss):
    cases, rows, width = u.shape
    diag = 4.0 + ext[...]
    us = [u[c] for c in range(cases)]
    fl = [f[c] for c in range(cases)]
    u_halo = [both(before, after, k) for k in range(3)]
    f_halo = [both(before, after, 3 + k) for k in range(2)]
    d_halo = [4.0 + both(before, after, 5 + k) for k in range(2)]
    valid = both(before, after, 7)
    x, res = two_sweeps(us, u_halo, fl, f_halo, diag, d_halo, valid)
    for c in range(cases):
        smooth[c] = x[c]
    key = lab[...]
    row, col = iotas(key.shape)
    one = jnp.ones(key.shape, F32)
    zero = jnp.zeros(key.shape, F32)
    m = jnp.where((pltpu.roll(key, 1, 0) == key) & (row > 0), one, zero)
    m = m + jnp.where((pltpu.roll(key, rows - 1, 0) == key) & (row < rows - 1), one, zero)
    m = m + jnp.where((pltpu.roll(key, 1, 1) == key) & (col > 0), one, zero)
    m = m + jnp.where((pltpu.roll(key, width - 1, 1) == key) & (col < width - 1), one, zero)
    seg_sum(key, res + [diag - m], lab, ls, fs, ss)
    half = damping_coarse / ss[cases]
    h[...] = half
    for c in range(cases):
        b[c] = ss[c]
        v = half * ss[c]
        x0[c] = v
        first[pl.ds(c, 1), :] = v[0:1]
        last[pl.ds(c, 1), :] = v[rows - 1 : rows]
    rsum[...] = lane_row([(c, total(res[c])) for c in range(cases)])


def coarse_step(x, above, below, ext, lab, b, h, ls, fs, ss):
    cases = len(x)
    diag = 4.0 + ext[...]
    w = [
        diag * x[c] - neighbours(x[c], above[c], below[c])
        for c in range(cases)
    ]
    seg_sum(lab[...], w, lab, ls, fs, ss)
    return [x[c] + h[...] * (b[c] - ss[c]) for c in range(cases)]


def store_edges(x, first, last):
    rows = x[0].shape[0]
    for c in range(len(x)):
        first[pl.ds(c, 1), :] = x[c][0:1]
        last[pl.ds(c, 1), :] = x[c][rows - 1 : rows]


def coarse_kernel_a(x0, ext, lab, b, h, rsum, before, after, x1, first, last, gather, ls, fs, ss):
    cases, rows, width = x0.shape
    x = coarse_step(
        [x0[c] for c in range(cases)],
        [before[pl.ds(c, 1), :] for c in range(cases)],
        [after[pl.ds(c, 1), :] for c in range(cases)],
        ext, lab, b, h, ls, fs, ss,
    )
    store_edges(x, first, last)
    row, col = iotas((rows, width))
    one = jnp.ones((rows, width), F32)
    zero = jnp.zeros((rows, width), F32)
    weight = ext[...]
    for at_edge in (row == 0, row == rows - 1, col == 0, col == width - 1):
        weight = weight + jnp.where(at_edge, one, zero)
    values = []
    for c in range(cases):
        x1[c] = x[c]
        own = rsum[:, c : c + 1] - total(weight * x[c])
        values.append((c, own))
        values.append((cases + c, total(x[c][0:1])))
        values.append((2 * cases + c, total(x[c][rows - 1 : rows])))
    values.append((3 * cases, total(ext[...])))
    gather[...] = jnp.broadcast_to(lane_row(values), gather.shape)


def solve_slabs(g, cases, groups, cells):
    n = g.shape[0]
    row, lane = iotas(g.shape)
    top = pltpu.roll(pltpu.roll(g, 128 - cases, 1), n - 1, 0)
    bottom = pltpu.roll(pltpu.roll(g, 128 - 2 * cases, 1), 1, 0)
    b = g + jnp.where(row == n - 1, 0.0, top) + jnp.where(row == 0, 0.0, bottom)
    b = jnp.where(lane < cases, b / (groups * float(n)), 0.0)
    mean = jnp.broadcast_to(g[:, 3 * cases : 3 * cases + 1], g.shape) / float(cells)
    d = 2.0 + mean / (float(n) * float(n))
    lower = jnp.where(row == 0, 0.0, 1.0)
    upper = jnp.where(row == n - 1, 0.0, 1.0)
    excess = (d - lower) - upper
    s = 1
    while s < n:
        inv = 1.0 / (lower + upper + excess)
        alpha = lower * pltpu.roll(inv, s, 0)
        gamma = upper * pltpu.roll(inv, n - s, 0)
        b = b + alpha * pltpu.roll(b, s, 0) + gamma * pltpu.roll(b, n - s, 0)
        excess = excess + alpha * pltpu.roll(excess, s, 0) + gamma * pltpu.roll(excess, n - s, 0)
        lower = alpha * pltpu.roll(lower, s, 0)
        upper = gamma * pltpu.roll(upper, n - s, 0)
        s *= 2
    return b / (lower + upper + excess)


def coarse_kernel_b(groups, at, x1, ext, lab, b, h, before, after, gathered, x3, first, last, ls, fs, ss, e_ref):
    cases, rows, width = x1.shape
    n = gathered.shape[0]
    i = at[0]
    e_ref[pl.ds(8, n), :] = solve_slabs(gathered[...], cases, groups, rows * width)
    e_ref[pl.ds(0, 8), :] = jnp.zeros((8, 128), F32)
    e_ref[pl.ds(8 + n, 8), :] = jnp.zeros((8, 128), F32)
    e_above = e_ref[pl.ds(i + 7, 1), :]
    e_own = e_ref[pl.ds(i + 8, 1), :]
    e_below = e_ref[pl.ds(i + 9, 1), :]
    x = coarse_step(
        [x1[c] + e_own[:, c : c + 1] for c in range(cases)],
        [before[pl.ds(c, 1), :] + e_above[:, c : c + 1] for c in range(cases)],
        [after[pl.ds(c, 1), :] + e_below[:, c : c + 1] for c in range(cases)],
        ext, lab, b, h, ls, fs, ss,
    )
    store_edges(x, first, last)
    for c in range(cases):
        x3[c] = x[c]


def coarse_kernel_c(x3, ext, lab, b, h, smooth, before, after, v, first, last, ls, fs, ss):
    cases, rows, width = x3.shape
    x = coarse_step(
        [x3[c] for c in range(cases)],
        [before[pl.ds(c, 1), :] for c in range(cases)],
        [after[pl.ds(c, 1), :] for c in range(cases)],
        ext, lab, b, h, ls, fs, ss,
    )
    for c in range(cases):
        y = smooth[c] + x[c]
        v[c] = y
        for k in range(3):
            first[k, pl.ds(c, 1), :] = y[k : k + 1]
            last[k, pl.ds(c, 1), :] = y[rows - 1 - k : rows - k]


def post_kernel(v, f, ext, before, after, before_v, after_v, out, gather):
    cases, rows, width = v.shape
    diag = 4.0 + ext[...]
    fl = [f[c] for c in range(cases)]
    v_halo = [both(before_v, after_v, k) for k in range(3)]
    f_halo = [both(before, after, 3 + k) for k in range(2)]
    d_halo = [4.0 + both(before, after, 5 + k) for k in range(2)]
    valid = both(before, after, 7)
    x, res = two_sweeps([v[c] for c in range(cases)], v_halo, fl, f_halo, diag, d_halo, valid)
    values = []
    for c in range(cases):
        out[c] = x[c]
        values.append((c, total(res[c] * res[c])))
        values.append((cases + c, total(fl[c] * fl[c])))
    gather[...] = jnp.broadcast_to(lane_row(values), gather.shape)


def ratio_kernel(cases, g, out):
    s = jnp.sum(g[...], axis=0, keepdims=True)
    ratio = jnp.sqrt(s / pltpu.roll(s, 128 - cases, 1))
    lane = lax.broadcasted_iota(jnp.int32, s.shape, 1)
    out[...] = jnp.broadcast_to(jnp.where(lane < cases, ratio, 0.0), out.shape)


def local(thermal_solution, heat_forcing, extinction_factor, cluster_label):
    cases, rows, width = thermal_solution.shape
    n = lax.axis_size("blk")
    n_rhs = lax.axis_size("rhs")
    groups = rows * width // 16
    field = (cases, rows, width)
    up = [(i, i + 1) for i in range(n - 1)]
    down = [(j, i) for i, j in up]

    def exchange(first, last):
        return lax.ppermute(last, "blk", up), lax.ppermute(first, "blk", down)

    def to_all(x, axis):
        return lax.all_to_all(x, axis, 0, 0, tiled=True)

    seg4 = seg_scratch(cases, rows, width)
    edge = (cases, width)
    u, f, ext, lab = thermal_solution, heat_forcing, extinction_factor, cluster_label
    first, last = vmem_call(pack_kernel, [(8, cases, width)] * 2, n_in=3)(u, f, ext)
    before, after = exchange(first, last)
    smooth, b, h, x0, first, last, rsum = vmem_call(
        pre_kernel,
        [field, field, (rows, width), field, edge, edge, (1, 128)],
        seg_scratch(cases + 1, rows, width),
        n_in=6,
    )(u, f, ext, lab, before, after)
    ab, be = exchange(first, last)
    x1, first, last, mine = vmem_call(
        coarse_kernel_a, [field, edge, edge, (n, 128)], seg4, n_in=8
    )(x0, ext, lab, b, h, rsum, ab, be)
    ab, be = exchange(first, last)
    gathered = to_all(mine, "blk")
    at = lax.axis_index("blk").astype(jnp.int32).reshape(1)
    x3, first, last = vmem_call(
        functools.partial(coarse_kernel_b, groups),
        [field, edge, edge],
        seg4 + [pltpu.VMEM((n + 16, 128), F32)],
        smem_args=(0,),
        n_in=9,
    )(at, x1, ext, lab, b, h, ab, be, gathered)
    ab, be = exchange(first, last)
    v, first, last = vmem_call(
        coarse_kernel_c, [field, (3, cases, width), (3, cases, width)], seg4, n_in=8
    )(x3, ext, lab, b, h, smooth, ab, be)
    ab, be = exchange(first, last)
    corrected, mine = vmem_call(post_kernel, [field, (n, 128)], n_in=7)(
        v, f, ext, before, after, ab, be
    )
    gathered = to_all(mine, "blk")
    (ratio,) = vmem_call(
        functools.partial(ratio_kernel, cases), [(n_rhs, 128)], n_in=1
    )(gathered)
    every = to_all(ratio, "rhs")
    return corrected, every[:, :cases].reshape(n_rhs * cases)


def solution(mesh):
    in_specs = (P("rhs", "blk", None), P("rhs", "blk", None), P("blk", None), P("blk", None))
    out_specs = (P("rhs", "blk", None), P())
    return jax.shard_map(local, mesh=mesh, in_specs=in_specs, out_specs=out_specs, check_vma=False)
```

time: 1340 us -> 120 us (0.09)
  the two profiles are of different devices: /device:TPU:256 before, /device:TPU:1 now
where the time goes in v1:
time: 120 us; the launch traced here: 119 us
  starting transfers between devices  48.3 us (40%)
  blocking collectives  35 us (29%)
  Pallas kernels  16.4 us (14%)
  waiting for transfers between devices  15.6 us (13%)
  local copies, waits for them, and re-layouts  3.16 us (3%)
    all_to_all x2, blocking collectives, to_all(): return lax.all_to_all(x, axis, 0, 0, tiled=True)  35 us
    ppermute x10, starting transfers between devices, exchange(): return (lax.ppermute(last, 'blk', up), lax.ppermute(first, 'blk', down))  29 us
    all_to_all x1, starting transfers between devices, to_all(): return lax.all_to_all(x, axis, 0, 0, tiled=True)  19.3 us
    ppermute x10, waiting for transfers between devices, exchange(): return (lax.ppermute(last, 'blk', up), lax.ppermute(first, 'blk', down))  13.1 us
    pallas_call x1, Pallas kernels, local(): vmem_call(pre_kernel, [field, field, (rows, width), field, edge, edge, (1...  4.11 us
    pallas_call x1, Pallas kernels, local(): vmem_call(coarse_kernel_a, [field, edge, edge, (n, 128)], seg4, n_in=8)  4.08 us
    pallas_call x1, Pallas kernels, local(): vmem_call(functools.partial(coarse_kernel_b, groups), [field, edge, edge]...  3.77 us
    pallas_call x1, Pallas kernels, local(): vmem_call(coarse_kernel_c, [field, (3, cases, width), (3, cases, width)],...  3.28 us
  transfers between devices with their start and end apart: 11, of which 6 were waited for; matrix products, arithmetic and copies ran while one was open for 0% of the time, Pallas kernels for 0%

profile of v1, /device:TPU:1, one launch (start us, length us, event | category | flops | bytes accessed | tf_op | source)
XLA Modules:
  0.0 119.3 jit_solution(5673987380316630897)
XLA Ops:
  0.6 0.0 copy-start
  0.6 0.7 copy-done
  1.4 0.0 copy-start.2
  1.4 0.9 copy-done.2
  2.3 0.0 copy-start.5
  2.3 0.9 copy-done.5
  3.2 0.0 copy-start.4
  3.3 4.6 %collective-permute-start = (f32[8,4,1024]{2,1,0:T(4,128)S(1)}, f32[8,4,1024]{2,1,0:T(4,128)S(1)}, u32[]{:S(2)}, u32[]{:S(2)}) collective-permute-start(f32[8,4,1024]{2,1,0:T(4,128)S(1)} %get-tuple-element.23), channel_id=1, source_target_pairs={{0,4},{4,8},{8,12},{12,16},{16,20},{20,24},{24,28},{28,32},{32,36}... | collective-permute-start | bytes 393224 | tf_op jit(solution)/shard_map/ppermute | solution.py:332
  7.9 5.5 %collective-permute-start.1 = (f32[8,4,1024]{2,1,0:T(4,128)S(1)}, f32[8,4,1024]{2,1,0:T(4,128)S(1)}, u32[]{:S(2)}, u32[]{:S(2)}) collective-permute-start(f32[8,4,1024]{2,1,0:T(4,128)S(1)} %get-tuple-element.24), channel_id=1, source_target_pairs={{4,0},{8,4},{12,8},{16,12},{20,16},{24,20},{28,24},{32,28},{36,32}... | collective-permute-start | bytes 393224 | tf_op jit(solution)/shard_map/ppermute | solution.py:332
  13.4 0.0 collective-permute-done.before
  13.4 1.0 collective-permute-done.1.after
  14.3 0.0 copy-done.4
  14.3 0.0 copy-start.1
  14.3 4.1 %shard_map.60 = (f32[4,8,1024]{2,1,0:T(8,128)S(1)}, f32[4,8,1024]{2,1,0:T(8,128)S(1)}, f32[8,1024]{1,0:T(8,128)S(1)}, f32[4,8,1024]{2,1,0:T(8,128)S(1)}, f32[4,1...) custom-call(f32[4,8,1024]{2,1,0:T(8,128)S(1)} %copy-done.5, f32[4,8,1024]{2,1,0:T(8,128)S(1)} %copy-done.2, ...), custom_call_target="tpu_custom_call" | custom-call | tf_op jit(solution)/shard_map/pallas_call | solution.py:342
  18.4 1.9 %collective-permute-start.2 = (f32[4,1024]{1,0:T(4,128)S(1)}, f32[4,1024]{1,0:T(4,128)S(1)}, u32[]{:S(2)}, u32[]{:S(2)}) collective-permute-start(f32[4,1024]{1,0:T(4,128)S(1)} %get-tuple-element.29), channel_id=1, source_target_pairs={{0,4},{4,8},{8,12},{12,16},{16,20},{20,24},{24,28},{28,32},{32,36}... | collective-permute-start | bytes 49160 | tf_op jit(solution)/shard_map/ppermute | solution.py:332
  20.4 2.4 %collective-permute-start.3 = (f32[4,1024]{1,0:T(4,128)S(1)}, f32[4,1024]{1,0:T(4,128)S(1)}, u32[]{:S(2)}, u32[]{:S(2)}) collective-permute-start(f32[4,1024]{1,0:T(4,128)S(1)} %get-tuple-element.30), channel_id=1, source_target_pairs={{4,0},{8,4},{12,8},{16,12},{20,16},{24,20},{28,24},{32,28},{36,32}... | collective-permute-start | bytes 49160 | tf_op jit(solution)/shard_map/ppermute | solution.py:332
  22.8 0.0 collective-permute-done.2.before
  22.8 2.6 %collective-permute-done.3.after = f32[4,1024]{1,0:T(4,128)S(1)} collective-permute-done((f32[4,1024]{1,0:T(4,128)S(1)}, f32[4,1024]{1,0:T(4,128)S(1)}, u32[]{:S(2)}, u32[]{:S(2)}) %collective-permute-start.3) | collective-permute-done | bytes 16416 | tf_op jit(solution)/shard_map/ppermute | solution.py:332
  25.4 0.0 copy-done.1
  25.4 4.1 %shard_map.61 = (f32[4,8,1024]{2,1,0:T(8,128)S(1)}, f32[4,1024]{1,0:T(4,128)S(1)}, f32[4,1024]{1,0:T(4,128)S(1)}, f32[128,128]{1,0:T(8,128)}) custom-call(f32[4,8,1024]{2,1,0:T(8,128)S(1)} %get-tuple-element.25.x0, f32[8,1024]{1,0:T(8,128)S(1)} %copy-done.1, s32[8,1024]{1,0:T(8,128)S(1)} %copy-done.4, f32[4,8,1024]{2,1,0:T(8,128)S(1)} %get-tuple-element.26.b, ...), custom_call_target="tpu_custom_call" | custom-call | tf_op jit(solution)/shard_map/pallas_call | solution.py:349
  29.5 19.3 %all-to-all-start = ((f32[128,1,128]{2,1,0:T(1,128)}), f32[128,1,128]{2,1,0:T(1,128)S(1)}, u32[]{:S(2)}, u32[]{:S(2)}) async-start(f32[128,1,128]{2,1,0:T(1,128)} %bitcast.2), calls=%async_computation | async-start | bytes 131072 | tf_op jit(solution)/shard_map/all_to_all | solution.py:335
  48.8 3.5 %collective-permute-start.4 = (f32[4,1024]{1,0:T(4,128)S(1)}, f32[4,1024]{1,0:T(4,128)S(1)}, u32[]{:S(2)}, u32[]{:S(2)}) collective-permute-start(f32[4,1024]{1,0:T(4,128)S(1)} %get-tuple-element.32), channel_id=1, source_target_pairs={{0,4},{4,8},{8,12},{12,16},{16,20},{20,24},{24,28},{28,32},{32,36}... | collective-permute-start | bytes 49160 | tf_op jit(solution)/shard_map/ppermute | solution.py:332
  52.4 1.9 %collective-permute-start.5 = (f32[4,1024]{1,0:T(4,128)S(1)}, f32[4,1024]{1,0:T(4,128)S(1)}, u32[]{:S(2)}, u32[]{:S(2)}) collective-permute-start(f32[4,1024]{1,0:T(4,128)S(1)} %get-tuple-element.33), channel_id=1, source_target_pairs={{4,0},{8,4},{12,8},{16,12},{20,16},{24,20},{28,24},{32,28},{36,32}... | collective-permute-start | bytes 49160 | tf_op jit(solution)/shard_map/ppermute | solution.py:332
  54.3 0.0 collective-permute-done.4.before
  54.3 3.4 %collective-permute-done.5.after = f32[4,1024]{1,0:T(4,128)S(1)} collective-permute-done((f32[4,1024]{1,0:T(4,128)S(1)}, f32[4,1024]{1,0:T(4,128)S(1)}, u32[]{:S(2)}, u32[]{:S(2)}) %collective-permute-start.5) | collective-permute-done | bytes 16416 | tf_op jit(solution)/shard_map/ppermute | solution.py:332
  57.7 2.5 %all-to-all-done = f32[128,1,128]{2,1,0:T(1,128)S(1)} async-done(((f32[128,1,128]{2,1,0:T(1,128)}), f32[128,1,128]{2,1,0:T(1,128)S(1)}, u32[]{:S(2)}, u32[]{:S(2)}) %all-to-all-start) | async-done | bytes 65568 | tf_op jit(solution)/shard_map/all_to_all | solution.py:335
  60.2 3.8 %shard_map.62 = (f32[4,8,1024]{2,1,0:T(8,128)S(1)}, f32[4,1024]{1,0:T(4,128)S(1)}, f32[4,1024]{1,0:T(4,128)S(1)}) custom-call(s32[1]{0:T(128)} %bitcast.at, f32[4,8,1024]{2,1,0:T(8,128)S(1)} %get-tuple-element.31.x1, f32[8,1024]{1,0:T(8,128)S(1)} %copy-done.1, s32[8,1024]{1,0:T(8,128)S(1)} %copy-done.4, f32[4,8,1024]{2,1,0:T(8,128)S(1)} %get-tuple-element.26.b, ...), custom_call_target="tpu_custom_call" | custom-call | tf_op jit(solution)/shard_map/pallas_call | solution.py:355
  64.0 2.9 %collective-permute-start.6 = (f32[4,1024]{1,0:T(4,128)S(1)}, f32[4,1024]{1,0:T(4,128)S(1)}, u32[]{:S(2)}, u32[]{:S(2)}) collective-permute-start(f32[4,1024]{1,0:T(4,128)S(1)} %get-tuple-element.37), channel_id=1, source_target_pairs={{0,4},{4,8},{8,12},{12,16},{16,20},{20,24},{24,28},{28,32},{32,36}... | collective-permute-start | bytes 49160 | tf_op jit(solution)/shard_map/ppermute | solution.py:332
  66.9 1.9 %collective-permute-start.7 = (f32[4,1024]{1,0:T(4,128)S(1)}, f32[4,1024]{1,0:T(4,128)S(1)}, u32[]{:S(2)}, u32[]{:S(2)}) collective-permute-start(f32[4,1024]{1,0:T(4,128)S(1)} %get-tuple-element.38), channel_id=1, source_target_pairs={{4,0},{8,4},{12,8},{16,12},{20,16},{24,20},{28,24},{32,28},{36,32}... | collective-permute-start | bytes 49160 | tf_op jit(solution)/shard_map/ppermute | solution.py:332
  68.8 0.0 collective-permute-done.6.before
  68.8 3.1 %collective-permute-done.7.after = f32[4,1024]{1,0:T(4,128)S(1)} collective-permute-done((f32[4,1024]{1,0:T(4,128)S(1)}, f32[4,1024]{1,0:T(4,128)S(1)}, u32[]{:S(2)}, u32[]{:S(2)}) %collective-permute-start.7) | collective-permute-done | bytes 16416 | tf_op jit(solution)/shard_map/ppermute | solution.py:332
  71.9 0.0 copy-start.3
  72.0 3.3 %shard_map.63 = (f32[4,8,1024]{2,1,0:T(8,128)S(1)}, f32[3,4,1024]{2,1,0:T(4,128)S(1)}, f32[3,4,1024]{2,1,0:T(4,128)S(1)}) custom-call(f32[4,8,1024]{2,1,0:T(8,128)S(1)} %get-tuple-element.35.x3, f32[8,1024]{1,0:T(8,128)S(1)} %copy-done.1, s32[8,1024]{1,0:T(8,128)S(1)} %copy-done.4, f32[4,8,1024]{2,1,0:T(8,128)S(1)} %get-tuple-element.26.b, ...), custom_call_target="tpu_custom_call" | custom-call | tf_op jit(solution)/shard_map/pallas_call | solution.py:363
  75.2 1.9 %collective-permute-start.8 = (f32[3,4,1024]{2,1,0:T(4,128)S(1)}, f32[3,4,1024]{2,1,0:T(4,128)S(1)}, u32[]{:S(2)}, u32[]{:S(2)}) collective-permute-start(f32[3,4,1024]{2,1,0:T(4,128)S(1)} %get-tuple-element.40), channel_id=1, source_target_pairs={{0,4},{4,8},{8,12},{12,16},{16,20},{20,24},{24,28},{28,32},{32,36}... | collective-permute-start | bytes 147464 | tf_op jit(solution)/shard_map/ppermute | solution.py:332
  77.2 2.4 %collective-permute-start.9 = (f32[3,4,1024]{2,1,0:T(4,128)S(1)}, f32[3,4,1024]{2,1,0:T(4,128)S(1)}, u32[]{:S(2)}, u32[]{:S(2)}) collective-permute-start(f32[3,4,1024]{2,1,0:T(4,128)S(1)} %get-tuple-element.41), channel_id=1, source_target_pairs={{4,0},{8,4},{12,8},{16,12},{20,16},{24,20},{28,24},{32,28},{36,32}... | collective-permute-start | bytes 147464 | tf_op jit(solution)/shard_map/ppermute | solution.py:332
  79.6 0.0 collective-permute-done.8.before_v
  79.6 3.0 %collective-permute-done.9.after_v = f32[3,4,1024]{2,1,0:T(4,128)S(1)} collective-permute-done((f32[3,4,1024]{2,1,0:T(4,128)S(1)}, f32[3,4,1024]{2,1,0:T(4,128)S(1)}, u32[]{:S(2)}, u32[]{:S(2)}) %collective-permute-start.9) | collective-permute-done | bytes 49184 | tf_op jit(solution)/shard_map/ppermute | solution.py:332
  82.6 0.0 copy-done.3
  82.6 1.0 shard_map.64
  83.6 27.1 %all_to_all.34 = f32[128,1,128]{2,1,0:T(1,128)S(1)} all-to-all(f32[128,1,128]{2,1,0:T(1,128)S(1)} %bitcast.16), channel_id=1, replica_groups=mesh['blk'=128,'rhs'=4] {'blk'}, dimensions={0} | all-to-all | bytes 131072 | tf_op jit(solution)/shard_map/all_to_all | solution.py:335
  110.7 0.1 shard_map.65
  110.8 7.9 %all_to_all.35 = f32[4,1,128]{2,1,0:T(1,128)S(1)} all-to-all(f32[4,1,128]{2,1,0:T(1,128)S(1)} %bitcast.17), channel_id=1, replica_groups=mesh['blk'=128,'rhs'=4] {'rhs'}, dimensions={0} | all-to-all | bytes 4096 | tf_op jit(solution)/shard_map/all_to_all | solution.py:335
  118.7 0.6 reshape.17
  (1 shorter events, 0.0 us)
Async XLA Ops:
  0.6 0.8 copy-start
  1.4 0.9 copy-start.2
  2.3 0.9 copy-start.5
  3.2 11.1 %copy-start.4 = (s32[8,1024]{1,0:T(8,128)S(1)}, s32[8,1024]{1,0:T(8,128)}, u32[]{:S(2)}) copy-start(s32[8,1024]{1,0:T(8,128)} %lab.7) | copy-start | bytes 98308
  3.3 10.1 %collective-permute-start = (f32[8,4,1024]{2,1,0:T(4,128)S(1)}, f32[8,4,1024]{2,1,0:T(4,128)S(1)}, u32[]{:S(2)}, u32[]{:S(2)}) collective-permute-start(f32[8,4,1024]{2,1,0:T(4,128)S(1)} %get-tuple-element.23), channel_id=1, source_target_pairs={{0,4},{4,8},{8,12},{12,16},{16,20},{20,24},{24,28},{28,32},{32,36}... | collective-permute-start | bytes 393224 | tf_op jit(solution)/shard_map/ppermute | solution.py:332
  7.9 6.5 %collective-permute-start.1 = (f32[8,4,1024]{2,1,0:T(4,128)S(1)}, f32[8,4,1024]{2,1,0:T(4,128)S(1)}, u32[]{:S(2)}, u32[]{:S(2)}) collective-permute-start(f32[8,4,1024]{2,1,0:T(4,128)S(1)} %get-tuple-element.24), channel_id=1, source_target_pairs={{4,0},{8,4},{12,8},{16,12},{20,16},{24,20},{28,24},{32,28},{36,32}... | collective-permute-start | bytes 393224 | tf_op jit(solution)/shard_map/ppermute | solution.py:332
  14.3 11.1 %copy-start.1 = (f32[8,1024]{1,0:T(8,128)S(1)}, f32[8,1024]{1,0:T(8,128)}, u32[]{:S(2)}) copy-start(f32[8,1024]{1,0:T(8,128)} %ext.11) | copy-start | bytes 98308
  18.4 4.3 %collective-permute-start.2 = (f32[4,1024]{1,0:T(4,128)S(1)}, f32[4,1024]{1,0:T(4,128)S(1)}, u32[]{:S(2)}, u32[]{:S(2)}) collective-permute-start(f32[4,1024]{1,0:T(4,128)S(1)} %get-tuple-element.29), channel_id=1, source_target_pairs={{0,4},{4,8},{8,12},{12,16},{16,20},{20,24},{24,28},{28,32},{32,36}... | collective-permute-start | bytes 49160 | tf_op jit(solution)/shard_map/ppermute | solution.py:332
  20.4 5.1 %collective-permute-start.3 = (f32[4,1024]{1,0:T(4,128)S(1)}, f32[4,1024]{1,0:T(4,128)S(1)}, u32[]{:S(2)}, u32[]{:S(2)}) collective-permute-start(f32[4,1024]{1,0:T(4,128)S(1)} %get-tuple-element.30), channel_id=1, source_target_pairs={{4,0},{8,4},{12,8},{16,12},{20,16},{24,20},{28,24},{32,28},{36,32}... | collective-permute-start | bytes 49160 | tf_op jit(solution)/shard_map/ppermute | solution.py:332
  29.5 30.7 %all-to-all-start = ((f32[128,1,128]{2,1,0:T(1,128)}), f32[128,1,128]{2,1,0:T(1,128)S(1)}, u32[]{:S(2)}, u32[]{:S(2)}) async-start(f32[128,1,128]{2,1,0:T(1,128)} %bitcast.2), calls=%async_computation | async-start | bytes 131072 | tf_op jit(solution)/shard_map/all_to_all | solution.py:335
  48.8 5.5 %collective-permute-start.4 = (f32[4,1024]{1,0:T(4,128)S(1)}, f32[4,1024]{1,0:T(4,128)S(1)}, u32[]{:S(2)}, u32[]{:S(2)}) collective-permute-start(f32[4,1024]{1,0:T(4,128)S(1)} %get-tuple-element.32), channel_id=1, source_target_pairs={{0,4},{4,8},{8,12},{12,16},{16,20},{20,24},{24,28},{28,32},{32,36}... | collective-permute-start | bytes 49160 | tf_op jit(solution)/shard_map/ppermute | solution.py:332
  52.4 5.4 %collective-permute-start.5 = (f32[4,1024]{1,0:T(4,128)S(1)}, f32[4,1024]{1,0:T(4,128)S(1)}, u32[]{:S(2)}, u32[]{:S(2)}) collective-permute-start(f32[4,1024]{1,0:T(4,128)S(1)} %get-tuple-element.33), channel_id=1, source_target_pairs={{4,0},{8,4},{12,8},{16,12},{20,16},{24,20},{28,24},{32,28},{36,32}... | collective-permute-start | bytes 49160 | tf_op jit(solution)/shard_map/ppermute | solution.py:332
  64.0 4.8 %collective-permute-start.6 = (f32[4,1024]{1,0:T(4,128)S(1)}, f32[4,1024]{1,0:T(4,128)S(1)}, u32[]{:S(2)}, u32[]{:S(2)}) collective-permute-start(f32[4,1024]{1,0:T(4,128)S(1)} %get-tuple-element.37), channel_id=1, source_target_pairs={{0,4},{4,8},{8,12},{12,16},{16,20},{20,24},{24,28},{28,32},{32,36}... | collective-permute-start | bytes 49160 | tf_op jit(solution)/shard_map/ppermute | solution.py:332
  66.9 5.1 %collective-permute-start.7 = (f32[4,1024]{1,0:T(4,128)S(1)}, f32[4,1024]{1,0:T(4,128)S(1)}, u32[]{:S(2)}, u32[]{:S(2)}) collective-permute-start(f32[4,1024]{1,0:T(4,128)S(1)} %get-tuple-element.38), channel_id=1, source_target_pairs={{4,0},{8,4},{12,8},{16,12},{20,16},{24,20},{28,24},{32,28},{36,32}... | collective-permute-start | bytes 49160 | tf_op jit(solution)/shard_map/ppermute | solution.py:332
  71.9 10.6 %copy-start.3 = (f32[4,8,1024]{2,1,0:T(8,128)S(1)}, f32[4,8,1024]{2,1,0:T(8,128)}, u32[]{:S(2)}) copy-start(f32[4,8,1024]{2,1,0:T(8,128)} %f.5) | copy-start | bytes 393220
  75.2 4.3 %collective-permute-start.8 = (f32[3,4,1024]{2,1,0:T(4,128)S(1)}, f32[3,4,1024]{2,1,0:T(4,128)S(1)}, u32[]{:S(2)}, u32[]{:S(2)}) collective-permute-start(f32[3,4,1024]{2,1,0:T(4,128)S(1)} %get-tuple-element.40), channel_id=1, source_target_pairs={{0,4},{4,8},{8,12},{12,16},{16,20},{20,24},{24,28},{28,32},{32,36}... | collective-permute-start | bytes 147464 | tf_op jit(solution)/shard_map/ppermute | solution.py:332
  77.2 5.4 %collective-permute-start.9 = (f32[3,4,1024]{2,1,0:T(4,128)S(1)}, f32[3,4,1024]{2,1,0:T(4,128)S(1)}, u32[]{:S(2)}, u32[]{:S(2)}) collective-permute-start(f32[3,4,1024]{2,1,0:T(4,128)S(1)} %get-tuple-element.41), channel_id=1, source_target_pairs={{4,0},{8,4},{12,8},{16,12},{20,16},{24,20},{28,24},{32,28},{36,32}... | collective-permute-start | bytes 147464 | tf_op jit(solution)/shard_map/ppermute | solution.py:332

commit v2 on v1

--- a/solution.py
+++ b/solution.py
@@ -20,7 +20,9 @@
     ]
     return pl.pallas_call(
         body,
-        out_shape=[jax.ShapeDtypeStruct(s, F32) for s in outs],
+        out_shape=[
+            jax.ShapeDtypeStruct(*(s if isinstance(s[0], tuple) else (s, F32))) for s in outs
+        ],
         in_specs=in_specs,
         out_specs=[pl.BlockSpec(memory_space=pltpu.VMEM)] * len(outs),
         scratch_shapes=list(scratch),
@@ -51,42 +53,52 @@
     return up + down + sideways(x)
 
 
-def seg_sum(lab, fields, lab_ref, lab_shift, field_shift, out_ref):
-    rows, width = lab.shape
-    n = len(fields)
-    shifts = list(range(-REACH, REACH + 1))
-    for d, dx in enumerate(shifts):
-        amount = (-dx) % width
-        lab_shift[d] = pltpu.roll(lab, amount, 1) if amount else lab
-        for f in range(n):
-            field_shift[d, f] = pltpu.roll(fields[f], amount, 1) if amount else fields[f]
-    chunk = 256
-
-    def step(j, carry):
-        at = pl.ds(pl.multiple_of(j * chunk, chunk), chunk)
-        own = lab_ref[:, at]
-        sums = [jnp.zeros((rows, chunk), F32) for _ in range(n)]
-        for d in range(len(shifts)):
-            for r in range(rows):
-                there = jnp.broadcast_to(lab_shift[d, pl.ds(r, 1), at], (rows, chunk))
-                same = there == own
-                for f in range(n):
-                    w = jnp.broadcast_to(field_shift[d, f, pl.ds(r, 1), at], (rows, chunk))
-                    sums[f] = sums[f] + jnp.where(same, w, 0.0)
-        for f in range(n):
-            out_ref[f, :, at] = sums[f]
-        return carry
-
-    lax.fori_loop(0, width // chunk, step, 0)
-
-
-def seg_scratch(n, rows, width):
-    d = 2 * REACH + 1
-    return [
-        pltpu.VMEM((d, rows, width), jnp.int32),
-        pltpu.VMEM((d, n, rows, width), F32),
-        pltpu.VMEM((n, rows, width), F32),
-    ]
+def offsets():
+    return [d for d in range(-REACH, REACH + 1) if d]
+
+
+def seg_sum(fields, tables):
+    row_at, row_ok, same_col = tables
+    rows, width = fields[0].shape
+    col = list(fields)
+    for k in range(1, rows):
+        m = same_col[k - 1]
+        col = [s + m * pltpu.roll(w, k, 0) for s, w in zip(col, fields)]
+    out = list(col)
+    for d, dx in enumerate(offsets()):
+        at, ok = row_at[d], row_ok[d]
+        out = [
+            t
+            + ok
+            * jnp.take_along_axis(
+                pltpu.roll(s, (-dx) % width, 1), at, axis=0, mode="promise_in_bounds"
+            )
+            for t, s in zip(out, col)
+        ]
+    return out
+
+
+def table_kernel(ext, lab, row_at, row_ok, same_col, h):
+    key = lab[...]
+    rows, width = key.shape
+    for k in range(1, rows):
+        same_col[k - 1] = jnp.where(pltpu.roll(key, k, 0) == key, 1.0, 0.0)
+    for d, dx in enumerate(offsets()):
+        there = pltpu.roll(key, (-dx) % width, 1)
+        at = jnp.full(key.shape, -1, jnp.int32)
+        for r in range(rows):
+            at = jnp.where(jnp.broadcast_to(there[r : r + 1], key.shape) == key, r, at)
+        row_ok[d] = jnp.where(at >= 0, 1.0, 0.0)
+        row_at[d] = jnp.maximum(at, 0)
+    row, col = iotas(key.shape)
+    one = jnp.ones(key.shape, F32)
+    zero = jnp.zeros(key.shape, F32)
+    m = jnp.where((pltpu.roll(key, 1, 0) == key) & (row > 0), one, zero)
+    m = m + jnp.where((pltpu.roll(key, rows - 1, 0) == key) & (row < rows - 1), one, zero)
+    m = m + jnp.where((pltpu.roll(key, 1, 1) == key) & (col > 0), one, zero)
+    m = m + jnp.where((pltpu.roll(key, width - 1, 1) == key) & (col < width - 1), one, zero)
+    (diag1,) = seg_sum([4.0 + ext[...] - m], (row_at, row_ok, same_col))
+    h[...] = damping_coarse / diag1
 
 
 def pack_kernel(u, f, ext, first, last):
@@ -157,7 +169,7 @@
     return row
 
 
-def pre_kernel(u, f, ext, lab, before, after, smooth, b, h, x0, first, last, rsum, ls, fs, ss):
+def pre_kernel(u, f, ext, before, after, row_at, row_ok, same_col, h, smooth, b, x0, first, last, rsum):
     cases, rows, width = u.shape
     diag = 4.0 + ext[...]
     us = [u[c] for c in range(cases)]
@@ -169,35 +181,22 @@
     x, res = two_sweeps(us, u_halo, fl, f_halo, diag, d_halo, valid)
     for c in range(cases):
         smooth[c] = x[c]
-    key = lab[...]
-    row, col = iotas(key.shape)
-    one = jnp.ones(key.shape, F32)
-    zero = jnp.zeros(key.shape, F32)
-    m = jnp.where((pltpu.roll(key, 1, 0) == key) & (row > 0), one, zero)
-    m = m + jnp.where((pltpu.roll(key, rows - 1, 0) == key) & (row < rows - 1), one, zero)
-    m = m + jnp.where((pltpu.roll(key, 1, 1) == key) & (col > 0), one, zero)
-    m = m + jnp.where((pltpu.roll(key, width - 1, 1) == key) & (col < width - 1), one, zero)
-    seg_sum(key, res + [diag - m], lab, ls, fs, ss)
-    half = damping_coarse / ss[cases]
-    h[...] = half
-    for c in range(cases):
-        b[c] = ss[c]
-        v = half * ss[c]
+    sums = seg_sum(res, (row_at, row_ok, same_col))
+    for c in range(cases):
+        b[c] = sums[c]
+        v = h[...] * sums[c]
         x0[c] = v
         first[pl.ds(c, 1), :] = v[0:1]
         last[pl.ds(c, 1), :] = v[rows - 1 : rows]
     rsum[...] = lane_row([(c, total(res[c])) for c in range(cases)])
 
 
-def coarse_step(x, above, below, ext, lab, b, h, ls, fs, ss):
+def coarse_step(x, above, below, ext, b, h, tables):
     cases = len(x)
     diag = 4.0 + ext[...]
-    w = [
-        diag * x[c] - neighbours(x[c], above[c], below[c])
-        for c in range(cases)
-    ]
-    seg_sum(lab[...], w, lab, ls, fs, ss)
-    return [x[c] + h[...] * (b[c] - ss[c]) for c in range(cases)]
+    w = [diag * x[c] - neighbours(x[c], above[c], below[c]) for c in range(cases)]
+    sums = seg_sum(w, tables)
+    return [x[c] + h[...] * (b[c] - sums[c]) for c in range(cases)]
 
 
 def store_edges(x, first, last):
@@ -207,13 +206,13 @@
         last[pl.ds(c, 1), :] = x[c][rows - 1 : rows]
 
 
-def coarse_kernel_a(x0, ext, lab, b, h, rsum, before, after, x1, first, last, gather, ls, fs, ss):
+def coarse_kernel_a(x0, ext, b, row_at, row_ok, same_col, h, rsum, before, after, x1, first, last, gather):
     cases, rows, width = x0.shape
     x = coarse_step(
         [x0[c] for c in range(cases)],
         [before[pl.ds(c, 1), :] for c in range(cases)],
         [after[pl.ds(c, 1), :] for c in range(cases)],
-        ext, lab, b, h, ls, fs, ss,
+        ext, b, h, (row_at, row_ok, same_col),
     )
     store_edges(x, first, last)
     row, col = iotas((rows, width))
@@ -258,7 +257,7 @@
     return b / (lower + upper + excess)
 
 
-def coarse_kernel_b(groups, at, x1, ext, lab, b, h, before, after, gathered, x3, first, last, ls, fs, ss, e_ref):
+def coarse_kernel_b(groups, at, x1, ext, b, row_at, row_ok, same_col, h, before, after, gathered, x3, first, last, e_ref):
     cases, rows, width = x1.shape
     n = gathered.shape[0]
     i = at[0]
@@ -272,20 +271,20 @@
         [x1[c] + e_own[:, c : c + 1] for c in range(cases)],
         [before[pl.ds(c, 1), :] + e_above[:, c : c + 1] for c in range(cases)],
         [after[pl.ds(c, 1), :] + e_below[:, c : c + 1] for c in range(cases)],
-        ext, lab, b, h, ls, fs, ss,
+        ext, b, h, (row_at, row_ok, same_col),
     )
     store_edges(x, first, last)
     for c in range(cases):
         x3[c] = x[c]
 
 
-def coarse_kernel_c(x3, ext, lab, b, h, smooth, before, after, v, first, last, ls, fs, ss):
+def coarse_kernel_c(x3, ext, b, row_at, row_ok, same_col, h, smooth, before, after, v, first, last):
     cases, rows, width = x3.shape
     x = coarse_step(
         [x3[c] for c in range(cases)],
         [before[pl.ds(c, 1), :] for c in range(cases)],
         [after[pl.ds(c, 1), :] for c in range(cases)],
-        ext, lab, b, h, ls, fs, ss,
+        ext, b, h, (row_at, row_ok, same_col),
     )
     for c in range(cases):
         y = smooth[c] + x[c]
@@ -334,35 +333,38 @@
     def to_all(x, axis):
         return lax.all_to_all(x, axis, 0, 0, tiled=True)
 
-    seg4 = seg_scratch(cases, rows, width)
     edge = (cases, width)
     u, f, ext, lab = thermal_solution, heat_forcing, extinction_factor, cluster_label
     first, last = vmem_call(pack_kernel, [(8, cases, width)] * 2, n_in=3)(u, f, ext)
     before, after = exchange(first, last)
-    smooth, b, h, x0, first, last, rsum = vmem_call(
-        pre_kernel,
-        [field, field, (rows, width), field, edge, edge, (1, 128)],
-        seg_scratch(cases + 1, rows, width),
-        n_in=6,
-    )(u, f, ext, lab, before, after)
+    shifts = len(offsets())
+    cells = (rows, width)
+    tables = vmem_call(
+        table_kernel,
+        [((shifts, rows, width), jnp.int32), (shifts, rows, width), (rows - 1, rows, width), cells],
+        n_in=2,
+    )(ext, lab)
+    smooth, b, x0, first, last, rsum = vmem_call(
+        pre_kernel, [field, field, field, edge, edge, (1, 128)], n_in=9
+    )(u, f, ext, before, after, *tables)
     ab, be = exchange(first, last)
     x1, first, last, mine = vmem_call(
-        coarse_kernel_a, [field, edge, edge, (n, 128)], seg4, n_in=8
-    )(x0, ext, lab, b, h, rsum, ab, be)
+        coarse_kernel_a, [field, edge, edge, (n, 128)], n_in=10
+    )(x0, ext, b, *tables, rsum, ab, be)
     ab, be = exchange(first, last)
     gathered = to_all(mine, "blk")
     at = lax.axis_index("blk").astype(jnp.int32).reshape(1)
     x3, first, last = vmem_call(
         functools.partial(coarse_kernel_b, groups),
         [field, edge, edge],
-        seg4 + [pltpu.VMEM((n + 16, 128), F32)],
+        [pltpu.VMEM((n + 16, 128), F32)],
         smem_args=(0,),
-        n_in=9,
-    )(at, x1, ext, lab, b, h, ab, be, gathered)
+        n_in=11,
+    )(at, x1, ext, b, *tables, ab, be, gathered)
     ab, be = exchange(first, last)
     v, first, last = vmem_call(
-        coarse_kernel_c, [field, (3, cases, width), (3, cases, width)], seg4, n_in=8
-    )(x3, ext, lab, b, h, smooth, ab, be)
+        coarse_kernel_c, [field, (3, cases, width), (3, cases, width)], n_in=10
+    )(x3, ext, b, *tables, smooth, ab, be)
     ab, be = exchange(first, last)
     corrected, mine = vmem_call(post_kernel, [field, (n, 128)], n_in=7)(
         v, f, ext, before, after, ab, be

time: 120 us -> 109 us (0.908)
  Pallas kernels: 16.4 us -> 6.38 us
    pallas_call x2 -> x3, Pallas kernels: 8.2 us -> 3.25 us  [the longest x1 1.56 us: local(): vmem_call(coarse_kernel_a, [field, edge, edge, (n, 128)], n_in=10)]
    pallas_call x1, Pallas kernels: 3.77 us -> 1.23 us  [local(): vmem_call(functools.partial(coarse_kernel_b, groups), [field, edge, edge]...]
    pallas_call x1, Pallas kernels: 3.28 us -> 0.75 us  [local(): vmem_call(coarse_kernel_c, [field, (3, cases, width), (3, cases, width)],...]
    unnamed x12 -> x14, local copies, waits for them, and re-layouts: 2.57 us -> 2.58 us
  transfers between devices with their start and end apart: 11 -> 11, of which waited for: 6 -> 6; matrix products, arithmetic and copies ran while one was open for 0% -> 0% of each run, Pallas kernels for 0% -> 1%
where the time goes in v2:
time: 109 us
  starting transfers between devices  48.6 us (45%)
  blocking collectives  35 us (32%)
  waiting for transfers between devices  14.9 us (14%)
  Pallas kernels  6.38 us (6%)
  local copies, waits for them, and re-layouts  3.17 us (3%)
    all_to_all x2, blocking collectives, to_all(): return lax.all_to_all(x, axis, 0, 0, tiled=True)  35 us
    ppermute x10, starting transfers between devices, exchange(): return (lax.ppermute(last, 'blk', up), lax.ppermute(first, 'blk', down))  29.1 us
    all_to_all x1, starting transfers between devices, to_all(): return lax.all_to_all(x, axis, 0, 0, tiled=True)  19.4 us
    ppermute x10, waiting for transfers between devices, exchange(): return (lax.ppermute(last, 'blk', up), lax.ppermute(first, 'blk', down))  12.4 us
    unnamed x14, local copies, waits for them, and re-layouts  2.58 us
    all_to_all x1, waiting for transfers between devices, to_all(): return lax.all_to_all(x, axis, 0, 0, tiled=True)  2.48 us
  transfers between devices with their start and end apart: 11, of which 6 were waited for; matrix products, arithmetic and copies ran while one was open for 0% of the time, Pallas kernels for 1%

profile of v2, /device:TPU:1, one launch (start us, length us, event | category | flops | bytes accessed | tf_op | source)
XLA Modules:
  0.0 108.8 jit_solution(16103483172821571795)
XLA Ops:
  0.6 0.0 copy-start
  0.6 0.7 copy-done
  1.4 0.0 copy-start.2
  1.4 0.9 copy-done.2
  2.3 0.0 copy-start.4
  2.3 0.9 copy-done.4
  3.2 0.0 copy-start.6
  3.2 0.0 copy-start.5
  3.3 4.7 %collective-permute-start = (f32[8,4,1024]{2,1,0:T(4,128)S(1)}, f32[8,4,1024]{2,1,0:T(4,128)S(1)}, u32[]{:S(2)}, u32[]{:S(2)}) collective-permute-start(f32[8,4,1024]{2,1,0:T(4,128)S(1)} %get-tuple-element.26), channel_id=1, source_target_pairs={{0,4},{4,8},{8,12},{12,16},{16,20},{20,24},{24,28},{28,32},{32,36}... | collective-permute-start | bytes 393224 | tf_op jit(solution)/shard_map/ppermute | solution.py:331
  8.0 5.5 %collective-permute-start.1 = (f32[8,4,1024]{2,1,0:T(4,128)S(1)}, f32[8,4,1024]{2,1,0:T(4,128)S(1)}, u32[]{:S(2)}, u32[]{:S(2)}) collective-permute-start(f32[8,4,1024]{2,1,0:T(4,128)S(1)} %get-tuple-element.27), channel_id=1, source_target_pairs={{4,0},{8,4},{12,8},{16,12},{20,16},{24,20},{28,24},{32,28},{36,32}... | collective-permute-start | bytes 393224 | tf_op jit(solution)/shard_map/ppermute | solution.py:331
  13.5 0.0 copy-done.6
  13.5 0.7 shard_map.60
  14.2 0.0 collective-permute-done.before
  14.2 0.2 collective-permute-done.1.after
  14.4 0.0 copy-done.5
  14.5 1.0 shard_map.61
  15.4 1.9 %collective-permute-start.2 = (f32[4,1024]{1,0:T(4,128)S(1)}, f32[4,1024]{1,0:T(4,128)S(1)}, u32[]{:S(2)}, u32[]{:S(2)}) collective-permute-start(f32[4,1024]{1,0:T(4,128)S(1)} %get-tuple-element.35), channel_id=1, source_target_pairs={{0,4},{4,8},{8,12},{12,16},{16,20},{20,24},{24,28},{28,32},{32,36}... | collective-permute-start | bytes 49160 | tf_op jit(solution)/shard_map/ppermute | solution.py:331
  17.4 2.4 %collective-permute-start.3 = (f32[4,1024]{1,0:T(4,128)S(1)}, f32[4,1024]{1,0:T(4,128)S(1)}, u32[]{:S(2)}, u32[]{:S(2)}) collective-permute-start(f32[4,1024]{1,0:T(4,128)S(1)} %get-tuple-element.36), channel_id=1, source_target_pairs={{4,0},{8,4},{12,8},{16,12},{20,16},{24,20},{28,24},{32,28},{36,32}... | collective-permute-start | bytes 49160 | tf_op jit(solution)/shard_map/ppermute | solution.py:331
  19.8 0.0 collective-permute-done.2.before
  19.8 2.6 %collective-permute-done.3.after = f32[4,1024]{1,0:T(4,128)S(1)} collective-permute-done((f32[4,1024]{1,0:T(4,128)S(1)}, f32[4,1024]{1,0:T(4,128)S(1)}, u32[]{:S(2)}, u32[]{:S(2)}) %collective-permute-start.3) | collective-permute-done | bytes 16416 | tf_op jit(solution)/shard_map/ppermute | solution.py:331
  22.4 1.6 %shard_map.62 = (f32[4,8,1024]{2,1,0:T(8,128)S(1)}, f32[4,1024]{1,0:T(4,128)S(1)}, f32[4,1024]{1,0:T(4,128)S(1)}, f32[128,128]{1,0:T(8,128)}) custom-call(f32[4,8,1024]{2,1,0:T(8,128)S(1)} %get-tuple-element.32.x0, f32[8,1024]{1,0:T(8,128)S(1)} %copy-done, f32[4,8,1024]{2,1,0:T(8,128)S(1)} %get-tuple-element.33.b, ...), custom_call_target="tpu_custom_call" | custom-call | tf_op jit(solution)/shard_map/pallas_call | solution.py:351
  24.0 0.0 copy-start.1
  24.0 19.4 %all-to-all-start = ((f32[128,1,128]{2,1,0:T(1,128)}), f32[128,1,128]{2,1,0:T(1,128)S(1)}, u32[]{:S(2)}, u32[]{:S(2)}) async-start(f32[128,1,128]{2,1,0:T(1,128)} %bitcast.2), calls=%async_computation | async-start | bytes 131072 | tf_op jit(solution)/shard_map/all_to_all | solution.py:334
  43.4 3.5 %collective-permute-start.4 = (f32[4,1024]{1,0:T(4,128)S(1)}, f32[4,1024]{1,0:T(4,128)S(1)}, u32[]{:S(2)}, u32[]{:S(2)}) collective-permute-start(f32[4,1024]{1,0:T(4,128)S(1)} %get-tuple-element.38), channel_id=1, source_target_pairs={{0,4},{4,8},{8,12},{12,16},{16,20},{20,24},{24,28},{28,32},{32,36}... | collective-permute-start | bytes 49160 | tf_op jit(solution)/shard_map/ppermute | solution.py:331
  47.0 1.9 %collective-permute-start.5 = (f32[4,1024]{1,0:T(4,128)S(1)}, f32[4,1024]{1,0:T(4,128)S(1)}, u32[]{:S(2)}, u32[]{:S(2)}) collective-permute-start(f32[4,1024]{1,0:T(4,128)S(1)} %get-tuple-element.39), channel_id=1, source_target_pairs={{4,0},{8,4},{12,8},{16,12},{20,16},{24,20},{28,24},{32,28},{36,32}... | collective-permute-start | bytes 49160 | tf_op jit(solution)/shard_map/ppermute | solution.py:331
  48.9 0.0 collective-permute-done.4.before
  48.9 3.4 %collective-permute-done.5.after = f32[4,1024]{1,0:T(4,128)S(1)} collective-permute-done((f32[4,1024]{1,0:T(4,128)S(1)}, f32[4,1024]{1,0:T(4,128)S(1)}, u32[]{:S(2)}, u32[]{:S(2)}) %collective-permute-start.5) | collective-permute-done | bytes 16416 | tf_op jit(solution)/shard_map/ppermute | solution.py:331
  52.3 2.5 %all-to-all-done = f32[128,1,128]{2,1,0:T(1,128)S(1)} async-done(((f32[128,1,128]{2,1,0:T(1,128)}), f32[128,1,128]{2,1,0:T(1,128)S(1)}, u32[]{:S(2)}, u32[]{:S(2)}) %all-to-all-start) | async-done | bytes 65568 | tf_op jit(solution)/shard_map/all_to_all | solution.py:334
  54.8 0.0 copy-done.1
  54.8 1.2 %shard_map.63 = (f32[4,8,1024]{2,1,0:T(8,128)S(1)}, f32[4,1024]{1,0:T(4,128)S(1)}, f32[4,1024]{1,0:T(4,128)S(1)}) custom-call(s32[1]{0:T(128)} %bitcast.at, f32[4,8,1024]{2,1,0:T(8,128)S(1)} %get-tuple-element.37.x1, f32[8,1024]{1,0:T(8,128)S(1)} %copy-done.1, f32[4,8,1024]{2,1,0:T(8,128)S(1)} %get-tuple-element.33.b, ...), custom_call_target="tpu_custom_call" | custom-call | tf_op jit(solution)/shard_map/pallas_call | solution.py:357
  56.1 2.9 %collective-permute-start.6 = (f32[4,1024]{1,0:T(4,128)S(1)}, f32[4,1024]{1,0:T(4,128)S(1)}, u32[]{:S(2)}, u32[]{:S(2)}) collective-permute-start(f32[4,1024]{1,0:T(4,128)S(1)} %get-tuple-element.43), channel_id=1, source_target_pairs={{0,4},{4,8},{8,12},{12,16},{16,20},{20,24},{24,28},{28,32},{32,36}... | collective-permute-start | bytes 49160 | tf_op jit(solution)/shard_map/ppermute | solution.py:331
  59.0 1.9 %collective-permute-start.7 = (f32[4,1024]{1,0:T(4,128)S(1)}, f32[4,1024]{1,0:T(4,128)S(1)}, u32[]{:S(2)}, u32[]{:S(2)}) collective-permute-start(f32[4,1024]{1,0:T(4,128)S(1)} %get-tuple-element.44), channel_id=1, source_target_pairs={{4,0},{8,4},{12,8},{16,12},{20,16},{24,20},{28,24},{32,28},{36,32}... | collective-permute-start | bytes 49160 | tf_op jit(solution)/shard_map/ppermute | solution.py:331
  60.9 0.0 collective-permute-done.6.before
  60.9 3.1 %collective-permute-done.7.after = f32[4,1024]{1,0:T(4,128)S(1)} collective-permute-done((f32[4,1024]{1,0:T(4,128)S(1)}, f32[4,1024]{1,0:T(4,128)S(1)}, u32[]{:S(2)}, u32[]{:S(2)}) %collective-permute-start.7) | collective-permute-done | bytes 16416 | tf_op jit(solution)/shard_map/ppermute | solution.py:331
  64.0 0.0 copy-start.3
  64.0 0.7 shard_map.64
  64.8 1.9 %collective-permute-start.8 = (f32[3,4,1024]{2,1,0:T(4,128)S(1)}, f32[3,4,1024]{2,1,0:T(4,128)S(1)}, u32[]{:S(2)}, u32[]{:S(2)}) collective-permute-start(f32[3,4,1024]{2,1,0:T(4,128)S(1)} %get-tuple-element.46), channel_id=1, source_target_pairs={{0,4},{4,8},{8,12},{12,16},{16,20},{20,24},{24,28},{28,32},{32,36}... | collective-permute-start | bytes 147464 | tf_op jit(solution)/shard_map/ppermute | solution.py:331
  66.7 2.4 %collective-permute-start.9 = (f32[3,4,1024]{2,1,0:T(4,128)S(1)}, f32[3,4,1024]{2,1,0:T(4,128)S(1)}, u32[]{:S(2)}, u32[]{:S(2)}) collective-permute-start(f32[3,4,1024]{2,1,0:T(4,128)S(1)} %get-tuple-element.47), channel_id=1, source_target_pairs={{4,0},{8,4},{12,8},{16,12},{20,16},{24,20},{28,24},{32,28},{36,32}... | collective-permute-start | bytes 147464 | tf_op jit(solution)/shard_map/ppermute | solution.py:331
  69.1 0.0 collective-permute-done.8.before_v
  69.1 3.0 %collective-permute-done.9.after_v = f32[3,4,1024]{2,1,0:T(4,128)S(1)} collective-permute-done((f32[3,4,1024]{2,1,0:T(4,128)S(1)}, f32[3,4,1024]{2,1,0:T(4,128)S(1)}, u32[]{:S(2)}, u32[]{:S(2)}) %collective-permute-start.9) | collective-permute-done | bytes 49184 | tf_op jit(solution)/shard_map/ppermute | solution.py:331
  72.1 0.0 copy-done.3
  72.1 1.0 shard_map.65
  73.1 27.1 %all_to_all.34 = f32[128,1,128]{2,1,0:T(1,128)S(1)} all-to-all(f32[128,1,128]{2,1,0:T(1,128)S(1)} %bitcast.16), channel_id=1, replica_groups=mesh['blk'=128,'rhs'=4] {'blk'}, dimensions={0} | all-to-all | bytes 131072 | tf_op jit(solution)/shard_map/all_to_all | solution.py:334
  100.2 0.1 shard_map.66
  100.3 7.9 %all_to_all.35 = f32[4,1,128]{2,1,0:T(1,128)S(1)} all-to-all(f32[4,1,128]{2,1,0:T(1,128)S(1)} %bitcast.17), channel_id=1, replica_groups=mesh['blk'=128,'rhs'=4] {'rhs'}, dimensions={0} | all-to-all | bytes 4096 | tf_op jit(solution)/shard_map/all_to_all | solution.py:334
  108.3 0.6 reshape.17
  (1 shorter events, 0.0 us)
Async XLA Ops:
  0.6 0.8 copy-start
  1.4 0.9 copy-start.2
  2.3 0.9 copy-start.4
  3.2 10.3 %copy-start.6 = (s32[8,1024]{1,0:T(8,128)S(1)}, s32[8,1024]{1,0:T(8,128)}, u32[]{:S(2)}) copy-start(s32[8,1024]{1,0:T(8,128)} %lab.1) | copy-start | bytes 98308
  3.2 11.2 %copy-start.5 = (f32[4,8,1024]{2,1,0:T(8,128)S(1)}, f32[4,8,1024]{2,1,0:T(8,128)}, u32[]{:S(2)}) copy-start(f32[4,8,1024]{2,1,0:T(8,128)} %u.3) | copy-start | bytes 393220
  3.3 10.9 %collective-permute-start = (f32[8,4,1024]{2,1,0:T(4,128)S(1)}, f32[8,4,1024]{2,1,0:T(4,128)S(1)}, u32[]{:S(2)}, u32[]{:S(2)}) collective-permute-start(f32[8,4,1024]{2,1,0:T(4,128)S(1)} %get-tuple-element.26), channel_id=1, source_target_pairs={{0,4},{4,8},{8,12},{12,16},{16,20},{20,24},{24,28},{28,32},{32,36}... | collective-permute-start | bytes 393224 | tf_op jit(solution)/shard_map/ppermute | solution.py:331
  8.0 6.5 %collective-permute-start.1 = (f32[8,4,1024]{2,1,0:T(4,128)S(1)}, f32[8,4,1024]{2,1,0:T(4,128)S(1)}, u32[]{:S(2)}, u32[]{:S(2)}) collective-permute-start(f32[8,4,1024]{2,1,0:T(4,128)S(1)} %get-tuple-element.27), channel_id=1, source_target_pairs={{4,0},{8,4},{12,8},{16,12},{20,16},{24,20},{28,24},{32,28},{36,32}... | collective-permute-start | bytes 393224 | tf_op jit(solution)/shard_map/ppermute | solution.py:331
  15.4 4.3 %collective-permute-start.2 = (f32[4,1024]{1,0:T(4,128)S(1)}, f32[4,1024]{1,0:T(4,128)S(1)}, u32[]{:S(2)}, u32[]{:S(2)}) collective-permute-start(f32[4,1024]{1,0:T(4,128)S(1)} %get-tuple-element.35), channel_id=1, source_target_pairs={{0,4},{4,8},{8,12},{12,16},{16,20},{20,24},{24,28},{28,32},{32,36}... | collective-permute-start | bytes 49160 | tf_op jit(solution)/shard_map/ppermute | solution.py:331
  17.4 5.1 %collective-permute-start.3 = (f32[4,1024]{1,0:T(4,128)S(1)}, f32[4,1024]{1,0:T(4,128)S(1)}, u32[]{:S(2)}, u32[]{:S(2)}) collective-permute-start(f32[4,1024]{1,0:T(4,128)S(1)} %get-tuple-element.36), channel_id=1, source_target_pairs={{4,0},{8,4},{12,8},{16,12},{20,16},{24,20},{28,24},{32,28},{36,32}... | collective-permute-start | bytes 49160 | tf_op jit(solution)/shard_map/ppermute | solution.py:331
  24.0 30.8 %copy-start.1 = (f32[8,1024]{1,0:T(8,128)S(1)}, f32[8,1024]{1,0:T(8,128)}, u32[]{:S(2)}) copy-start(f32[8,1024]{1,0:T(8,128)} %ext.13) | copy-start | bytes 98308
  24.0 30.8 %all-to-all-start = ((f32[128,1,128]{2,1,0:T(1,128)}), f32[128,1,128]{2,1,0:T(1,128)S(1)}, u32[]{:S(2)}, u32[]{:S(2)}) async-start(f32[128,1,128]{2,1,0:T(1,128)} %bitcast.2), calls=%async_computation | async-start | bytes 131072 | tf_op jit(solution)/shard_map/all_to_all | solution.py:334
  43.4 5.5 %collective-permute-start.4 = (f32[4,1024]{1,0:T(4,128)S(1)}, f32[4,1024]{1,0:T(4,128)S(1)}, u32[]{:S(2)}, u32[]{:S(2)}) collective-permute-start(f32[4,1024]{1,0:T(4,128)S(1)} %get-tuple-element.38), channel_id=1, source_target_pairs={{0,4},{4,8},{8,12},{12,16},{16,20},{20,24},{24,28},{28,32},{32,36}... | collective-permute-start | bytes 49160 | tf_op jit(solution)/shard_map/ppermute | solution.py:331
  47.0 5.4 %collective-permute-start.5 = (f32[4,1024]{1,0:T(4,128)S(1)}, f32[4,1024]{1,0:T(4,128)S(1)}, u32[]{:S(2)}, u32[]{:S(2)}) collective-permute-start(f32[4,1024]{1,0:T(4,128)S(1)} %get-tuple-element.39), channel_id=1, source_target_pairs={{4,0},{8,4},{12,8},{16,12},{20,16},{24,20},{28,24},{32,28},{36,32}... | collective-permute-start | bytes 49160 | tf_op jit(solution)/shard_map/ppermute | solution.py:331
  56.1 4.8 %collective-permute-start.6 = (f32[4,1024]{1,0:T(4,128)S(1)}, f32[4,1024]{1,0:T(4,128)S(1)}, u32[]{:S(2)}, u32[]{:S(2)}) collective-permute-start(f32[4,1024]{1,0:T(4,128)S(1)} %get-tuple-element.43), channel_id=1, source_target_pairs={{0,4},{4,8},{8,12},{12,16},{16,20},{20,24},{24,28},{28,32},{32,36}... | collective-permute-start | bytes 49160 | tf_op jit(solution)/shard_map/ppermute | solution.py:331
  59.0 5.1 %collective-permute-start.7 = (f32[4,1024]{1,0:T(4,128)S(1)}, f32[4,1024]{1,0:T(4,128)S(1)}, u32[]{:S(2)}, u32[]{:S(2)}) collective-permute-start(f32[4,1024]{1,0:T(4,128)S(1)} %get-tuple-element.44), channel_id=1, source_target_pairs={{4,0},{8,4},{12,8},{16,12},{20,16},{24,20},{28,24},{32,28},{36,32}... | collective-permute-start | bytes 49160 | tf_op jit(solution)/shard_map/ppermute | solution.py:331
  64.0 8.1 %copy-start.3 = (f32[4,8,1024]{2,1,0:T(8,128)S(1)}, f32[4,8,1024]{2,1,0:T(8,128)}, u32[]{:S(2)}) copy-start(f32[4,8,1024]{2,1,0:T(8,128)} %f.5) | copy-start | bytes 393220
  64.8 4.3 %collective-permute-start.8 = (f32[3,4,1024]{2,1,0:T(4,128)S(1)}, f32[3,4,1024]{2,1,0:T(4,128)S(1)}, u32[]{:S(2)}, u32[]{:S(2)}) collective-permute-start(f32[3,4,1024]{2,1,0:T(4,128)S(1)} %get-tuple-element.46), channel_id=1, source_target_pairs={{0,4},{4,8},{8,12},{12,16},{16,20},{20,24},{24,28},{28,32},{32,36}... | collective-permute-start | bytes 147464 | tf_op jit(solution)/shard_map/ppermute | solution.py:331
  66.7 5.4 %collective-permute-start.9 = (f32[3,4,1024]{2,1,0:T(4,128)S(1)}, f32[3,4,1024]{2,1,0:T(4,128)S(1)}, u32[]{:S(2)}, u32[]{:S(2)}) collective-permute-start(f32[3,4,1024]{2,1,0:T(4,128)S(1)} %get-tuple-element.47), channel_id=1, source_target_pairs={{4,0},{8,4},{12,8},{16,12},{20,16},{24,20},{28,24},{32,28},{36,32}... | collective-permute-start | bytes 147464 | tf_op jit(solution)/shard_map/ppermute | solution.py:331

commit v3 on v2

--- a/solution.py
+++ b/solution.py
@@ -78,7 +78,7 @@
     return out
 
 
-def table_kernel(ext, lab, row_at, row_ok, same_col, h):
+def table_kernel(n, me, ext, lab, row_at, row_ok, same_col, h, y3):
     key = lab[...]
     rows, width = key.shape
     for k in range(1, rows):
@@ -97,8 +97,30 @@
     m = m + jnp.where((pltpu.roll(key, rows - 1, 0) == key) & (row < rows - 1), one, zero)
     m = m + jnp.where((pltpu.roll(key, 1, 1) == key) & (col > 0), one, zero)
     m = m + jnp.where((pltpu.roll(key, width - 1, 1) == key) & (col < width - 1), one, zero)
-    (diag1,) = seg_sum([4.0 + ext[...] - m], (row_at, row_ok, same_col))
-    h[...] = damping_coarse / diag1
+    above = jnp.where(me[0] > 0, 1.0, 0.0)
+    below = jnp.where(me[0] < n - 1, 1.0, 0.0)
+    top = jnp.where(row == 0, one, zero)
+    bottom = jnp.where(row == rows - 1, one, zero)
+    open_sides = open_weight(ext[...])
+    diag1, s_top, s_own, s_bottom = seg_sum(
+        [4.0 + ext[...] - m, top, open_sides, bottom], (row_at, row_ok, same_col)
+    )
+    half = damping_coarse / diag1
+    h[...] = half
+    y3[0] = above * (half * s_top)
+    y3[1] = 1.0 - half * s_own
+    y3[2] = below * (half * s_bottom)
+
+
+def open_weight(ext):
+    rows, width = ext.shape
+    row, col = iotas(ext.shape)
+    one = jnp.ones(ext.shape, F32)
+    zero = jnp.zeros(ext.shape, F32)
+    weight = ext
+    for at_edge in (row == 0, row == rows - 1, col == 0, col == width - 1):
+        weight = weight + jnp.where(at_edge, one, zero)
+    return weight
 
 
 def pack_kernel(u, f, ext, first, last):
@@ -125,31 +147,30 @@
     keep = 1.0 - damping_fine
 
     def edge(x):
-        return jnp.concatenate(
-            [v[0:1] for v in x] + [v[rows - 1 : rows] for v in x], axis=0
-        )
+        return jnp.concatenate([v[0:1] for v in x] + [v[rows - 1 : rows] for v in x], axis=0)
+
+    def around(x, halo, c):
+        return neighbours(x[c], halo[0][c : c + 1], halo[0][cases + c : cases + c + 1])
 
     def sweep(x, halo, depth):
-        new = [
-            keep * x[c]
-            + gain * (f[c] + neighbours(x[c], halo[0][c : c + 1], halo[0][cases + c : cases + c + 1]))
-            for c in range(cases)
-        ]
+        new = []
+        for c in range(cases):
+            push = around(x, halo, c)
+            new.append(keep * x[c] + gain * (push if f is None else f[c] + push))
         inner = [edge(x)] + halo
         new_halo = []
         for k in range(depth):
-            v = keep * halo[k] + gain_halo[k] * (
-                f_halo[k] + inner[k] + inner[k + 2] + sideways(halo[k])
-            )
-            new_halo.append(v * valid)
+            push = inner[k] + inner[k + 2] + sideways(halo[k])
+            push = push if f is None else f_halo[k] + push
+            new_halo.append((keep * halo[k] + gain_halo[k] * push) * valid)
         return new, new_halo
 
     x, h = sweep(u, u_halo, 2)
     x, h = sweep(x, h, 1)
-    res = [
-        f[c] - diag * x[c] + neighbours(x[c], h[0][c : c + 1], h[0][cases + c : cases + c + 1])
-        for c in range(cases)
-    ]
+    res = []
+    for c in range(cases):
+        r = around(x, h, c) - diag * x[c]
+        res.append(r if f is None else f[c] + r)
     return x, res
 
 
@@ -169,7 +190,7 @@
     return row
 
 
-def pre_kernel(u, f, ext, before, after, row_at, row_ok, same_col, h, smooth, b, x0, first, last, rsum):
+def pre_kernel(u, f, ext, before, after, row_at, row_ok, same_col, h, y3, smooth, b, x0, first, last, rsum):
     cases, rows, width = u.shape
     diag = 4.0 + ext[...]
     us = [u[c] for c in range(cases)]
@@ -188,6 +209,12 @@
         x0[c] = v
         first[pl.ds(c, 1), :] = v[0:1]
         last[pl.ds(c, 1), :] = v[rows - 1 : rows]
+    for j in range(3):
+        y = y3[j]
+        first[pl.ds(cases + j, 1), :] = y[0:1]
+        last[pl.ds(cases + j, 1), :] = y[rows - 1 : rows]
+    for out in (first, last):
+        out[pl.ds(cases + 3, 1), :] = jnp.zeros((1, width), F32)
     rsum[...] = lane_row([(c, total(res[c])) for c in range(cases)])
 
 
@@ -206,21 +233,31 @@
         last[pl.ds(c, 1), :] = x[c][rows - 1 : rows]
 
 
-def coarse_kernel_a(x0, ext, b, row_at, row_ok, same_col, h, rsum, before, after, x1, first, last, gather):
+def coarse_kernel_a(x0, ext, b, row_at, row_ok, same_col, h, y3, rsum, before, after, x1, y4, first, last, part):
     cases, rows, width = x0.shape
-    x = coarse_step(
-        [x0[c] for c in range(cases)],
-        [before[pl.ds(c, 1), :] for c in range(cases)],
-        [after[pl.ds(c, 1), :] for c in range(cases)],
-        ext, b, h, (row_at, row_ok, same_col),
-    )
-    store_edges(x, first, last)
-    row, col = iotas((rows, width))
-    one = jnp.ones((rows, width), F32)
-    zero = jnp.zeros((rows, width), F32)
-    weight = ext[...]
-    for at_edge in (row == 0, row == rows - 1, col == 0, col == width - 1):
-        weight = weight + jnp.where(at_edge, one, zero)
+    tables = (row_at, row_ok, same_col)
+    none = jnp.zeros((rows, width), F32)
+    no_row = jnp.zeros((1, width), F32)
+    old = [x0[c] for c in range(cases)] + [none] + [y3[j] for j in range(3)] + [none]
+    above = [before[pl.ds(c, 1), :] for c in range(cases + 3)] + [no_row, no_row]
+    below = [after[pl.ds(c, 1), :] for c in range(cases)] + [no_row, no_row]
+    below = below + [after[pl.ds(cases + j, 1), :] for j in range(3)]
+    rhs = [b[c] for c in range(cases)] + [none] * 5
+    x = coarse_step(old, above, below, ext, rhs, h, tables)
+    no_rows = jnp.zeros((8, width), F32)
+    for out in (first, last):
+        for k in range(4):
+            out[k] = no_rows
+    for c in range(cases):
+        first[0, pl.ds(c, 1), :] = x[c][0:1]
+        last[0, pl.ds(c, 1), :] = x[c][rows - 1 : rows]
+    for j in range(5):
+        y = x[cases + j]
+        y4[j] = y
+        for k in range(3):
+            first[1 + k, pl.ds(j, 1), :] = y[k : k + 1]
+            last[1 + k, pl.ds(j, 1), :] = y[rows - 1 - k : rows - k]
+    weight = open_weight(ext[...])
     values = []
     for c in range(cases):
         x1[c] = x[c]
@@ -229,7 +266,55 @@
         values.append((cases + c, total(x[c][0:1])))
         values.append((2 * cases + c, total(x[c][rows - 1 : rows])))
     values.append((3 * cases, total(ext[...])))
-    gather[...] = jnp.broadcast_to(lane_row(values), gather.shape)
+    part[...] = lane_row(values)
+
+
+REACH_E = 3
+ORDER = [0, -1, 1, -2, 2, -3, 3]
+LANE_PERP, LANE_LOAD, LANE_D, LANE_C, LANE_L = 16, 20, 24, 32, 64
+
+
+def dot(x, y):
+    return total(x * y)
+
+
+def response_kernel(ext, before, after, y4, ab, be, phi, q, part):
+    rows, width = ext.shape
+    m = 2 * REACH_E + 1
+    diag = 4.0 + ext[...]
+    none = jnp.zeros((rows, width), F32)
+    fields = [none] + [y4[j] for j in range(5)] + [none]
+    two_rows = jnp.zeros((2, width), F32)
+    halo = []
+    for k in range(3):
+        up, down = ab[1 + k], be[1 + k]
+        halo.append(jnp.concatenate([up[0:5], two_rows, two_rows, down[0:5]], axis=0))
+
+    def spread(k):
+        up = jnp.broadcast_to(before[k][0:1], (m, width))
+        down = jnp.broadcast_to(after[k][0:1], (m, width))
+        return jnp.concatenate([up, down], axis=0)
+
+    d_halo = [4.0 + spread(5 + k) for k in range(2)]
+    x, res = two_sweeps(fields, halo, None, None, diag, d_halo, spread(7))
+    for j in range(m):
+        phi[j] = x[j]
+    every = res[0]
+    for j in range(1, m):
+        every = every + res[j]
+    basis = [every] + [res[REACH_E + j] for j in ORDER[1:]]
+    values = []
+    for j in range(m):
+        v = basis[j]
+        q[j] = v
+        d = dot(v, v)
+        inv = jnp.where(d > 0.0, 1.0 / jnp.where(d > 0.0, d, 1.0), 0.0)
+        values.append((LANE_D + j, d))
+        for k in range(j + 1, m):
+            factor = dot(v, basis[k]) * inv
+            values.append((LANE_L + m * j + k, factor))
+            basis[k] = basis[k] - factor * v
+    part[...] = lane_row(values)
 
 
 def solve_slabs(g, cases, groups, cells):
@@ -257,20 +342,12 @@
     return b / (lower + upper + excess)
 
 
-def coarse_kernel_b(groups, at, x1, ext, b, row_at, row_ok, same_col, h, before, after, gathered, x3, first, last, e_ref):
-    cases, rows, width = x1.shape
-    n = gathered.shape[0]
-    i = at[0]
-    e_ref[pl.ds(8, n), :] = solve_slabs(gathered[...], cases, groups, rows * width)
-    e_ref[pl.ds(0, 8), :] = jnp.zeros((8, 128), F32)
-    e_ref[pl.ds(8 + n, 8), :] = jnp.zeros((8, 128), F32)
-    e_above = e_ref[pl.ds(i + 7, 1), :]
-    e_own = e_ref[pl.ds(i + 8, 1), :]
-    e_below = e_ref[pl.ds(i + 9, 1), :]
+def coarse_kernel_b(x1, ext, b, row_at, row_ok, same_col, h, ab, be, x3, first, last):
+    cases = x1.shape[0]
     x = coarse_step(
-        [x1[c] + e_own[:, c : c + 1] for c in range(cases)],
-        [before[pl.ds(c, 1), :] + e_above[:, c : c + 1] for c in range(cases)],
-        [after[pl.ds(c, 1), :] + e_below[:, c : c + 1] for c in range(cases)],
+        [x1[c] for c in range(cases)],
+        [ab[0, pl.ds(c, 1), :] for c in range(cases)],
+        [be[0, pl.ds(c, 1), :] for c in range(cases)],
         ext, b, h, (row_at, row_ok, same_col),
     )
     store_edges(x, first, last)
@@ -294,8 +371,9 @@
             last[k, pl.ds(c, 1), :] = y[rows - 1 - k : rows - k]
 
 
-def post_kernel(v, f, ext, before, after, before_v, after_v, out, gather):
+def post_kernel(v, f, ext, before, after, before_v, after_v, q, part_a, part_e, out, gather):
     cases, rows, width = v.shape
+    m = q.shape[0]
     diag = 4.0 + ext[...]
     fl = [f[c] for c in range(cases)]
     v_halo = [both(before_v, after_v, k) for k in range(3)]
@@ -303,19 +381,66 @@
     d_halo = [4.0 + both(before, after, 5 + k) for k in range(2)]
     valid = both(before, after, 7)
     x, res = two_sweeps([v[c] for c in range(cases)], v_halo, fl, f_halo, diag, d_halo, valid)
+    for c in range(cases):
+        out[c] = x[c]
+    inv = []
+    for j in range(m):
+        d = part_e[:, LANE_D + j : LANE_D + j + 1]
+        inv.append(jnp.where(d > 0.0, 1.0 / jnp.where(d > 0.0, d, 1.0), 0.0))
     values = []
     for c in range(cases):
-        out[c] = x[c]
-        values.append((c, total(res[c] * res[c])))
-        values.append((cases + c, total(fl[c] * fl[c])))
-    gather[...] = jnp.broadcast_to(lane_row(values), gather.shape)
-
-
-def ratio_kernel(cases, g, out):
-    s = jnp.sum(g[...], axis=0, keepdims=True)
-    ratio = jnp.sqrt(s / pltpu.roll(s, 128 - cases, 1))
-    lane = lax.broadcasted_iota(jnp.int32, s.shape, 1)
-    out[...] = jnp.broadcast_to(jnp.where(lane < cases, ratio, 0.0), out.shape)
+        r = res[c]
+        share = None
+        for _ in range(2):
+            step = [dot(r, q[j]) * inv[j] for j in range(m)]
+            for j in range(m):
+                r = r - step[j] * q[j]
+            share = step if share is None else [p + t for p, t in zip(share, step)]
+        values.append((LANE_PERP + c, dot(r, r)))
+        values.append((LANE_LOAD + c, dot(fl[c], fl[c])))
+        for j in range(m):
+            values.append((LANE_C + cases * j + c, share[j]))
+    row = part_a[...] + part_e[...] + lane_row(values)
+    gather[...] = jnp.broadcast_to(row, gather.shape)
+
+
+def final_kernel(groups, at, base, phi, gathered, out, ratio, e_ref):
+    cases, rows, width = base.shape
+    n = gathered.shape[0]
+    m = phi.shape[0]
+    i = at[0]
+    g = gathered[...]
+    row, lane = iotas(g.shape)
+    e = solve_slabs(g, cases, groups, rows * width)
+    margin = 8
+    e_ref[pl.ds(0, margin), :] = jnp.zeros((margin, 128), F32)
+    e_ref[pl.ds(margin, n), :] = e
+    e_ref[pl.ds(margin + n, margin), :] = jnp.zeros((margin, 128), F32)
+    near = [e_ref[pl.ds(i + margin + j, 1), :] for j in range(-REACH_E, REACH_E + 1)]
+    for c in range(cases):
+        x = base[c]
+        for j in range(m):
+            x = x + near[j][:, c : c + 1] * phi[j]
+        out[c] = x
+
+    def lanes(k):
+        return pltpu.roll(g, 128 - k, 1)
+
+    def column(k):
+        return jnp.broadcast_to(g[:, k : k + 1], g.shape)
+
+    t = [e] + [e_ref[pl.ds(margin + j, n), :] - e for j in ORDER[1:]]
+    norm = lanes(LANE_PERP)
+    for j in range(m):
+        z = lanes(LANE_C + cases * j) + t[j]
+        for k in range(j + 1, m):
+            z = z + column(LANE_L + m * j + k) * t[k]
+        norm = norm + column(LANE_D + j) * (z * z)
+    norm = jnp.sum(norm, axis=0, keepdims=True)
+    load = jnp.sum(lanes(LANE_LOAD), axis=0, keepdims=True)
+    first = lax.broadcasted_iota(jnp.int32, norm.shape, 1) < cases
+    r = jnp.sqrt(jnp.where(first, norm, 0.0) / jnp.where(first, load, 1.0))
+    ratio[...] = jnp.broadcast_to(r, ratio.shape)
 
 
 def local(thermal_solution, heat_forcing, extinction_factor, cluster_label):
@@ -334,45 +459,57 @@
         return lax.all_to_all(x, axis, 0, 0, tiled=True)
 
     edge = (cases, width)
+    edges = (8, width)
+    deep = (4, 8, width)
     u, f, ext, lab = thermal_solution, heat_forcing, extinction_factor, cluster_label
+    at = lax.axis_index("blk").astype(jnp.int32).reshape(1)
     first, last = vmem_call(pack_kernel, [(8, cases, width)] * 2, n_in=3)(u, f, ext)
     before, after = exchange(first, last)
     shifts = len(offsets())
     cells = (rows, width)
-    tables = vmem_call(
-        table_kernel,
-        [((shifts, rows, width), jnp.int32), (shifts, rows, width), (rows - 1, rows, width), cells],
-        n_in=2,
-    )(ext, lab)
+    *tables, y3 = vmem_call(
+        functools.partial(table_kernel, n),
+        [
+            ((shifts, rows, width), jnp.int32),
+            (shifts, rows, width),
+            (rows - 1, rows, width),
+            cells,
+            (3, rows, width),
+        ],
+        smem_args=(0,),
+        n_in=3,
+    )(at, ext, lab)
     smooth, b, x0, first, last, rsum = vmem_call(
-        pre_kernel, [field, field, field, edge, edge, (1, 128)], n_in=9
-    )(u, f, ext, before, after, *tables)
+        pre_kernel, [field, field, field, edges, edges, (1, 128)], n_in=10
+    )(u, f, ext, before, after, *tables, y3)
     ab, be = exchange(first, last)
-    x1, first, last, mine = vmem_call(
-        coarse_kernel_a, [field, edge, edge, (n, 128)], n_in=10
-    )(x0, ext, b, *tables, rsum, ab, be)
+    x1, y4, first, last, part_a = vmem_call(
+        coarse_kernel_a, [field, (5, rows, width), deep, deep, (1, 128)], n_in=11
+    )(x0, ext, b, *tables, y3, rsum, ab, be)
     ab, be = exchange(first, last)
-    gathered = to_all(mine, "blk")
-    at = lax.axis_index("blk").astype(jnp.int32).reshape(1)
-    x3, first, last = vmem_call(
-        functools.partial(coarse_kernel_b, groups),
-        [field, edge, edge],
-        [pltpu.VMEM((n + 16, 128), F32)],
-        smem_args=(0,),
-        n_in=11,
-    )(at, x1, ext, b, *tables, ab, be, gathered)
+    m = 2 * REACH_E + 1
+    phi, q, part_e = vmem_call(
+        response_kernel, [(m, rows, width), (m, rows, width), (1, 128)], n_in=6
+    )(ext, before, after, y4, ab, be)
+    x3, first, last = vmem_call(coarse_kernel_b, [field, edge, edge], n_in=9)(
+        x1, ext, b, *tables, ab, be
+    )
     ab, be = exchange(first, last)
     v, first, last = vmem_call(
         coarse_kernel_c, [field, (3, cases, width), (3, cases, width)], n_in=10
     )(x3, ext, b, *tables, smooth, ab, be)
     ab, be = exchange(first, last)
-    corrected, mine = vmem_call(post_kernel, [field, (n, 128)], n_in=7)(
-        v, f, ext, before, after, ab, be
+    base, mine = vmem_call(post_kernel, [field, (n, 128)], n_in=10)(
+        v, f, ext, before, after, ab, be, q, part_a, part_e
     )
     gathered = to_all(mine, "blk")
-    (ratio,) = vmem_call(
-        functools.partial(ratio_kernel, cases), [(n_rhs, 128)], n_in=1
-    )(gathered)
+    corrected, ratio = vmem_call(
+        functools.partial(final_kernel, groups),
+        [field, (n_rhs, 128)],
+        [pltpu.VMEM((n + 16, 128), F32)],
+        smem_args=(0,),
+        n_in=4,
+    )(at, base, phi, gathered)
     every = to_all(ratio, "rhs")
     return corrected, every[:, :cases].reshape(n_rhs * cases)
 

time: 109 us -> 101 us (0.927)
  starting transfers between devices: 48.6 us -> 27.5 us
  blocking collectives: 35 us -> 45.1 us
  Pallas kernels: 6.38 us -> 9.66 us
  waiting for transfers between devices: 14.9 us -> 13.5 us
    all_to_all x1 -> x0, starting transfers between devices: 19.4 us -> none  [to_all(): return lax.all_to_all(x, axis, 0, 0, tiled=True)]
    all_to_all x2, blocking collectives: 35 us -> 45.1 us  [to_all(): return lax.all_to_all(x, axis, 0, 0, tiled=True)]
    pallas_call x6 -> x7, Pallas kernels: 5.58 us -> 8.84 us  [the longest x1 1.83 us: local(): vmem_call(functools.partial(final_kernel, groups), [field, (n_rhs, 128)],...]
    all_to_all x1 -> x0, waiting for transfers between devices: 2.48 us -> none  [to_all(): return lax.all_to_all(x, axis, 0, 0, tiled=True)]
    ppermute x10, starting transfers between devices: 29.1 us -> 27.5 us  [exchange(): return (lax.ppermute(last, 'blk', up), lax.ppermute(first, 'blk', down))]
  transfers between devices with their start and end apart: 11 -> 10, of which waited for: 6 -> 4; matrix products, arithmetic and copies ran while one was open for 0% -> 0% of each run, Pallas kernels for 1% -> 2%
where the time goes in v3:
time: 101 us
  blocking collectives  45.1 us (45%)
  starting transfers between devices  27.5 us (27%)
  waiting for transfers between devices  13.5 us (13%)
  Pallas kernels  9.66 us (10%)
  local copies, waits for them, and re-layouts  3.92 us (4%)
    all_to_all x2, blocking collectives, to_all(): return lax.all_to_all(x, axis, 0, 0, tiled=True)  45.1 us
    ppermute x10, starting transfers between devices, exchange(): return (lax.ppermute(last, 'blk', up), lax.ppermute(first, 'blk', down))  27.5 us
    ppermute x10, waiting for transfers between devices, exchange(): return (lax.ppermute(last, 'blk', up), lax.ppermute(first, 'blk', down))  13.5 us
    unnamed x14, local copies, waits for them, and re-layouts  3.32 us
  transfers between devices with their start and end apart: 10, of which 4 were waited for; matrix products, arithmetic and copies ran while one was open for 0% of the time, Pallas kernels for 2%

profile of v3, /device:TPU:1, one launch (start us, length us, event | category | flops | bytes accessed | tf_op | source)
XLA Modules:
  0.0 100.5 jit_solution(3006724414681243298)
XLA Ops:
  0.6 0.0 copy-start
  0.6 0.7 copy-done
  1.4 0.0 copy-start.2
  1.4 0.9 copy-done.2
  2.3 0.0 copy-start.4
  2.3 0.9 copy-done.4
  3.2 0.0 copy-start.1
  3.2 0.0 copy-start.3
  3.2 0.0 copy-start.5
  3.3 4.7 %collective-permute-start = (f32[8,4,1024]{2,1,0:T(4,128)S(1)}, f32[8,4,1024]{2,1,0:T(4,128)S(1)}, u32[]{:S(2)}, u32[]{:S(2)}) collective-permute-start(f32[8,4,1024]{2,1,0:T(4,128)S(1)} %get-tuple-element.33), channel_id=1, source_target_pairs={{0,4},{4,8},{8,12},{12,16},{16,20},{20,24},{24,28},{28,32},{32,36}... | collective-permute-start | bytes 393224 | tf_op jit(solution)/shard_map/ppermute | solution.py:456
  8.0 5.5 %collective-permute-start.1 = (f32[8,4,1024]{2,1,0:T(4,128)S(1)}, f32[8,4,1024]{2,1,0:T(4,128)S(1)}, u32[]{:S(2)}, u32[]{:S(2)}) collective-permute-start(f32[8,4,1024]{2,1,0:T(4,128)S(1)} %get-tuple-element.34), channel_id=1, source_target_pairs={{4,0},{8,4},{12,8},{16,12},{20,16},{24,20},{28,24},{32,28},{36,32}... | collective-permute-start | bytes 393224 | tf_op jit(solution)/shard_map/ppermute | solution.py:456
  13.5 0.0 copy-done.1
  13.5 0.0 copy-start.6
  13.5 0.7 copy-done.6
  14.3 1.1 %shard_map.60 = (s32[14,8,1024]{2,1,0:T(8,128)S(1)}, f32[14,8,1024]{2,1,0:T(8,128)S(1)}, f32[7,8,1024]{2,1,0:T(8,128)S(1)}, f32[8,1024]{1,0:T(8,128)S(1)}, f32[3,8,1024]{2,1,0:T(8,128)S(1)}) custom-call(s32[1]{0:T(128)} %bitcast.me.at, f32[8,1024]{1,0:T(8,128)S(1)} %copy-done.1, s32[8,1024]{1,0:T(8,128)S(1)} %copy-done.6), custom_call_target="tpu_custom_call" | custom-call | tf_op jit(solution)/shard_map/pallas_call | solution.py:470
  15.3 0.0 collective-permute-done.before
  15.3 0.0 collective-permute-done.1.after
  15.3 0.0 copy-done.3
  15.4 0.0 copy-done.5
  15.4 1.0 %shard_map.61 = (f32[4,8,1024]{2,1,0:T(8,128)S(1)}, f32[4,8,1024]{2,1,0:T(8,128)S(1)}, f32[4,8,1024]{2,1,0:T(8,128)S(1)}, f32[8,1024]{1,0:T(8,128)S(1)}, f32[8,1024]{1,0:T(8,128)S(1)}, /*index=5*/f32[1,128]{1,0:T(1,128)S(1)}) custom-call(f32[4,8,1024]{2,1,0:T(8,128)S(1)} %copy-done.5, f32[4,8,1024]{2,1,0:T(8,128)S(1)} %copy-done.3, f32[8,1024]{1,0:T(8,128)S(1)} %copy-done.1, ...), custom_call_target="tpu_custom_call" | custom-call | tf_op jit(solution)/shard_map/pallas_call | solution.py:482
  16.4 1.9 %collective-permute-start.2 = (f32[8,1024]{1,0:T(8,128)S(1)}, f32[8,1024]{1,0:T(8,128)S(1)}, u32[]{:S(2)}, u32[]{:S(2)}) collective-permute-start(f32[8,1024]{1,0:T(8,128)S(1)} %get-tuple-element.43), channel_id=1, source_target_pairs={{0,4},{4,8},{8,12},{12,16},{16,20},{20,24},{24,28},{28,32},{32,36}... | collective-permute-start | bytes 98312 | tf_op jit(solution)/shard_map/ppermute | solution.py:456
  18.3 2.4 %collective-permute-start.3 = (f32[8,1024]{1,0:T(8,128)S(1)}, f32[8,1024]{1,0:T(8,128)S(1)}, u32[]{:S(2)}, u32[]{:S(2)}) collective-permute-start(f32[8,1024]{1,0:T(8,128)S(1)} %get-tuple-element.44), channel_id=1, source_target_pairs={{4,0},{8,4},{12,8},{16,12},{20,16},{24,20},{28,24},{32,28},{36,32}... | collective-permute-start | bytes 98312 | tf_op jit(solution)/shard_map/ppermute | solution.py:456
  20.7 0.0 collective-permute-done.2.before
  20.8 2.8 %collective-permute-done.3.after = f32[8,1024]{1,0:T(8,128)S(1)} collective-permute-done((f32[8,1024]{1,0:T(8,128)S(1)}, f32[8,1024]{1,0:T(8,128)S(1)}, u32[]{:S(2)}, u32[]{:S(2)}) %collective-permute-start.3) | collective-permute-done | bytes 32800 | tf_op jit(solution)/shard_map/ppermute | solution.py:456
  23.6 1.7 %shard_map.62 = (f32[4,8,1024]{2,1,0:T(8,128)S(1)}, f32[5,8,1024]{2,1,0:T(8,128)S(1)}, f32[4,8,1024]{2,1,0:T(8,128)S(1)}, f32[4,8,1024]{2,1,0:T(8,128)S(1)}, f32[1,128]{1,0:T(1,128)S(1)}) custom-call(f32[4,8,1024]{2,1,0:T(8,128)S(1)} %get-tuple-element.40.x0, f32[8,1024]{1,0:T(8,128)S(1)} %copy-done.1, f32[4,8,1024]{2,1,0:T(8,128)S(1)} %get-tuple-element.41.b, ...), custom_call_target="tpu_custom_call" | custom-call | tf_op jit(solution)/shard_map/pallas_call | solution.py:486
  25.3 1.9 %collective-permute-start.4 = (f32[4,8,1024]{2,1,0:T(8,128)S(1)}, f32[4,8,1024]{2,1,0:T(8,128)S(1)}, u32[]{:S(2)}, u32[]{:S(2)}) collective-permute-start(f32[4,8,1024]{2,1,0:T(8,128)S(1)} %get-tuple-element.46), channel_id=1, source_target_pairs={{0,4},{4,8},{8,12},{12,16},{16,20},{20,24},{24,28},{28,32},{32,36}... | collective-permute-start | bytes 393224 | tf_op jit(solution)/shard_map/ppermute | solution.py:456
  27.2 2.4 %collective-permute-start.5 = (f32[4,8,1024]{2,1,0:T(8,128)S(1)}, f32[4,8,1024]{2,1,0:T(8,128)S(1)}, u32[]{:S(2)}, u32[]{:S(2)}) collective-permute-start(f32[4,8,1024]{2,1,0:T(8,128)S(1)} %get-tuple-element.47), channel_id=1, source_target_pairs={{4,0},{8,4},{12,8},{16,12},{20,16},{24,20},{28,24},{32,28},{36,32}... | collective-permute-start | bytes 393224 | tf_op jit(solution)/shard_map/ppermute | solution.py:456
  29.7 0.0 collective-permute-done.4.ab
  29.7 3.9 %collective-permute-done.5.be = f32[4,8,1024]{2,1,0:T(8,128)S(1)} collective-permute-done((f32[4,8,1024]{2,1,0:T(8,128)S(1)}, f32[4,8,1024]{2,1,0:T(8,128)S(1)}, u32[]{:S(2)}, u32[]{:S(2)}) %collective-permute-start.5) | collective-permute-done | bytes 131104 | tf_op jit(solution)/shard_map/ppermute | solution.py:456
  33.5 0.8 shard_map.63
  34.3 1.9 %collective-permute-start.6 = (f32[4,1024]{1,0:T(4,128)S(1)}, f32[4,1024]{1,0:T(4,128)S(1)}, u32[]{:S(2)}, u32[]{:S(2)}) collective-permute-start(f32[4,1024]{1,0:T(4,128)S(1)} %get-tuple-element.50), channel_id=1, source_target_pairs={{0,4},{4,8},{8,12},{12,16},{16,20},{20,24},{24,28},{28,32},{32,36}... | collective-permute-start | bytes 49160 | tf_op jit(solution)/shard_map/ppermute | solution.py:456
  36.2 2.4 %collective-permute-start.7 = (f32[4,1024]{1,0:T(4,128)S(1)}, f32[4,1024]{1,0:T(4,128)S(1)}, u32[]{:S(2)}, u32[]{:S(2)}) collective-permute-start(f32[4,1024]{1,0:T(4,128)S(1)} %get-tuple-element.51), channel_id=1, source_target_pairs={{4,0},{8,4},{12,8},{16,12},{20,16},{24,20},{28,24},{32,28},{36,32}... | collective-permute-start | bytes 49160 | tf_op jit(solution)/shard_map/ppermute | solution.py:456
  38.6 0.0 collective-permute-done.6.before
  38.7 3.8 %collective-permute-done.7.after = f32[4,1024]{1,0:T(4,128)S(1)} collective-permute-done((f32[4,1024]{1,0:T(4,128)S(1)}, f32[4,1024]{1,0:T(4,128)S(1)}, u32[]{:S(2)}, u32[]{:S(2)}) %collective-permute-start.7) | collective-permute-done | bytes 16416 | tf_op jit(solution)/shard_map/ppermute | solution.py:456
  42.5 0.8 shard_map.64
  43.2 1.9 %collective-permute-start.8 = (f32[3,4,1024]{2,1,0:T(4,128)S(1)}, f32[3,4,1024]{2,1,0:T(4,128)S(1)}, u32[]{:S(2)}, u32[]{:S(2)}) collective-permute-start(f32[3,4,1024]{2,1,0:T(4,128)S(1)} %get-tuple-element.53), channel_id=1, source_target_pairs={{0,4},{4,8},{8,12},{12,16},{16,20},{20,24},{24,28},{28,32},{32,36}... | collective-permute-start | bytes 147464 | tf_op jit(solution)/shard_map/ppermute | solution.py:456
  45.2 2.4 %collective-permute-start.9 = (f32[3,4,1024]{2,1,0:T(4,128)S(1)}, f32[3,4,1024]{2,1,0:T(4,128)S(1)}, u32[]{:S(2)}, u32[]{:S(2)}) collective-permute-start(f32[3,4,1024]{2,1,0:T(4,128)S(1)} %get-tuple-element.54), channel_id=1, source_target_pairs={{4,0},{8,4},{12,8},{16,12},{20,16},{24,20},{28,24},{32,28},{36,32}... | collective-permute-start | bytes 147464 | tf_op jit(solution)/shard_map/ppermute | solution.py:456
  47.6 1.2 %shard_map.65 = (f32[7,8,1024]{2,1,0:T(8,128)S(1)}, f32[7,8,1024]{2,1,0:T(8,128)S(1)}, f32[1,128]{1,0:T(1,128)S(1)}) custom-call(f32[8,1024]{1,0:T(8,128)S(1)} %copy-done.1, f32[8,4,1024]{2,1,0:T(4,128)S(1)} %collective-permute-done.before, f32[8,4,1024]{2,1,0:T(4,128)S(1)} %collective-permute-done.1.after, f32[5,8,1024]{2,1,0:T(8,128)S(1)} %get-tuple-element.55.y4, ...), custom_call_target="tpu_custom_call" | custom-call | tf_op jit(solution)/shard_map/pallas_call | solution.py:491
  48.8 0.0 collective-permute-done.8.before_v
  48.8 3.0 %collective-permute-done.9.after_v = f32[3,4,1024]{2,1,0:T(4,128)S(1)} collective-permute-done((f32[3,4,1024]{2,1,0:T(4,128)S(1)}, f32[3,4,1024]{2,1,0:T(4,128)S(1)}, u32[]{:S(2)}, u32[]{:S(2)}) %collective-permute-start.9) | collective-permute-done | bytes 49184 | tf_op jit(solution)/shard_map/ppermute | solution.py:456
  51.8 1.2 %shard_map.66 = (f32[4,8,1024]{2,1,0:T(8,128)S(1)}, f32[128,128]{1,0:T(8,128)S(1)}) custom-call(f32[4,8,1024]{2,1,0:T(8,128)S(1)} %get-tuple-element.52.v, f32[4,8,1024]{2,1,0:T(8,128)S(1)} %copy-done.3, f32[8,1024]{1,0:T(8,128)S(1)} %copy-done.1, f32[8,4,1024]{2,1,0:T(4,128)S(1)} %collective-permute-done.before, ...), custom_call_target="tpu_custom_call" | custom-call | tf_op jit(solution)/shard_map/pallas_call | solution.py:502
  53.0 37.2 %all_to_all.23 = f32[128,1,128]{2,1,0:T(1,128)S(1)} all-to-all(f32[128,1,128]{2,1,0:T(1,128)S(1)} %bitcast.11), channel_id=1, replica_groups=mesh['blk'=128,'rhs'=4] {'blk'}, dimensions={0} | all-to-all | bytes 131072 | tf_op jit(solution)/shard_map/all_to_all | solution.py:459
  90.2 1.8 %shard_map.67 = (f32[4,8,1024]{2,1,0:T(8,128)}, f32[4,128]{1,0:T(4,128)S(1)}) custom-call(s32[1]{0:T(128)} %bitcast.me.at, f32[4,8,1024]{2,1,0:T(8,128)S(1)} %get-tuple-element.59.base, f32[7,8,1024]{2,1,0:T(8,128)S(1)} %get-tuple-element.60.phi, f32[128,128]{1,0:T(8,128)S(1)} %bitcast.10), custom_call_target="tpu_custom_call" | custom-call | tf_op jit(solution)/shard_map/pallas_call | solution.py:506
  92.0 7.9 %all_to_all.24 = f32[4,1,128]{2,1,0:T(1,128)S(1)} all-to-all(f32[4,1,128]{2,1,0:T(1,128)S(1)} %bitcast.12), channel_id=1, replica_groups=mesh['blk'=128,'rhs'=4] {'rhs'}, dimensions={0} | all-to-all | bytes 4096 | tf_op jit(solution)/shard_map/all_to_all | solution.py:459
  99.9 0.6 reshape.15
  (1 shorter events, 0.0 us)
Async XLA Ops:
  0.6 0.8 copy-start
  1.4 0.9 copy-start.2
  2.3 0.9 copy-start.4
  3.2 10.3 %copy-start.1 = (f32[8,1024]{1,0:T(8,128)S(1)}, f32[8,1024]{1,0:T(8,128)}, u32[]{:S(2)}) copy-start(f32[8,1024]{1,0:T(8,128)} %ext.15) | copy-start | bytes 98308
  3.2 12.1 %copy-start.3 = (f32[4,8,1024]{2,1,0:T(8,128)S(1)}, f32[4,8,1024]{2,1,0:T(8,128)}, u32[]{:S(2)}) copy-start(f32[4,8,1024]{2,1,0:T(8,128)} %f.5) | copy-start | bytes 393220
  3.2 12.2 %copy-start.5 = (f32[4,8,1024]{2,1,0:T(8,128)S(1)}, f32[4,8,1024]{2,1,0:T(8,128)}, u32[]{:S(2)}) copy-start(f32[4,8,1024]{2,1,0:T(8,128)} %u.3) | copy-start | bytes 393220
  3.3 12.1 %collective-permute-start = (f32[8,4,1024]{2,1,0:T(4,128)S(1)}, f32[8,4,1024]{2,1,0:T(4,128)S(1)}, u32[]{:S(2)}, u32[]{:S(2)}) collective-permute-start(f32[8,4,1024]{2,1,0:T(4,128)S(1)} %get-tuple-element.33), channel_id=1, source_target_pairs={{0,4},{4,8},{8,12},{12,16},{16,20},{20,24},{24,28},{28,32},{32,36}... | collective-permute-start | bytes 393224 | tf_op jit(solution)/shard_map/ppermute | solution.py:456
  8.0 7.3 %collective-permute-start.1 = (f32[8,4,1024]{2,1,0:T(4,128)S(1)}, f32[8,4,1024]{2,1,0:T(4,128)S(1)}, u32[]{:S(2)}, u32[]{:S(2)}) collective-permute-start(f32[8,4,1024]{2,1,0:T(4,128)S(1)} %get-tuple-element.34), channel_id=1, source_target_pairs={{4,0},{8,4},{12,8},{16,12},{20,16},{24,20},{28,24},{32,28},{36,32}... | collective-permute-start | bytes 393224 | tf_op jit(solution)/shard_map/ppermute | solution.py:456
  13.5 0.8 copy-start.6
  16.4 4.3 %collective-permute-start.2 = (f32[8,1024]{1,0:T(8,128)S(1)}, f32[8,1024]{1,0:T(8,128)S(1)}, u32[]{:S(2)}, u32[]{:S(2)}) collective-permute-start(f32[8,1024]{1,0:T(8,128)S(1)} %get-tuple-element.43), channel_id=1, source_target_pairs={{0,4},{4,8},{8,12},{12,16},{16,20},{20,24},{24,28},{28,32},{32,36}... | collective-permute-start | bytes 98312 | tf_op jit(solution)/shard_map/ppermute | solution.py:456
  18.3 5.2 %collective-permute-start.3 = (f32[8,1024]{1,0:T(8,128)S(1)}, f32[8,1024]{1,0:T(8,128)S(1)}, u32[]{:S(2)}, u32[]{:S(2)}) collective-permute-start(f32[8,1024]{1,0:T(8,128)S(1)} %get-tuple-element.44), channel_id=1, source_target_pairs={{4,0},{8,4},{12,8},{16,12},{20,16},{24,20},{28,24},{32,28},{36,32}... | collective-permute-start | bytes 98312 | tf_op jit(solution)/shard_map/ppermute | solution.py:456
  25.3 4.3 %collective-permute-start.4 = (f32[4,8,1024]{2,1,0:T(8,128)S(1)}, f32[4,8,1024]{2,1,0:T(8,128)S(1)}, u32[]{:S(2)}, u32[]{:S(2)}) collective-permute-start(f32[4,8,1024]{2,1,0:T(8,128)S(1)} %get-tuple-element.46), channel_id=1, source_target_pairs={{0,4},{4,8},{8,12},{12,16},{16,20},{20,24},{24,28},{28,32},{32,36}... | collective-permute-start | bytes 393224 | tf_op jit(solution)/shard_map/ppermute | solution.py:456
  27.2 6.3 %collective-permute-start.5 = (f32[4,8,1024]{2,1,0:T(8,128)S(1)}, f32[4,8,1024]{2,1,0:T(8,128)S(1)}, u32[]{:S(2)}, u32[]{:S(2)}) collective-permute-start(f32[4,8,1024]{2,1,0:T(8,128)S(1)} %get-tuple-element.47), channel_id=1, source_target_pairs={{4,0},{8,4},{12,8},{16,12},{20,16},{24,20},{28,24},{32,28},{36,32}... | collective-permute-start | bytes 393224 | tf_op jit(solution)/shard_map/ppermute | solution.py:456
  34.3 4.3 %collective-permute-start.6 = (f32[4,1024]{1,0:T(4,128)S(1)}, f32[4,1024]{1,0:T(4,128)S(1)}, u32[]{:S(2)}, u32[]{:S(2)}) collective-permute-start(f32[4,1024]{1,0:T(4,128)S(1)} %get-tuple-element.50), channel_id=1, source_target_pairs={{0,4},{4,8},{8,12},{12,16},{16,20},{20,24},{24,28},{28,32},{32,36}... | collective-permute-start | bytes 49160 | tf_op jit(solution)/shard_map/ppermute | solution.py:456
  36.2 6.2 %collective-permute-start.7 = (f32[4,1024]{1,0:T(4,128)S(1)}, f32[4,1024]{1,0:T(4,128)S(1)}, u32[]{:S(2)}, u32[]{:S(2)}) collective-permute-start(f32[4,1024]{1,0:T(4,128)S(1)} %get-tuple-element.51), channel_id=1, source_target_pairs={{4,0},{8,4},{12,8},{16,12},{20,16},{24,20},{28,24},{32,28},{36,32}... | collective-permute-start | bytes 49160 | tf_op jit(solution)/shard_map/ppermute | solution.py:456
  43.2 5.6 %collective-permute-start.8 = (f32[3,4,1024]{2,1,0:T(4,128)S(1)}, f32[3,4,1024]{2,1,0:T(4,128)S(1)}, u32[]{:S(2)}, u32[]{:S(2)}) collective-permute-start(f32[3,4,1024]{2,1,0:T(4,128)S(1)} %get-tuple-element.53), channel_id=1, source_target_pairs={{0,4},{4,8},{8,12},{12,16},{16,20},{20,24},{24,28},{28,32},{32,36}... | collective-permute-start | bytes 147464 | tf_op jit(solution)/shard_map/ppermute | solution.py:456
  45.2 6.6 %collective-permute-start.9 = (f32[3,4,1024]{2,1,0:T(4,128)S(1)}, f32[3,4,1024]{2,1,0:T(4,128)S(1)}, u32[]{:S(2)}, u32[]{:S(2)}) collective-permute-start(f32[3,4,1024]{2,1,0:T(4,128)S(1)} %get-tuple-element.54), channel_id=1, source_target_pairs={{4,0},{8,4},{12,8},{16,12},{20,16},{24,20},{28,24},{32,28},{36,32}... | collective-permute-start | bytes 147464 | tf_op jit(solution)/shard_map/ppermute | solution.py:456

commit v4 on v3

--- a/solution.py
+++ b/solution.py
@@ -28,6 +28,34 @@
         scratch_shapes=list(scratch),
         compiler_params=pltpu.CompilerParams(vmem_limit_bytes=48 << 20),
     )
+
+
+class View:
+    def __init__(self, own_chip, cross, chip):
+        self.own_chip = own_chip
+        self.chip, self.cross = chip, cross
+
+    def __getitem__(self, k):
+        return jnp.where(self.own_chip, self.chip[k], self.cross[k])
+
+
+def sides(me, cross, chip):
+    odd = (me[0] & 1) == 1
+    return View(odd, cross, chip), View(jnp.logical_not(odd), cross, chip)
+
+
+def row_of(c):
+    return (pl.ds(c, 1), slice(None))
+
+
+def sender(me, cross, chip):
+    odd = (me[0] & 1) == 1
+
+    def put(k, first, last):
+        chip[k] = jnp.where(odd, first, last)
+        cross[k] = jnp.where(odd, last, first)
+
+    return put
 
 
 def iotas(shape):
@@ -123,16 +151,29 @@
     return weight
 
 
-def pack_kernel(u, f, ext, first, last):
+def pack_kernel(me, u_hbm, f_hbm, ext_hbm, cross, chip, u, f, ext, sem):
+    copies = [
+        pltpu.make_async_copy(src, dst, sem.at[k])
+        for k, (src, dst) in enumerate(((u_hbm, u), (f_hbm, f), (ext_hbm, ext)))
+    ]
+    for copy in copies:
+        copy.start()
+    for copy in copies:
+        copy.wait()
     cases, rows, width = u.shape
+    put = sender(me, cross, chip)
     ones = jnp.ones((cases, width), F32)
-    for out, order in ((first, (0, 1, 2)), (last, (rows - 1, rows - 2, rows - 3))):
-        for k in range(3):
-            out[k] = u[:, order[k], :]
-        for k in range(2):
-            out[3 + k] = f[:, order[k], :]
-            out[5 + k] = jnp.broadcast_to(ext[pl.ds(order[k], 1), :], (cases, width))
-        out[7] = ones
+    end = rows - 1
+    for k in range(3):
+        put(k, u[:, k, :], u[:, end - k, :])
+    for k in range(2):
+        put(3 + k, f[:, k, :], f[:, end - k, :])
+        put(
+            5 + k,
+            jnp.broadcast_to(ext[pl.ds(k, 1), :], (cases, width)),
+            jnp.broadcast_to(ext[pl.ds(end - k, 1), :], (cases, width)),
+        )
+    put(7, ones, ones)
 
 
 def both(before, after, k):
@@ -190,7 +231,9 @@
     return row
 
 
-def pre_kernel(u, f, ext, before, after, row_at, row_ok, same_col, h, y3, smooth, b, x0, first, last, rsum):
+def pre_kernel(me, u, f, ext, cross, chip, row_at, row_ok, same_col, h, y3, smooth, b, x0, to_cross, to_chip, rsum):
+    before, after = sides(me, cross, chip)
+    put = sender(me, to_cross, to_chip)
     cases, rows, width = u.shape
     diag = 4.0 + ext[...]
     us = [u[c] for c in range(cases)]
@@ -207,14 +250,11 @@
         b[c] = sums[c]
         v = h[...] * sums[c]
         x0[c] = v
-        first[pl.ds(c, 1), :] = v[0:1]
-        last[pl.ds(c, 1), :] = v[rows - 1 : rows]
+        put(row_of(c), v[0:1], v[rows - 1 : rows])
     for j in range(3):
         y = y3[j]
-        first[pl.ds(cases + j, 1), :] = y[0:1]
-        last[pl.ds(cases + j, 1), :] = y[rows - 1 : rows]
-    for out in (first, last):
-        out[pl.ds(cases + 3, 1), :] = jnp.zeros((1, width), F32)
+        put(row_of(cases + j), y[0:1], y[rows - 1 : rows])
+    put(row_of(cases + 3), jnp.zeros((1, width), F32), jnp.zeros((1, width), F32))
     rsum[...] = lane_row([(c, total(res[c])) for c in range(cases)])
 
 
@@ -226,14 +266,9 @@
     return [x[c] + h[...] * (b[c] - sums[c]) for c in range(cases)]
 
 
-def store_edges(x, first, last):
-    rows = x[0].shape[0]
-    for c in range(len(x)):
-        first[pl.ds(c, 1), :] = x[c][0:1]
-        last[pl.ds(c, 1), :] = x[c][rows - 1 : rows]
-
-
-def coarse_kernel_a(x0, ext, b, row_at, row_ok, same_col, h, y3, rsum, before, after, x1, y4, first, last, part):
+def coarse_kernel_a(me, x0, ext, b, row_at, row_ok, same_col, h, y3, rsum, cross, chip, x1, y4, to_cross, to_chip, part):
+    before, after = sides(me, cross, chip)
+    put = sender(me, to_cross, to_chip)
     cases, rows, width = x0.shape
     tables = (row_at, row_ok, same_col)
     none = jnp.zeros((rows, width), F32)
@@ -245,18 +280,15 @@
     rhs = [b[c] for c in range(cases)] + [none] * 5
     x = coarse_step(old, above, below, ext, rhs, h, tables)
     no_rows = jnp.zeros((8, width), F32)
-    for out in (first, last):
-        for k in range(4):
-            out[k] = no_rows
-    for c in range(cases):
-        first[0, pl.ds(c, 1), :] = x[c][0:1]
-        last[0, pl.ds(c, 1), :] = x[c][rows - 1 : rows]
+    for k in range(4):
+        put(k, no_rows, no_rows)
+    for c in range(cases):
+        put((0,) + row_of(c), x[c][0:1], x[c][rows - 1 : rows])
     for j in range(5):
         y = x[cases + j]
         y4[j] = y
         for k in range(3):
-            first[1 + k, pl.ds(j, 1), :] = y[k : k + 1]
-            last[1 + k, pl.ds(j, 1), :] = y[rows - 1 - k : rows - k]
+            put((1 + k,) + row_of(j), y[k : k + 1], y[rows - 1 - k : rows - k])
     weight = open_weight(ext[...])
     values = []
     for c in range(cases):
@@ -278,7 +310,9 @@
     return total(x * y)
 
 
-def response_kernel(ext, before, after, y4, ab, be, phi, q, part):
+def response_kernel(me, ext, cross, chip, y4, cross_y, chip_y, phi, q, part):
+    before, after = sides(me, cross, chip)
+    ab, be = sides(me, cross_y, chip_y)
     rows, width = ext.shape
     m = 2 * REACH_E + 1
     diag = 4.0 + ext[...]
@@ -342,20 +376,24 @@
     return b / (lower + upper + excess)
 
 
-def coarse_kernel_b(x1, ext, b, row_at, row_ok, same_col, h, ab, be, x3, first, last):
-    cases = x1.shape[0]
+def coarse_kernel_b(me, x1, ext, b, row_at, row_ok, same_col, h, cross, chip, x3, to_cross, to_chip):
+    ab, be = sides(me, cross, chip)
+    put = sender(me, to_cross, to_chip)
+    cases, rows, _ = x1.shape
     x = coarse_step(
         [x1[c] for c in range(cases)],
-        [ab[0, pl.ds(c, 1), :] for c in range(cases)],
-        [be[0, pl.ds(c, 1), :] for c in range(cases)],
+        [ab[(0,) + row_of(c)] for c in range(cases)],
+        [be[(0,) + row_of(c)] for c in range(cases)],
         ext, b, h, (row_at, row_ok, same_col),
     )
-    store_edges(x, first, last)
     for c in range(cases):
         x3[c] = x[c]
-
-
-def coarse_kernel_c(x3, ext, b, row_at, row_ok, same_col, h, smooth, before, after, v, first, last):
+        put(row_of(c), x[c][0:1], x[c][rows - 1 : rows])
+
+
+def coarse_kernel_c(me, x3, ext, b, row_at, row_ok, same_col, h, smooth, cross, chip, v, to_cross, to_chip):
+    before, after = sides(me, cross, chip)
+    put = sender(me, to_cross, to_chip)
     cases, rows, width = x3.shape
     x = coarse_step(
         [x3[c] for c in range(cases)],
@@ -367,11 +405,12 @@
         y = smooth[c] + x[c]
         v[c] = y
         for k in range(3):
-            first[k, pl.ds(c, 1), :] = y[k : k + 1]
-            last[k, pl.ds(c, 1), :] = y[rows - 1 - k : rows - k]
-
-
-def post_kernel(v, f, ext, before, after, before_v, after_v, q, part_a, part_e, out, gather):
+            put((k,) + row_of(c), y[k : k + 1], y[rows - 1 - k : rows - k])
+
+
+def post_kernel(me, v, f, ext, cross, chip, cross_v, chip_v, q, part_a, part_e, out, gather):
+    before, after = sides(me, cross, chip)
+    before_v, after_v = sides(me, cross_v, chip_v)
     cases, rows, width = v.shape
     m = q.shape[0]
     diag = 4.0 + ext[...]
@@ -404,11 +443,11 @@
     gather[...] = jnp.broadcast_to(row, gather.shape)
 
 
-def final_kernel(groups, at, base, phi, gathered, out, ratio, e_ref):
+def final_kernel(groups, me, base, phi, gathered, out, ratio, e_ref):
     cases, rows, width = base.shape
     n = gathered.shape[0]
     m = phi.shape[0]
-    i = at[0]
+    i = me[0]
     g = gathered[...]
     row, lane = iotas(g.shape)
     e = solve_slabs(g, cases, groups, rows * width)
@@ -440,7 +479,8 @@
     load = jnp.sum(lanes(LANE_LOAD), axis=0, keepdims=True)
     first = lax.broadcasted_iota(jnp.int32, norm.shape, 1) < cases
     r = jnp.sqrt(jnp.where(first, norm, 0.0) / jnp.where(first, load, 1.0))
-    ratio[...] = jnp.broadcast_to(r, ratio.shape)
+    mine = pltpu.roll(jnp.where(first, r, 0.0), me[1] * cases, 1)
+    ratio[...] = mine[:, : ratio.shape[1]]
 
 
 def local(thermal_solution, heat_forcing, extinction_factor, cluster_label):
@@ -449,24 +489,35 @@
     n_rhs = lax.axis_size("rhs")
     groups = rows * width // 16
     field = (cases, rows, width)
-    up = [(i, i + 1) for i in range(n - 1)]
-    down = [(j, i) for i, j in up]
-
-    def exchange(first, last):
-        return lax.ppermute(last, "blk", up), lax.ppermute(first, "blk", down)
-
-    def to_all(x, axis):
-        return lax.all_to_all(x, axis, 0, 0, tiled=True)
+    pairs = [(i, i + 1) for i in range(1, n - 1, 2)]
+    cross_chip = pairs + [(j, i) for i, j in pairs]
+    on_chip = [(i, i ^ 1) for i in range(n)]
+
+    def exchange(cross, chip):
+        cross = lax.ppermute(cross, "blk", cross_chip)
+        return cross, lax.ppermute(chip, "blk", on_chip)
 
     edge = (cases, width)
     edges = (8, width)
     deep = (4, 8, width)
     u, f, ext, lab = thermal_solution, heat_forcing, extinction_factor, cluster_label
-    at = lax.axis_index("blk").astype(jnp.int32).reshape(1)
-    first, last = vmem_call(pack_kernel, [(8, cases, width)] * 2, n_in=3)(u, f, ext)
-    before, after = exchange(first, last)
+    me = jnp.stack([lax.axis_index("blk"), lax.axis_index("rhs")]).astype(jnp.int32)
+    cells = (rows, width)
+    hbm = pl.BlockSpec(memory_space=pl.ANY)
+    sent = pl.pallas_call(
+        pack_kernel,
+        out_shape=[jax.ShapeDtypeStruct((8, cases, width), F32)] * 2,
+        in_specs=[pl.BlockSpec(memory_space=pltpu.SMEM), hbm, hbm, hbm],
+        out_specs=[pl.BlockSpec(memory_space=pltpu.VMEM)] * 2,
+        scratch_shapes=[
+            pltpu.VMEM(field, F32),
+            pltpu.VMEM(field, F32),
+            pltpu.VMEM(cells, F32),
+            pltpu.SemaphoreType.DMA((3,)),
+        ],
+    )(me, u, f, ext)
+    halo = exchange(*sent)
     shifts = len(offsets())
-    cells = (rows, width)
     *tables, y3 = vmem_call(
         functools.partial(table_kernel, n),
         [
@@ -478,40 +529,39 @@
         ],
         smem_args=(0,),
         n_in=3,
-    )(at, ext, lab)
-    smooth, b, x0, first, last, rsum = vmem_call(
-        pre_kernel, [field, field, field, edges, edges, (1, 128)], n_in=10
-    )(u, f, ext, before, after, *tables, y3)
-    ab, be = exchange(first, last)
-    x1, y4, first, last, part_a = vmem_call(
-        coarse_kernel_a, [field, (5, rows, width), deep, deep, (1, 128)], n_in=11
-    )(x0, ext, b, *tables, y3, rsum, ab, be)
-    ab, be = exchange(first, last)
+    )(me, ext, lab)
+    call = functools.partial(vmem_call, smem_args=(0,))
+    smooth, b, x0, *sent, rsum = call(
+        pre_kernel, [field, field, field, edges, edges, (1, 128)], n_in=11
+    )(me, u, f, ext, *halo, *tables, y3)
+    rows_x = exchange(*sent)
+    x1, y4, *sent, part_a = call(
+        coarse_kernel_a, [field, (5, rows, width), deep, deep, (1, 128)], n_in=12
+    )(me, x0, ext, b, *tables, y3, rsum, *rows_x)
+    rows_x = exchange(*sent)
     m = 2 * REACH_E + 1
-    phi, q, part_e = vmem_call(
-        response_kernel, [(m, rows, width), (m, rows, width), (1, 128)], n_in=6
-    )(ext, before, after, y4, ab, be)
-    x3, first, last = vmem_call(coarse_kernel_b, [field, edge, edge], n_in=9)(
-        x1, ext, b, *tables, ab, be
-    )
-    ab, be = exchange(first, last)
-    v, first, last = vmem_call(
-        coarse_kernel_c, [field, (3, cases, width), (3, cases, width)], n_in=10
-    )(x3, ext, b, *tables, smooth, ab, be)
-    ab, be = exchange(first, last)
-    base, mine = vmem_call(post_kernel, [field, (n, 128)], n_in=10)(
-        v, f, ext, before, after, ab, be, q, part_a, part_e
-    )
-    gathered = to_all(mine, "blk")
-    corrected, ratio = vmem_call(
+    phi, q, part_e = call(
+        response_kernel, [(m, rows, width), (m, rows, width), (1, 128)], n_in=7
+    )(me, ext, *halo, y4, *rows_x)
+    x3, *sent = call(coarse_kernel_b, [field, edge, edge], n_in=10)(
+        me, x1, ext, b, *tables, *rows_x
+    )
+    rows_x = exchange(*sent)
+    v, *sent = call(
+        coarse_kernel_c, [field, (3, cases, width), (3, cases, width)], n_in=11
+    )(me, x3, ext, b, *tables, smooth, *rows_x)
+    rows_x = exchange(*sent)
+    base, mine = call(post_kernel, [field, (n, 128)], n_in=11)(
+        me, v, f, ext, *halo, *rows_x, q, part_a, part_e
+    )
+    gathered = lax.all_to_all(mine, "blk", 0, 0, tiled=True)
+    corrected, ratio = call(
         functools.partial(final_kernel, groups),
-        [field, (n_rhs, 128)],
+        [field, (1, n_rhs * cases)],
         [pltpu.VMEM((n + 16, 128), F32)],
-        smem_args=(0,),
         n_in=4,
-    )(at, base, phi, gathered)
-    every = to_all(ratio, "rhs")
-    return corrected, every[:, :cases].reshape(n_rhs * cases)
+    )(me, base, phi, gathered)
+    return corrected, lax.psum(ratio.reshape(n_rhs * cases), "rhs")
 
 
 def solution(mesh):

time: 101 us -> 93.3 us (0.924)
  waiting for transfers between devices: 13.5 us -> 3.86 us
  Pallas kernels: 9.66 us -> 16.2 us
  blocking collectives: 45.1 us -> 41.9 us
  local copies, waits for them, and re-layouts: 3.92 us -> 0.77 us
    all_to_all x2 -> x1, blocking collectives: 45.1 us -> 33 us  [local(): gathered = lax.all_to_all(mine, 'blk', 0, 0, tiled=True)]
    ppermute x10, waiting for transfers between devices: 13.5 us -> 3.86 us  [the longest x5 2.38 us: exchange(): cross = lax.ppermute(cross, 'blk', cross_chip)]
    psum x0 -> x1, blocking collectives: none -> 8.95 us  [local(): return (corrected, lax.psum(ratio.reshape(n_rhs * cases), 'rhs'))]
    pallas_call x8, Pallas kernels: 8.61 us -> 14.6 us  [the longest x1 2.54 us: local(): pl.pallas_call(pack_kernel, out_shape=[jax.ShapeDtypeStruct((8, cases, wi...]
    unnamed x14 -> x10, local copies, waits for them, and re-layouts: 3.32 us -> 0.77 us
  transfers between devices with their start and end apart: 10 -> 10, of which waited for: 4 -> 5; matrix products, arithmetic and copies ran while one was open for 0% -> 0% of each run, Pallas kernels for 2% -> 4%
where the time goes in v4:
time: 93.3 us; the launch traced here: 92.5 us
  blocking collectives  41.9 us (45%)
  starting transfers between devices  28.3 us (30%)
  Pallas kernels  16.2 us (17%)
  waiting for transfers between devices  3.86 us (4%)
    all_to_all x1, blocking collectives, local(): gathered = lax.all_to_all(mine, 'blk', 0, 0, tiled=True)  33 us
    ppermute x5, starting transfers between devices, exchange(): cross = lax.ppermute(cross, 'blk', cross_chip)  15.8 us
    ppermute x5, starting transfers between devices, exchange(): return (cross, lax.ppermute(chip, 'blk', on_chip))  12.5 us
    psum x1, blocking collectives, local(): return (corrected, lax.psum(ratio.reshape(n_rhs * cases), 'rhs'))  8.95 us
    pallas_call x1, Pallas kernels, local(): pl.pallas_call(pack_kernel, out_shape=[jax.ShapeDtypeStruct((8, cases, wi...  2.54 us
    ppermute x5, waiting for transfers between devices, exchange(): cross = lax.ppermute(cross, 'blk', cross_chip)  2.38 us
    pallas_call x1, Pallas kernels, local(): call(coarse_kernel_a, [field, (5, rows, width), deep, deep, (1, 128)], n_...  2.33 us
  transfers between devices with their start and end apart: 10, of which 5 were waited for; matrix products, arithmetic and copies ran while one was open for 0% of the time, Pallas kernels for 4%

profile of v4, /device:TPU:1, one launch (start us, length us, event | category | flops | bytes accessed | tf_op | source)
XLA Modules:
  0.0 92.5 jit_solution(3821504966896968492)
XLA Ops:
  0.6 0.6 pad_add_fusion.me
  1.2 0.0 copy-start
  1.2 0.0 copy-start.1
  1.2 0.0 copy-start.2
  1.2 2.5 %shard_map.59 = (f32[8,4,1024]{2,1,0:T(4,128)}, f32[8,4,1024]{2,1,0:T(4,128)}) custom-call(s32[2]{0:T(128)} %pad_add_fusion.me, f32[4,8,1024]{2,1,0:T(8,128)} %u.1, f32[4,8,1024]{2,1,0:T(8,128)} %f.3, f32[8,1024]{1,0:T(8,128)} %ext.13), custom_call_target="tpu_custom_call" | custom-call | tf_op jit(solution)/shard_map/pallas_call | solution.py:507
  3.8 0.0 copy-start.3
  3.8 4.6 %collective-permute-start = (f32[8,4,1024]{2,1,0:T(4,128)}, f32[8,4,1024]{2,1,0:T(4,128)S(1)}, u32[]{:S(2)}, u32[]{:S(2)}) collective-permute-start(f32[8,4,1024]{2,1,0:T(4,128)} %get-tuple-element.33), channel_id=1, source_target_pairs={{4,8},{12,16},{20,24},{28,32},{36,40},{44,48},{52,56},{60,64},{68,... | collective-permute-start | bytes 393224 | tf_op jit(solution)/shard_map/ppermute | solution.py:497
  8.4 4.9 %collective-permute-start.1 = (f32[8,4,1024]{2,1,0:T(4,128)}, f32[8,4,1024]{2,1,0:T(4,128)S(1)}, u32[]{:S(2)}, u32[]{:S(2)}) collective-permute-start(f32[8,4,1024]{2,1,0:T(4,128)} %get-tuple-element.34), channel_id=1, source_target_pairs={{0,4},{4,0},{8,12},{12,8},{16,20},{20,16},{24,28},{28,24},{32,36},... | collective-permute-start | bytes 393224 | tf_op jit(solution)/shard_map/ppermute | solution.py:498
  13.3 0.0 copy-done
  13.3 0.0 copy-done.3
  13.3 0.0 copy-start.4
  13.3 0.7 copy-done.4
  14.1 1.6 %shard_map.60 = (s32[14,8,1024]{2,1,0:T(8,128)S(1)}, f32[14,8,1024]{2,1,0:T(8,128)S(1)}, f32[7,8,1024]{2,1,0:T(8,128)S(1)}, f32[8,1024]{1,0:T(8,128)S(1)}, f32[3,8,1024]{2,1,0:T(8,128)S(1)}) custom-call(s32[2]{0:T(128)S(1)} %copy-done.3, f32[8,1024]{1,0:T(8,128)S(1)} %copy-done, s32[8,1024]{1,0:T(8,128)S(1)} %copy-done.4), custom_call_target="tpu_custom_call" | custom-call | tf_op jit(solution)/shard_map/pallas_call | solution.py:521
  15.7 0.0 collective-permute-done.cross
  15.7 0.0 collective-permute-done.1.chip
  15.7 0.0 copy-done.1
  15.7 0.0 copy-done.2
  15.7 1.6 %shard_map.61 = (f32[4,8,1024]{2,1,0:T(8,128)S(1)}, f32[4,8,1024]{2,1,0:T(8,128)S(1)}, f32[4,8,1024]{2,1,0:T(8,128)S(1)}, f32[8,1024]{1,0:T(8,128)S(1)}, f32[8,1024]{1,0:T(8,128)S(1)}, /*index=5*/f32[1,128]{1,0:T(1,128)S(1)}) custom-call(s32[2]{0:T(128)S(1)} %copy-done.3, f32[4,8,1024]{2,1,0:T(8,128)S(1)} %copy-done.2, f32[4,8,1024]{2,1,0:T(8,128)S(1)} %copy-done.1, ...), custom_call_target="tpu_custom_call" | custom-call | tf_op jit(solution)/shard_map/pallas_call | solution.py:534
  17.3 1.9 %collective-permute-start.2 = (f32[8,1024]{1,0:T(8,128)S(1)}, f32[8,1024]{1,0:T(8,128)S(1)}, u32[]{:S(2)}, u32[]{:S(2)}) collective-permute-start(f32[8,1024]{1,0:T(8,128)S(1)} %get-tuple-element.43), channel_id=1, source_target_pairs={{4,8},{12,16},{20,24},{28,32},{36,40},{44,48},{52,56},{60,64},{68,... | collective-permute-start | bytes 98312 | tf_op jit(solution)/shard_map/ppermute | solution.py:497
  19.2 1.9 %collective-permute-start.3 = (f32[8,1024]{1,0:T(8,128)S(1)}, f32[8,1024]{1,0:T(8,128)S(1)}, u32[]{:S(2)}, u32[]{:S(2)}) collective-permute-start(f32[8,1024]{1,0:T(8,128)S(1)} %get-tuple-element.44), channel_id=1, source_target_pairs={{0,4},{4,0},{8,12},{12,8},{16,20},{20,16},{24,28},{28,24},{32,36},... | collective-permute-start | bytes 98312 | tf_op jit(solution)/shard_map/ppermute | solution.py:498
  21.2 1.4 %collective-permute-done.2.cross = f32[8,1024]{1,0:T(8,128)S(1)} collective-permute-done((f32[8,1024]{1,0:T(8,128)S(1)}, f32[8,1024]{1,0:T(8,128)S(1)}, u32[]{:S(2)}, u32[]{:S(2)}) %collective-permute-start.2) | collective-permute-done | bytes 32800 | tf_op jit(solution)/shard_map/ppermute | solution.py:497
  22.5 0.0 collective-permute-done.3.chip
  22.5 2.3 %shard_map.62 = (f32[4,8,1024]{2,1,0:T(8,128)S(1)}, f32[5,8,1024]{2,1,0:T(8,128)S(1)}, f32[4,8,1024]{2,1,0:T(8,128)S(1)}, f32[4,8,1024]{2,1,0:T(8,128)S(1)}, f32[1,128]{1,0:T(1,128)S(1)}) custom-call(s32[2]{0:T(128)S(1)} %copy-done.3, f32[4,8,1024]{2,1,0:T(8,128)S(1)} %get-tuple-element.40.x0, f32[8,1024]{1,0:T(8,128)S(1)} %copy-done, ...), custom_call_target="tpu_custom_call" | custom-call | tf_op jit(solution)/shard_map/pallas_call | solution.py:538
  24.9 3.4 %collective-permute-start.4 = (f32[4,8,1024]{2,1,0:T(8,128)S(1)}, f32[4,8,1024]{2,1,0:T(8,128)S(1)}, u32[]{:S(2)}, u32[]{:S(2)}) collective-permute-start(f32[4,8,1024]{2,1,0:T(8,128)S(1)} %get-tuple-element.46), channel_id=1, source_target_pairs={{4,8},{12,16},{20,24},{28,32},{36,40},{44,48},{52,56},{60,64},{68,... | collective-permute-start | bytes 393224 | tf_op jit(solution)/shard_map/ppermute | solution.py:497
  28.3 1.9 %collective-permute-start.5 = (f32[4,8,1024]{2,1,0:T(8,128)S(1)}, f32[4,8,1024]{2,1,0:T(8,128)S(1)}, u32[]{:S(2)}, u32[]{:S(2)}) collective-permute-start(f32[4,8,1024]{2,1,0:T(8,128)S(1)} %get-tuple-element.47), channel_id=1, source_target_pairs={{0,4},{4,0},{8,12},{12,8},{16,20},{20,16},{24,28},{28,24},{32,36},... | collective-permute-start | bytes 393224 | tf_op jit(solution)/shard_map/ppermute | solution.py:498
  30.3 0.9 collective-permute-done.4.cross.cross_y
  31.2 0.4 collective-permute-done.5.chip.chip_y
  31.6 1.3 %shard_map.63 = (f32[4,8,1024]{2,1,0:T(8,128)S(1)}, f32[4,1024]{1,0:T(4,128)S(1)}, f32[4,1024]{1,0:T(4,128)S(1)}) custom-call(s32[2]{0:T(128)S(1)} %copy-done.3, f32[4,8,1024]{2,1,0:T(8,128)S(1)} %get-tuple-element.45.x1, f32[8,1024]{1,0:T(8,128)S(1)} %copy-done, f32[4,8,1024]{2,1,0:T(8,128)S(1)} %get-tuple-element.41.b, ...), custom_call_target="tpu_custom_call" | custom-call | tf_op jit(solution)/shard_map/pallas_call | solution.py:546
  32.9 3.0 %collective-permute-start.6 = (f32[4,1024]{1,0:T(4,128)S(1)}, f32[4,1024]{1,0:T(4,128)S(1)}, u32[]{:S(2)}, u32[]{:S(2)}) collective-permute-start(f32[4,1024]{1,0:T(4,128)S(1)} %get-tuple-element.50), channel_id=1, source_target_pairs={{4,8},{12,16},{20,24},{28,32},{36,40},{44,48},{52,56},{60,64},{68,... | collective-permute-start | bytes 49160 | tf_op jit(solution)/shard_map/ppermute | solution.py:497
  36.0 1.9 %collective-permute-start.7 = (f32[4,1024]{1,0:T(4,128)S(1)}, f32[4,1024]{1,0:T(4,128)S(1)}, u32[]{:S(2)}, u32[]{:S(2)}) collective-permute-start(f32[4,1024]{1,0:T(4,128)S(1)} %get-tuple-element.51), channel_id=1, source_target_pairs={{0,4},{4,0},{8,12},{12,8},{16,20},{20,16},{24,28},{28,24},{32,36},... | collective-permute-start | bytes 49160 | tf_op jit(solution)/shard_map/ppermute | solution.py:498
  37.9 0.1 collective-permute-done.6.cross
  38.0 1.1 %collective-permute-done.7.chip = f32[4,1024]{1,0:T(4,128)S(1)} collective-permute-done((f32[4,1024]{1,0:T(4,128)S(1)}, f32[4,1024]{1,0:T(4,128)S(1)}, u32[]{:S(2)}, u32[]{:S(2)}) %collective-permute-start.7) | collective-permute-done | bytes 16416 | tf_op jit(solution)/shard_map/ppermute | solution.py:498
  39.0 1.4 %shard_map.64 = (f32[4,8,1024]{2,1,0:T(8,128)S(1)}, f32[3,4,1024]{2,1,0:T(4,128)S(1)}, f32[3,4,1024]{2,1,0:T(4,128)S(1)}) custom-call(s32[2]{0:T(128)S(1)} %copy-done.3, f32[4,8,1024]{2,1,0:T(8,128)S(1)} %get-tuple-element.48.x3, f32[8,1024]{1,0:T(8,128)S(1)} %copy-done, f32[4,8,1024]{2,1,0:T(8,128)S(1)} %get-tuple-element.41.b, ...), custom_call_target="tpu_custom_call" | custom-call | tf_op jit(solution)/shard_map/pallas_call | solution.py:550
  40.4 2.8 %collective-permute-start.8 = (f32[3,4,1024]{2,1,0:T(4,128)S(1)}, f32[3,4,1024]{2,1,0:T(4,128)S(1)}, u32[]{:S(2)}, u32[]{:S(2)}) collective-permute-start(f32[3,4,1024]{2,1,0:T(4,128)S(1)} %get-tuple-element.53), channel_id=1, source_target_pairs={{4,8},{12,16},{20,24},{28,32},{36,40},{44,48},{52,56},{60,64},{68,... | collective-permute-start | bytes 147464 | tf_op jit(solution)/shard_map/ppermute | solution.py:497
  43.2 1.9 %collective-permute-start.9 = (f32[3,4,1024]{2,1,0:T(4,128)S(1)}, f32[3,4,1024]{2,1,0:T(4,128)S(1)}, u32[]{:S(2)}, u32[]{:S(2)}) collective-permute-start(f32[3,4,1024]{2,1,0:T(4,128)S(1)} %get-tuple-element.54), channel_id=1, source_target_pairs={{0,4},{4,0},{8,12},{12,8},{16,20},{20,16},{24,28},{28,24},{32,36},... | collective-permute-start | bytes 147464 | tf_op jit(solution)/shard_map/ppermute | solution.py:498
  45.2 1.8 %shard_map.65 = (f32[7,8,1024]{2,1,0:T(8,128)S(1)}, f32[7,8,1024]{2,1,0:T(8,128)S(1)}, f32[1,128]{1,0:T(1,128)S(1)}) custom-call(s32[2]{0:T(128)S(1)} %copy-done.3, f32[8,1024]{1,0:T(8,128)S(1)} %copy-done, f32[8,4,1024]{2,1,0:T(4,128)S(1)} %collective-permute-done.cross, f32[8,4,1024]{2,1,0:T(4,128)S(1)} %collective-permute-done.1.chip, ...), custom_call_target="tpu_custom_call" | custom-call | tf_op jit(solution)/shard_map/pallas_call | solution.py:543
  47.0 0.0 collective-permute-done.8.cross_v
  47.0 0.0 collective-permute-done.9.chip_v
  47.0 1.7 %shard_map.66 = (f32[4,8,1024]{2,1,0:T(8,128)S(1)}, f32[128,128]{1,0:T(8,128)S(1)}) custom-call(s32[2]{0:T(128)S(1)} %copy-done.3, f32[4,8,1024]{2,1,0:T(8,128)S(1)} %get-tuple-element.52.v, f32[4,8,1024]{2,1,0:T(8,128)S(1)} %copy-done.1, f32[8,1024]{1,0:T(8,128)S(1)} %copy-done, f32[8,4,1024]{2,1,0:T(4,128)S(1)} %collective-permute-done.cross, ...), custom_call_target="tpu_custom_call" | custom-call | tf_op jit(solution)/shard_map/pallas_call | solution.py:554
  48.7 33.0 %all_to_all.11 = f32[128,1,128]{2,1,0:T(1,128)S(1)} all-to-all(f32[128,1,128]{2,1,0:T(1,128)S(1)} %bitcast.8), channel_id=1, replica_groups=mesh['blk'=128,'rhs'=4] {'blk'}, dimensions={0} | all-to-all | bytes 131072 | tf_op jit(solution)/shard_map/all_to_all | solution.py:557
  81.7 1.9 %shard_map.67 = (f32[4,8,1024]{2,1,0:T(8,128)}, f32[1,16]{1,0:T(1,128)S(1)}) custom-call(s32[2]{0:T(128)S(1)} %copy-done.3, f32[4,8,1024]{2,1,0:T(8,128)S(1)} %get-tuple-element.59.base, f32[7,8,1024]{2,1,0:T(8,128)S(1)} %get-tuple-element.60.phi, f32[128,128]{1,0:T(8,128)S(1)} %bitcast.7), custom_call_target="tpu_custom_call" | custom-call | tf_op jit(solution)/shard_map/pallas_call | solution.py:558
  83.6 9.0 %psum.7 = f32[16]{0:T(128)} all-reduce(f32[16]{0:T(128)S(1)} %bitcast.9), channel_id=1, replica_groups=mesh['blk'=128,'rhs'=4] {'rhs'}, use_global_device_ids=true, to_apply=%region_0.0 | all-reduce | flops 16 | bytes 128 | tf_op jit(solution)/shard_map/psum | solution.py:564
Async XLA Ops:
  1.2 12.0 %copy-start = (f32[8,1024]{1,0:T(8,128)S(1)}, f32[8,1024]{1,0:T(8,128)}, u32[]{:S(2)}) copy-start(f32[8,1024]{1,0:T(8,128)} %ext.13) | copy-start | bytes 98308
  1.2 14.4 %copy-start.1 = (f32[4,8,1024]{2,1,0:T(8,128)S(1)}, f32[4,8,1024]{2,1,0:T(8,128)}, u32[]{:S(2)}) copy-start(f32[4,8,1024]{2,1,0:T(8,128)} %f.3) | copy-start | bytes 393220
  1.2 14.4 %copy-start.2 = (f32[4,8,1024]{2,1,0:T(8,128)S(1)}, f32[4,8,1024]{2,1,0:T(8,128)}, u32[]{:S(2)}) copy-start(f32[4,8,1024]{2,1,0:T(8,128)} %u.1) | copy-start | bytes 393220
  3.8 9.5 %copy-start.3 = (s32[2]{0:T(128)S(1)}, s32[2]{0:T(128)}, u32[]{:S(2)}) copy-start(s32[2]{0:T(128)} %pad_add_fusion.me) | copy-start | bytes 28
  3.8 11.9 %collective-permute-start = (f32[8,4,1024]{2,1,0:T(4,128)}, f32[8,4,1024]{2,1,0:T(4,128)S(1)}, u32[]{:S(2)}, u32[]{:S(2)}) collective-permute-start(f32[8,4,1024]{2,1,0:T(4,128)} %get-tuple-element.33), channel_id=1, source_target_pairs={{4,8},{12,16},{20,24},{28,32},{36,40},{44,48},{52,56},{60,64},{68,... | collective-permute-start | bytes 393224 | tf_op jit(solution)/shard_map/ppermute | solution.py:497
  8.4 7.3 %collective-permute-start.1 = (f32[8,4,1024]{2,1,0:T(4,128)}, f32[8,4,1024]{2,1,0:T(4,128)S(1)}, u32[]{:S(2)}, u32[]{:S(2)}) collective-permute-start(f32[8,4,1024]{2,1,0:T(4,128)} %get-tuple-element.34), channel_id=1, source_target_pairs={{0,4},{4,0},{8,12},{12,8},{16,20},{20,16},{24,28},{28,24},{32,36},... | collective-permute-start | bytes 393224 | tf_op jit(solution)/shard_map/ppermute | solution.py:498
  13.3 0.8 copy-start.4
  17.3 5.2 %collective-permute-start.2 = (f32[8,1024]{1,0:T(8,128)S(1)}, f32[8,1024]{1,0:T(8,128)S(1)}, u32[]{:S(2)}, u32[]{:S(2)}) collective-permute-start(f32[8,1024]{1,0:T(8,128)S(1)} %get-tuple-element.43), channel_id=1, source_target_pairs={{4,8},{12,16},{20,24},{28,32},{36,40},{44,48},{52,56},{60,64},{68,... | collective-permute-start | bytes 98312 | tf_op jit(solution)/shard_map/ppermute | solution.py:497
  19.2 3.3 %collective-permute-start.3 = (f32[8,1024]{1,0:T(8,128)S(1)}, f32[8,1024]{1,0:T(8,128)S(1)}, u32[]{:S(2)}, u32[]{:S(2)}) collective-permute-start(f32[8,1024]{1,0:T(8,128)S(1)} %get-tuple-element.44), channel_id=1, source_target_pairs={{0,4},{4,0},{8,12},{12,8},{16,20},{20,16},{24,28},{28,24},{32,36},... | collective-permute-start | bytes 98312 | tf_op jit(solution)/shard_map/ppermute | solution.py:498
  24.9 6.3 %collective-permute-start.4 = (f32[4,8,1024]{2,1,0:T(8,128)S(1)}, f32[4,8,1024]{2,1,0:T(8,128)S(1)}, u32[]{:S(2)}, u32[]{:S(2)}) collective-permute-start(f32[4,8,1024]{2,1,0:T(8,128)S(1)} %get-tuple-element.46), channel_id=1, source_target_pairs={{4,8},{12,16},{20,24},{28,32},{36,40},{44,48},{52,56},{60,64},{68,... | collective-permute-start | bytes 393224 | tf_op jit(solution)/shard_map/ppermute | solution.py:497
  28.3 3.2 %collective-permute-start.5 = (f32[4,8,1024]{2,1,0:T(8,128)S(1)}, f32[4,8,1024]{2,1,0:T(8,128)S(1)}, u32[]{:S(2)}, u32[]{:S(2)}) collective-permute-start(f32[4,8,1024]{2,1,0:T(8,128)S(1)} %get-tuple-element.47), channel_id=1, source_target_pairs={{0,4},{4,0},{8,12},{12,8},{16,20},{20,16},{24,28},{28,24},{32,36},... | collective-permute-start | bytes 393224 | tf_op jit(solution)/shard_map/ppermute | solution.py:498
  32.9 5.1 %collective-permute-start.6 = (f32[4,1024]{1,0:T(4,128)S(1)}, f32[4,1024]{1,0:T(4,128)S(1)}, u32[]{:S(2)}, u32[]{:S(2)}) collective-permute-start(f32[4,1024]{1,0:T(4,128)S(1)} %get-tuple-element.50), channel_id=1, source_target_pairs={{4,8},{12,16},{20,24},{28,32},{36,40},{44,48},{52,56},{60,64},{68,... | collective-permute-start | bytes 49160 | tf_op jit(solution)/shard_map/ppermute | solution.py:497
  36.0 3.1 %collective-permute-start.7 = (f32[4,1024]{1,0:T(4,128)S(1)}, f32[4,1024]{1,0:T(4,128)S(1)}, u32[]{:S(2)}, u32[]{:S(2)}) collective-permute-start(f32[4,1024]{1,0:T(4,128)S(1)} %get-tuple-element.51), channel_id=1, source_target_pairs={{0,4},{4,0},{8,12},{12,8},{16,20},{20,16},{24,28},{28,24},{32,36},... | collective-permute-start | bytes 49160 | tf_op jit(solution)/shard_map/ppermute | solution.py:498
  40.4 6.5 %collective-permute-start.8 = (f32[3,4,1024]{2,1,0:T(4,128)S(1)}, f32[3,4,1024]{2,1,0:T(4,128)S(1)}, u32[]{:S(2)}, u32[]{:S(2)}) collective-permute-start(f32[3,4,1024]{2,1,0:T(4,128)S(1)} %get-tuple-element.53), channel_id=1, source_target_pairs={{4,8},{12,16},{20,24},{28,32},{36,40},{44,48},{52,56},{60,64},{68,... | collective-permute-start | bytes 147464 | tf_op jit(solution)/shard_map/ppermute | solution.py:497
  43.2 3.7 %collective-permute-start.9 = (f32[3,4,1024]{2,1,0:T(4,128)S(1)}, f32[3,4,1024]{2,1,0:T(4,128)S(1)}, u32[]{:S(2)}, u32[]{:S(2)}) collective-permute-start(f32[3,4,1024]{2,1,0:T(4,128)S(1)} %get-tuple-element.54), channel_id=1, source_target_pairs={{0,4},{4,0},{8,12},{12,8},{16,20},{20,16},{24,28},{28,24},{32,36},... | collective-permute-start | bytes 147464 | tf_op jit(solution)/shard_map/ppermute | solution.py:498

commit v5 on v4

--- a/solution.py
+++ b/solution.py
@@ -13,20 +13,27 @@
 F32 = jnp.float32
 
 
-def vmem_call(body, outs, scratch=(), smem_args=(), n_in=0):
-    in_specs = [
-        pl.BlockSpec(memory_space=pltpu.SMEM if k in smem_args else pltpu.VMEM)
-        for k in range(n_in)
-    ]
+VMEM = pl.BlockSpec(memory_space=pltpu.VMEM)
+
+
+def with_place(body):
+    def kernel(*refs):
+        body((lax.axis_index("blk"), lax.axis_index("rhs")), *refs)
+
+    return kernel
+
+
+def vmem_call(body, outs, scratch=(), n_in=0, in_space=pltpu.VMEM):
+    limit = 48 << 20 if in_space == pltpu.VMEM else None
     return pl.pallas_call(
-        body,
+        with_place(body),
         out_shape=[
             jax.ShapeDtypeStruct(*(s if isinstance(s[0], tuple) else (s, F32))) for s in outs
         ],
-        in_specs=in_specs,
-        out_specs=[pl.BlockSpec(memory_space=pltpu.VMEM)] * len(outs),
+        in_specs=[pl.BlockSpec(memory_space=in_space)] * n_in,
+        out_specs=[VMEM] * len(outs),
         scratch_shapes=list(scratch),
-        compiler_params=pltpu.CompilerParams(vmem_limit_bytes=48 << 20),
+        compiler_params=pltpu.CompilerParams(vmem_limit_bytes=limit),
     )
 
 
@@ -151,33 +158,39 @@
     return weight
 
 
+GROUP_EXT = 5
+
+
 def pack_kernel(me, u_hbm, f_hbm, ext_hbm, cross, chip, u, f, ext, sem):
-    copies = [
-        pltpu.make_async_copy(src, dst, sem.at[k])
-        for k, (src, dst) in enumerate(((u_hbm, u), (f_hbm, f), (ext_hbm, ext)))
-    ]
+    pairs = ((u_hbm, u), (f_hbm, f), (ext_hbm, ext))
+    copies = [pltpu.make_async_copy(src, dst, sem.at[k]) for k, (src, dst) in enumerate(pairs)]
     for copy in copies:
         copy.start()
     for copy in copies:
         copy.wait()
     cases, rows, width = u.shape
     put = sender(me, cross, chip)
-    ones = jnp.ones((cases, width), F32)
+    ones = jnp.ones((1, width), F32)
     end = rows - 1
     for k in range(3):
         put(k, u[:, k, :], u[:, end - k, :])
     for k in range(2):
         put(3 + k, f[:, k, :], f[:, end - k, :])
-        put(
-            5 + k,
-            jnp.broadcast_to(ext[pl.ds(k, 1), :], (cases, width)),
-            jnp.broadcast_to(ext[pl.ds(end - k, 1), :], (cases, width)),
-        )
-    put(7, ones, ones)
+        at = (GROUP_EXT,) + row_of(k)
+        put(at, ext[pl.ds(k, 1), :], ext[pl.ds(end - k, 1), :])
+    for k in range(2, cases):
+        put((GROUP_EXT,) + row_of(k), ones, ones)
 
 
 def both(before, after, k):
     return jnp.concatenate([before[k], after[k]], axis=0)
+
+
+def spread(before, after, k, times):
+    at = (GROUP_EXT,) + row_of(k)
+    up, down = before[at], after[at]
+    shape = (times, up.shape[1])
+    return jnp.concatenate([jnp.broadcast_to(up, shape), jnp.broadcast_to(down, shape)], axis=0)
 
 
 def two_sweeps(u, u_halo, f, f_halo, diag, diag_halo, valid):
@@ -240,8 +253,8 @@
     fl = [f[c] for c in range(cases)]
     u_halo = [both(before, after, k) for k in range(3)]
     f_halo = [both(before, after, 3 + k) for k in range(2)]
-    d_halo = [4.0 + both(before, after, 5 + k) for k in range(2)]
-    valid = both(before, after, 7)
+    d_halo = [4.0 + spread(before, after, k, cases) for k in range(2)]
+    valid = spread(before, after, 2, cases)
     x, res = two_sweeps(us, u_halo, fl, f_halo, diag, d_halo, valid)
     for c in range(cases):
         smooth[c] = x[c]
@@ -264,6 +277,10 @@
     w = [diag * x[c] - neighbours(x[c], above[c], below[c]) for c in range(cases)]
     sums = seg_sum(w, tables)
     return [x[c] + h[...] * (b[c] - sums[c]) for c in range(cases)]
+
+
+def x1_row(c):
+    return (c // 3,) + row_of(5 + c % 3)
 
 
 def coarse_kernel_a(me, x0, ext, b, row_at, row_ok, same_col, h, y3, rsum, cross, chip, x1, y4, to_cross, to_chip, part):
@@ -279,16 +296,16 @@
     below = below + [after[pl.ds(cases + j, 1), :] for j in range(3)]
     rhs = [b[c] for c in range(cases)] + [none] * 5
     x = coarse_step(old, above, below, ext, rhs, h, tables)
-    no_rows = jnp.zeros((8, width), F32)
-    for k in range(4):
-        put(k, no_rows, no_rows)
-    for c in range(cases):
-        put((0,) + row_of(c), x[c][0:1], x[c][rows - 1 : rows])
+    for c in range(cases):
+        put(x1_row(c), x[c][0:1], x[c][rows - 1 : rows])
+    no_row = jnp.zeros((1, width), F32)
+    for c in range(cases, 9):
+        put(x1_row(c), no_row, no_row)
     for j in range(5):
         y = x[cases + j]
         y4[j] = y
         for k in range(3):
-            put((1 + k,) + row_of(j), y[k : k + 1], y[rows - 1 - k : rows - k])
+            put((k,) + row_of(j), y[k : k + 1], y[rows - 1 - k : rows - k])
     weight = open_weight(ext[...])
     values = []
     for c in range(cases):
@@ -321,16 +338,11 @@
     two_rows = jnp.zeros((2, width), F32)
     halo = []
     for k in range(3):
-        up, down = ab[1 + k], be[1 + k]
+        up, down = ab[k], be[k]
         halo.append(jnp.concatenate([up[0:5], two_rows, two_rows, down[0:5]], axis=0))
 
-    def spread(k):
-        up = jnp.broadcast_to(before[k][0:1], (m, width))
-        down = jnp.broadcast_to(after[k][0:1], (m, width))
-        return jnp.concatenate([up, down], axis=0)
-
-    d_halo = [4.0 + spread(5 + k) for k in range(2)]
-    x, res = two_sweeps(fields, halo, None, None, diag, d_halo, spread(7))
+    d_halo = [4.0 + spread(before, after, k, m) for k in range(2)]
+    x, res = two_sweeps(fields, halo, None, None, diag, d_halo, spread(before, after, 2, m))
     for j in range(m):
         phi[j] = x[j]
     every = res[0]
@@ -382,8 +394,8 @@
     cases, rows, _ = x1.shape
     x = coarse_step(
         [x1[c] for c in range(cases)],
-        [ab[(0,) + row_of(c)] for c in range(cases)],
-        [be[(0,) + row_of(c)] for c in range(cases)],
+        [ab[x1_row(c)] for c in range(cases)],
+        [be[x1_row(c)] for c in range(cases)],
         ext, b, h, (row_at, row_ok, same_col),
     )
     for c in range(cases):
@@ -417,8 +429,8 @@
     fl = [f[c] for c in range(cases)]
     v_halo = [both(before_v, after_v, k) for k in range(3)]
     f_halo = [both(before, after, 3 + k) for k in range(2)]
-    d_halo = [4.0 + both(before, after, 5 + k) for k in range(2)]
-    valid = both(before, after, 7)
+    d_halo = [4.0 + spread(before, after, k, cases) for k in range(2)]
+    valid = spread(before, after, 2, cases)
     x, res = two_sweeps([v[c] for c in range(cases)], v_halo, fl, f_halo, diag, d_halo, valid)
     for c in range(cases):
         out[c] = x[c]
@@ -483,6 +495,14 @@
     ratio[...] = mine[:, : ratio.shape[1]]
 
 
+def doubling(n):
+    step, steps = 1, []
+    while step < n:
+        steps.append([(i, i ^ (2 * step - 1)) for i in range(n)])
+        step *= 2
+    return steps
+
+
 def local(thermal_solution, heat_forcing, extinction_factor, cluster_label):
     cases, rows, width = thermal_solution.shape
     n = lax.axis_size("blk")
@@ -499,23 +519,21 @@
 
     edge = (cases, width)
     edges = (8, width)
-    deep = (4, 8, width)
+    deep = (3, 8, width)
+    cells = (rows, width)
     u, f, ext, lab = thermal_solution, heat_forcing, extinction_factor, cluster_label
-    me = jnp.stack([lax.axis_index("blk"), lax.axis_index("rhs")]).astype(jnp.int32)
-    cells = (rows, width)
-    hbm = pl.BlockSpec(memory_space=pl.ANY)
-    sent = pl.pallas_call(
+    sent = vmem_call(
         pack_kernel,
-        out_shape=[jax.ShapeDtypeStruct((8, cases, width), F32)] * 2,
-        in_specs=[pl.BlockSpec(memory_space=pltpu.SMEM), hbm, hbm, hbm],
-        out_specs=[pl.BlockSpec(memory_space=pltpu.VMEM)] * 2,
-        scratch_shapes=[
+        [(6, cases, width)] * 2,
+        [
             pltpu.VMEM(field, F32),
             pltpu.VMEM(field, F32),
             pltpu.VMEM(cells, F32),
             pltpu.SemaphoreType.DMA((3,)),
         ],
-    )(me, u, f, ext)
+        n_in=3,
+        in_space=pl.ANY,
+    )(u, f, ext)
     halo = exchange(*sent)
     shifts = len(offsets())
     *tables, y3 = vmem_call(
@@ -527,41 +545,43 @@
             cells,
             (3, rows, width),
         ],
-        smem_args=(0,),
-        n_in=3,
-    )(me, ext, lab)
-    call = functools.partial(vmem_call, smem_args=(0,))
+        n_in=2,
+    )(ext, lab)
+    call = vmem_call
     smooth, b, x0, *sent, rsum = call(
-        pre_kernel, [field, field, field, edges, edges, (1, 128)], n_in=11
-    )(me, u, f, ext, *halo, *tables, y3)
+        pre_kernel, [field, field, field, edges, edges, (1, 128)], n_in=10
+    )(u, f, ext, *halo, *tables, y3)
     rows_x = exchange(*sent)
     x1, y4, *sent, part_a = call(
-        coarse_kernel_a, [field, (5, rows, width), deep, deep, (1, 128)], n_in=12
-    )(me, x0, ext, b, *tables, y3, rsum, *rows_x)
+        coarse_kernel_a, [field, (5, rows, width), deep, deep, (1, 128)], n_in=11
+    )(x0, ext, b, *tables, y3, rsum, *rows_x)
     rows_x = exchange(*sent)
     m = 2 * REACH_E + 1
     phi, q, part_e = call(
-        response_kernel, [(m, rows, width), (m, rows, width), (1, 128)], n_in=7
-    )(me, ext, *halo, y4, *rows_x)
-    x3, *sent = call(coarse_kernel_b, [field, edge, edge], n_in=10)(
-        me, x1, ext, b, *tables, *rows_x
+        response_kernel, [(m, rows, width), (m, rows, width), (1, 128)], n_in=6
+    )(ext, *halo, y4, *rows_x)
+    x3, *sent = call(coarse_kernel_b, [field, edge, edge], n_in=9)(
+        x1, ext, b, *tables, *rows_x
     )
     rows_x = exchange(*sent)
     v, *sent = call(
-        coarse_kernel_c, [field, (3, cases, width), (3, cases, width)], n_in=11
-    )(me, x3, ext, b, *tables, smooth, *rows_x)
+        coarse_kernel_c, [field, (3, cases, width), (3, cases, width)], n_in=10
+    )(x3, ext, b, *tables, smooth, *rows_x)
     rows_x = exchange(*sent)
-    base, mine = call(post_kernel, [field, (n, 128)], n_in=11)(
-        me, v, f, ext, *halo, *rows_x, q, part_a, part_e
+    base, mine = call(post_kernel, [field, (n, 128)], n_in=10)(
+        v, f, ext, *halo, *rows_x, q, part_a, part_e
     )
     gathered = lax.all_to_all(mine, "blk", 0, 0, tiled=True)
     corrected, ratio = call(
         functools.partial(final_kernel, groups),
         [field, (1, n_rhs * cases)],
         [pltpu.VMEM((n + 16, 128), F32)],
-        n_in=4,
-    )(me, base, phi, gathered)
-    return corrected, lax.psum(ratio.reshape(n_rhs * cases), "rhs")
+        n_in=3,
+    )(base, phi, gathered)
+    ratio = ratio.reshape(n_rhs * cases)
+    for step in doubling(n_rhs):
+        ratio = ratio + lax.ppermute(ratio, "rhs", step)
+    return corrected, ratio
 
 
 def solution(mesh):

time: 93.3 us -> 90.8 us (0.973)
  the two profiles are of different devices: /device:TPU:1 before, /device:TPU:6 now
where the time goes in v5:
time: 90.8 us; the launch traced here: 90.3 us
  starting transfers between devices  33.8 us (37%)
  blocking collectives  33.3 us (37%)
  Pallas kernels  11.4 us (13%)
  waiting for transfers between devices  9.51 us (10%)
    all_to_all x1, blocking collectives, local(): gathered = lax.all_to_all(mine, 'blk', 0, 0, tiled=True)  33.3 us
    ppermute x5, starting transfers between devices, exchange(): return (cross, lax.ppermute(chip, 'blk', on_chip))  25.4 us
    ppermute x2, waiting for transfers between devices, local(): ratio = ratio + lax.ppermute(ratio, 'rhs', step)  6.94 us
    ppermute x2, starting transfers between devices, local(): ratio = ratio + lax.ppermute(ratio, 'rhs', step)  5.1 us
    ppermute x5, starting transfers between devices, exchange(): cross = lax.ppermute(cross, 'blk', cross_chip)  3.32 us
    ppermute x5, waiting for transfers between devices, exchange(): return (cross, lax.ppermute(chip, 'blk', on_chip))  2.55 us
  transfers between devices with their start and end apart: 12, of which 5 were waited for; matrix products, arithmetic and copies ran while one was open for 0% of the time, Pallas kernels for 3%

profile of v5, /device:TPU:6, one launch (start us, length us, event | category | flops | bytes accessed | tf_op | source)
XLA Modules:
  0.0 90.3 jit_solution(17567215841035357256)
XLA Ops:
  0.6 0.0 copy-start
  0.6 0.0 copy-start.1
  0.6 0.0 copy-start.2
  0.7 1.7 %shard_map.59 = (f32[6,4,1024]{2,1,0:T(4,128)}, f32[6,4,1024]{2,1,0:T(4,128)}) custom-call(f32[4,8,1024]{2,1,0:T(8,128)} %refs_0_.6, f32[4,8,1024]{2,1,0:T(8,128)} %refs_1_.13, f32[8,1024]{1,0:T(8,128)} %refs_2_.5), custom_call_target="tpu_custom_call" | custom-call | tf_op jit(solution)/shard_map/pallas_call | solution.py:525
  2.4 0.7 collective-permute-start
  3.1 4.8 %collective-permute-start.1 = (f32[6,4,1024]{2,1,0:T(4,128)}, f32[6,4,1024]{2,1,0:T(4,128)S(1)}, u32[]{:S(2)}, u32[]{:S(2)}) collective-permute-start(f32[6,4,1024]{2,1,0:T(4,128)} %get-tuple-element.34), channel_id=1, source_target_pairs={{0,4},{4,0},{8,12},{12,8},{16,20},{20,16},{24,28},{28,24},{32,36},... | collective-permute-start | bytes 294920 | tf_op jit(solution)/shard_map/ppermute | solution.py:518
  7.9 0.0 copy-done
  7.9 0.0 copy-start.3
  8.0 0.7 copy-done.3
  8.7 1.1 %shard_map.60 = (s32[14,8,1024]{2,1,0:T(8,128)S(1)}, f32[14,8,1024]{2,1,0:T(8,128)S(1)}, f32[7,8,1024]{2,1,0:T(8,128)S(1)}, f32[8,1024]{1,0:T(8,128)S(1)}, f32[3,8,1024]{2,1,0:T(8,128)S(1)}) custom-call(f32[8,1024]{1,0:T(8,128)S(1)} %copy-done, s32[8,1024]{1,0:T(8,128)S(1)} %copy-done.3), custom_call_target="tpu_custom_call" | custom-call | tf_op jit(solution)/shard_map/pallas_call | solution.py:539
  9.8 0.0 collective-permute-done.refs_3_.refs_1_
  9.8 0.0 collective-permute-done.1.refs_4_.refs_2_
  9.8 0.0 copy-done.1
  9.8 0.0 copy-done.2
  9.8 1.0 %shard_map.61 = (f32[4,8,1024]{2,1,0:T(8,128)S(1)}, f32[4,8,1024]{2,1,0:T(8,128)S(1)}, f32[4,8,1024]{2,1,0:T(8,128)S(1)}, f32[8,1024]{1,0:T(8,128)S(1)}, f32[8,1024]{1,0:T(8,128)S(1)}, /*index=5*/f32[1,128]{1,0:T(1,128)S(1)}) custom-call(f32[4,8,1024]{2,1,0:T(8,128)S(1)} %copy-done.2, f32[4,8,1024]{2,1,0:T(8,128)S(1)} %copy-done.1, f32[8,1024]{1,0:T(8,128)S(1)} %copy-done, ...), custom_call_target="tpu_custom_call" | custom-call | tf_op jit(solution)/shard_map/pallas_call | solution.py:551
  10.9 0.7 collective-permute-start.2
  11.5 4.8 %collective-permute-start.3 = (f32[8,1024]{1,0:T(8,128)S(1)}, f32[8,1024]{1,0:T(8,128)S(1)}, u32[]{:S(2)}, u32[]{:S(2)}) collective-permute-start(f32[8,1024]{1,0:T(8,128)S(1)} %get-tuple-element.44), channel_id=1, source_target_pairs={{0,4},{4,0},{8,12},{12,8},{16,20},{20,16},{24,28},{28,24},{32,36},... | collective-permute-start | bytes 98312 | tf_op jit(solution)/shard_map/ppermute | solution.py:518
  16.4 0.0 collective-permute-done.2.refs_9_
  16.4 0.8 collective-permute-done.3.refs_10_
  17.2 1.8 %shard_map.62 = (f32[4,8,1024]{2,1,0:T(8,128)S(1)}, f32[5,8,1024]{2,1,0:T(8,128)S(1)}, f32[3,8,1024]{2,1,0:T(8,128)S(1)}, f32[3,8,1024]{2,1,0:T(8,128)S(1)}, f32[1,128]{1,0:T(1,128)S(1)}) custom-call(f32[4,8,1024]{2,1,0:T(8,128)S(1)} %get-tuple-element.40.refs_0_, f32[8,1024]{1,0:T(8,128)S(1)} %copy-done, f32[4,8,1024]{2,1,0:T(8,128)S(1)} %get-tuple-element.41.refs_2_, ...), custom_call_target="tpu_custom_call" | custom-call | tf_op jit(solution)/shard_map/pallas_call | solution.py:555
  19.0 0.7 collective-permute-start.4
  19.7 4.8 %collective-permute-start.5 = (f32[3,8,1024]{2,1,0:T(8,128)S(1)}, f32[3,8,1024]{2,1,0:T(8,128)S(1)}, u32[]{:S(2)}, u32[]{:S(2)}) collective-permute-start(f32[3,8,1024]{2,1,0:T(8,128)S(1)} %get-tuple-element.47), channel_id=1, source_target_pairs={{0,4},{4,0},{8,12},{12,8},{16,20},{20,16},{24,28},{28,24},{32,36},... | collective-permute-start | bytes 294920 | tf_op jit(solution)/shard_map/ppermute | solution.py:518
  24.5 0.0 collective-permute-done.4.refs_7_.refs_4_
  24.5 0.9 %collective-permute-done.5.refs_8_.refs_5_ = f32[3,8,1024]{2,1,0:T(8,128)S(1)} collective-permute-done((f32[3,8,1024]{2,1,0:T(8,128)S(1)}, f32[3,8,1024]{2,1,0:T(8,128)S(1)}, u32[]{:S(2)}, u32[]{:S(2)}) %collective-permute-start.5) | collective-permute-done | bytes 98336 | tf_op jit(solution)/shard_map/ppermute | solution.py:518
  25.4 0.8 shard_map.63
  26.2 0.7 collective-permute-start.6
  26.9 6.1 %collective-permute-start.7 = (f32[4,1024]{1,0:T(4,128)S(1)}, f32[4,1024]{1,0:T(4,128)S(1)}, u32[]{:S(2)}, u32[]{:S(2)}) collective-permute-start(f32[4,1024]{1,0:T(4,128)S(1)} %get-tuple-element.51), channel_id=1, source_target_pairs={{0,4},{4,0},{8,12},{12,8},{16,20},{20,16},{24,28},{28,24},{32,36},... | collective-permute-start | bytes 49160 | tf_op jit(solution)/shard_map/ppermute | solution.py:518
  33.0 0.0 collective-permute-done.6.refs_8_
  33.0 0.8 collective-permute-done.7.refs_9_
  33.8 0.8 shard_map.64
  34.6 0.7 collective-permute-start.8
  35.3 4.8 %collective-permute-start.9 = (f32[3,4,1024]{2,1,0:T(4,128)S(1)}, f32[3,4,1024]{2,1,0:T(4,128)S(1)}, u32[]{:S(2)}, u32[]{:S(2)}) collective-permute-start(f32[3,4,1024]{2,1,0:T(4,128)S(1)} %get-tuple-element.54), channel_id=1, source_target_pairs={{0,4},{4,0},{8,12},{12,8},{16,20},{20,16},{24,28},{28,24},{32,36},... | collective-permute-start | bytes 147464 | tf_op jit(solution)/shard_map/ppermute | solution.py:518
  40.1 1.3 %shard_map.65 = (f32[7,8,1024]{2,1,0:T(8,128)S(1)}, f32[7,8,1024]{2,1,0:T(8,128)S(1)}, f32[1,128]{1,0:T(1,128)S(1)}) custom-call(f32[8,1024]{1,0:T(8,128)S(1)} %copy-done, f32[6,4,1024]{2,1,0:T(4,128)S(1)} %collective-permute-done.refs_3_.refs_1_, f32[6,4,1024]{2,1,0:T(4,128)S(1)} %collective-permute-done.1.refs_4_.refs_2_, ...), custom_call_target="tpu_custom_call" | custom-call | tf_op jit(solution)/shard_map/pallas_call | solution.py:560
  41.4 0.0 collective-permute-done.8.refs_5_
  41.4 0.0 collective-permute-done.9.refs_6_
  41.4 1.2 %shard_map.66 = (f32[4,8,1024]{2,1,0:T(8,128)S(1)}, f32[128,128]{1,0:T(8,128)S(1)}) custom-call(f32[4,8,1024]{2,1,0:T(8,128)S(1)} %get-tuple-element.52.refs_0_, f32[4,8,1024]{2,1,0:T(8,128)S(1)} %copy-done.1, f32[8,1024]{1,0:T(8,128)S(1)} %copy-done, f32[6,4,1024]{2,1,0:T(4,128)S(1)} %collective-permute-done.refs_3_.refs_1_, ...), custom_call_target="tpu_custom_call" | custom-call | tf_op jit(solution)/shard_map/pallas_call | solution.py:571
  42.6 33.3 %all_to_all.11 = f32[128,1,128]{2,1,0:T(1,128)S(1)} all-to-all(f32[128,1,128]{2,1,0:T(1,128)S(1)} %bitcast.7), channel_id=1, replica_groups=mesh['blk'=128,'rhs'=4] {'blk'}, dimensions={0} | all-to-all | bytes 131072 | tf_op jit(solution)/shard_map/all_to_all | solution.py:574
  75.9 1.8 %shard_map.67 = (f32[4,8,1024]{2,1,0:T(8,128)}, f32[1,16]{1,0:T(1,128)S(1)}) custom-call(f32[4,8,1024]{2,1,0:T(8,128)S(1)} %get-tuple-element.59.refs_0_, f32[7,8,1024]{2,1,0:T(8,128)S(1)} %get-tuple-element.60.refs_1_, f32[128,128]{1,0:T(8,128)S(1)} %bitcast.6), custom_call_target="tpu_custom_call" | custom-call | tf_op jit(solution)/shard_map/pallas_call | solution.py:575
  77.7 2.7 %collective-permute-start.10 = (f32[16]{0:T(128)S(1)}, f32[16]{0:T(128)S(1)}, u32[]{:S(2)}, u32[]{:S(2)}) collective-permute-start(f32[16]{0:T(128)S(1)} %bitcast.8), channel_id=1, source_target_pairs={{0,1},{1,0},{2,3},{3,2},{4,5},{5,4},{6,7},{7,6},{8,9},{9,8},{10,11... | collective-permute-start | bytes 200 | tf_op jit(solution)/shard_map/ppermute | solution.py:583
  80.4 2.7 %collective-permute-done.10 = f32[16]{0:T(128)S(1)} collective-permute-done((f32[16]{0:T(128)S(1)}, f32[16]{0:T(128)S(1)}, u32[]{:S(2)}, u32[]{:S(2)}) %collective-permute-start.10) | collective-permute-done | bytes 96 | tf_op jit(solution)/shard_map/ppermute | solution.py:583
  83.1 2.4 %collective-permute-start.11 = (f32[16]{0:T(128)S(1)}, f32[16]{0:T(128)S(1)}, u32[]{:S(2)}, u32[]{:S(2)}) collective-permute-start(f32[16]{0:T(128)S(1)} %bitcast_add_fusion), channel_id=1, source_target_pairs={{0,3},{1,2},{2,1},{3,0},{4,7},{5,6},{6,5},{7,4},{8,11},{9,10},{10,... | collective-permute-start | bytes 200 | tf_op jit(solution)/shard_map/ppermute | solution.py:583
  85.5 4.3 %collective-permute-done.11 = f32[16]{0:T(128)S(1)} collective-permute-done((f32[16]{0:T(128)S(1)}, f32[16]{0:T(128)S(1)}, u32[]{:S(2)}, u32[]{:S(2)}) %collective-permute-start.11) | collective-permute-done | bytes 96 | tf_op jit(solution)/shard_map/ppermute | solution.py:583
  89.8 0.5 add.7
  (1 shorter events, 0.0 us)
Async XLA Ops:
  0.6 7.3 %copy-start = (f32[8,1024]{1,0:T(8,128)S(1)}, f32[8,1024]{1,0:T(8,128)}, u32[]{:S(2)}) copy-start(f32[8,1024]{1,0:T(8,128)} %refs_2_.5) | copy-start | bytes 98308
  0.6 9.2 %copy-start.1 = (f32[4,8,1024]{2,1,0:T(8,128)S(1)}, f32[4,8,1024]{2,1,0:T(8,128)}, u32[]{:S(2)}) copy-start(f32[4,8,1024]{2,1,0:T(8,128)} %refs_1_.13) | copy-start | bytes 393220
  0.6 9.2 %copy-start.2 = (f32[4,8,1024]{2,1,0:T(8,128)S(1)}, f32[4,8,1024]{2,1,0:T(8,128)}, u32[]{:S(2)}) copy-start(f32[4,8,1024]{2,1,0:T(8,128)} %refs_0_.6) | copy-start | bytes 393220
  2.4 7.4 %collective-permute-start = (f32[6,4,1024]{2,1,0:T(4,128)}, f32[6,4,1024]{2,1,0:T(4,128)S(1)}, u32[]{:S(2)}, u32[]{:S(2)}) collective-permute-start(f32[6,4,1024]{2,1,0:T(4,128)} %get-tuple-element.33), channel_id=1, source_target_pairs={{4,8},{12,16},{20,24},{28,32},{36,40},{44,48},{52,56},{60,64},{68,... | collective-permute-start | bytes 294920 | tf_op jit(solution)/shard_map/ppermute | solution.py:517
  3.1 6.7 %collective-permute-start.1 = (f32[6,4,1024]{2,1,0:T(4,128)}, f32[6,4,1024]{2,1,0:T(4,128)S(1)}, u32[]{:S(2)}, u32[]{:S(2)}) collective-permute-start(f32[6,4,1024]{2,1,0:T(4,128)} %get-tuple-element.34), channel_id=1, source_target_pairs={{0,4},{4,0},{8,12},{12,8},{16,20},{20,16},{24,28},{28,24},{32,36},... | collective-permute-start | bytes 294920 | tf_op jit(solution)/shard_map/ppermute | solution.py:518
  7.9 0.8 copy-start.3
  10.9 5.5 %collective-permute-start.2 = (f32[8,1024]{1,0:T(8,128)S(1)}, f32[8,1024]{1,0:T(8,128)S(1)}, u32[]{:S(2)}, u32[]{:S(2)}) collective-permute-start(f32[8,1024]{1,0:T(8,128)S(1)} %get-tuple-element.43), channel_id=1, source_target_pairs={{4,8},{12,16},{20,24},{28,32},{36,40},{44,48},{52,56},{60,64},{68,... | collective-permute-start | bytes 98312 | tf_op jit(solution)/shard_map/ppermute | solution.py:517
  11.5 5.7 %collective-permute-start.3 = (f32[8,1024]{1,0:T(8,128)S(1)}, f32[8,1024]{1,0:T(8,128)S(1)}, u32[]{:S(2)}, u32[]{:S(2)}) collective-permute-start(f32[8,1024]{1,0:T(8,128)S(1)} %get-tuple-element.44), channel_id=1, source_target_pairs={{0,4},{4,0},{8,12},{12,8},{16,20},{20,16},{24,28},{28,24},{32,36},... | collective-permute-start | bytes 98312 | tf_op jit(solution)/shard_map/ppermute | solution.py:518
  19.0 5.5 %collective-permute-start.4 = (f32[3,8,1024]{2,1,0:T(8,128)S(1)}, f32[3,8,1024]{2,1,0:T(8,128)S(1)}, u32[]{:S(2)}, u32[]{:S(2)}) collective-permute-start(f32[3,8,1024]{2,1,0:T(8,128)S(1)} %get-tuple-element.46), channel_id=1, source_target_pairs={{4,8},{12,16},{20,24},{28,32},{36,40},{44,48},{52,56},{60,64},{68,... | collective-permute-start | bytes 294920 | tf_op jit(solution)/shard_map/ppermute | solution.py:517
  19.7 5.8 %collective-permute-start.5 = (f32[3,8,1024]{2,1,0:T(8,128)S(1)}, f32[3,8,1024]{2,1,0:T(8,128)S(1)}, u32[]{:S(2)}, u32[]{:S(2)}) collective-permute-start(f32[3,8,1024]{2,1,0:T(8,128)S(1)} %get-tuple-element.47), channel_id=1, source_target_pairs={{0,4},{4,0},{8,12},{12,8},{16,20},{20,16},{24,28},{28,24},{32,36},... | collective-permute-start | bytes 294920 | tf_op jit(solution)/shard_map/ppermute | solution.py:518
  26.2 6.7 %collective-permute-start.6 = (f32[4,1024]{1,0:T(4,128)S(1)}, f32[4,1024]{1,0:T(4,128)S(1)}, u32[]{:S(2)}, u32[]{:S(2)}) collective-permute-start(f32[4,1024]{1,0:T(4,128)S(1)} %get-tuple-element.50), channel_id=1, source_target_pairs={{4,8},{12,16},{20,24},{28,32},{36,40},{44,48},{52,56},{60,64},{68,... | collective-permute-start | bytes 49160 | tf_op jit(solution)/shard_map/ppermute | solution.py:517
  26.9 6.9 %collective-permute-start.7 = (f32[4,1024]{1,0:T(4,128)S(1)}, f32[4,1024]{1,0:T(4,128)S(1)}, u32[]{:S(2)}, u32[]{:S(2)}) collective-permute-start(f32[4,1024]{1,0:T(4,128)S(1)} %get-tuple-element.51), channel_id=1, source_target_pairs={{0,4},{4,0},{8,12},{12,8},{16,20},{20,16},{24,28},{28,24},{32,36},... | collective-permute-start | bytes 49160 | tf_op jit(solution)/shard_map/ppermute | solution.py:518
  34.6 6.8 %collective-permute-start.8 = (f32[3,4,1024]{2,1,0:T(4,128)S(1)}, f32[3,4,1024]{2,1,0:T(4,128)S(1)}, u32[]{:S(2)}, u32[]{:S(2)}) collective-permute-start(f32[3,4,1024]{2,1,0:T(4,128)S(1)} %get-tuple-element.53), channel_id=1, source_target_pairs={{4,8},{12,16},{20,24},{28,32},{36,40},{44,48},{52,56},{60,64},{68,... | collective-permute-start | bytes 147464 | tf_op jit(solution)/shard_map/ppermute | solution.py:517
  35.3 6.1 %collective-permute-start.9 = (f32[3,4,1024]{2,1,0:T(4,128)S(1)}, f32[3,4,1024]{2,1,0:T(4,128)S(1)}, u32[]{:S(2)}, u32[]{:S(2)}) collective-permute-start(f32[3,4,1024]{2,1,0:T(4,128)S(1)} %get-tuple-element.54), channel_id=1, source_target_pairs={{0,4},{4,0},{8,12},{12,8},{16,20},{20,16},{24,28},{28,24},{32,36},... | collective-permute-start | bytes 147464 | tf_op jit(solution)/shard_map/ppermute | solution.py:518
  77.7 5.4 %collective-permute-start.10 = (f32[16]{0:T(128)S(1)}, f32[16]{0:T(128)S(1)}, u32[]{:S(2)}, u32[]{:S(2)}) collective-permute-start(f32[16]{0:T(128)S(1)} %bitcast.8), channel_id=1, source_target_pairs={{0,1},{1,0},{2,3},{3,2},{4,5},{5,4},{6,7},{7,6},{8,9},{9,8},{10,11... | collective-permute-start | bytes 200 | tf_op jit(solution)/shard_map/ppermute | solution.py:583
  83.1 6.6 %collective-permute-start.11 = (f32[16]{0:T(128)S(1)}, f32[16]{0:T(128)S(1)}, u32[]{:S(2)}, u32[]{:S(2)}) collective-permute-start(f32[16]{0:T(128)S(1)} %bitcast_add_fusion), channel_id=1, source_target_pairs={{0,3},{1,2},{2,1},{3,0},{4,7},{5,6},{6,5},{7,4},{8,11},{9,10},{10,... | collective-permute-start | bytes 200 | tf_op jit(solution)/shard_map/ppermute | solution.py:583

commit v6 on v5

--- a/solution.py
+++ b/solution.py
@@ -279,48 +279,53 @@
     return [x[c] + h[...] * (b[c] - sums[c]) for c in range(cases)]
 
 
-def x1_row(c):
+def edge_row(c):
     return (c // 3,) + row_of(5 + c % 3)
 
 
-def coarse_kernel_a(me, x0, ext, b, row_at, row_ok, same_col, h, y3, rsum, cross, chip, x1, y4, to_cross, to_chip, part):
+def coarse_kernel_a(me, x0, ext, b, row_at, row_ok, same_col, h, rsum, cross, chip, x1, to_cross, to_chip, part):
     before, after = sides(me, cross, chip)
     put = sender(me, to_cross, to_chip)
     cases, rows, width = x0.shape
-    tables = (row_at, row_ok, same_col)
+    x = coarse_step(
+        [x0[c] for c in range(cases)],
+        [before[row_of(c)] for c in range(cases)],
+        [after[row_of(c)] for c in range(cases)],
+        ext, b, h, (row_at, row_ok, same_col),
+    )
+    weight = open_weight(ext[...])
+    values = []
+    for c in range(cases):
+        x1[c] = x[c]
+        put(row_of(c), x[c][0:1], x[c][rows - 1 : rows])
+        own = rsum[:, c : c + 1] - total(weight * x[c])
+        values.append((LANE_OWN + c, own))
+        values.append((LANE_TOP + c, total(x[c][0:1])))
+        values.append((LANE_BOTTOM + c, total(x[c][rows - 1 : rows])))
+    values.append((LANE_EXT, total(ext[...])))
+    part[...] = lane_row(values)
+
+
+def answer_kernel(cases, me, ext, row_at, row_ok, same_col, h, y3, cross, chip, y4):
+    before, after = sides(me, cross, chip)
+    rows, width = ext.shape
     none = jnp.zeros((rows, width), F32)
     no_row = jnp.zeros((1, width), F32)
-    old = [x0[c] for c in range(cases)] + [none] + [y3[j] for j in range(3)] + [none]
-    above = [before[pl.ds(c, 1), :] for c in range(cases + 3)] + [no_row, no_row]
-    below = [after[pl.ds(c, 1), :] for c in range(cases)] + [no_row, no_row]
-    below = below + [after[pl.ds(cases + j, 1), :] for j in range(3)]
-    rhs = [b[c] for c in range(cases)] + [none] * 5
-    x = coarse_step(old, above, below, ext, rhs, h, tables)
-    for c in range(cases):
-        put(x1_row(c), x[c][0:1], x[c][rows - 1 : rows])
-    no_row = jnp.zeros((1, width), F32)
-    for c in range(cases, 9):
-        put(x1_row(c), no_row, no_row)
+    above = [before[row_of(cases + j)] for j in range(3)] + [no_row, no_row]
+    below = [no_row, no_row] + [after[row_of(cases + j)] for j in range(3)]
+    y = coarse_step(
+        [none] + [y3[j] for j in range(3)] + [none],
+        above, below, ext, [none] * 5, h, (row_at, row_ok, same_col),
+    )
     for j in range(5):
-        y = x[cases + j]
-        y4[j] = y
-        for k in range(3):
-            put((k,) + row_of(j), y[k : k + 1], y[rows - 1 - k : rows - k])
-    weight = open_weight(ext[...])
-    values = []
-    for c in range(cases):
-        x1[c] = x[c]
-        own = rsum[:, c : c + 1] - total(weight * x[c])
-        values.append((c, own))
-        values.append((cases + c, total(x[c][0:1])))
-        values.append((2 * cases + c, total(x[c][rows - 1 : rows])))
-    values.append((3 * cases, total(ext[...])))
-    part[...] = lane_row(values)
+        y4[j] = y[j]
 
 
 REACH_E = 3
 ORDER = [0, -1, 1, -2, 2, -3, 3]
-LANE_PERP, LANE_LOAD, LANE_D, LANE_C, LANE_L = 16, 20, 24, 32, 64
+LANE_OWN, LANE_TOP, LANE_BOTTOM, LANE_EXT, LANE_D = 0, 8, 16, 24, 25
+LANE_PERP, LANE_LOAD, LANE_C, LANE_L = 32, 40, 48, 104
+FACTORS = [(j, k) for j in range(7) for k in range(j + 1, 7)]
 
 
 def dot(x, y):
@@ -358,49 +363,56 @@
         values.append((LANE_D + j, d))
         for k in range(j + 1, m):
             factor = dot(v, basis[k]) * inv
-            values.append((LANE_L + m * j + k, factor))
+            values.append((LANE_L + FACTORS.index((j, k)), factor))
             basis[k] = basis[k] - factor * v
     part[...] = lane_row(values)
 
 
-def solve_slabs(g, cases, groups, cells):
-    n = g.shape[0]
-    row, lane = iotas(g.shape)
-    top = pltpu.roll(pltpu.roll(g, 128 - cases, 1), n - 1, 0)
-    bottom = pltpu.roll(pltpu.roll(g, 128 - 2 * cases, 1), 1, 0)
-    b = g + jnp.where(row == n - 1, 0.0, top) + jnp.where(row == 0, 0.0, bottom)
-    b = jnp.where(lane < cases, b / (groups * float(n)), 0.0)
-    mean = jnp.broadcast_to(g[:, 3 * cases : 3 * cases + 1], g.shape) / float(cells)
+def solve_slabs(g, groups, cells):
+    own, top, bottom = (g[k : k + 8] for k in (LANE_OWN, LANE_TOP, LANE_BOTTOM))
+    n = own.shape[1]
+    lane = lax.broadcasted_iota(jnp.int32, own.shape, 1)
+    b = own + jnp.where(lane == n - 1, 0.0, pltpu.roll(top, n - 1, 1))
+    b = b + jnp.where(lane == 0, 0.0, pltpu.roll(bottom, 1, 1))
+    b = b / (groups * float(n))
+    mean = jnp.broadcast_to(g[LANE_EXT : LANE_EXT + 1], own.shape) / float(cells)
     d = 2.0 + mean / (float(n) * float(n))
-    lower = jnp.where(row == 0, 0.0, 1.0)
-    upper = jnp.where(row == n - 1, 0.0, 1.0)
+    lower = jnp.where(lane == 0, 0.0, 1.0)
+    upper = jnp.where(lane == n - 1, 0.0, 1.0)
     excess = (d - lower) - upper
     s = 1
     while s < n:
         inv = 1.0 / (lower + upper + excess)
-        alpha = lower * pltpu.roll(inv, s, 0)
-        gamma = upper * pltpu.roll(inv, n - s, 0)
-        b = b + alpha * pltpu.roll(b, s, 0) + gamma * pltpu.roll(b, n - s, 0)
-        excess = excess + alpha * pltpu.roll(excess, s, 0) + gamma * pltpu.roll(excess, n - s, 0)
-        lower = alpha * pltpu.roll(lower, s, 0)
-        upper = gamma * pltpu.roll(upper, n - s, 0)
+        alpha = lower * pltpu.roll(inv, s, 1)
+        gamma = upper * pltpu.roll(inv, n - s, 1)
+        b = b + alpha * pltpu.roll(b, s, 1) + gamma * pltpu.roll(b, n - s, 1)
+        excess = excess + alpha * pltpu.roll(excess, s, 1) + gamma * pltpu.roll(excess, n - s, 1)
+        lower = alpha * pltpu.roll(lower, s, 1)
+        upper = gamma * pltpu.roll(upper, n - s, 1)
         s *= 2
     return b / (lower + upper + excess)
 
 
-def coarse_kernel_b(me, x1, ext, b, row_at, row_ok, same_col, h, cross, chip, x3, to_cross, to_chip):
-    ab, be = sides(me, cross, chip)
+def coarse_kernel_b(me, x1, ext, b, row_at, row_ok, same_col, h, y4, cross, chip, x3, to_cross, to_chip):
+    before, after = sides(me, cross, chip)
     put = sender(me, to_cross, to_chip)
-    cases, rows, _ = x1.shape
+    cases, rows, width = x1.shape
     x = coarse_step(
         [x1[c] for c in range(cases)],
-        [ab[x1_row(c)] for c in range(cases)],
-        [be[x1_row(c)] for c in range(cases)],
+        [before[row_of(c)] for c in range(cases)],
+        [after[row_of(c)] for c in range(cases)],
         ext, b, h, (row_at, row_ok, same_col),
     )
     for c in range(cases):
         x3[c] = x[c]
-        put(row_of(c), x[c][0:1], x[c][rows - 1 : rows])
+        put(edge_row(c), x[c][0:1], x[c][rows - 1 : rows])
+    no_row = jnp.zeros((1, width), F32)
+    for c in range(cases, 9):
+        put(edge_row(c), no_row, no_row)
+    for j in range(5):
+        y = y4[j]
+        for k in range(3):
+            put((k,) + row_of(j), y[k : k + 1], y[rows - 1 - k : rows - k])
 
 
 def coarse_kernel_c(me, x3, ext, b, row_at, row_ok, same_col, h, smooth, cross, chip, v, to_cross, to_chip):
@@ -409,8 +421,8 @@
     cases, rows, width = x3.shape
     x = coarse_step(
         [x3[c] for c in range(cases)],
-        [before[pl.ds(c, 1), :] for c in range(cases)],
-        [after[pl.ds(c, 1), :] for c in range(cases)],
+        [before[edge_row(c)] for c in range(cases)],
+        [after[edge_row(c)] for c in range(cases)],
         ext, b, h, (row_at, row_ok, same_col),
     )
     for c in range(cases):
@@ -450,57 +462,47 @@
         values.append((LANE_PERP + c, dot(r, r)))
         values.append((LANE_LOAD + c, dot(fl[c], fl[c])))
         for j in range(m):
-            values.append((LANE_C + cases * j + c, share[j]))
+            values.append((LANE_C + 8 * j + c, share[j]))
     row = part_a[...] + part_e[...] + lane_row(values)
     gather[...] = jnp.broadcast_to(row, gather.shape)
 
 
-def final_kernel(groups, me, base, phi, gathered, out, ratio, e_ref):
+def final_kernel(groups, me, base, phi, gathered, out, ratio):
     cases, rows, width = base.shape
     n = gathered.shape[0]
     m = phi.shape[0]
-    i = me[0]
-    g = gathered[...]
-    row, lane = iotas(g.shape)
-    e = solve_slabs(g, cases, groups, rows * width)
-    margin = 8
-    e_ref[pl.ds(0, margin), :] = jnp.zeros((margin, 128), F32)
-    e_ref[pl.ds(margin, n), :] = e
-    e_ref[pl.ds(margin + n, margin), :] = jnp.zeros((margin, 128), F32)
-    near = [e_ref[pl.ds(i + margin + j, 1), :] for j in range(-REACH_E, REACH_E + 1)]
+    g = jnp.transpose(gathered[...])
+    e = solve_slabs(g, groups, rows * width)
+    lane = lax.broadcasted_iota(jnp.int32, e.shape, 1)
+    near = [
+        jnp.sum(jnp.where(lane == me[0] + j, e, 0.0), axis=1, keepdims=True)
+        for j in range(-REACH_E, REACH_E + 1)
+    ]
     for c in range(cases):
         x = base[c]
         for j in range(m):
-            x = x + near[j][:, c : c + 1] * phi[j]
+            x = x + near[j][c : c + 1] * phi[j]
         out[c] = x
 
-    def lanes(k):
-        return pltpu.roll(g, 128 - k, 1)
-
-    def column(k):
-        return jnp.broadcast_to(g[:, k : k + 1], g.shape)
-
-    t = [e] + [e_ref[pl.ds(margin + j, n), :] - e for j in ORDER[1:]]
-    norm = lanes(LANE_PERP)
+    def shifted(j):
+        inside = (lane + j >= 0) & (lane + j < n)
+        return jnp.where(inside, pltpu.roll(e, (-j) % n, 1), 0.0)
+
+    def spread_row(k):
+        return jnp.broadcast_to(g[k : k + 1], e.shape)
+
+    t = [e] + [shifted(j) - e for j in ORDER[1:]]
+    norm = g[LANE_PERP : LANE_PERP + 8]
     for j in range(m):
-        z = lanes(LANE_C + cases * j) + t[j]
+        z = g[LANE_C + 8 * j : LANE_C + 8 * j + 8] + t[j]
         for k in range(j + 1, m):
-            z = z + column(LANE_L + m * j + k) * t[k]
-        norm = norm + column(LANE_D + j) * (z * z)
-    norm = jnp.sum(norm, axis=0, keepdims=True)
-    load = jnp.sum(lanes(LANE_LOAD), axis=0, keepdims=True)
-    first = lax.broadcasted_iota(jnp.int32, norm.shape, 1) < cases
-    r = jnp.sqrt(jnp.where(first, norm, 0.0) / jnp.where(first, load, 1.0))
-    mine = pltpu.roll(jnp.where(first, r, 0.0), me[1] * cases, 1)
-    ratio[...] = mine[:, : ratio.shape[1]]
-
-
-def doubling(n):
-    step, steps = 1, []
-    while step < n:
-        steps.append([(i, i ^ (2 * step - 1)) for i in range(n)])
-        step *= 2
-    return steps
+            z = z + spread_row(LANE_L + FACTORS.index((j, k))) * t[k]
+        norm = norm + spread_row(LANE_D + j) * (z * z)
+    norm = jnp.sum(norm, axis=1, keepdims=True)
+    load = jnp.sum(g[LANE_LOAD : LANE_LOAD + 8], axis=1, keepdims=True)
+    case = lax.broadcasted_iota(jnp.int32, norm.shape, 0)
+    r = jnp.sqrt(jnp.where(case < cases, norm, 0.0) / jnp.where(case < cases, load, 1.0))
+    ratio[...] = jnp.broadcast_to(lane_row([(c, r[c : c + 1]) for c in range(cases)]), ratio.shape)
 
 
 def local(thermal_solution, heat_forcing, extinction_factor, cluster_label):
@@ -552,18 +554,21 @@
         pre_kernel, [field, field, field, edges, edges, (1, 128)], n_in=10
     )(u, f, ext, *halo, *tables, y3)
     rows_x = exchange(*sent)
-    x1, y4, *sent, part_a = call(
-        coarse_kernel_a, [field, (5, rows, width), deep, deep, (1, 128)], n_in=11
-    )(x0, ext, b, *tables, y3, rsum, *rows_x)
+    x1, *sent, part_a = call(coarse_kernel_a, [field, edge, edge, (1, 128)], n_in=10)(
+        x0, ext, b, *tables, rsum, *rows_x
+    )
+    (y4,) = call(functools.partial(answer_kernel, cases), [(5, rows, width)], n_in=8)(
+        ext, *tables, y3, *rows_x
+    )
+    rows_x = exchange(*sent)
+    x3, *sent = call(coarse_kernel_b, [field, deep, deep], n_in=10)(
+        x1, ext, b, *tables, y4, *rows_x
+    )
     rows_x = exchange(*sent)
     m = 2 * REACH_E + 1
     phi, q, part_e = call(
         response_kernel, [(m, rows, width), (m, rows, width), (1, 128)], n_in=6
     )(ext, *halo, y4, *rows_x)
-    x3, *sent = call(coarse_kernel_b, [field, edge, edge], n_in=9)(
-        x1, ext, b, *tables, *rows_x
-    )
-    rows_x = exchange(*sent)
     v, *sent = call(
         coarse_kernel_c, [field, (3, cases, width), (3, cases, width)], n_in=10
     )(x3, ext, b, *tables, smooth, *rows_x)
@@ -573,15 +578,10 @@
     )
     gathered = lax.all_to_all(mine, "blk", 0, 0, tiled=True)
     corrected, ratio = call(
-        functools.partial(final_kernel, groups),
-        [field, (1, n_rhs * cases)],
-        [pltpu.VMEM((n + 16, 128), F32)],
-        n_in=3,
+        functools.partial(final_kernel, groups), [field, (n_rhs, 128)], n_in=3
     )(base, phi, gathered)
-    ratio = ratio.reshape(n_rhs * cases)
-    for step in doubling(n_rhs):
-        ratio = ratio + lax.ppermute(ratio, "rhs", step)
-    return corrected, ratio
+    every = lax.all_to_all(ratio, "rhs", 0, 0, tiled=True)
+    return corrected, every[:, :cases].reshape(n_rhs * cases)
 
 
 def solution(mesh):

time: 90.8 us -> 86.6 us (0.954)
  the two profiles are of different devices: /device:TPU:6 before, /device:TPU:1 now
where the time goes in v6:
time: 86.6 us; the launch traced here: 86.1 us
  blocking collectives  41.1 us (47%)
  starting transfers between devices  28.6 us (33%)
  Pallas kernels  11.3 us (13%)
  waiting for transfers between devices  2.88 us (3%)
  local copies, waits for them, and re-layouts  1.36 us (2%)
    all_to_all x1, blocking collectives, local(): gathered = lax.all_to_all(mine, 'blk', 0, 0, tiled=True)  33.2 us
    ppermute x5, starting transfers between devices, exchange(): cross = lax.ppermute(cross, 'blk', cross_chip)  16.1 us
    ppermute x5, starting transfers between devices, exchange(): return (cross, lax.ppermute(chip, 'blk', on_chip))  12.5 us
    all_to_all x1, blocking collectives, local(): every = lax.all_to_all(ratio, 'rhs', 0, 0, tiled=True)  7.91 us
    ppermute x5, waiting for transfers between devices, exchange(): cross = lax.ppermute(cross, 'blk', cross_chip)  2.46 us
    pallas_call x1, Pallas kernels, local(): vmem_call(pack_kernel, [(6, cases, width)] * 2, [pltpu.VMEM(field, F32),...  1.75 us
  transfers between devices with their start and end apart: 10, of which 4 were waited for; matrix products, arithmetic and copies ran while one was open for 0% of the time, Pallas kernels for 4%

profile of v6, /device:TPU:1, one launch (start us, length us, event | category | flops | bytes accessed | tf_op | source)
XLA Modules:
  0.0 86.1 jit_solution(6105453852830422807)
XLA Ops:
  0.6 0.0 copy-start
  0.6 0.0 copy-start.1
  0.6 0.0 copy-start.2
  0.7 1.7 %shard_map.59 = (f32[6,4,1024]{2,1,0:T(4,128)}, f32[6,4,1024]{2,1,0:T(4,128)}) custom-call(f32[4,8,1024]{2,1,0:T(8,128)} %refs_0_.7, f32[4,8,1024]{2,1,0:T(8,128)} %refs_1_.13, f32[8,1024]{1,0:T(8,128)} %refs_2_.5), custom_call_target="tpu_custom_call" | custom-call | tf_op jit(solution)/shard_map/pallas_call | solution.py:527
  2.4 4.6 %collective-permute-start = (f32[6,4,1024]{2,1,0:T(4,128)}, f32[6,4,1024]{2,1,0:T(4,128)S(1)}, u32[]{:S(2)}, u32[]{:S(2)}) collective-permute-start(f32[6,4,1024]{2,1,0:T(4,128)} %get-tuple-element.32), channel_id=1, source_target_pairs={{4,8},{12,16},{20,24},{28,32},{36,40},{44,48},{52,56},{60,64},{68,... | collective-permute-start | bytes 294920 | tf_op jit(solution)/shard_map/ppermute | solution.py:519
  7.0 4.9 %collective-permute-start.1 = (f32[6,4,1024]{2,1,0:T(4,128)}, f32[6,4,1024]{2,1,0:T(4,128)S(1)}, u32[]{:S(2)}, u32[]{:S(2)}) collective-permute-start(f32[6,4,1024]{2,1,0:T(4,128)} %get-tuple-element.33), channel_id=1, source_target_pairs={{0,4},{4,0},{8,12},{12,8},{16,20},{20,16},{24,28},{28,24},{32,36},... | collective-permute-start | bytes 294920 | tf_op jit(solution)/shard_map/ppermute | solution.py:520
  11.9 0.0 copy-done
  11.9 0.0 copy-start.3
  11.9 0.7 copy-done.3
  12.7 1.1 %shard_map.60 = (s32[14,8,1024]{2,1,0:T(8,128)S(1)}, f32[14,8,1024]{2,1,0:T(8,128)S(1)}, f32[7,8,1024]{2,1,0:T(8,128)S(1)}, f32[8,1024]{1,0:T(8,128)S(1)}, f32[3,8,1024]{2,1,0:T(8,128)S(1)}) custom-call(f32[8,1024]{1,0:T(8,128)S(1)} %copy-done, s32[8,1024]{1,0:T(8,128)S(1)} %copy-done.3), custom_call_target="tpu_custom_call" | custom-call | tf_op jit(solution)/shard_map/pallas_call | solution.py:541
  13.7 0.0 collective-permute-done.refs_3_.refs_1_
  13.7 0.0 collective-permute-done.1.refs_4_.refs_2_
  13.7 0.0 copy-done.1
  13.7 0.0 copy-done.2
  13.8 1.0 %shard_map.61 = (f32[4,8,1024]{2,1,0:T(8,128)S(1)}, f32[4,8,1024]{2,1,0:T(8,128)S(1)}, f32[4,8,1024]{2,1,0:T(8,128)S(1)}, f32[8,1024]{1,0:T(8,128)S(1)}, f32[8,1024]{1,0:T(8,128)S(1)}, /*index=5*/f32[1,128]{1,0:T(1,128)S(1)}) custom-call(f32[4,8,1024]{2,1,0:T(8,128)S(1)} %copy-done.2, f32[4,8,1024]{2,1,0:T(8,128)S(1)} %copy-done.1, f32[8,1024]{1,0:T(8,128)S(1)} %copy-done, ...), custom_call_target="tpu_custom_call" | custom-call | tf_op jit(solution)/shard_map/pallas_call | solution.py:553
  14.8 1.9 %collective-permute-start.2 = (f32[8,1024]{1,0:T(8,128)S(1)}, f32[8,1024]{1,0:T(8,128)S(1)}, u32[]{:S(2)}, u32[]{:S(2)}) collective-permute-start(f32[8,1024]{1,0:T(8,128)S(1)} %get-tuple-element.42), channel_id=1, source_target_pairs={{4,8},{12,16},{20,24},{28,32},{36,40},{44,48},{52,56},{60,64},{68,... | collective-permute-start | bytes 98312 | tf_op jit(solution)/shard_map/ppermute | solution.py:519
  16.7 1.9 %collective-permute-start.3 = (f32[8,1024]{1,0:T(8,128)S(1)}, f32[8,1024]{1,0:T(8,128)S(1)}, u32[]{:S(2)}, u32[]{:S(2)}) collective-permute-start(f32[8,1024]{1,0:T(8,128)S(1)} %get-tuple-element.43), channel_id=1, source_target_pairs={{0,4},{4,0},{8,12},{12,8},{16,20},{20,16},{24,28},{28,24},{32,36},... | collective-permute-start | bytes 98312 | tf_op jit(solution)/shard_map/ppermute | solution.py:520
  18.7 1.4 %collective-permute-done.2.refs_8_.refs_6_ = f32[8,1024]{1,0:T(8,128)S(1)} collective-permute-done((f32[8,1024]{1,0:T(8,128)S(1)}, f32[8,1024]{1,0:T(8,128)S(1)}, u32[]{:S(2)}, u32[]{:S(2)}) %collective-permute-start.2) | collective-permute-done | bytes 32800 | tf_op jit(solution)/shard_map/ppermute | solution.py:519
  20.0 0.0 collective-permute-done.3.refs_9_.refs_7_
  20.0 0.9 %shard_map.62 = (f32[4,8,1024]{2,1,0:T(8,128)S(1)}, f32[4,1024]{1,0:T(4,128)S(1)}, f32[4,1024]{1,0:T(4,128)S(1)}, f32[1,128]{1,0:T(1,128)S(1)}) custom-call(f32[4,8,1024]{2,1,0:T(8,128)S(1)} %get-tuple-element.39.refs_0_, f32[8,1024]{1,0:T(8,128)S(1)} %copy-done, f32[4,8,1024]{2,1,0:T(8,128)S(1)} %get-tuple-element.40.refs_2_, ...), custom_call_target="tpu_custom_call" | custom-call | tf_op jit(solution)/shard_map/pallas_call | solution.py:557
  21.0 3.4 %collective-permute-start.4 = (f32[4,1024]{1,0:T(4,128)S(1)}, f32[4,1024]{1,0:T(4,128)S(1)}, u32[]{:S(2)}, u32[]{:S(2)}) collective-permute-start(f32[4,1024]{1,0:T(4,128)S(1)} %get-tuple-element.45), channel_id=1, source_target_pairs={{4,8},{12,16},{20,24},{28,32},{36,40},{44,48},{52,56},{60,64},{68,... | collective-permute-start | bytes 49160 | tf_op jit(solution)/shard_map/ppermute | solution.py:519
  24.4 1.9 %collective-permute-start.5 = (f32[4,1024]{1,0:T(4,128)S(1)}, f32[4,1024]{1,0:T(4,128)S(1)}, u32[]{:S(2)}, u32[]{:S(2)}) collective-permute-start(f32[4,1024]{1,0:T(4,128)S(1)} %get-tuple-element.46), channel_id=1, source_target_pairs={{0,4},{4,0},{8,12},{12,8},{16,20},{20,16},{24,28},{28,24},{32,36},... | collective-permute-start | bytes 49160 | tf_op jit(solution)/shard_map/ppermute | solution.py:520
  26.4 0.9 %shard_map.63.refs_7_.refs_3_ = f32[5,8,1024]{2,1,0:T(8,128)S(1)} custom-call(f32[8,1024]{1,0:T(8,128)S(1)} %copy-done, s32[14,8,1024]{2,1,0:T(8,128)S(1)} %get-tuple-element.34.refs_5_.refs_3_.refs_1_, f32[14,8,1024]{2,1,0:T(8,128)S(1)} %get-tuple-element.35.refs_6_.refs_4_.refs_2_, f32[7,8,1024]{2,1,0:T(8,128)S(1)} %get-tuple-element.36.refs_7_.refs_5_.refs_3_, ...), custom_call_target="tpu_custom_call" | custom-call | tf_op jit(solution)/shard_map/pallas_call | solution.py:560
  27.3 0.0 collective-permute-done.4.refs_8_
  27.3 0.2 collective-permute-done.5.refs_9_
  27.5 0.8 shard_map.64
  28.4 2.9 %collective-permute-start.6 = (f32[3,8,1024]{2,1,0:T(8,128)S(1)}, f32[3,8,1024]{2,1,0:T(8,128)S(1)}, u32[]{:S(2)}, u32[]{:S(2)}) collective-permute-start(f32[3,8,1024]{2,1,0:T(8,128)S(1)} %get-tuple-element.49), channel_id=1, source_target_pairs={{4,8},{12,16},{20,24},{28,32},{36,40},{44,48},{52,56},{60,64},{68,... | collective-permute-start | bytes 294920 | tf_op jit(solution)/shard_map/ppermute | solution.py:519
  31.3 1.9 %collective-permute-start.7 = (f32[3,8,1024]{2,1,0:T(8,128)S(1)}, f32[3,8,1024]{2,1,0:T(8,128)S(1)}, u32[]{:S(2)}, u32[]{:S(2)}) collective-permute-start(f32[3,8,1024]{2,1,0:T(8,128)S(1)} %get-tuple-element.50), channel_id=1, source_target_pairs={{0,4},{4,0},{8,12},{12,8},{16,20},{20,16},{24,28},{28,24},{32,36},... | collective-permute-start | bytes 294920 | tf_op jit(solution)/shard_map/ppermute | solution.py:520
  33.2 1.1 %collective-permute-done.6.refs_8_.refs_4_ = f32[3,8,1024]{2,1,0:T(8,128)S(1)} collective-permute-done((f32[3,8,1024]{2,1,0:T(8,128)S(1)}, f32[3,8,1024]{2,1,0:T(8,128)S(1)}, u32[]{:S(2)}, u32[]{:S(2)}) %collective-permute-start.6) | collective-permute-done | bytes 98336 | tf_op jit(solution)/shard_map/ppermute | solution.py:519
  34.3 0.2 collective-permute-done.7.refs_9_.refs_5_
  34.5 0.8 shard_map.65
  35.3 3.2 %collective-permute-start.8 = (f32[3,4,1024]{2,1,0:T(4,128)S(1)}, f32[3,4,1024]{2,1,0:T(4,128)S(1)}, u32[]{:S(2)}, u32[]{:S(2)}) collective-permute-start(f32[3,4,1024]{2,1,0:T(4,128)S(1)} %get-tuple-element.52), channel_id=1, source_target_pairs={{4,8},{12,16},{20,24},{28,32},{36,40},{44,48},{52,56},{60,64},{68,... | collective-permute-start | bytes 147464 | tf_op jit(solution)/shard_map/ppermute | solution.py:519
  38.6 1.9 %collective-permute-start.9 = (f32[3,4,1024]{2,1,0:T(4,128)S(1)}, f32[3,4,1024]{2,1,0:T(4,128)S(1)}, u32[]{:S(2)}, u32[]{:S(2)}) collective-permute-start(f32[3,4,1024]{2,1,0:T(4,128)S(1)} %get-tuple-element.53), channel_id=1, source_target_pairs={{0,4},{4,0},{8,12},{12,8},{16,20},{20,16},{24,28},{28,24},{32,36},... | collective-permute-start | bytes 147464 | tf_op jit(solution)/shard_map/ppermute | solution.py:520
  40.5 1.2 %shard_map.66 = (f32[7,8,1024]{2,1,0:T(8,128)S(1)}, f32[7,8,1024]{2,1,0:T(8,128)S(1)}, f32[1,128]{1,0:T(1,128)S(1)}) custom-call(f32[8,1024]{1,0:T(8,128)S(1)} %copy-done, f32[6,4,1024]{2,1,0:T(4,128)S(1)} %collective-permute-done.refs_3_.refs_1_, f32[6,4,1024]{2,1,0:T(4,128)S(1)} %collective-permute-done.1.refs_4_.refs_2_, ...), custom_call_target="tpu_custom_call" | custom-call | tf_op jit(solution)/shard_map/pallas_call | solution.py:569
  41.7 0.0 collective-permute-done.8.refs_5_
  41.7 0.0 collective-permute-done.9.refs_6_
  41.8 1.2 %shard_map.67 = (f32[4,8,1024]{2,1,0:T(8,128)S(1)}, f32[128,128]{1,0:T(8,128)S(1)}) custom-call(f32[4,8,1024]{2,1,0:T(8,128)S(1)} %get-tuple-element.51.refs_0_, f32[4,8,1024]{2,1,0:T(8,128)S(1)} %copy-done.1, f32[8,1024]{1,0:T(8,128)S(1)} %copy-done, f32[6,4,1024]{2,1,0:T(4,128)S(1)} %collective-permute-done.refs_3_.refs_1_, ...), custom_call_target="tpu_custom_call" | custom-call | tf_op jit(solution)/shard_map/pallas_call | solution.py:576
  42.9 33.2 %all_to_all.23 = f32[128,1,128]{2,1,0:T(1,128)S(1)} all-to-all(f32[128,1,128]{2,1,0:T(1,128)S(1)} %bitcast.10), channel_id=1, replica_groups=mesh['blk'=128,'rhs'=4] {'blk'}, dimensions={0} | all-to-all | bytes 131072 | tf_op jit(solution)/shard_map/all_to_all | solution.py:579
  76.1 1.6 %shard_map.68 = (f32[4,8,1024]{2,1,0:T(8,128)}, f32[4,128]{1,0:T(4,128)S(1)}) custom-call(f32[4,8,1024]{2,1,0:T(8,128)S(1)} %get-tuple-element.57.refs_0_, f32[7,8,1024]{2,1,0:T(8,128)S(1)} %get-tuple-element.58.refs_1_, f32[128,128]{1,0:T(8,128)S(1)} %bitcast.9), custom_call_target="tpu_custom_call" | custom-call | tf_op jit(solution)/shard_map/pallas_call | solution.py:580
  77.6 7.9 %all_to_all.24 = f32[4,1,128]{2,1,0:T(1,128)S(1)} all-to-all(f32[4,1,128]{2,1,0:T(1,128)S(1)} %bitcast.11), channel_id=1, replica_groups=mesh['blk'=128,'rhs'=4] {'rhs'}, dimensions={0} | all-to-all | bytes 4096 | tf_op jit(solution)/shard_map/all_to_all | solution.py:583
  85.5 0.6 reshape.11
Async XLA Ops:
  0.6 11.3 %copy-start = (f32[8,1024]{1,0:T(8,128)S(1)}, f32[8,1024]{1,0:T(8,128)}, u32[]{:S(2)}) copy-start(f32[8,1024]{1,0:T(8,128)} %refs_2_.5) | copy-start | bytes 98308
  0.6 13.1 %copy-start.1 = (f32[4,8,1024]{2,1,0:T(8,128)S(1)}, f32[4,8,1024]{2,1,0:T(8,128)}, u32[]{:S(2)}) copy-start(f32[4,8,1024]{2,1,0:T(8,128)} %refs_1_.13) | copy-start | bytes 393220
  0.6 13.1 %copy-start.2 = (f32[4,8,1024]{2,1,0:T(8,128)S(1)}, f32[4,8,1024]{2,1,0:T(8,128)}, u32[]{:S(2)}) copy-start(f32[4,8,1024]{2,1,0:T(8,128)} %refs_0_.7) | copy-start | bytes 393220
  2.4 11.3 %collective-permute-start = (f32[6,4,1024]{2,1,0:T(4,128)}, f32[6,4,1024]{2,1,0:T(4,128)S(1)}, u32[]{:S(2)}, u32[]{:S(2)}) collective-permute-start(f32[6,4,1024]{2,1,0:T(4,128)} %get-tuple-element.32), channel_id=1, source_target_pairs={{4,8},{12,16},{20,24},{28,32},{36,40},{44,48},{52,56},{60,64},{68,... | collective-permute-start | bytes 294920 | tf_op jit(solution)/shard_map/ppermute | solution.py:519
  7.0 6.7 %collective-permute-start.1 = (f32[6,4,1024]{2,1,0:T(4,128)}, f32[6,4,1024]{2,1,0:T(4,128)S(1)}, u32[]{:S(2)}, u32[]{:S(2)}) collective-permute-start(f32[6,4,1024]{2,1,0:T(4,128)} %get-tuple-element.33), channel_id=1, source_target_pairs={{0,4},{4,0},{8,12},{12,8},{16,20},{20,16},{24,28},{28,24},{32,36},... | collective-permute-start | bytes 294920 | tf_op jit(solution)/shard_map/ppermute | solution.py:520
  11.9 0.8 copy-start.3
  14.8 5.2 %collective-permute-start.2 = (f32[8,1024]{1,0:T(8,128)S(1)}, f32[8,1024]{1,0:T(8,128)S(1)}, u32[]{:S(2)}, u32[]{:S(2)}) collective-permute-start(f32[8,1024]{1,0:T(8,128)S(1)} %get-tuple-element.42), channel_id=1, source_target_pairs={{4,8},{12,16},{20,24},{28,32},{36,40},{44,48},{52,56},{60,64},{68,... | collective-permute-start | bytes 98312 | tf_op jit(solution)/shard_map/ppermute | solution.py:519
  16.7 3.3 %collective-permute-start.3 = (f32[8,1024]{1,0:T(8,128)S(1)}, f32[8,1024]{1,0:T(8,128)S(1)}, u32[]{:S(2)}, u32[]{:S(2)}) collective-permute-start(f32[8,1024]{1,0:T(8,128)S(1)} %get-tuple-element.43), channel_id=1, source_target_pairs={{0,4},{4,0},{8,12},{12,8},{16,20},{20,16},{24,28},{28,24},{32,36},... | collective-permute-start | bytes 98312 | tf_op jit(solution)/shard_map/ppermute | solution.py:520
  21.0 6.3 %collective-permute-start.4 = (f32[4,1024]{1,0:T(4,128)S(1)}, f32[4,1024]{1,0:T(4,128)S(1)}, u32[]{:S(2)}, u32[]{:S(2)}) collective-permute-start(f32[4,1024]{1,0:T(4,128)S(1)} %get-tuple-element.45), channel_id=1, source_target_pairs={{4,8},{12,16},{20,24},{28,32},{36,40},{44,48},{52,56},{60,64},{68,... | collective-permute-start | bytes 49160 | tf_op jit(solution)/shard_map/ppermute | solution.py:519
  24.4 3.1 %collective-permute-start.5 = (f32[4,1024]{1,0:T(4,128)S(1)}, f32[4,1024]{1,0:T(4,128)S(1)}, u32[]{:S(2)}, u32[]{:S(2)}) collective-permute-start(f32[4,1024]{1,0:T(4,128)S(1)} %get-tuple-element.46), channel_id=1, source_target_pairs={{0,4},{4,0},{8,12},{12,8},{16,20},{20,16},{24,28},{28,24},{32,36},... | collective-permute-start | bytes 49160 | tf_op jit(solution)/shard_map/ppermute | solution.py:520
  28.4 5.9 %collective-permute-start.6 = (f32[3,8,1024]{2,1,0:T(8,128)S(1)}, f32[3,8,1024]{2,1,0:T(8,128)S(1)}, u32[]{:S(2)}, u32[]{:S(2)}) collective-permute-start(f32[3,8,1024]{2,1,0:T(8,128)S(1)} %get-tuple-element.49), channel_id=1, source_target_pairs={{4,8},{12,16},{20,24},{28,32},{36,40},{44,48},{52,56},{60,64},{68,... | collective-permute-start | bytes 294920 | tf_op jit(solution)/shard_map/ppermute | solution.py:519
  31.3 3.2 %collective-permute-start.7 = (f32[3,8,1024]{2,1,0:T(8,128)S(1)}, f32[3,8,1024]{2,1,0:T(8,128)S(1)}, u32[]{:S(2)}, u32[]{:S(2)}) collective-permute-start(f32[3,8,1024]{2,1,0:T(8,128)S(1)} %get-tuple-element.50), channel_id=1, source_target_pairs={{0,4},{4,0},{8,12},{12,8},{16,20},{20,16},{24,28},{28,24},{32,36},... | collective-permute-start | bytes 294920 | tf_op jit(solution)/shard_map/ppermute | solution.py:520
  35.3 6.4 %collective-permute-start.8 = (f32[3,4,1024]{2,1,0:T(4,128)S(1)}, f32[3,4,1024]{2,1,0:T(4,128)S(1)}, u32[]{:S(2)}, u32[]{:S(2)}) collective-permute-start(f32[3,4,1024]{2,1,0:T(4,128)S(1)} %get-tuple-element.52), channel_id=1, source_target_pairs={{4,8},{12,16},{20,24},{28,32},{36,40},{44,48},{52,56},{60,64},{68,... | collective-permute-start | bytes 147464 | tf_op jit(solution)/shard_map/ppermute | solution.py:519
  38.6 3.2 %collective-permute-start.9 = (f32[3,4,1024]{2,1,0:T(4,128)S(1)}, f32[3,4,1024]{2,1,0:T(4,128)S(1)}, u32[]{:S(2)}, u32[]{:S(2)}) collective-permute-start(f32[3,4,1024]{2,1,0:T(4,128)S(1)} %get-tuple-element.53), channel_id=1, source_target_pairs={{0,4},{4,0},{8,12},{12,8},{16,20},{20,16},{24,28},{28,24},{32,36},... | collective-permute-start | bytes 147464 | tf_op jit(solution)/shard_map/ppermute | solution.py:520

commit v7 on v6

--- a/solution.py
+++ b/solution.py
@@ -279,8 +279,12 @@
     return [x[c] + h[...] * (b[c] - sums[c]) for c in range(cases)]
 
 
-def edge_row(c):
-    return (c // 3,) + row_of(5 + c % 3)
+def flat_row(r):
+    return (r // 4,) + row_of(r % 4)
+
+
+def response_row(k, j):
+    return flat_row(4 + 5 * k + j)
 
 
 def coarse_kernel_a(me, x0, ext, b, row_at, row_ok, same_col, h, rsum, cross, chip, x1, to_cross, to_chip, part):
@@ -343,8 +347,9 @@
     two_rows = jnp.zeros((2, width), F32)
     halo = []
     for k in range(3):
-        up, down = ab[k], be[k]
-        halo.append(jnp.concatenate([up[0:5], two_rows, two_rows, down[0:5]], axis=0))
+        up = [ab[response_row(k, j)] for j in range(5)]
+        down = [be[response_row(k, j)] for j in range(5)]
+        halo.append(jnp.concatenate(up + [two_rows, two_rows] + down, axis=0))
 
     d_halo = [4.0 + spread(before, after, k, m) for k in range(2)]
     x, res = two_sweeps(fields, halo, None, None, diag, d_halo, spread(before, after, 2, m))
@@ -405,14 +410,13 @@
     )
     for c in range(cases):
         x3[c] = x[c]
-        put(edge_row(c), x[c][0:1], x[c][rows - 1 : rows])
+        put(flat_row(c), x[c][0:1], x[c][rows - 1 : rows])
     no_row = jnp.zeros((1, width), F32)
-    for c in range(cases, 9):
-        put(edge_row(c), no_row, no_row)
+    put(flat_row(19), no_row, no_row)
     for j in range(5):
         y = y4[j]
         for k in range(3):
-            put((k,) + row_of(j), y[k : k + 1], y[rows - 1 - k : rows - k])
+            put(response_row(k, j), y[k : k + 1], y[rows - 1 - k : rows - k])
 
 
 def coarse_kernel_c(me, x3, ext, b, row_at, row_ok, same_col, h, smooth, cross, chip, v, to_cross, to_chip):
@@ -421,8 +425,8 @@
     cases, rows, width = x3.shape
     x = coarse_step(
         [x3[c] for c in range(cases)],
-        [before[edge_row(c)] for c in range(cases)],
-        [after[edge_row(c)] for c in range(cases)],
+        [before[flat_row(c)] for c in range(cases)],
+        [after[flat_row(c)] for c in range(cases)],
         ext, b, h, (row_at, row_ok, same_col),
     )
     for c in range(cases):
@@ -453,12 +457,9 @@
     values = []
     for c in range(cases):
         r = res[c]
-        share = None
-        for _ in range(2):
-            step = [dot(r, q[j]) * inv[j] for j in range(m)]
-            for j in range(m):
-                r = r - step[j] * q[j]
-            share = step if share is None else [p + t for p, t in zip(share, step)]
+        share = [dot(r, q[j]) * inv[j] for j in range(m)]
+        for j in range(m):
+            r = r - share[j] * q[j]
         values.append((LANE_PERP + c, dot(r, r)))
         values.append((LANE_LOAD + c, dot(fl[c], fl[c])))
         for j in range(m):
@@ -467,22 +468,16 @@
     gather[...] = jnp.broadcast_to(row, gather.shape)
 
 
-def final_kernel(groups, me, base, phi, gathered, out, ratio):
-    cases, rows, width = base.shape
+def ratio_kernel(groups, cases, cells, me, gathered, ratio, near):
     n = gathered.shape[0]
-    m = phi.shape[0]
+    m = 2 * REACH_E + 1
     g = jnp.transpose(gathered[...])
-    e = solve_slabs(g, groups, rows * width)
+    e = solve_slabs(g, groups, cells)
     lane = lax.broadcasted_iota(jnp.int32, e.shape, 1)
-    near = [
-        jnp.sum(jnp.where(lane == me[0] + j, e, 0.0), axis=1, keepdims=True)
-        for j in range(-REACH_E, REACH_E + 1)
-    ]
-    for c in range(cases):
-        x = base[c]
-        for j in range(m):
-            x = x + near[j][c : c + 1] * phi[j]
-        out[c] = x
+    for j in range(m):
+        at = lane == me[0] + j - REACH_E
+        own = jnp.sum(jnp.where(at, e, 0.0), axis=1, keepdims=True)
+        near[j] = jnp.broadcast_to(own, near.shape[1:])
 
     def shifted(j):
         inside = (lane + j >= 0) & (lane + j < n)
@@ -505,6 +500,15 @@
     ratio[...] = jnp.broadcast_to(lane_row([(c, r[c : c + 1]) for c in range(cases)]), ratio.shape)
 
 
+def final_kernel(me, base, phi, near, out):
+    cases, rows, width = base.shape
+    for c in range(cases):
+        x = base[c]
+        for j in range(phi.shape[0]):
+            x = x + near[j, pl.ds(c, 1), 0:1] * phi[j]
+        out[c] = x
+
+
 def local(thermal_solution, heat_forcing, extinction_factor, cluster_label):
     cases, rows, width = thermal_solution.shape
     n = lax.axis_size("blk")
@@ -521,7 +525,7 @@
 
     edge = (cases, width)
     edges = (8, width)
-    deep = (3, 8, width)
+    deep = (5, 4, width)
     cells = (rows, width)
     u, f, ext, lab = thermal_solution, heat_forcing, extinction_factor, cluster_label
     sent = vmem_call(
@@ -577,10 +581,13 @@
         v, f, ext, *halo, *rows_x, q, part_a, part_e
     )
     gathered = lax.all_to_all(mine, "blk", 0, 0, tiled=True)
-    corrected, ratio = call(
-        functools.partial(final_kernel, groups), [field, (n_rhs, 128)], n_in=3
-    )(base, phi, gathered)
+    ratio, near = call(
+        functools.partial(ratio_kernel, groups, cases, rows * width),
+        [(n_rhs, 128), (m, 8, 128)],
+        n_in=1,
+    )(gathered)
     every = lax.all_to_all(ratio, "rhs", 0, 0, tiled=True)
+    (corrected,) = call(final_kernel, [field], n_in=3)(base, phi, near)
     return corrected, every[:, :cases].reshape(n_rhs * cases)
 
 

time: 86.6 us -> 86.1 us (level)
  blocking collectives: 41.1 us -> 33 us
  starting transfers between devices: 28.6 us -> 32.7 us
  waiting for transfers between devices: 2.88 us -> 6.06 us
    all_to_all x1 -> x0, blocking collectives: 7.91 us -> none  [local(): every = lax.all_to_all(ratio, 'rhs', 0, 0, tiled=True)]
    all_to_all x0 -> x1, starting transfers between devices: none -> 4.01 us  [local(): every = lax.all_to_all(ratio, 'rhs', 0, 0, tiled=True)]
    all_to_all x0 -> x1, waiting for transfers between devices: none -> 3.2 us  [local(): every = lax.all_to_all(ratio, 'rhs', 0, 0, tiled=True)]
    pallas_call x1 -> x2, Pallas kernels: 1.55 us -> 2.17 us  [the longest x1 1.42 us: local(): call(functools.partial(ratio_kernel, groups, cases, rows * width), [(n_rh...]
  transfers between devices with their start and end apart: 10 -> 11, of which waited for: 4 -> 5; matrix products, arithmetic and copies ran while one was open for 0% -> 0% of each run, Pallas kernels for 4% -> 5%
where the time goes in v7:
time: 86.1 us; the launch traced here: 85.6 us
  blocking collectives  33 us (38%)
  starting transfers between devices  32.7 us (38%)
  Pallas kernels  11.7 us (14%)
  waiting for transfers between devices  6.06 us (7%)
  local copies, waits for them, and re-layouts  1.36 us (2%)
    all_to_all x1, blocking collectives, local(): gathered = lax.all_to_all(mine, 'blk', 0, 0, tiled=True)  33 us
    ppermute x5, starting transfers between devices, exchange(): cross = lax.ppermute(cross, 'blk', cross_chip)  16.1 us
    ppermute x5, starting transfers between devices, exchange(): return (cross, lax.ppermute(chip, 'blk', on_chip))  12.5 us
    all_to_all x1, starting transfers between devices, local(): every = lax.all_to_all(ratio, 'rhs', 0, 0, tiled=True)  4.01 us
    all_to_all x1, waiting for transfers between devices, local(): every = lax.all_to_all(ratio, 'rhs', 0, 0, tiled=True)  3.2 us
    ppermute x5, waiting for transfers between devices, exchange(): cross = lax.ppermute(cross, 'blk', cross_chip)  2.28 us
    pallas_call x1, Pallas kernels, local(): vmem_call(pack_kernel, [(6, cases, width)] * 2, [pltpu.VMEM(field, F32),...  1.75 us
  transfers between devices with their start and end apart: 11, of which 5 were waited for; matrix products, arithmetic and copies ran while one was open for 0% of the time, Pallas kernels for 5%

profile of v7, /device:TPU:1, one launch (start us, length us, event | category | flops | bytes accessed | tf_op | source)
XLA Modules:
  0.0 85.6 jit_solution(16639204463088025382)
XLA Ops:
  0.6 0.0 copy-start
  0.6 0.0 copy-start.1
  0.6 0.0 copy-start.2
  0.7 1.7 %shard_map.59 = (f32[6,4,1024]{2,1,0:T(4,128)}, f32[6,4,1024]{2,1,0:T(4,128)}) custom-call(f32[4,8,1024]{2,1,0:T(8,128)} %refs_0_.7, f32[4,8,1024]{2,1,0:T(8,128)} %refs_1_.13, f32[8,1024]{1,0:T(8,128)} %refs_2_.5), custom_call_target="tpu_custom_call" | custom-call | tf_op jit(solution)/shard_map/pallas_call | solution.py:531
  2.4 4.6 %collective-permute-start = (f32[6,4,1024]{2,1,0:T(4,128)}, f32[6,4,1024]{2,1,0:T(4,128)S(1)}, u32[]{:S(2)}, u32[]{:S(2)}) collective-permute-start(f32[6,4,1024]{2,1,0:T(4,128)} %get-tuple-element.32), channel_id=1, source_target_pairs={{4,8},{12,16},{20,24},{28,32},{36,40},{44,48},{52,56},{60,64},{68,... | collective-permute-start | bytes 294920 | tf_op jit(solution)/shard_map/ppermute | solution.py:523
  7.0 4.9 %collective-permute-start.1 = (f32[6,4,1024]{2,1,0:T(4,128)}, f32[6,4,1024]{2,1,0:T(4,128)S(1)}, u32[]{:S(2)}, u32[]{:S(2)}) collective-permute-start(f32[6,4,1024]{2,1,0:T(4,128)} %get-tuple-element.33), channel_id=1, source_target_pairs={{0,4},{4,0},{8,12},{12,8},{16,20},{20,16},{24,28},{28,24},{32,36},... | collective-permute-start | bytes 294920 | tf_op jit(solution)/shard_map/ppermute | solution.py:524
  11.9 0.0 copy-done
  11.9 0.0 copy-start.3
  11.9 0.7 copy-done.3
  12.7 1.1 %shard_map.60 = (s32[14,8,1024]{2,1,0:T(8,128)S(1)}, f32[14,8,1024]{2,1,0:T(8,128)S(1)}, f32[7,8,1024]{2,1,0:T(8,128)S(1)}, f32[8,1024]{1,0:T(8,128)S(1)}, f32[3,8,1024]{2,1,0:T(8,128)S(1)}) custom-call(f32[8,1024]{1,0:T(8,128)S(1)} %copy-done, s32[8,1024]{1,0:T(8,128)S(1)} %copy-done.3), custom_call_target="tpu_custom_call" | custom-call | tf_op jit(solution)/shard_map/pallas_call | solution.py:545
  13.7 0.0 collective-permute-done.refs_3_.refs_1_
  13.7 0.0 collective-permute-done.1.refs_4_.refs_2_
  13.7 0.0 copy-done.1
  13.7 0.0 copy-done.2
  13.8 1.0 %shard_map.61 = (f32[4,8,1024]{2,1,0:T(8,128)S(1)}, f32[4,8,1024]{2,1,0:T(8,128)S(1)}, f32[4,8,1024]{2,1,0:T(8,128)S(1)}, f32[8,1024]{1,0:T(8,128)S(1)}, f32[8,1024]{1,0:T(8,128)S(1)}, /*index=5*/f32[1,128]{1,0:T(1,128)S(1)}) custom-call(f32[4,8,1024]{2,1,0:T(8,128)S(1)} %copy-done.2, f32[4,8,1024]{2,1,0:T(8,128)S(1)} %copy-done.1, f32[8,1024]{1,0:T(8,128)S(1)} %copy-done, ...), custom_call_target="tpu_custom_call" | custom-call | tf_op jit(solution)/shard_map/pallas_call | solution.py:557
  14.8 1.9 %collective-permute-start.2 = (f32[8,1024]{1,0:T(8,128)S(1)}, f32[8,1024]{1,0:T(8,128)S(1)}, u32[]{:S(2)}, u32[]{:S(2)}) collective-permute-start(f32[8,1024]{1,0:T(8,128)S(1)} %get-tuple-element.42), channel_id=1, source_target_pairs={{4,8},{12,16},{20,24},{28,32},{36,40},{44,48},{52,56},{60,64},{68,... | collective-permute-start | bytes 98312 | tf_op jit(solution)/shard_map/ppermute | solution.py:523
  16.7 1.9 %collective-permute-start.3 = (f32[8,1024]{1,0:T(8,128)S(1)}, f32[8,1024]{1,0:T(8,128)S(1)}, u32[]{:S(2)}, u32[]{:S(2)}) collective-permute-start(f32[8,1024]{1,0:T(8,128)S(1)} %get-tuple-element.43), channel_id=1, source_target_pairs={{0,4},{4,0},{8,12},{12,8},{16,20},{20,16},{24,28},{28,24},{32,36},... | collective-permute-start | bytes 98312 | tf_op jit(solution)/shard_map/ppermute | solution.py:524
  18.7 1.4 %collective-permute-done.2.refs_8_.refs_6_ = f32[8,1024]{1,0:T(8,128)S(1)} collective-permute-done((f32[8,1024]{1,0:T(8,128)S(1)}, f32[8,1024]{1,0:T(8,128)S(1)}, u32[]{:S(2)}, u32[]{:S(2)}) %collective-permute-start.2) | collective-permute-done | bytes 32800 | tf_op jit(solution)/shard_map/ppermute | solution.py:523
  20.0 0.0 collective-permute-done.3.refs_9_.refs_7_
  20.0 1.0 %shard_map.62 = (f32[4,8,1024]{2,1,0:T(8,128)S(1)}, f32[4,1024]{1,0:T(4,128)S(1)}, f32[4,1024]{1,0:T(4,128)S(1)}, f32[1,128]{1,0:T(1,128)S(1)}) custom-call(f32[4,8,1024]{2,1,0:T(8,128)S(1)} %get-tuple-element.39.refs_0_, f32[8,1024]{1,0:T(8,128)S(1)} %copy-done, f32[4,8,1024]{2,1,0:T(8,128)S(1)} %get-tuple-element.40.refs_2_, ...), custom_call_target="tpu_custom_call" | custom-call | tf_op jit(solution)/shard_map/pallas_call | solution.py:561
  21.0 3.4 %collective-permute-start.4 = (f32[4,1024]{1,0:T(4,128)S(1)}, f32[4,1024]{1,0:T(4,128)S(1)}, u32[]{:S(2)}, u32[]{:S(2)}) collective-permute-start(f32[4,1024]{1,0:T(4,128)S(1)} %get-tuple-element.45), channel_id=1, source_target_pairs={{4,8},{12,16},{20,24},{28,32},{36,40},{44,48},{52,56},{60,64},{68,... | collective-permute-start | bytes 49160 | tf_op jit(solution)/shard_map/ppermute | solution.py:523
  24.4 1.9 %collective-permute-start.5 = (f32[4,1024]{1,0:T(4,128)S(1)}, f32[4,1024]{1,0:T(4,128)S(1)}, u32[]{:S(2)}, u32[]{:S(2)}) collective-permute-start(f32[4,1024]{1,0:T(4,128)S(1)} %get-tuple-element.46), channel_id=1, source_target_pairs={{0,4},{4,0},{8,12},{12,8},{16,20},{20,16},{24,28},{28,24},{32,36},... | collective-permute-start | bytes 49160 | tf_op jit(solution)/shard_map/ppermute | solution.py:524
  26.4 0.9 %shard_map.63.refs_7_.refs_3_ = f32[5,8,1024]{2,1,0:T(8,128)S(1)} custom-call(f32[8,1024]{1,0:T(8,128)S(1)} %copy-done, s32[14,8,1024]{2,1,0:T(8,128)S(1)} %get-tuple-element.34.refs_5_.refs_3_.refs_1_, f32[14,8,1024]{2,1,0:T(8,128)S(1)} %get-tuple-element.35.refs_6_.refs_4_.refs_2_, f32[7,8,1024]{2,1,0:T(8,128)S(1)} %get-tuple-element.36.refs_7_.refs_5_.refs_3_, ...), custom_call_target="tpu_custom_call" | custom-call | tf_op jit(solution)/shard_map/pallas_call | solution.py:564
  27.3 0.0 collective-permute-done.4.refs_8_
  27.3 0.2 collective-permute-done.5.refs_9_
  27.5 0.8 shard_map.64
  28.4 2.9 %collective-permute-start.6 = (f32[5,4,1024]{2,1,0:T(4,128)S(1)}, f32[5,4,1024]{2,1,0:T(4,128)S(1)}, u32[]{:S(2)}, u32[]{:S(2)}) collective-permute-start(f32[5,4,1024]{2,1,0:T(4,128)S(1)} %get-tuple-element.49), channel_id=1, source_target_pairs={{4,8},{12,16},{20,24},{28,32},{36,40},{44,48},{52,56},{60,64},{68,... | collective-permute-start | bytes 245768 | tf_op jit(solution)/shard_map/ppermute | solution.py:523
  31.3 1.9 %collective-permute-start.7 = (f32[5,4,1024]{2,1,0:T(4,128)S(1)}, f32[5,4,1024]{2,1,0:T(4,128)S(1)}, u32[]{:S(2)}, u32[]{:S(2)}) collective-permute-start(f32[5,4,1024]{2,1,0:T(4,128)S(1)} %get-tuple-element.50), channel_id=1, source_target_pairs={{0,4},{4,0},{8,12},{12,8},{16,20},{20,16},{24,28},{28,24},{32,36},... | collective-permute-start | bytes 245768 | tf_op jit(solution)/shard_map/ppermute | solution.py:524
  33.2 0.9 %collective-permute-done.6.refs_8_.refs_4_ = f32[5,4,1024]{2,1,0:T(4,128)S(1)} collective-permute-done((f32[5,4,1024]{2,1,0:T(4,128)S(1)}, f32[5,4,1024]{2,1,0:T(4,128)S(1)}, u32[]{:S(2)}, u32[]{:S(2)}) %collective-permute-start.6) | collective-permute-done | bytes 81952 | tf_op jit(solution)/shard_map/ppermute | solution.py:523
  34.1 0.3 collective-permute-done.7.refs_9_.refs_5_
  34.5 0.8 shard_map.65
  35.3 3.2 %collective-permute-start.8 = (f32[3,4,1024]{2,1,0:T(4,128)S(1)}, f32[3,4,1024]{2,1,0:T(4,128)S(1)}, u32[]{:S(2)}, u32[]{:S(2)}) collective-permute-start(f32[3,4,1024]{2,1,0:T(4,128)S(1)} %get-tuple-element.52), channel_id=1, source_target_pairs={{4,8},{12,16},{20,24},{28,32},{36,40},{44,48},{52,56},{60,64},{68,... | collective-permute-start | bytes 147464 | tf_op jit(solution)/shard_map/ppermute | solution.py:523
  38.5 1.9 %collective-permute-start.9 = (f32[3,4,1024]{2,1,0:T(4,128)S(1)}, f32[3,4,1024]{2,1,0:T(4,128)S(1)}, u32[]{:S(2)}, u32[]{:S(2)}) collective-permute-start(f32[3,4,1024]{2,1,0:T(4,128)S(1)} %get-tuple-element.53), channel_id=1, source_target_pairs={{0,4},{4,0},{8,12},{12,8},{16,20},{20,16},{24,28},{28,24},{32,36},... | collective-permute-start | bytes 147464 | tf_op jit(solution)/shard_map/ppermute | solution.py:524
  40.5 1.3 %shard_map.66 = (f32[7,8,1024]{2,1,0:T(8,128)S(1)}, f32[7,8,1024]{2,1,0:T(8,128)S(1)}, f32[1,128]{1,0:T(1,128)S(1)}) custom-call(f32[8,1024]{1,0:T(8,128)S(1)} %copy-done, f32[6,4,1024]{2,1,0:T(4,128)S(1)} %collective-permute-done.refs_3_.refs_1_, f32[6,4,1024]{2,1,0:T(4,128)S(1)} %collective-permute-done.1.refs_4_.refs_2_, ...), custom_call_target="tpu_custom_call" | custom-call | tf_op jit(solution)/shard_map/pallas_call | solution.py:573
  41.7 0.0 collective-permute-done.8.refs_5_
  41.7 0.0 collective-permute-done.9.refs_6_
  41.7 0.9 %shard_map.67 = (f32[4,8,1024]{2,1,0:T(8,128)S(1)}, f32[128,128]{1,0:T(8,128)S(1)}) custom-call(f32[4,8,1024]{2,1,0:T(8,128)S(1)} %get-tuple-element.51.refs_0_, f32[4,8,1024]{2,1,0:T(8,128)S(1)} %copy-done.1, f32[8,1024]{1,0:T(8,128)S(1)} %copy-done, f32[6,4,1024]{2,1,0:T(4,128)S(1)} %collective-permute-done.refs_3_.refs_1_, ...), custom_call_target="tpu_custom_call" | custom-call | tf_op jit(solution)/shard_map/pallas_call | solution.py:580
  42.6 33.0 %all_to_all.23 = f32[128,1,128]{2,1,0:T(1,128)S(1)} all-to-all(f32[128,1,128]{2,1,0:T(1,128)S(1)} %bitcast.10), channel_id=1, replica_groups=mesh['blk'=128,'rhs'=4] {'blk'}, dimensions={0} | all-to-all | bytes 131072 | tf_op jit(solution)/shard_map/all_to_all | solution.py:583
  75.6 1.4 %shard_map.68 = (f32[4,128]{1,0:T(4,128)}, f32[7,8,128]{2,1,0:T(8,128)S(1)}) custom-call(f32[128,128]{1,0:T(8,128)S(1)} %bitcast.9), custom_call_target="tpu_custom_call" | custom-call | tf_op jit(solution)/shard_map/pallas_call | solution.py:584
  77.0 4.0 %all-to-all-start.1 = ((f32[4,1,128]{2,1,0:T(1,128)}), f32[4,1,128]{2,1,0:T(1,128)S(1)}, u32[]{:S(2)}, u32[]{:S(2)}) async-start(f32[4,1,128]{2,1,0:T(1,128)} %bitcast.4), calls=%async_computation.1 | async-start | bytes 4096 | tf_op jit(solution)/shard_map/all_to_all | solution.py:589
  81.0 0.8 shard_map.69
  81.8 3.2 %all-to-all-done.1 = f32[4,1,128]{2,1,0:T(1,128)S(1)} async-done(((f32[4,1,128]{2,1,0:T(1,128)}), f32[4,1,128]{2,1,0:T(1,128)S(1)}, u32[]{:S(2)}, u32[]{:S(2)}) %all-to-all-start.1) | async-done | bytes 2080 | tf_op jit(solution)/shard_map/all_to_all | solution.py:589
  85.0 0.6 reshape.11
Async XLA Ops:
  0.6 11.3 %copy-start = (f32[8,1024]{1,0:T(8,128)S(1)}, f32[8,1024]{1,0:T(8,128)}, u32[]{:S(2)}) copy-start(f32[8,1024]{1,0:T(8,128)} %refs_2_.5) | copy-start | bytes 98308
  0.6 13.1 %copy-start.1 = (f32[4,8,1024]{2,1,0:T(8,128)S(1)}, f32[4,8,1024]{2,1,0:T(8,128)}, u32[]{:S(2)}) copy-start(f32[4,8,1024]{2,1,0:T(8,128)} %refs_1_.13) | copy-start | bytes 393220
  0.6 13.1 %copy-start.2 = (f32[4,8,1024]{2,1,0:T(8,128)S(1)}, f32[4,8,1024]{2,1,0:T(8,128)}, u32[]{:S(2)}) copy-start(f32[4,8,1024]{2,1,0:T(8,128)} %refs_0_.7) | copy-start | bytes 393220
  2.4 11.3 %collective-permute-start = (f32[6,4,1024]{2,1,0:T(4,128)}, f32[6,4,1024]{2,1,0:T(4,128)S(1)}, u32[]{:S(2)}, u32[]{:S(2)}) collective-permute-start(f32[6,4,1024]{2,1,0:T(4,128)} %get-tuple-element.32), channel_id=1, source_target_pairs={{4,8},{12,16},{20,24},{28,32},{36,40},{44,48},{52,56},{60,64},{68,... | collective-permute-start | bytes 294920 | tf_op jit(solution)/shard_map/ppermute | solution.py:523
  7.0 6.7 %collective-permute-start.1 = (f32[6,4,1024]{2,1,0:T(4,128)}, f32[6,4,1024]{2,1,0:T(4,128)S(1)}, u32[]{:S(2)}, u32[]{:S(2)}) collective-permute-start(f32[6,4,1024]{2,1,0:T(4,128)} %get-tuple-element.33), channel_id=1, source_target_pairs={{0,4},{4,0},{8,12},{12,8},{16,20},{20,16},{24,28},{28,24},{32,36},... | collective-permute-start | bytes 294920 | tf_op jit(solution)/shard_map/ppermute | solution.py:524
  11.9 0.8 copy-start.3
  14.8 5.2 %collective-permute-start.2 = (f32[8,1024]{1,0:T(8,128)S(1)}, f32[8,1024]{1,0:T(8,128)S(1)}, u32[]{:S(2)}, u32[]{:S(2)}) collective-permute-start(f32[8,1024]{1,0:T(8,128)S(1)} %get-tuple-element.42), channel_id=1, source_target_pairs={{4,8},{12,16},{20,24},{28,32},{36,40},{44,48},{52,56},{60,64},{68,... | collective-permute-start | bytes 98312 | tf_op jit(solution)/shard_map/ppermute | solution.py:523
  16.7 3.3 %collective-permute-start.3 = (f32[8,1024]{1,0:T(8,128)S(1)}, f32[8,1024]{1,0:T(8,128)S(1)}, u32[]{:S(2)}, u32[]{:S(2)}) collective-permute-start(f32[8,1024]{1,0:T(8,128)S(1)} %get-tuple-element.43), channel_id=1, source_target_pairs={{0,4},{4,0},{8,12},{12,8},{16,20},{20,16},{24,28},{28,24},{32,36},... | collective-permute-start | bytes 98312 | tf_op jit(solution)/shard_map/ppermute | solution.py:524
  21.0 6.3 %collective-permute-start.4 = (f32[4,1024]{1,0:T(4,128)S(1)}, f32[4,1024]{1,0:T(4,128)S(1)}, u32[]{:S(2)}, u32[]{:S(2)}) collective-permute-start(f32[4,1024]{1,0:T(4,128)S(1)} %get-tuple-element.45), channel_id=1, source_target_pairs={{4,8},{12,16},{20,24},{28,32},{36,40},{44,48},{52,56},{60,64},{68,... | collective-permute-start | bytes 49160 | tf_op jit(solution)/shard_map/ppermute | solution.py:523
  24.4 3.1 %collective-permute-start.5 = (f32[4,1024]{1,0:T(4,128)S(1)}, f32[4,1024]{1,0:T(4,128)S(1)}, u32[]{:S(2)}, u32[]{:S(2)}) collective-permute-start(f32[4,1024]{1,0:T(4,128)S(1)} %get-tuple-element.46), channel_id=1, source_target_pairs={{0,4},{4,0},{8,12},{12,8},{16,20},{20,16},{24,28},{28,24},{32,36},... | collective-permute-start | bytes 49160 | tf_op jit(solution)/shard_map/ppermute | solution.py:524
  28.4 5.8 %collective-permute-start.6 = (f32[5,4,1024]{2,1,0:T(4,128)S(1)}, f32[5,4,1024]{2,1,0:T(4,128)S(1)}, u32[]{:S(2)}, u32[]{:S(2)}) collective-permute-start(f32[5,4,1024]{2,1,0:T(4,128)S(1)} %get-tuple-element.49), channel_id=1, source_target_pairs={{4,8},{12,16},{20,24},{28,32},{36,40},{44,48},{52,56},{60,64},{68,... | collective-permute-start | bytes 245768 | tf_op jit(solution)/shard_map/ppermute | solution.py:523
  31.3 3.2 %collective-permute-start.7 = (f32[5,4,1024]{2,1,0:T(4,128)S(1)}, f32[5,4,1024]{2,1,0:T(4,128)S(1)}, u32[]{:S(2)}, u32[]{:S(2)}) collective-permute-start(f32[5,4,1024]{2,1,0:T(4,128)S(1)} %get-tuple-element.50), channel_id=1, source_target_pairs={{0,4},{4,0},{8,12},{12,8},{16,20},{20,16},{24,28},{28,24},{32,36},... | collective-permute-start | bytes 245768 | tf_op jit(solution)/shard_map/ppermute | solution.py:524
  35.3 6.4 %collective-permute-start.8 = (f32[3,4,1024]{2,1,0:T(4,128)S(1)}, f32[3,4,1024]{2,1,0:T(4,128)S(1)}, u32[]{:S(2)}, u32[]{:S(2)}) collective-permute-start(f32[3,4,1024]{2,1,0:T(4,128)S(1)} %get-tuple-element.52), channel_id=1, source_target_pairs={{4,8},{12,16},{20,24},{28,32},{36,40},{44,48},{52,56},{60,64},{68,... | collective-permute-start | bytes 147464 | tf_op jit(solution)/shard_map/ppermute | solution.py:523
  38.5 3.2 %collective-permute-start.9 = (f32[3,4,1024]{2,1,0:T(4,128)S(1)}, f32[3,4,1024]{2,1,0:T(4,128)S(1)}, u32[]{:S(2)}, u32[]{:S(2)}) collective-permute-start(f32[3,4,1024]{2,1,0:T(4,128)S(1)} %get-tuple-element.53), channel_id=1, source_target_pairs={{0,4},{4,0},{8,12},{12,8},{16,20},{20,16},{24,28},{28,24},{32,36},... | collective-permute-start | bytes 147464 | tf_op jit(solution)/shard_map/ppermute | solution.py:524
  77.0 8.0 %all-to-all-start.1 = ((f32[4,1,128]{2,1,0:T(1,128)}), f32[4,1,128]{2,1,0:T(1,128)S(1)}, u32[]{:S(2)}, u32[]{:S(2)}) async-start(f32[4,1,128]{2,1,0:T(1,128)} %bitcast.4), calls=%async_computation.1 | async-start | bytes 4096 | tf_op jit(solution)/shard_map/all_to_all | solution.py:589

commit v8 on v7

--- a/solution.py
+++ b/solution.py
@@ -165,7 +165,7 @@
     pairs = ((u_hbm, u), (f_hbm, f), (ext_hbm, ext))
     copies = [pltpu.make_async_copy(src, dst, sem.at[k]) for k, (src, dst) in enumerate(pairs)]
     for copy in copies:
-        copy.start()
+        copy.start(priority=1)
     for copy in copies:
         copy.wait()
     cases, rows, width = u.shape
@@ -287,7 +287,7 @@
     return flat_row(4 + 5 * k + j)
 
 
-def coarse_kernel_a(me, x0, ext, b, row_at, row_ok, same_col, h, rsum, cross, chip, x1, to_cross, to_chip, part):
+def coarse_kernel_a(me, x0, ext, b, row_at, row_ok, same_col, h, cross, chip, x1, to_cross, to_chip):
     before, after = sides(me, cross, chip)
     put = sender(me, to_cross, to_chip)
     cases, rows, width = x0.shape
@@ -297,16 +297,21 @@
         [after[row_of(c)] for c in range(cases)],
         ext, b, h, (row_at, row_ok, same_col),
     )
-    weight = open_weight(ext[...])
-    values = []
     for c in range(cases):
         x1[c] = x[c]
         put(row_of(c), x[c][0:1], x[c][rows - 1 : rows])
-        own = rsum[:, c : c + 1] - total(weight * x[c])
-        values.append((LANE_OWN + c, own))
-        values.append((LANE_TOP + c, total(x[c][0:1])))
-        values.append((LANE_BOTTOM + c, total(x[c][rows - 1 : rows])))
-    values.append((LANE_EXT, total(ext[...])))
+
+
+def sum_kernel(me, x1, ext, f, rsum, part):
+    cases, rows, width = x1.shape
+    weight = open_weight(ext[...])
+    values = [(LANE_EXT, total(ext[...]))]
+    for c in range(cases):
+        x = x1[c]
+        values.append((LANE_OWN + c, rsum[:, c : c + 1] - total(weight * x)))
+        values.append((LANE_TOP + c, total(x[0:1])))
+        values.append((LANE_BOTTOM + c, total(x[rows - 1 : rows])))
+        values.append((LANE_LOAD + c, dot(f[c], f[c])))
     part[...] = lane_row(values)
 
 
@@ -419,7 +424,7 @@
             put(response_row(k, j), y[k : k + 1], y[rows - 1 - k : rows - k])
 
 
-def coarse_kernel_c(me, x3, ext, b, row_at, row_ok, same_col, h, smooth, cross, chip, v, to_cross, to_chip):
+def coarse_kernel_c(me, x3, ext, b, row_at, row_ok, same_col, h, smooth, cross, chip, part, v, to_cross, to_chip):
     before, after = sides(me, cross, chip)
     put = sender(me, to_cross, to_chip)
     cases, rows, width = x3.shape
@@ -461,7 +466,6 @@
         for j in range(m):
             r = r - share[j] * q[j]
         values.append((LANE_PERP + c, dot(r, r)))
-        values.append((LANE_LOAD + c, dot(fl[c], fl[c])))
         for j in range(m):
             values.append((LANE_C + 8 * j + c, share[j]))
     row = part_a[...] + part_e[...] + lane_row(values)
@@ -558,9 +562,10 @@
         pre_kernel, [field, field, field, edges, edges, (1, 128)], n_in=10
     )(u, f, ext, *halo, *tables, y3)
     rows_x = exchange(*sent)
-    x1, *sent, part_a = call(coarse_kernel_a, [field, edge, edge, (1, 128)], n_in=10)(
-        x0, ext, b, *tables, rsum, *rows_x
-    )
+    x1, *sent = call(coarse_kernel_a, [field, edge, edge], n_in=9)(
+        x0, ext, b, *tables, *rows_x
+    )
+    (part_a,) = call(sum_kernel, [(1, 128)], n_in=4)(x1, ext, f, rsum)
     (y4,) = call(functools.partial(answer_kernel, cases), [(5, rows, width)], n_in=8)(
         ext, *tables, y3, *rows_x
     )
@@ -574,8 +579,8 @@
         response_kernel, [(m, rows, width), (m, rows, width), (1, 128)], n_in=6
     )(ext, *halo, y4, *rows_x)
     v, *sent = call(
-        coarse_kernel_c, [field, (3, cases, width), (3, cases, width)], n_in=10
-    )(x3, ext, b, *tables, smooth, *rows_x)
+        coarse_kernel_c, [field, (3, cases, width), (3, cases, width)], n_in=11
+    )(x3, ext, b, *tables, smooth, *rows_x, part_a)
     rows_x = exchange(*sent)
     base, mine = call(post_kernel, [field, (n, 128)], n_in=10)(
         v, f, ext, *halo, *rows_x, q, part_a, part_e

time: 86.1 us -> 85.9 us (level)
  no operation moved by 1% of the time
where the time goes in v8:
time: 85.9 us; the launch traced here: 85.4 us
  blocking collectives  33 us (38%)
  starting transfers between devices  32.7 us (38%)
  Pallas kernels  11.8 us (14%)
  waiting for transfers between devices  5.82 us (7%)
  local copies, waits for them, and re-layouts  1.36 us (2%)
  between operations  0.86 us (1%)
    all_to_all x1, blocking collectives, local(): gathered = lax.all_to_all(mine, 'blk', 0, 0, tiled=True)  33 us
    ppermute x5, starting transfers between devices, exchange(): cross = lax.ppermute(cross, 'blk', cross_chip)  16.1 us
    ppermute x5, starting transfers between devices, exchange(): return (cross, lax.ppermute(chip, 'blk', on_chip))  12.5 us
    all_to_all x1, starting transfers between devices, local(): every = lax.all_to_all(ratio, 'rhs', 0, 0, tiled=True)  4.01 us
    all_to_all x1, waiting for transfers between devices, local(): every = lax.all_to_all(ratio, 'rhs', 0, 0, tiled=True)  3.2 us
    ppermute x5, waiting for transfers between devices, exchange(): cross = lax.ppermute(cross, 'blk', cross_chip)  2.04 us
    pallas_call x1, Pallas kernels, local(): vmem_call(pack_kernel, [(6, cases, width)] * 2, [pltpu.VMEM(field, F32),...  1.75 us
  transfers between devices with their start and end apart: 11, of which 5 were waited for; matrix products, arithmetic and copies ran while one was open for 0% of the time, Pallas kernels for 5%

profile of v8, /device:TPU:1, one launch (start us, length us, event | category | flops | bytes accessed | tf_op | source)
XLA Modules:
  0.0 85.4 jit_solution(12276949172856095229)
XLA Ops:
  0.6 0.0 copy-start
  0.6 0.0 copy-start.1
  0.6 0.0 copy-start.2
  0.7 1.7 %shard_map.59 = (f32[6,4,1024]{2,1,0:T(4,128)}, f32[6,4,1024]{2,1,0:T(4,128)}) custom-call(f32[4,8,1024]{2,1,0:T(8,128)} %refs_0_.7, f32[4,8,1024]{2,1,0:T(8,128)} %refs_1_.15, f32[8,1024]{1,0:T(8,128)} %refs_2_.7), custom_call_target="tpu_custom_call" | custom-call | tf_op jit(solution)/shard_map/pallas_call | solution.py:535
  2.4 4.6 %collective-permute-start = (f32[6,4,1024]{2,1,0:T(4,128)}, f32[6,4,1024]{2,1,0:T(4,128)S(1)}, u32[]{:S(2)}, u32[]{:S(2)}) collective-permute-start(f32[6,4,1024]{2,1,0:T(4,128)} %get-tuple-element.31), channel_id=1, source_target_pairs={{4,8},{12,16},{20,24},{28,32},{36,40},{44,48},{52,56},{60,64},{68,... | collective-permute-start | bytes 294920 | tf_op jit(solution)/shard_map/ppermute | solution.py:527
  7.0 4.9 %collective-permute-start.1 = (f32[6,4,1024]{2,1,0:T(4,128)}, f32[6,4,1024]{2,1,0:T(4,128)S(1)}, u32[]{:S(2)}, u32[]{:S(2)}) collective-permute-start(f32[6,4,1024]{2,1,0:T(4,128)} %get-tuple-element.32), channel_id=1, source_target_pairs={{0,4},{4,0},{8,12},{12,8},{16,20},{20,16},{24,28},{28,24},{32,36},... | collective-permute-start | bytes 294920 | tf_op jit(solution)/shard_map/ppermute | solution.py:528
  11.9 0.0 copy-done
  11.9 0.0 copy-start.3
  11.9 0.7 copy-done.3
  12.7 1.1 %shard_map.60 = (s32[14,8,1024]{2,1,0:T(8,128)S(1)}, f32[14,8,1024]{2,1,0:T(8,128)S(1)}, f32[7,8,1024]{2,1,0:T(8,128)S(1)}, f32[8,1024]{1,0:T(8,128)S(1)}, f32[3,8,1024]{2,1,0:T(8,128)S(1)}) custom-call(f32[8,1024]{1,0:T(8,128)S(1)} %copy-done, s32[8,1024]{1,0:T(8,128)S(1)} %copy-done.3), custom_call_target="tpu_custom_call" | custom-call | tf_op jit(solution)/shard_map/pallas_call | solution.py:549
  13.7 0.0 collective-permute-done.refs_3_.refs_1_
  13.7 0.0 collective-permute-done.1.refs_4_.refs_2_
  13.7 0.0 copy-done.1
  13.7 0.0 copy-done.2
  13.8 1.0 %shard_map.61 = (f32[4,8,1024]{2,1,0:T(8,128)S(1)}, f32[4,8,1024]{2,1,0:T(8,128)S(1)}, f32[4,8,1024]{2,1,0:T(8,128)S(1)}, f32[8,1024]{1,0:T(8,128)S(1)}, f32[8,1024]{1,0:T(8,128)S(1)}, /*index=5*/f32[1,128]{1,0:T(1,128)S(1)}) custom-call(f32[4,8,1024]{2,1,0:T(8,128)S(1)} %copy-done.2, f32[4,8,1024]{2,1,0:T(8,128)S(1)} %copy-done.1, f32[8,1024]{1,0:T(8,128)S(1)} %copy-done, ...), custom_call_target="tpu_custom_call" | custom-call | tf_op jit(solution)/shard_map/pallas_call | solution.py:561
  14.8 1.9 %collective-permute-start.2 = (f32[8,1024]{1,0:T(8,128)S(1)}, f32[8,1024]{1,0:T(8,128)S(1)}, u32[]{:S(2)}, u32[]{:S(2)}) collective-permute-start(f32[8,1024]{1,0:T(8,128)S(1)} %get-tuple-element.40), channel_id=1, source_target_pairs={{4,8},{12,16},{20,24},{28,32},{36,40},{44,48},{52,56},{60,64},{68,... | collective-permute-start | bytes 98312 | tf_op jit(solution)/shard_map/ppermute | solution.py:527
  16.7 1.9 %collective-permute-start.3 = (f32[8,1024]{1,0:T(8,128)S(1)}, f32[8,1024]{1,0:T(8,128)S(1)}, u32[]{:S(2)}, u32[]{:S(2)}) collective-permute-start(f32[8,1024]{1,0:T(8,128)S(1)} %get-tuple-element.41), channel_id=1, source_target_pairs={{0,4},{4,0},{8,12},{12,8},{16,20},{20,16},{24,28},{28,24},{32,36},... | collective-permute-start | bytes 98312 | tf_op jit(solution)/shard_map/ppermute | solution.py:528
  18.7 1.4 %collective-permute-done.2.refs_7_.refs_6_ = f32[8,1024]{1,0:T(8,128)S(1)} collective-permute-done((f32[8,1024]{1,0:T(8,128)S(1)}, f32[8,1024]{1,0:T(8,128)S(1)}, u32[]{:S(2)}, u32[]{:S(2)}) %collective-permute-start.2) | collective-permute-done | bytes 32800 | tf_op jit(solution)/shard_map/ppermute | solution.py:527
  20.0 0.0 collective-permute-done.3.refs_8_.refs_7_
  20.0 0.8 shard_map.62
  20.8 3.4 %collective-permute-start.4 = (f32[4,1024]{1,0:T(4,128)S(1)}, f32[4,1024]{1,0:T(4,128)S(1)}, u32[]{:S(2)}, u32[]{:S(2)}) collective-permute-start(f32[4,1024]{1,0:T(4,128)S(1)} %get-tuple-element.43), channel_id=1, source_target_pairs={{4,8},{12,16},{20,24},{28,32},{36,40},{44,48},{52,56},{60,64},{68,... | collective-permute-start | bytes 49160 | tf_op jit(solution)/shard_map/ppermute | solution.py:527
  24.3 1.9 %collective-permute-start.5 = (f32[4,1024]{1,0:T(4,128)S(1)}, f32[4,1024]{1,0:T(4,128)S(1)}, u32[]{:S(2)}, u32[]{:S(2)}) collective-permute-start(f32[4,1024]{1,0:T(4,128)S(1)} %get-tuple-element.44), channel_id=1, source_target_pairs={{0,4},{4,0},{8,12},{12,8},{16,20},{20,16},{24,28},{28,24},{32,36},... | collective-permute-start | bytes 49160 | tf_op jit(solution)/shard_map/ppermute | solution.py:528
  26.2 0.9 %shard_map.63.refs_7_.refs_3_ = f32[5,8,1024]{2,1,0:T(8,128)S(1)} custom-call(f32[8,1024]{1,0:T(8,128)S(1)} %copy-done, s32[14,8,1024]{2,1,0:T(8,128)S(1)} %get-tuple-element.33.refs_5_.refs_3_.refs_1_, f32[14,8,1024]{2,1,0:T(8,128)S(1)} %get-tuple-element.34.refs_6_.refs_4_.refs_2_, f32[7,8,1024]{2,1,0:T(8,128)S(1)} %get-tuple-element.35.refs_7_.refs_5_.refs_3_, ...), custom_call_target="tpu_custom_call" | custom-call | tf_op jit(solution)/shard_map/pallas_call | solution.py:569
  27.1 0.0 collective-permute-done.4.refs_8_
  27.1 0.2 collective-permute-done.5.refs_9_
  27.4 0.9 shard_map.64
  28.2 2.9 %collective-permute-start.6 = (f32[5,4,1024]{2,1,0:T(4,128)S(1)}, f32[5,4,1024]{2,1,0:T(4,128)S(1)}, u32[]{:S(2)}, u32[]{:S(2)}) collective-permute-start(f32[5,4,1024]{2,1,0:T(4,128)S(1)} %get-tuple-element.47), channel_id=1, source_target_pairs={{4,8},{12,16},{20,24},{28,32},{36,40},{44,48},{52,56},{60,64},{68,... | collective-permute-start | bytes 245768 | tf_op jit(solution)/shard_map/ppermute | solution.py:527
  31.2 1.9 %collective-permute-start.7 = (f32[5,4,1024]{2,1,0:T(4,128)S(1)}, f32[5,4,1024]{2,1,0:T(4,128)S(1)}, u32[]{:S(2)}, u32[]{:S(2)}) collective-permute-start(f32[5,4,1024]{2,1,0:T(4,128)S(1)} %get-tuple-element.48), channel_id=1, source_target_pairs={{0,4},{4,0},{8,12},{12,8},{16,20},{20,16},{24,28},{28,24},{32,36},... | collective-permute-start | bytes 245768 | tf_op jit(solution)/shard_map/ppermute | solution.py:528
  33.1 0.2 shard_map.65.refs_10_.refs_8_
  33.3 0.7 collective-permute-done.6.refs_8_.refs_4_
  34.0 0.4 collective-permute-done.7.refs_9_.refs_5_
  34.3 0.8 shard_map.66
  35.2 3.2 %collective-permute-start.8 = (f32[3,4,1024]{2,1,0:T(4,128)S(1)}, f32[3,4,1024]{2,1,0:T(4,128)S(1)}, u32[]{:S(2)}, u32[]{:S(2)}) collective-permute-start(f32[3,4,1024]{2,1,0:T(4,128)S(1)} %get-tuple-element.51), channel_id=1, source_target_pairs={{4,8},{12,16},{20,24},{28,32},{36,40},{44,48},{52,56},{60,64},{68,... | collective-permute-start | bytes 147464 | tf_op jit(solution)/shard_map/ppermute | solution.py:527
  38.4 1.9 %collective-permute-start.9 = (f32[3,4,1024]{2,1,0:T(4,128)S(1)}, f32[3,4,1024]{2,1,0:T(4,128)S(1)}, u32[]{:S(2)}, u32[]{:S(2)}) collective-permute-start(f32[3,4,1024]{2,1,0:T(4,128)S(1)} %get-tuple-element.52), channel_id=1, source_target_pairs={{0,4},{4,0},{8,12},{12,8},{16,20},{20,16},{24,28},{28,24},{32,36},... | collective-permute-start | bytes 147464 | tf_op jit(solution)/shard_map/ppermute | solution.py:528
  40.3 1.3 %shard_map.67 = (f32[7,8,1024]{2,1,0:T(8,128)S(1)}, f32[7,8,1024]{2,1,0:T(8,128)S(1)}, f32[1,128]{1,0:T(1,128)S(1)}) custom-call(f32[8,1024]{1,0:T(8,128)S(1)} %copy-done, f32[6,4,1024]{2,1,0:T(4,128)S(1)} %collective-permute-done.refs_3_.refs_1_, f32[6,4,1024]{2,1,0:T(4,128)S(1)} %collective-permute-done.1.refs_4_.refs_2_, ...), custom_call_target="tpu_custom_call" | custom-call | tf_op jit(solution)/shard_map/pallas_call | solution.py:578
  41.6 0.0 collective-permute-done.8.refs_5_
  41.6 0.0 collective-permute-done.9.refs_6_
  41.6 0.9 shard_map.68
  42.5 33.0 %all_to_all.23 = f32[128,1,128]{2,1,0:T(1,128)S(1)} all-to-all(f32[128,1,128]{2,1,0:T(1,128)S(1)} %bitcast.10), channel_id=1, replica_groups=mesh['blk'=128,'rhs'=4] {'blk'}, dimensions={0} | all-to-all | bytes 131072 | tf_op jit(solution)/shard_map/all_to_all | solution.py:588
  75.4 1.4 %shard_map.69 = (f32[4,128]{1,0:T(4,128)}, f32[7,8,128]{2,1,0:T(8,128)S(1)}) custom-call(f32[128,128]{1,0:T(8,128)S(1)} %bitcast.9), custom_call_target="tpu_custom_call" | custom-call | tf_op jit(solution)/shard_map/pallas_call | solution.py:589
  76.9 4.0 %all-to-all-start.1 = ((f32[4,1,128]{2,1,0:T(1,128)}), f32[4,1,128]{2,1,0:T(1,128)S(1)}, u32[]{:S(2)}, u32[]{:S(2)}) async-start(f32[4,1,128]{2,1,0:T(1,128)} %bitcast.4), calls=%async_computation.1 | async-start | bytes 4096 | tf_op jit(solution)/shard_map/all_to_all | solution.py:594
  80.9 0.8 shard_map.70
  81.6 3.2 %all-to-all-done.1 = f32[4,1,128]{2,1,0:T(1,128)S(1)} async-done(((f32[4,1,128]{2,1,0:T(1,128)}), f32[4,1,128]{2,1,0:T(1,128)S(1)}, u32[]{:S(2)}, u32[]{:S(2)}) %all-to-all-start.1) | async-done | bytes 2080 | tf_op jit(solution)/shard_map/all_to_all | solution.py:594
  84.8 0.6 reshape.11
Async XLA Ops:
  0.6 11.3 %copy-start = (f32[8,1024]{1,0:T(8,128)S(1)}, f32[8,1024]{1,0:T(8,128)}, u32[]{:S(2)}) copy-start(f32[8,1024]{1,0:T(8,128)} %refs_2_.7) | copy-start | bytes 98308
  0.6 13.1 %copy-start.1 = (f32[4,8,1024]{2,1,0:T(8,128)S(1)}, f32[4,8,1024]{2,1,0:T(8,128)}, u32[]{:S(2)}) copy-start(f32[4,8,1024]{2,1,0:T(8,128)} %refs_1_.15) | copy-start | bytes 393220
  0.6 13.1 %copy-start.2 = (f32[4,8,1024]{2,1,0:T(8,128)S(1)}, f32[4,8,1024]{2,1,0:T(8,128)}, u32[]{:S(2)}) copy-start(f32[4,8,1024]{2,1,0:T(8,128)} %refs_0_.7) | copy-start | bytes 393220
  2.4 11.3 %collective-permute-start = (f32[6,4,1024]{2,1,0:T(4,128)}, f32[6,4,1024]{2,1,0:T(4,128)S(1)}, u32[]{:S(2)}, u32[]{:S(2)}) collective-permute-start(f32[6,4,1024]{2,1,0:T(4,128)} %get-tuple-element.31), channel_id=1, source_target_pairs={{4,8},{12,16},{20,24},{28,32},{36,40},{44,48},{52,56},{60,64},{68,... | collective-permute-start | bytes 294920 | tf_op jit(solution)/shard_map/ppermute | solution.py:527
  7.0 6.7 %collective-permute-start.1 = (f32[6,4,1024]{2,1,0:T(4,128)}, f32[6,4,1024]{2,1,0:T(4,128)S(1)}, u32[]{:S(2)}, u32[]{:S(2)}) collective-permute-start(f32[6,4,1024]{2,1,0:T(4,128)} %get-tuple-element.32), channel_id=1, source_target_pairs={{0,4},{4,0},{8,12},{12,8},{16,20},{20,16},{24,28},{28,24},{32,36},... | collective-permute-start | bytes 294920 | tf_op jit(solution)/shard_map/ppermute | solution.py:528
  11.9 0.8 copy-start.3
  14.8 5.2 %collective-permute-start.2 = (f32[8,1024]{1,0:T(8,128)S(1)}, f32[8,1024]{1,0:T(8,128)S(1)}, u32[]{:S(2)}, u32[]{:S(2)}) collective-permute-start(f32[8,1024]{1,0:T(8,128)S(1)} %get-tuple-element.40), channel_id=1, source_target_pairs={{4,8},{12,16},{20,24},{28,32},{36,40},{44,48},{52,56},{60,64},{68,... | collective-permute-start | bytes 98312 | tf_op jit(solution)/shard_map/ppermute | solution.py:527
  16.7 3.3 %collective-permute-start.3 = (f32[8,1024]{1,0:T(8,128)S(1)}, f32[8,1024]{1,0:T(8,128)S(1)}, u32[]{:S(2)}, u32[]{:S(2)}) collective-permute-start(f32[8,1024]{1,0:T(8,128)S(1)} %get-tuple-element.41), channel_id=1, source_target_pairs={{0,4},{4,0},{8,12},{12,8},{16,20},{20,16},{24,28},{28,24},{32,36},... | collective-permute-start | bytes 98312 | tf_op jit(solution)/shard_map/ppermute | solution.py:528
  20.8 6.3 %collective-permute-start.4 = (f32[4,1024]{1,0:T(4,128)S(1)}, f32[4,1024]{1,0:T(4,128)S(1)}, u32[]{:S(2)}, u32[]{:S(2)}) collective-permute-start(f32[4,1024]{1,0:T(4,128)S(1)} %get-tuple-element.43), channel_id=1, source_target_pairs={{4,8},{12,16},{20,24},{28,32},{36,40},{44,48},{52,56},{60,64},{68,... | collective-permute-start | bytes 49160 | tf_op jit(solution)/shard_map/ppermute | solution.py:527
  24.3 3.1 %collective-permute-start.5 = (f32[4,1024]{1,0:T(4,128)S(1)}, f32[4,1024]{1,0:T(4,128)S(1)}, u32[]{:S(2)}, u32[]{:S(2)}) collective-permute-start(f32[4,1024]{1,0:T(4,128)S(1)} %get-tuple-element.44), channel_id=1, source_target_pairs={{0,4},{4,0},{8,12},{12,8},{16,20},{20,16},{24,28},{28,24},{32,36},... | collective-permute-start | bytes 49160 | tf_op jit(solution)/shard_map/ppermute | solution.py:528
  28.2 5.8 %collective-permute-start.6 = (f32[5,4,1024]{2,1,0:T(4,128)S(1)}, f32[5,4,1024]{2,1,0:T(4,128)S(1)}, u32[]{:S(2)}, u32[]{:S(2)}) collective-permute-start(f32[5,4,1024]{2,1,0:T(4,128)S(1)} %get-tuple-element.47), channel_id=1, source_target_pairs={{4,8},{12,16},{20,24},{28,32},{36,40},{44,48},{52,56},{60,64},{68,... | collective-permute-start | bytes 245768 | tf_op jit(solution)/shard_map/ppermute | solution.py:527
  31.2 3.2 %collective-permute-start.7 = (f32[5,4,1024]{2,1,0:T(4,128)S(1)}, f32[5,4,1024]{2,1,0:T(4,128)S(1)}, u32[]{:S(2)}, u32[]{:S(2)}) collective-permute-start(f32[5,4,1024]{2,1,0:T(4,128)S(1)} %get-tuple-element.48), channel_id=1, source_target_pairs={{0,4},{4,0},{8,12},{12,8},{16,20},{20,16},{24,28},{28,24},{32,36},... | collective-permute-start | bytes 245768 | tf_op jit(solution)/shard_map/ppermute | solution.py:528
  35.2 6.4 %collective-permute-start.8 = (f32[3,4,1024]{2,1,0:T(4,128)S(1)}, f32[3,4,1024]{2,1,0:T(4,128)S(1)}, u32[]{:S(2)}, u32[]{:S(2)}) collective-permute-start(f32[3,4,1024]{2,1,0:T(4,128)S(1)} %get-tuple-element.51), channel_id=1, source_target_pairs={{4,8},{12,16},{20,24},{28,32},{36,40},{44,48},{52,56},{60,64},{68,... | collective-permute-start | bytes 147464 | tf_op jit(solution)/shard_map/ppermute | solution.py:527
  38.4 3.2 %collective-permute-start.9 = (f32[3,4,1024]{2,1,0:T(4,128)S(1)}, f32[3,4,1024]{2,1,0:T(4,128)S(1)}, u32[]{:S(2)}, u32[]{:S(2)}) collective-permute-start(f32[3,4,1024]{2,1,0:T(4,128)S(1)} %get-tuple-element.52), channel_id=1, source_target_pairs={{0,4},{4,0},{8,12},{12,8},{16,20},{20,16},{24,28},{28,24},{32,36},... | collective-permute-start | bytes 147464 | tf_op jit(solution)/shard_map/ppermute | solution.py:528
  76.9 8.0 %all-to-all-start.1 = ((f32[4,1,128]{2,1,0:T(1,128)}), f32[4,1,128]{2,1,0:T(1,128)S(1)}, u32[]{:S(2)}, u32[]{:S(2)}) async-start(f32[4,1,128]{2,1,0:T(1,128)} %bitcast.4), calls=%async_computation.1 | async-start | bytes 4096 | tf_op jit(solution)/shard_map/all_to_all | solution.py:594

commit v9 on v8

--- a/solution.py
+++ b/solution.py
@@ -24,7 +24,7 @@
 
 
 def vmem_call(body, outs, scratch=(), n_in=0, in_space=pltpu.VMEM):
-    limit = 48 << 20 if in_space == pltpu.VMEM else None
+    limit = 48 << 20 if in_space == pltpu.VMEM else 56_288_000
     return pl.pallas_call(
         with_place(body),
         out_shape=[
@@ -165,7 +165,7 @@
     pairs = ((u_hbm, u), (f_hbm, f), (ext_hbm, ext))
     copies = [pltpu.make_async_copy(src, dst, sem.at[k]) for k, (src, dst) in enumerate(pairs)]
     for copy in copies:
-        copy.start(priority=1)
+        copy.start()
     for copy in copies:
         copy.wait()
     cases, rows, width = u.shape

time: 85.9 us -> 85.8 us (level)
  no operation moved by 1% of the time
where the time goes in v9:
time: 85.8 us; the launch traced here: 85.3 us
  starting transfers between devices  33.2 us (39%)
  blocking collectives  33 us (38%)
  Pallas kernels  11.1 us (13%)
  waiting for transfers between devices  5.82 us (7%)
  local copies, waits for them, and re-layouts  1.35 us (2%)
    all_to_all x1, blocking collectives, local(): gathered = lax.all_to_all(mine, 'blk', 0, 0, tiled=True)  33 us
    ppermute x5, starting transfers between devices, exchange(): cross = lax.ppermute(cross, 'blk', cross_chip)  16.6 us
    ppermute x5, starting transfers between devices, exchange(): return (cross, lax.ppermute(chip, 'blk', on_chip))  12.5 us
    all_to_all x1, starting transfers between devices, local(): every = lax.all_to_all(ratio, 'rhs', 0, 0, tiled=True)  4.01 us
    all_to_all x1, waiting for transfers between devices, local(): every = lax.all_to_all(ratio, 'rhs', 0, 0, tiled=True)  3.2 us
    ppermute x5, waiting for transfers between devices, exchange(): cross = lax.ppermute(cross, 'blk', cross_chip)  2.04 us
  transfers between devices with their start and end apart: 11, of which 5 were waited for; matrix products, arithmetic and copies ran while one was open for 0% of the time, Pallas kernels for 5%

profile of v9, /device:TPU:1, one launch (start us, length us, event | category | flops | bytes accessed | tf_op | source)
XLA Modules:
  0.0 85.3 jit_solution(3959340649080439774)
XLA Ops:
  0.6 0.0 copy-start
  0.6 0.7 copy-done
  1.4 0.0 copy-start.3
  1.4 0.0 copy-start.1
  1.4 0.0 copy-start.2
  1.4 1.1 %shard_map.59 = (f32[6,4,1024]{2,1,0:T(4,128)S(1)}, f32[6,4,1024]{2,1,0:T(4,128)S(1)}) custom-call(f32[4,8,1024]{2,1,0:T(8,128)} %refs_0_.7, f32[4,8,1024]{2,1,0:T(8,128)} %refs_1_.15, f32[8,1024]{1,0:T(8,128)S(1)} %copy-done), custom_call_target="tpu_custom_call" | custom-call | tf_op jit(solution)/shard_map/pallas_call | solution.py:535
  2.5 4.6 %collective-permute-start = (f32[6,4,1024]{2,1,0:T(4,128)S(1)}, f32[6,4,1024]{2,1,0:T(4,128)S(1)}, u32[]{:S(2)}, u32[]{:S(2)}) collective-permute-start(f32[6,4,1024]{2,1,0:T(4,128)S(1)} %get-tuple-element.31), channel_id=1, source_target_pairs={{4,8},{12,16},{20,24},{28,32},{36,40},{44,48},{52,56},{60,64},{68,... | collective-permute-start | bytes 294920 | tf_op jit(solution)/shard_map/ppermute | solution.py:527
  7.1 4.9 %collective-permute-start.1 = (f32[6,4,1024]{2,1,0:T(4,128)S(1)}, f32[6,4,1024]{2,1,0:T(4,128)S(1)}, u32[]{:S(2)}, u32[]{:S(2)}) collective-permute-start(f32[6,4,1024]{2,1,0:T(4,128)S(1)} %get-tuple-element.32), channel_id=1, source_target_pairs={{0,4},{4,0},{8,12},{12,8},{16,20},{20,16},{24,28},{28,24},{32,36},... | collective-permute-start | bytes 294920 | tf_op jit(solution)/shard_map/ppermute | solution.py:528
  11.9 0.0 copy-done.3
  12.0 1.1 %shard_map.60 = (s32[14,8,1024]{2,1,0:T(8,128)S(1)}, f32[14,8,1024]{2,1,0:T(8,128)S(1)}, f32[7,8,1024]{2,1,0:T(8,128)S(1)}, f32[8,1024]{1,0:T(8,128)S(1)}, f32[3,8,1024]{2,1,0:T(8,128)S(1)}) custom-call(f32[8,1024]{1,0:T(8,128)S(1)} %copy-done, s32[8,1024]{1,0:T(8,128)S(1)} %copy-done.3), custom_call_target="tpu_custom_call" | custom-call | tf_op jit(solution)/shard_map/pallas_call | solution.py:549
  13.0 0.0 collective-permute-done.refs_3_.refs_1_
  13.0 0.0 collective-permute-done.1.refs_4_.refs_2_
  13.0 0.0 copy-done.1
  13.1 0.0 copy-done.2
  13.1 1.0 %shard_map.61 = (f32[4,8,1024]{2,1,0:T(8,128)S(1)}, f32[4,8,1024]{2,1,0:T(8,128)S(1)}, f32[4,8,1024]{2,1,0:T(8,128)S(1)}, f32[8,1024]{1,0:T(8,128)S(1)}, f32[8,1024]{1,0:T(8,128)S(1)}, /*index=5*/f32[1,128]{1,0:T(1,128)S(1)}) custom-call(f32[4,8,1024]{2,1,0:T(8,128)S(1)} %copy-done.2, f32[4,8,1024]{2,1,0:T(8,128)S(1)} %copy-done.1, f32[8,1024]{1,0:T(8,128)S(1)} %copy-done, ...), custom_call_target="tpu_custom_call" | custom-call | tf_op jit(solution)/shard_map/pallas_call | solution.py:561
  14.1 1.9 %collective-permute-start.2 = (f32[8,1024]{1,0:T(8,128)S(1)}, f32[8,1024]{1,0:T(8,128)S(1)}, u32[]{:S(2)}, u32[]{:S(2)}) collective-permute-start(f32[8,1024]{1,0:T(8,128)S(1)} %get-tuple-element.40), channel_id=1, source_target_pairs={{4,8},{12,16},{20,24},{28,32},{36,40},{44,48},{52,56},{60,64},{68,... | collective-permute-start | bytes 98312 | tf_op jit(solution)/shard_map/ppermute | solution.py:527
  16.0 1.9 %collective-permute-start.3 = (f32[8,1024]{1,0:T(8,128)S(1)}, f32[8,1024]{1,0:T(8,128)S(1)}, u32[]{:S(2)}, u32[]{:S(2)}) collective-permute-start(f32[8,1024]{1,0:T(8,128)S(1)} %get-tuple-element.41), channel_id=1, source_target_pairs={{0,4},{4,0},{8,12},{12,8},{16,20},{20,16},{24,28},{28,24},{32,36},... | collective-permute-start | bytes 98312 | tf_op jit(solution)/shard_map/ppermute | solution.py:528
  18.0 1.4 %collective-permute-done.2.refs_7_.refs_6_ = f32[8,1024]{1,0:T(8,128)S(1)} collective-permute-done((f32[8,1024]{1,0:T(8,128)S(1)}, f32[8,1024]{1,0:T(8,128)S(1)}, u32[]{:S(2)}, u32[]{:S(2)}) %collective-permute-start.2) | collective-permute-done | bytes 32800 | tf_op jit(solution)/shard_map/ppermute | solution.py:527
  19.4 0.0 collective-permute-done.3.refs_8_.refs_7_
  19.4 0.8 shard_map.62
  20.2 3.4 %collective-permute-start.4 = (f32[4,1024]{1,0:T(4,128)S(1)}, f32[4,1024]{1,0:T(4,128)S(1)}, u32[]{:S(2)}, u32[]{:S(2)}) collective-permute-start(f32[4,1024]{1,0:T(4,128)S(1)} %get-tuple-element.43), channel_id=1, source_target_pairs={{4,8},{12,16},{20,24},{28,32},{36,40},{44,48},{52,56},{60,64},{68,... | collective-permute-start | bytes 49160 | tf_op jit(solution)/shard_map/ppermute | solution.py:527
  23.6 1.9 %collective-permute-start.5 = (f32[4,1024]{1,0:T(4,128)S(1)}, f32[4,1024]{1,0:T(4,128)S(1)}, u32[]{:S(2)}, u32[]{:S(2)}) collective-permute-start(f32[4,1024]{1,0:T(4,128)S(1)} %get-tuple-element.44), channel_id=1, source_target_pairs={{0,4},{4,0},{8,12},{12,8},{16,20},{20,16},{24,28},{28,24},{32,36},... | collective-permute-start | bytes 49160 | tf_op jit(solution)/shard_map/ppermute | solution.py:528
  25.5 0.9 %shard_map.63.refs_7_.refs_3_ = f32[5,8,1024]{2,1,0:T(8,128)S(1)} custom-call(f32[8,1024]{1,0:T(8,128)S(1)} %copy-done, s32[14,8,1024]{2,1,0:T(8,128)S(1)} %get-tuple-element.33.refs_5_.refs_3_.refs_1_, f32[14,8,1024]{2,1,0:T(8,128)S(1)} %get-tuple-element.34.refs_6_.refs_4_.refs_2_, f32[7,8,1024]{2,1,0:T(8,128)S(1)} %get-tuple-element.35.refs_7_.refs_5_.refs_3_, ...), custom_call_target="tpu_custom_call" | custom-call | tf_op jit(solution)/shard_map/pallas_call | solution.py:569
  26.4 0.0 collective-permute-done.4.refs_8_
  26.5 0.2 collective-permute-done.5.refs_9_
  26.7 0.9 shard_map.64
  27.5 2.9 %collective-permute-start.6 = (f32[5,4,1024]{2,1,0:T(4,128)S(1)}, f32[5,4,1024]{2,1,0:T(4,128)S(1)}, u32[]{:S(2)}, u32[]{:S(2)}) collective-permute-start(f32[5,4,1024]{2,1,0:T(4,128)S(1)} %get-tuple-element.47), channel_id=1, source_target_pairs={{4,8},{12,16},{20,24},{28,32},{36,40},{44,48},{52,56},{60,64},{68,... | collective-permute-start | bytes 245768 | tf_op jit(solution)/shard_map/ppermute | solution.py:527
  30.5 1.9 %collective-permute-start.7 = (f32[5,4,1024]{2,1,0:T(4,128)S(1)}, f32[5,4,1024]{2,1,0:T(4,128)S(1)}, u32[]{:S(2)}, u32[]{:S(2)}) collective-permute-start(f32[5,4,1024]{2,1,0:T(4,128)S(1)} %get-tuple-element.48), channel_id=1, source_target_pairs={{0,4},{4,0},{8,12},{12,8},{16,20},{20,16},{24,28},{28,24},{32,36},... | collective-permute-start | bytes 245768 | tf_op jit(solution)/shard_map/ppermute | solution.py:528
  32.4 0.2 shard_map.65.refs_10_.refs_8_
  32.6 0.7 collective-permute-done.6.refs_8_.refs_4_
  33.3 0.4 collective-permute-done.7.refs_9_.refs_5_
  33.6 0.8 shard_map.66
  34.5 3.8 %collective-permute-start.8 = (f32[3,4,1024]{2,1,0:T(4,128)S(1)}, f32[3,4,1024]{2,1,0:T(4,128)S(1)}, u32[]{:S(2)}, u32[]{:S(2)}) collective-permute-start(f32[3,4,1024]{2,1,0:T(4,128)S(1)} %get-tuple-element.51), channel_id=1, source_target_pairs={{4,8},{12,16},{20,24},{28,32},{36,40},{44,48},{52,56},{60,64},{68,... | collective-permute-start | bytes 147464 | tf_op jit(solution)/shard_map/ppermute | solution.py:527
  38.3 1.9 %collective-permute-start.9 = (f32[3,4,1024]{2,1,0:T(4,128)S(1)}, f32[3,4,1024]{2,1,0:T(4,128)S(1)}, u32[]{:S(2)}, u32[]{:S(2)}) collective-permute-start(f32[3,4,1024]{2,1,0:T(4,128)S(1)} %get-tuple-element.52), channel_id=1, source_target_pairs={{0,4},{4,0},{8,12},{12,8},{16,20},{20,16},{24,28},{28,24},{32,36},... | collective-permute-start | bytes 147464 | tf_op jit(solution)/shard_map/ppermute | solution.py:528
  40.2 1.3 %shard_map.67 = (f32[7,8,1024]{2,1,0:T(8,128)S(1)}, f32[7,8,1024]{2,1,0:T(8,128)S(1)}, f32[1,128]{1,0:T(1,128)S(1)}) custom-call(f32[8,1024]{1,0:T(8,128)S(1)} %copy-done, f32[6,4,1024]{2,1,0:T(4,128)S(1)} %collective-permute-done.refs_3_.refs_1_, f32[6,4,1024]{2,1,0:T(4,128)S(1)} %collective-permute-done.1.refs_4_.refs_2_, ...), custom_call_target="tpu_custom_call" | custom-call | tf_op jit(solution)/shard_map/pallas_call | solution.py:578
  41.4 0.0 collective-permute-done.8.refs_5_
  41.5 0.0 collective-permute-done.9.refs_6_
  41.5 0.9 %shard_map.68 = (f32[4,8,1024]{2,1,0:T(8,128)S(1)}, f32[128,128]{1,0:T(8,128)S(1)}) custom-call(f32[4,8,1024]{2,1,0:T(8,128)S(1)} %get-tuple-element.50.refs_0_, f32[4,8,1024]{2,1,0:T(8,128)S(1)} %copy-done.1, f32[8,1024]{1,0:T(8,128)S(1)} %copy-done, f32[6,4,1024]{2,1,0:T(4,128)S(1)} %collective-permute-done.refs_3_.refs_1_, ...), custom_call_target="tpu_custom_call" | custom-call | tf_op jit(solution)/shard_map/pallas_call | solution.py:585
  42.3 33.0 %all_to_all.23 = f32[128,1,128]{2,1,0:T(1,128)S(1)} all-to-all(f32[128,1,128]{2,1,0:T(1,128)S(1)} %bitcast.10), channel_id=1, replica_groups=mesh['blk'=128,'rhs'=4] {'blk'}, dimensions={0} | all-to-all | bytes 131072 | tf_op jit(solution)/shard_map/all_to_all | solution.py:588
  75.3 1.4 %shard_map.69 = (f32[4,128]{1,0:T(4,128)}, f32[7,8,128]{2,1,0:T(8,128)S(1)}) custom-call(f32[128,128]{1,0:T(8,128)S(1)} %bitcast.9), custom_call_target="tpu_custom_call" | custom-call | tf_op jit(solution)/shard_map/pallas_call | solution.py:589
  76.7 4.0 %all-to-all-start.1 = ((f32[4,1,128]{2,1,0:T(1,128)}), f32[4,1,128]{2,1,0:T(1,128)S(1)}, u32[]{:S(2)}, u32[]{:S(2)}) async-start(f32[4,1,128]{2,1,0:T(1,128)} %bitcast.4), calls=%async_computation.1 | async-start | bytes 4096 | tf_op jit(solution)/shard_map/all_to_all | solution.py:594
  80.7 0.8 shard_map.70
  81.5 3.2 %all-to-all-done.1 = f32[4,1,128]{2,1,0:T(1,128)S(1)} async-done(((f32[4,1,128]{2,1,0:T(1,128)}), f32[4,1,128]{2,1,0:T(1,128)S(1)}, u32[]{:S(2)}, u32[]{:S(2)}) %all-to-all-start.1) | async-done | bytes 2080 | tf_op jit(solution)/shard_map/all_to_all | solution.py:594
  84.7 0.6 reshape.11
Async XLA Ops:
  0.6 0.8 copy-start
  1.4 10.6 %copy-start.3 = (s32[8,1024]{1,0:T(8,128)S(1)}, s32[8,1024]{1,0:T(8,128)}, u32[]{:S(2)}) copy-start(s32[8,1024]{1,0:T(8,128)} %refs_1_.9) | copy-start | bytes 98308
  1.4 11.7 %copy-start.1 = (f32[4,8,1024]{2,1,0:T(8,128)S(1)}, f32[4,8,1024]{2,1,0:T(8,128)}, u32[]{:S(2)}) copy-start(f32[4,8,1024]{2,1,0:T(8,128)} %refs_1_.15) | copy-start | bytes 393220
  1.4 11.7 %copy-start.2 = (f32[4,8,1024]{2,1,0:T(8,128)S(1)}, f32[4,8,1024]{2,1,0:T(8,128)}, u32[]{:S(2)}) copy-start(f32[4,8,1024]{2,1,0:T(8,128)} %refs_0_.7) | copy-start | bytes 393220
  2.5 10.5 %collective-permute-start = (f32[6,4,1024]{2,1,0:T(4,128)S(1)}, f32[6,4,1024]{2,1,0:T(4,128)S(1)}, u32[]{:S(2)}, u32[]{:S(2)}) collective-permute-start(f32[6,4,1024]{2,1,0:T(4,128)S(1)} %get-tuple-element.31), channel_id=1, source_target_pairs={{4,8},{12,16},{20,24},{28,32},{36,40},{44,48},{52,56},{60,64},{68,... | collective-permute-start | bytes 294920 | tf_op jit(solution)/shard_map/ppermute | solution.py:527
  7.1 6.0 %collective-permute-start.1 = (f32[6,4,1024]{2,1,0:T(4,128)S(1)}, f32[6,4,1024]{2,1,0:T(4,128)S(1)}, u32[]{:S(2)}, u32[]{:S(2)}) collective-permute-start(f32[6,4,1024]{2,1,0:T(4,128)S(1)} %get-tuple-element.32), channel_id=1, source_target_pairs={{0,4},{4,0},{8,12},{12,8},{16,20},{20,16},{24,28},{28,24},{32,36},... | collective-permute-start | bytes 294920 | tf_op jit(solution)/shard_map/ppermute | solution.py:528
  14.1 5.2 %collective-permute-start.2 = (f32[8,1024]{1,0:T(8,128)S(1)}, f32[8,1024]{1,0:T(8,128)S(1)}, u32[]{:S(2)}, u32[]{:S(2)}) collective-permute-start(f32[8,1024]{1,0:T(8,128)S(1)} %get-tuple-element.40), channel_id=1, source_target_pairs={{4,8},{12,16},{20,24},{28,32},{36,40},{44,48},{52,56},{60,64},{68,... | collective-permute-start | bytes 98312 | tf_op jit(solution)/shard_map/ppermute | solution.py:527
  16.0 3.3 %collective-permute-start.3 = (f32[8,1024]{1,0:T(8,128)S(1)}, f32[8,1024]{1,0:T(8,128)S(1)}, u32[]{:S(2)}, u32[]{:S(2)}) collective-permute-start(f32[8,1024]{1,0:T(8,128)S(1)} %get-tuple-element.41), channel_id=1, source_target_pairs={{0,4},{4,0},{8,12},{12,8},{16,20},{20,16},{24,28},{28,24},{32,36},... | collective-permute-start | bytes 98312 | tf_op jit(solution)/shard_map/ppermute | solution.py:528
  20.2 6.3 %collective-permute-start.4 = (f32[4,1024]{1,0:T(4,128)S(1)}, f32[4,1024]{1,0:T(4,128)S(1)}, u32[]{:S(2)}, u32[]{:S(2)}) collective-permute-start(f32[4,1024]{1,0:T(4,128)S(1)} %get-tuple-element.43), channel_id=1, source_target_pairs={{4,8},{12,16},{20,24},{28,32},{36,40},{44,48},{52,56},{60,64},{68,... | collective-permute-start | bytes 49160 | tf_op jit(solution)/shard_map/ppermute | solution.py:527
  23.6 3.1 %collective-permute-start.5 = (f32[4,1024]{1,0:T(4,128)S(1)}, f32[4,1024]{1,0:T(4,128)S(1)}, u32[]{:S(2)}, u32[]{:S(2)}) collective-permute-start(f32[4,1024]{1,0:T(4,128)S(1)} %get-tuple-element.44), channel_id=1, source_target_pairs={{0,4},{4,0},{8,12},{12,8},{16,20},{20,16},{24,28},{28,24},{32,36},... | collective-permute-start | bytes 49160 | tf_op jit(solution)/shard_map/ppermute | solution.py:528
  27.5 5.8 %collective-permute-start.6 = (f32[5,4,1024]{2,1,0:T(4,128)S(1)}, f32[5,4,1024]{2,1,0:T(4,128)S(1)}, u32[]{:S(2)}, u32[]{:S(2)}) collective-permute-start(f32[5,4,1024]{2,1,0:T(4,128)S(1)} %get-tuple-element.47), channel_id=1, source_target_pairs={{4,8},{12,16},{20,24},{28,32},{36,40},{44,48},{52,56},{60,64},{68,... | collective-permute-start | bytes 245768 | tf_op jit(solution)/shard_map/ppermute | solution.py:527
  30.5 3.2 %collective-permute-start.7 = (f32[5,4,1024]{2,1,0:T(4,128)S(1)}, f32[5,4,1024]{2,1,0:T(4,128)S(1)}, u32[]{:S(2)}, u32[]{:S(2)}) collective-permute-start(f32[5,4,1024]{2,1,0:T(4,128)S(1)} %get-tuple-element.48), channel_id=1, source_target_pairs={{0,4},{4,0},{8,12},{12,8},{16,20},{20,16},{24,28},{28,24},{32,36},... | collective-permute-start | bytes 245768 | tf_op jit(solution)/shard_map/ppermute | solution.py:528
  34.5 7.0 %collective-permute-start.8 = (f32[3,4,1024]{2,1,0:T(4,128)S(1)}, f32[3,4,1024]{2,1,0:T(4,128)S(1)}, u32[]{:S(2)}, u32[]{:S(2)}) collective-permute-start(f32[3,4,1024]{2,1,0:T(4,128)S(1)} %get-tuple-element.51), channel_id=1, source_target_pairs={{4,8},{12,16},{20,24},{28,32},{36,40},{44,48},{52,56},{60,64},{68,... | collective-permute-start | bytes 147464 | tf_op jit(solution)/shard_map/ppermute | solution.py:527
  38.3 3.2 %collective-permute-start.9 = (f32[3,4,1024]{2,1,0:T(4,128)S(1)}, f32[3,4,1024]{2,1,0:T(4,128)S(1)}, u32[]{:S(2)}, u32[]{:S(2)}) collective-permute-start(f32[3,4,1024]{2,1,0:T(4,128)S(1)} %get-tuple-element.52), channel_id=1, source_target_pairs={{0,4},{4,0},{8,12},{12,8},{16,20},{20,16},{24,28},{28,24},{32,36},... | collective-permute-start | bytes 147464 | tf_op jit(solution)/shard_map/ppermute | solution.py:528
  76.7 8.0 %all-to-all-start.1 = ((f32[4,1,128]{2,1,0:T(1,128)}), f32[4,1,128]{2,1,0:T(1,128)S(1)}, u32[]{:S(2)}, u32[]{:S(2)}) async-start(f32[4,1,128]{2,1,0:T(1,128)} %bitcast.4), calls=%async_computation.1 | async-start | bytes 4096 | tf_op jit(solution)/shard_map/all_to_all | solution.py:594

commit v10 on v9

--- a/solution.py
+++ b/solution.py
@@ -389,18 +389,24 @@
     d = 2.0 + mean / (float(n) * float(n))
     lower = jnp.where(lane == 0, 0.0, 1.0)
     upper = jnp.where(lane == n - 1, 0.0, 1.0)
-    excess = (d - lower) - upper
+    half = b.shape[0] // 2
+    sub = lax.broadcasted_iota(jnp.int32, b.shape, 0)
+    both_rows = jnp.where(sub < half, b, (d - lower) - upper)
+
+    def excess():
+        return jnp.broadcast_to(both_rows[half : half + 1], b.shape)
+
     s = 1
     while s < n:
-        inv = 1.0 / (lower + upper + excess)
+        inv = 1.0 / (lower + upper + excess())
         alpha = lower * pltpu.roll(inv, s, 1)
         gamma = upper * pltpu.roll(inv, n - s, 1)
-        b = b + alpha * pltpu.roll(b, s, 1) + gamma * pltpu.roll(b, n - s, 1)
-        excess = excess + alpha * pltpu.roll(excess, s, 1) + gamma * pltpu.roll(excess, n - s, 1)
+        down, up = pltpu.roll(both_rows, s, 1), pltpu.roll(both_rows, n - s, 1)
+        both_rows = both_rows + alpha * down + gamma * up
         lower = alpha * pltpu.roll(lower, s, 1)
         upper = gamma * pltpu.roll(upper, n - s, 1)
         s *= 2
-    return b / (lower + upper + excess)
+    return jnp.where(sub < half, both_rows / excess(), 0.0)
 
 
 def coarse_kernel_b(me, x1, ext, b, row_at, row_ok, same_col, h, y4, cross, chip, x3, to_cross, to_chip):
@@ -472,16 +478,13 @@
     gather[...] = jnp.broadcast_to(row, gather.shape)
 
 
-def ratio_kernel(groups, cases, cells, me, gathered, ratio, near):
+def ratio_kernel(groups, cases, cells, me, gathered, ratio, corrections):
     n = gathered.shape[0]
     m = 2 * REACH_E + 1
     g = jnp.transpose(gathered[...])
     e = solve_slabs(g, groups, cells)
+    corrections[...] = e
     lane = lax.broadcasted_iota(jnp.int32, e.shape, 1)
-    for j in range(m):
-        at = lane == me[0] + j - REACH_E
-        own = jnp.sum(jnp.where(at, e, 0.0), axis=1, keepdims=True)
-        near[j] = jnp.broadcast_to(own, near.shape[1:])
 
     def shifted(j):
         inside = (lane + j >= 0) & (lane + j < n)
@@ -504,12 +507,18 @@
     ratio[...] = jnp.broadcast_to(lane_row([(c, r[c : c + 1]) for c in range(cases)]), ratio.shape)
 
 
-def final_kernel(me, base, phi, near, out):
+def final_kernel(me, base, phi, corrections, out):
     cases, rows, width = base.shape
+    e = corrections[...]
+    lane = lax.broadcasted_iota(jnp.int32, e.shape, 1)
+    near = [
+        jnp.sum(jnp.where(lane == me[0] + j, e, 0.0), axis=1, keepdims=True)
+        for j in range(-REACH_E, REACH_E + 1)
+    ]
     for c in range(cases):
         x = base[c]
         for j in range(phi.shape[0]):
-            x = x + near[j, pl.ds(c, 1), 0:1] * phi[j]
+            x = x + near[j][c : c + 1] * phi[j]
         out[c] = x
 
 
@@ -586,13 +595,13 @@
         v, f, ext, *halo, *rows_x, q, part_a, part_e
     )
     gathered = lax.all_to_all(mine, "blk", 0, 0, tiled=True)
-    ratio, near = call(
+    ratio, corrections = call(
         functools.partial(ratio_kernel, groups, cases, rows * width),
-        [(n_rhs, 128), (m, 8, 128)],
+        [(n_rhs, 128), (8, n)],
         n_in=1,
     )(gathered)
     every = lax.all_to_all(ratio, "rhs", 0, 0, tiled=True)
-    (corrected,) = call(final_kernel, [field], n_in=3)(base, phi, near)
+    (corrected,) = call(final_kernel, [field], n_in=3)(base, phi, corrections)
     return corrected, every[:, :cases].reshape(n_rhs * cases)
 
 

time: 85.8 us -> 85.8 us (level)
  no operation moved by 1% of the time
where the time goes in v10:
time: 85.8 us; the launch traced here: 85.3 us
  starting transfers between devices  33.2 us (39%)
  blocking collectives  33 us (38%)
  Pallas kernels  11.2 us (13%)
  waiting for transfers between devices  5.77 us (7%)
  local copies, waits for them, and re-layouts  1.35 us (2%)
    all_to_all x1, blocking collectives, local(): gathered = lax.all_to_all(mine, 'blk', 0, 0, tiled=True)  33 us
    ppermute x5, starting transfers between devices, exchange(): cross = lax.ppermute(cross, 'blk', cross_chip)  16.6 us
    ppermute x5, starting transfers between devices, exchange(): return (cross, lax.ppermute(chip, 'blk', on_chip))  12.5 us
    all_to_all x1, starting transfers between devices, local(): every = lax.all_to_all(ratio, 'rhs', 0, 0, tiled=True)  4.01 us
    all_to_all x1, waiting for transfers between devices, local(): every = lax.all_to_all(ratio, 'rhs', 0, 0, tiled=True)  3.15 us
    ppermute x5, waiting for transfers between devices, exchange(): cross = lax.ppermute(cross, 'blk', cross_chip)  2.04 us
  transfers between devices with their start and end apart: 11, of which 5 were waited for; matrix products, arithmetic and copies ran while one was open for 0% of the time, Pallas kernels for 5%

profile of v10, /device:TPU:1, one launch (start us, length us, event | category | flops | bytes accessed | tf_op | source)
XLA Modules:
  0.0 85.3 jit_solution(9629560976352477301)
XLA Ops:
  0.6 0.0 copy-start
  0.6 0.7 copy-done
  1.4 0.0 copy-start.3
  1.4 0.0 copy-start.1
  1.4 0.0 copy-start.2
  1.4 1.1 %shard_map.59 = (f32[6,4,1024]{2,1,0:T(4,128)S(1)}, f32[6,4,1024]{2,1,0:T(4,128)S(1)}) custom-call(f32[4,8,1024]{2,1,0:T(8,128)} %refs_0_.7, f32[4,8,1024]{2,1,0:T(8,128)} %refs_1_.15, f32[8,1024]{1,0:T(8,128)S(1)} %copy-done), custom_call_target="tpu_custom_call" | custom-call | tf_op jit(solution)/shard_map/pallas_call | solution.py:544
  2.5 4.6 %collective-permute-start = (f32[6,4,1024]{2,1,0:T(4,128)S(1)}, f32[6,4,1024]{2,1,0:T(4,128)S(1)}, u32[]{:S(2)}, u32[]{:S(2)}) collective-permute-start(f32[6,4,1024]{2,1,0:T(4,128)S(1)} %get-tuple-element.31), channel_id=1, source_target_pairs={{4,8},{12,16},{20,24},{28,32},{36,40},{44,48},{52,56},{60,64},{68,... | collective-permute-start | bytes 294920 | tf_op jit(solution)/shard_map/ppermute | solution.py:536
  7.1 4.9 %collective-permute-start.1 = (f32[6,4,1024]{2,1,0:T(4,128)S(1)}, f32[6,4,1024]{2,1,0:T(4,128)S(1)}, u32[]{:S(2)}, u32[]{:S(2)}) collective-permute-start(f32[6,4,1024]{2,1,0:T(4,128)S(1)} %get-tuple-element.32), channel_id=1, source_target_pairs={{0,4},{4,0},{8,12},{12,8},{16,20},{20,16},{24,28},{28,24},{32,36},... | collective-permute-start | bytes 294920 | tf_op jit(solution)/shard_map/ppermute | solution.py:537
  11.9 0.0 copy-done.3
  12.0 1.1 %shard_map.60 = (s32[14,8,1024]{2,1,0:T(8,128)S(1)}, f32[14,8,1024]{2,1,0:T(8,128)S(1)}, f32[7,8,1024]{2,1,0:T(8,128)S(1)}, f32[8,1024]{1,0:T(8,128)S(1)}, f32[3,8,1024]{2,1,0:T(8,128)S(1)}) custom-call(f32[8,1024]{1,0:T(8,128)S(1)} %copy-done, s32[8,1024]{1,0:T(8,128)S(1)} %copy-done.3), custom_call_target="tpu_custom_call" | custom-call | tf_op jit(solution)/shard_map/pallas_call | solution.py:558
  13.0 0.0 collective-permute-done.refs_3_.refs_1_
  13.0 0.0 collective-permute-done.1.refs_4_.refs_2_
  13.0 0.0 copy-done.1
  13.1 0.0 copy-done.2
  13.1 1.0 %shard_map.61 = (f32[4,8,1024]{2,1,0:T(8,128)S(1)}, f32[4,8,1024]{2,1,0:T(8,128)S(1)}, f32[4,8,1024]{2,1,0:T(8,128)S(1)}, f32[8,1024]{1,0:T(8,128)S(1)}, f32[8,1024]{1,0:T(8,128)S(1)}, /*index=5*/f32[1,128]{1,0:T(1,128)S(1)}) custom-call(f32[4,8,1024]{2,1,0:T(8,128)S(1)} %copy-done.2, f32[4,8,1024]{2,1,0:T(8,128)S(1)} %copy-done.1, f32[8,1024]{1,0:T(8,128)S(1)} %copy-done, ...), custom_call_target="tpu_custom_call" | custom-call | tf_op jit(solution)/shard_map/pallas_call | solution.py:570
  14.1 1.9 %collective-permute-start.2 = (f32[8,1024]{1,0:T(8,128)S(1)}, f32[8,1024]{1,0:T(8,128)S(1)}, u32[]{:S(2)}, u32[]{:S(2)}) collective-permute-start(f32[8,1024]{1,0:T(8,128)S(1)} %get-tuple-element.40), channel_id=1, source_target_pairs={{4,8},{12,16},{20,24},{28,32},{36,40},{44,48},{52,56},{60,64},{68,... | collective-permute-start | bytes 98312 | tf_op jit(solution)/shard_map/ppermute | solution.py:536
  16.0 1.9 %collective-permute-start.3 = (f32[8,1024]{1,0:T(8,128)S(1)}, f32[8,1024]{1,0:T(8,128)S(1)}, u32[]{:S(2)}, u32[]{:S(2)}) collective-permute-start(f32[8,1024]{1,0:T(8,128)S(1)} %get-tuple-element.41), channel_id=1, source_target_pairs={{0,4},{4,0},{8,12},{12,8},{16,20},{20,16},{24,28},{28,24},{32,36},... | collective-permute-start | bytes 98312 | tf_op jit(solution)/shard_map/ppermute | solution.py:537
  18.0 1.4 %collective-permute-done.2.refs_7_.refs_6_ = f32[8,1024]{1,0:T(8,128)S(1)} collective-permute-done((f32[8,1024]{1,0:T(8,128)S(1)}, f32[8,1024]{1,0:T(8,128)S(1)}, u32[]{:S(2)}, u32[]{:S(2)}) %collective-permute-start.2) | collective-permute-done | bytes 32800 | tf_op jit(solution)/shard_map/ppermute | solution.py:536
  19.4 0.0 collective-permute-done.3.refs_8_.refs_7_
  19.4 0.8 shard_map.62
  20.2 3.4 %collective-permute-start.4 = (f32[4,1024]{1,0:T(4,128)S(1)}, f32[4,1024]{1,0:T(4,128)S(1)}, u32[]{:S(2)}, u32[]{:S(2)}) collective-permute-start(f32[4,1024]{1,0:T(4,128)S(1)} %get-tuple-element.43), channel_id=1, source_target_pairs={{4,8},{12,16},{20,24},{28,32},{36,40},{44,48},{52,56},{60,64},{68,... | collective-permute-start | bytes 49160 | tf_op jit(solution)/shard_map/ppermute | solution.py:536
  23.6 1.9 %collective-permute-start.5 = (f32[4,1024]{1,0:T(4,128)S(1)}, f32[4,1024]{1,0:T(4,128)S(1)}, u32[]{:S(2)}, u32[]{:S(2)}) collective-permute-start(f32[4,1024]{1,0:T(4,128)S(1)} %get-tuple-element.44), channel_id=1, source_target_pairs={{0,4},{4,0},{8,12},{12,8},{16,20},{20,16},{24,28},{28,24},{32,36},... | collective-permute-start | bytes 49160 | tf_op jit(solution)/shard_map/ppermute | solution.py:537
  25.5 0.9 %shard_map.63.refs_7_.refs_3_ = f32[5,8,1024]{2,1,0:T(8,128)S(1)} custom-call(f32[8,1024]{1,0:T(8,128)S(1)} %copy-done, s32[14,8,1024]{2,1,0:T(8,128)S(1)} %get-tuple-element.33.refs_5_.refs_3_.refs_1_, f32[14,8,1024]{2,1,0:T(8,128)S(1)} %get-tuple-element.34.refs_6_.refs_4_.refs_2_, f32[7,8,1024]{2,1,0:T(8,128)S(1)} %get-tuple-element.35.refs_7_.refs_5_.refs_3_, ...), custom_call_target="tpu_custom_call" | custom-call | tf_op jit(solution)/shard_map/pallas_call | solution.py:578
  26.4 0.0 collective-permute-done.4.refs_8_
  26.5 0.2 collective-permute-done.5.refs_9_
  26.7 0.9 shard_map.64
  27.5 2.9 %collective-permute-start.6 = (f32[5,4,1024]{2,1,0:T(4,128)S(1)}, f32[5,4,1024]{2,1,0:T(4,128)S(1)}, u32[]{:S(2)}, u32[]{:S(2)}) collective-permute-start(f32[5,4,1024]{2,1,0:T(4,128)S(1)} %get-tuple-element.47), channel_id=1, source_target_pairs={{4,8},{12,16},{20,24},{28,32},{36,40},{44,48},{52,56},{60,64},{68,... | collective-permute-start | bytes 245768 | tf_op jit(solution)/shard_map/ppermute | solution.py:536
  30.5 1.9 %collective-permute-start.7 = (f32[5,4,1024]{2,1,0:T(4,128)S(1)}, f32[5,4,1024]{2,1,0:T(4,128)S(1)}, u32[]{:S(2)}, u32[]{:S(2)}) collective-permute-start(f32[5,4,1024]{2,1,0:T(4,128)S(1)} %get-tuple-element.48), channel_id=1, source_target_pairs={{0,4},{4,0},{8,12},{12,8},{16,20},{20,16},{24,28},{28,24},{32,36},... | collective-permute-start | bytes 245768 | tf_op jit(solution)/shard_map/ppermute | solution.py:537
  32.4 0.2 shard_map.65.refs_10_.refs_8_
  32.6 0.7 collective-permute-done.6.refs_8_.refs_4_
  33.3 0.4 collective-permute-done.7.refs_9_.refs_5_
  33.6 0.8 shard_map.66
  34.5 3.8 %collective-permute-start.8 = (f32[3,4,1024]{2,1,0:T(4,128)S(1)}, f32[3,4,1024]{2,1,0:T(4,128)S(1)}, u32[]{:S(2)}, u32[]{:S(2)}) collective-permute-start(f32[3,4,1024]{2,1,0:T(4,128)S(1)} %get-tuple-element.51), channel_id=1, source_target_pairs={{4,8},{12,16},{20,24},{28,32},{36,40},{44,48},{52,56},{60,64},{68,... | collective-permute-start | bytes 147464 | tf_op jit(solution)/shard_map/ppermute | solution.py:536
  38.3 1.9 %collective-permute-start.9 = (f32[3,4,1024]{2,1,0:T(4,128)S(1)}, f32[3,4,1024]{2,1,0:T(4,128)S(1)}, u32[]{:S(2)}, u32[]{:S(2)}) collective-permute-start(f32[3,4,1024]{2,1,0:T(4,128)S(1)} %get-tuple-element.52), channel_id=1, source_target_pairs={{0,4},{4,0},{8,12},{12,8},{16,20},{20,16},{24,28},{28,24},{32,36},... | collective-permute-start | bytes 147464 | tf_op jit(solution)/shard_map/ppermute | solution.py:537
  40.2 1.3 %shard_map.67 = (f32[7,8,1024]{2,1,0:T(8,128)S(1)}, f32[7,8,1024]{2,1,0:T(8,128)S(1)}, f32[1,128]{1,0:T(1,128)S(1)}) custom-call(f32[8,1024]{1,0:T(8,128)S(1)} %copy-done, f32[6,4,1024]{2,1,0:T(4,128)S(1)} %collective-permute-done.refs_3_.refs_1_, f32[6,4,1024]{2,1,0:T(4,128)S(1)} %collective-permute-done.1.refs_4_.refs_2_, ...), custom_call_target="tpu_custom_call" | custom-call | tf_op jit(solution)/shard_map/pallas_call | solution.py:587
  41.4 0.0 collective-permute-done.8.refs_5_
  41.5 0.0 collective-permute-done.9.refs_6_
  41.5 0.9 %shard_map.68 = (f32[4,8,1024]{2,1,0:T(8,128)S(1)}, f32[128,128]{1,0:T(8,128)S(1)}) custom-call(f32[4,8,1024]{2,1,0:T(8,128)S(1)} %get-tuple-element.50.refs_0_, f32[4,8,1024]{2,1,0:T(8,128)S(1)} %copy-done.1, f32[8,1024]{1,0:T(8,128)S(1)} %copy-done, f32[6,4,1024]{2,1,0:T(4,128)S(1)} %collective-permute-done.refs_3_.refs_1_, ...), custom_call_target="tpu_custom_call" | custom-call | tf_op jit(solution)/shard_map/pallas_call | solution.py:594
  42.3 33.0 %all_to_all.23 = f32[128,1,128]{2,1,0:T(1,128)S(1)} all-to-all(f32[128,1,128]{2,1,0:T(1,128)S(1)} %bitcast.10), channel_id=1, replica_groups=mesh['blk'=128,'rhs'=4] {'blk'}, dimensions={0} | all-to-all | bytes 131072 | tf_op jit(solution)/shard_map/all_to_all | solution.py:597
  75.3 1.5 %shard_map.69 = (f32[4,128]{1,0:T(4,128)}, f32[8,128]{1,0:T(8,128)S(1)}) custom-call(f32[128,128]{1,0:T(8,128)S(1)} %bitcast.9), custom_call_target="tpu_custom_call" | custom-call | tf_op jit(solution)/shard_map/pallas_call | solution.py:598
  76.8 4.0 %all-to-all-start.1 = ((f32[4,1,128]{2,1,0:T(1,128)}), f32[4,1,128]{2,1,0:T(1,128)S(1)}, u32[]{:S(2)}, u32[]{:S(2)}) async-start(f32[4,1,128]{2,1,0:T(1,128)} %bitcast.4), calls=%async_computation.1 | async-start | bytes 4096 | tf_op jit(solution)/shard_map/all_to_all | solution.py:603
  80.8 0.8 shard_map.70
  81.6 3.2 %all-to-all-done.1 = f32[4,1,128]{2,1,0:T(1,128)S(1)} async-done(((f32[4,1,128]{2,1,0:T(1,128)}), f32[4,1,128]{2,1,0:T(1,128)S(1)}, u32[]{:S(2)}, u32[]{:S(2)}) %all-to-all-start.1) | async-done | bytes 2080 | tf_op jit(solution)/shard_map/all_to_all | solution.py:603
  84.7 0.6 reshape.11
Async XLA Ops:
  0.6 0.8 copy-start
  1.4 10.6 %copy-start.3 = (s32[8,1024]{1,0:T(8,128)S(1)}, s32[8,1024]{1,0:T(8,128)}, u32[]{:S(2)}) copy-start(s32[8,1024]{1,0:T(8,128)} %refs_1_.9) | copy-start | bytes 98308
  1.4 11.7 %copy-start.1 = (f32[4,8,1024]{2,1,0:T(8,128)S(1)}, f32[4,8,1024]{2,1,0:T(8,128)}, u32[]{:S(2)}) copy-start(f32[4,8,1024]{2,1,0:T(8,128)} %refs_1_.15) | copy-start | bytes 393220
  1.4 11.7 %copy-start.2 = (f32[4,8,1024]{2,1,0:T(8,128)S(1)}, f32[4,8,1024]{2,1,0:T(8,128)}, u32[]{:S(2)}) copy-start(f32[4,8,1024]{2,1,0:T(8,128)} %refs_0_.7) | copy-start | bytes 393220
  2.5 10.5 %collective-permute-start = (f32[6,4,1024]{2,1,0:T(4,128)S(1)}, f32[6,4,1024]{2,1,0:T(4,128)S(1)}, u32[]{:S(2)}, u32[]{:S(2)}) collective-permute-start(f32[6,4,1024]{2,1,0:T(4,128)S(1)} %get-tuple-element.31), channel_id=1, source_target_pairs={{4,8},{12,16},{20,24},{28,32},{36,40},{44,48},{52,56},{60,64},{68,... | collective-permute-start | bytes 294920 | tf_op jit(solution)/shard_map/ppermute | solution.py:536
  7.1 6.0 %collective-permute-start.1 = (f32[6,4,1024]{2,1,0:T(4,128)S(1)}, f32[6,4,1024]{2,1,0:T(4,128)S(1)}, u32[]{:S(2)}, u32[]{:S(2)}) collective-permute-start(f32[6,4,1024]{2,1,0:T(4,128)S(1)} %get-tuple-element.32), channel_id=1, source_target_pairs={{0,4},{4,0},{8,12},{12,8},{16,20},{20,16},{24,28},{28,24},{32,36},... | collective-permute-start | bytes 294920 | tf_op jit(solution)/shard_map/ppermute | solution.py:537
  14.1 5.2 %collective-permute-start.2 = (f32[8,1024]{1,0:T(8,128)S(1)}, f32[8,1024]{1,0:T(8,128)S(1)}, u32[]{:S(2)}, u32[]{:S(2)}) collective-permute-start(f32[8,1024]{1,0:T(8,128)S(1)} %get-tuple-element.40), channel_id=1, source_target_pairs={{4,8},{12,16},{20,24},{28,32},{36,40},{44,48},{52,56},{60,64},{68,... | collective-permute-start | bytes 98312 | tf_op jit(solution)/shard_map/ppermute | solution.py:536
  16.0 3.3 %collective-permute-start.3 = (f32[8,1024]{1,0:T(8,128)S(1)}, f32[8,1024]{1,0:T(8,128)S(1)}, u32[]{:S(2)}, u32[]{:S(2)}) collective-permute-start(f32[8,1024]{1,0:T(8,128)S(1)} %get-tuple-element.41), channel_id=1, source_target_pairs={{0,4},{4,0},{8,12},{12,8},{16,20},{20,16},{24,28},{28,24},{32,36},... | collective-permute-start | bytes 98312 | tf_op jit(solution)/shard_map/ppermute | solution.py:537
  20.2 6.3 %collective-permute-start.4 = (f32[4,1024]{1,0:T(4,128)S(1)}, f32[4,1024]{1,0:T(4,128)S(1)}, u32[]{:S(2)}, u32[]{:S(2)}) collective-permute-start(f32[4,1024]{1,0:T(4,128)S(1)} %get-tuple-element.43), channel_id=1, source_target_pairs={{4,8},{12,16},{20,24},{28,32},{36,40},{44,48},{52,56},{60,64},{68,... | collective-permute-start | bytes 49160 | tf_op jit(solution)/shard_map/ppermute | solution.py:536
  23.6 3.1 %collective-permute-start.5 = (f32[4,1024]{1,0:T(4,128)S(1)}, f32[4,1024]{1,0:T(4,128)S(1)}, u32[]{:S(2)}, u32[]{:S(2)}) collective-permute-start(f32[4,1024]{1,0:T(4,128)S(1)} %get-tuple-element.44), channel_id=1, source_target_pairs={{0,4},{4,0},{8,12},{12,8},{16,20},{20,16},{24,28},{28,24},{32,36},... | collective-permute-start | bytes 49160 | tf_op jit(solution)/shard_map/ppermute | solution.py:537
  27.5 5.8 %collective-permute-start.6 = (f32[5,4,1024]{2,1,0:T(4,128)S(1)}, f32[5,4,1024]{2,1,0:T(4,128)S(1)}, u32[]{:S(2)}, u32[]{:S(2)}) collective-permute-start(f32[5,4,1024]{2,1,0:T(4,128)S(1)} %get-tuple-element.47), channel_id=1, source_target_pairs={{4,8},{12,16},{20,24},{28,32},{36,40},{44,48},{52,56},{60,64},{68,... | collective-permute-start | bytes 245768 | tf_op jit(solution)/shard_map/ppermute | solution.py:536
  30.5 3.2 %collective-permute-start.7 = (f32[5,4,1024]{2,1,0:T(4,128)S(1)}, f32[5,4,1024]{2,1,0:T(4,128)S(1)}, u32[]{:S(2)}, u32[]{:S(2)}) collective-permute-start(f32[5,4,1024]{2,1,0:T(4,128)S(1)} %get-tuple-element.48), channel_id=1, source_target_pairs={{0,4},{4,0},{8,12},{12,8},{16,20},{20,16},{24,28},{28,24},{32,36},... | collective-permute-start | bytes 245768 | tf_op jit(solution)/shard_map/ppermute | solution.py:537
  34.5 7.0 %collective-permute-start.8 = (f32[3,4,1024]{2,1,0:T(4,128)S(1)}, f32[3,4,1024]{2,1,0:T(4,128)S(1)}, u32[]{:S(2)}, u32[]{:S(2)}) collective-permute-start(f32[3,4,1024]{2,1,0:T(4,128)S(1)} %get-tuple-element.51), channel_id=1, source_target_pairs={{4,8},{12,16},{20,24},{28,32},{36,40},{44,48},{52,56},{60,64},{68,... | collective-permute-start | bytes 147464 | tf_op jit(solution)/shard_map/ppermute | solution.py:536
  38.3 3.2 %collective-permute-start.9 = (f32[3,4,1024]{2,1,0:T(4,128)S(1)}, f32[3,4,1024]{2,1,0:T(4,128)S(1)}, u32[]{:S(2)}, u32[]{:S(2)}) collective-permute-start(f32[3,4,1024]{2,1,0:T(4,128)S(1)} %get-tuple-element.52), channel_id=1, source_target_pairs={{0,4},{4,0},{8,12},{12,8},{16,20},{20,16},{24,28},{28,24},{32,36},... | collective-permute-start | bytes 147464 | tf_op jit(solution)/shard_map/ppermute | solution.py:537
  76.8 8.0 %all-to-all-start.1 = ((f32[4,1,128]{2,1,0:T(1,128)}), f32[4,1,128]{2,1,0:T(1,128)S(1)}, u32[]{:S(2)}, u32[]{:S(2)}) async-start(f32[4,1,128]{2,1,0:T(1,128)} %bitcast.4), calls=%async_computation.1 | async-start | bytes 4096 | tf_op jit(solution)/shard_map/all_to_all | solution.py:603

commit v11 on v9

--- a/solution.py
+++ b/solution.py
@@ -341,7 +341,7 @@
     return total(x * y)
 
 
-def response_kernel(me, ext, cross, chip, y4, cross_y, chip_y, phi, q, part):
+def response_kernel(me, ext, cross, chip, y4, cross_y, chip_y, phi, q, scaled, part):
     before, after = sides(me, cross, chip)
     ab, be = sides(me, cross_y, chip_y)
     rows, width = ext.shape
@@ -370,6 +370,7 @@
         q[j] = v
         d = dot(v, v)
         inv = jnp.where(d > 0.0, 1.0 / jnp.where(d > 0.0, d, 1.0), 0.0)
+        scaled[j] = inv * v
         values.append((LANE_D + j, d))
         for k in range(j + 1, m):
             factor = dot(v, basis[k]) * inv
@@ -441,7 +442,7 @@
             put((k,) + row_of(c), y[k : k + 1], y[rows - 1 - k : rows - k])
 
 
-def post_kernel(me, v, f, ext, cross, chip, cross_v, chip_v, q, part_a, part_e, out, gather):
+def post_kernel(me, v, f, ext, cross, chip, cross_v, chip_v, q, scaled, part_a, part_e, out, gather):
     before, after = sides(me, cross, chip)
     before_v, after_v = sides(me, cross_v, chip_v)
     cases, rows, width = v.shape
@@ -455,14 +456,10 @@
     x, res = two_sweeps([v[c] for c in range(cases)], v_halo, fl, f_halo, diag, d_halo, valid)
     for c in range(cases):
         out[c] = x[c]
-    inv = []
-    for j in range(m):
-        d = part_e[:, LANE_D + j : LANE_D + j + 1]
-        inv.append(jnp.where(d > 0.0, 1.0 / jnp.where(d > 0.0, d, 1.0), 0.0))
     values = []
     for c in range(cases):
         r = res[c]
-        share = [dot(r, q[j]) * inv[j] for j in range(m)]
+        share = [dot(r, scaled[j]) for j in range(m)]
         for j in range(m):
             r = r - share[j] * q[j]
         values.append((LANE_PERP + c, dot(r, r)))
@@ -575,15 +572,15 @@
     )
     rows_x = exchange(*sent)
     m = 2 * REACH_E + 1
-    phi, q, part_e = call(
-        response_kernel, [(m, rows, width), (m, rows, width), (1, 128)], n_in=6
+    phi, q, scaled, part_e = call(
+        response_kernel, [(m, rows, width)] * 3 + [(1, 128)], n_in=6
     )(ext, *halo, y4, *rows_x)
     v, *sent = call(
         coarse_kernel_c, [field, (3, cases, width), (3, cases, width)], n_in=11
     )(x3, ext, b, *tables, smooth, *rows_x, part_a)
     rows_x = exchange(*sent)
-    base, mine = call(post_kernel, [field, (n, 128)], n_in=10)(
-        v, f, ext, *halo, *rows_x, q, part_a, part_e
+    base, mine = call(post_kernel, [field, (n, 128)], n_in=11)(
+        v, f, ext, *halo, *rows_x, q, scaled, part_a, part_e
     )
     gathered = lax.all_to_all(mine, "blk", 0, 0, tiled=True)
     ratio, near = call(

time: 85.8 us -> 85.6 us (level)
  no operation moved by 1% of the time
where the time goes in v11:
time: 85.6 us; the launch traced here: 85.1 us
  starting transfers between devices  33.2 us (39%)
  blocking collectives  33 us (39%)
  Pallas kernels  10.9 us (13%)
  waiting for transfers between devices  5.82 us (7%)
  local copies, waits for them, and re-layouts  1.35 us (2%)
    all_to_all x1, blocking collectives, local(): gathered = lax.all_to_all(mine, 'blk', 0, 0, tiled=True)  33 us
    ppermute x5, starting transfers between devices, exchange(): cross = lax.ppermute(cross, 'blk', cross_chip)  16.6 us
    ppermute x5, starting transfers between devices, exchange(): return (cross, lax.ppermute(chip, 'blk', on_chip))  12.5 us
    all_to_all x1, starting transfers between devices, local(): every = lax.all_to_all(ratio, 'rhs', 0, 0, tiled=True)  4.01 us
    all_to_all x1, waiting for transfers between devices, local(): every = lax.all_to_all(ratio, 'rhs', 0, 0, tiled=True)  3.2 us
    ppermute x5, waiting for transfers between devices, exchange(): cross = lax.ppermute(cross, 'blk', cross_chip)  2.04 us
  transfers between devices with their start and end apart: 11, of which 5 were waited for; matrix products, arithmetic and copies ran while one was open for 0% of the time, Pallas kernels for 5%

profile of v11, /device:TPU:1, one launch (start us, length us, event | category | flops | bytes accessed | tf_op | source)
XLA Modules:
  0.0 85.1 jit_solution(475988062797452620)
XLA Ops:
  0.6 0.0 copy-start
  0.6 0.7 copy-done
  1.4 0.0 copy-start.3
  1.4 0.0 copy-start.1
  1.4 0.0 copy-start.2
  1.4 1.1 %shard_map.59 = (f32[6,4,1024]{2,1,0:T(4,128)S(1)}, f32[6,4,1024]{2,1,0:T(4,128)S(1)}) custom-call(f32[4,8,1024]{2,1,0:T(8,128)} %refs_0_.7, f32[4,8,1024]{2,1,0:T(8,128)} %refs_1_.15, f32[8,1024]{1,0:T(8,128)S(1)} %copy-done), custom_call_target="tpu_custom_call" | custom-call | tf_op jit(solution)/shard_map/pallas_call | solution.py:532
  2.5 4.6 %collective-permute-start = (f32[6,4,1024]{2,1,0:T(4,128)S(1)}, f32[6,4,1024]{2,1,0:T(4,128)S(1)}, u32[]{:S(2)}, u32[]{:S(2)}) collective-permute-start(f32[6,4,1024]{2,1,0:T(4,128)S(1)} %get-tuple-element.32), channel_id=1, source_target_pairs={{4,8},{12,16},{20,24},{28,32},{36,40},{44,48},{52,56},{60,64},{68,... | collective-permute-start | bytes 294920 | tf_op jit(solution)/shard_map/ppermute | solution.py:524
  7.1 4.9 %collective-permute-start.1 = (f32[6,4,1024]{2,1,0:T(4,128)S(1)}, f32[6,4,1024]{2,1,0:T(4,128)S(1)}, u32[]{:S(2)}, u32[]{:S(2)}) collective-permute-start(f32[6,4,1024]{2,1,0:T(4,128)S(1)} %get-tuple-element.33), channel_id=1, source_target_pairs={{0,4},{4,0},{8,12},{12,8},{16,20},{20,16},{24,28},{28,24},{32,36},... | collective-permute-start | bytes 294920 | tf_op jit(solution)/shard_map/ppermute | solution.py:525
  11.9 0.0 copy-done.3
  12.0 1.1 %shard_map.60 = (s32[14,8,1024]{2,1,0:T(8,128)S(1)}, f32[14,8,1024]{2,1,0:T(8,128)S(1)}, f32[7,8,1024]{2,1,0:T(8,128)S(1)}, f32[8,1024]{1,0:T(8,128)S(1)}, f32[3,8,1024]{2,1,0:T(8,128)S(1)}) custom-call(f32[8,1024]{1,0:T(8,128)S(1)} %copy-done, s32[8,1024]{1,0:T(8,128)S(1)} %copy-done.3), custom_call_target="tpu_custom_call" | custom-call | tf_op jit(solution)/shard_map/pallas_call | solution.py:546
  13.0 0.0 collective-permute-done.refs_3_.refs_1_
  13.0 0.0 collective-permute-done.1.refs_4_.refs_2_
  13.0 0.0 copy-done.1
  13.1 0.0 copy-done.2
  13.1 1.0 %shard_map.61 = (f32[4,8,1024]{2,1,0:T(8,128)S(1)}, f32[4,8,1024]{2,1,0:T(8,128)S(1)}, f32[4,8,1024]{2,1,0:T(8,128)S(1)}, f32[8,1024]{1,0:T(8,128)S(1)}, f32[8,1024]{1,0:T(8,128)S(1)}, /*index=5*/f32[1,128]{1,0:T(1,128)S(1)}) custom-call(f32[4,8,1024]{2,1,0:T(8,128)S(1)} %copy-done.2, f32[4,8,1024]{2,1,0:T(8,128)S(1)} %copy-done.1, f32[8,1024]{1,0:T(8,128)S(1)} %copy-done, ...), custom_call_target="tpu_custom_call" | custom-call | tf_op jit(solution)/shard_map/pallas_call | solution.py:558
  14.1 1.9 %collective-permute-start.2 = (f32[8,1024]{1,0:T(8,128)S(1)}, f32[8,1024]{1,0:T(8,128)S(1)}, u32[]{:S(2)}, u32[]{:S(2)}) collective-permute-start(f32[8,1024]{1,0:T(8,128)S(1)} %get-tuple-element.41), channel_id=1, source_target_pairs={{4,8},{12,16},{20,24},{28,32},{36,40},{44,48},{52,56},{60,64},{68,... | collective-permute-start | bytes 98312 | tf_op jit(solution)/shard_map/ppermute | solution.py:524
  16.0 1.9 %collective-permute-start.3 = (f32[8,1024]{1,0:T(8,128)S(1)}, f32[8,1024]{1,0:T(8,128)S(1)}, u32[]{:S(2)}, u32[]{:S(2)}) collective-permute-start(f32[8,1024]{1,0:T(8,128)S(1)} %get-tuple-element.42), channel_id=1, source_target_pairs={{0,4},{4,0},{8,12},{12,8},{16,20},{20,16},{24,28},{28,24},{32,36},... | collective-permute-start | bytes 98312 | tf_op jit(solution)/shard_map/ppermute | solution.py:525
  18.0 1.4 %collective-permute-done.2.refs_7_.refs_6_ = f32[8,1024]{1,0:T(8,128)S(1)} collective-permute-done((f32[8,1024]{1,0:T(8,128)S(1)}, f32[8,1024]{1,0:T(8,128)S(1)}, u32[]{:S(2)}, u32[]{:S(2)}) %collective-permute-start.2) | collective-permute-done | bytes 32800 | tf_op jit(solution)/shard_map/ppermute | solution.py:524
  19.4 0.0 collective-permute-done.3.refs_8_.refs_7_
  19.4 0.8 shard_map.62
  20.2 3.4 %collective-permute-start.4 = (f32[4,1024]{1,0:T(4,128)S(1)}, f32[4,1024]{1,0:T(4,128)S(1)}, u32[]{:S(2)}, u32[]{:S(2)}) collective-permute-start(f32[4,1024]{1,0:T(4,128)S(1)} %get-tuple-element.44), channel_id=1, source_target_pairs={{4,8},{12,16},{20,24},{28,32},{36,40},{44,48},{52,56},{60,64},{68,... | collective-permute-start | bytes 49160 | tf_op jit(solution)/shard_map/ppermute | solution.py:524
  23.6 1.9 %collective-permute-start.5 = (f32[4,1024]{1,0:T(4,128)S(1)}, f32[4,1024]{1,0:T(4,128)S(1)}, u32[]{:S(2)}, u32[]{:S(2)}) collective-permute-start(f32[4,1024]{1,0:T(4,128)S(1)} %get-tuple-element.45), channel_id=1, source_target_pairs={{0,4},{4,0},{8,12},{12,8},{16,20},{20,16},{24,28},{28,24},{32,36},... | collective-permute-start | bytes 49160 | tf_op jit(solution)/shard_map/ppermute | solution.py:525
  25.5 0.9 %shard_map.63.refs_7_.refs_3_ = f32[5,8,1024]{2,1,0:T(8,128)S(1)} custom-call(f32[8,1024]{1,0:T(8,128)S(1)} %copy-done, s32[14,8,1024]{2,1,0:T(8,128)S(1)} %get-tuple-element.34.refs_5_.refs_3_.refs_1_, f32[14,8,1024]{2,1,0:T(8,128)S(1)} %get-tuple-element.35.refs_6_.refs_4_.refs_2_, f32[7,8,1024]{2,1,0:T(8,128)S(1)} %get-tuple-element.36.refs_7_.refs_5_.refs_3_, ...), custom_call_target="tpu_custom_call" | custom-call | tf_op jit(solution)/shard_map/pallas_call | solution.py:566
  26.4 0.0 collective-permute-done.4.refs_8_
  26.5 0.2 collective-permute-done.5.refs_9_
  26.7 0.9 %shard_map.64 = (f32[4,8,1024]{2,1,0:T(8,128)S(1)}, f32[5,4,1024]{2,1,0:T(4,128)S(1)}, f32[5,4,1024]{2,1,0:T(4,128)S(1)}) custom-call(f32[4,8,1024]{2,1,0:T(8,128)S(1)} %get-tuple-element.43.refs_0_, f32[8,1024]{1,0:T(8,128)S(1)} %copy-done, f32[4,8,1024]{2,1,0:T(8,128)S(1)} %get-tuple-element.40.refs_2_, ...), custom_call_target="tpu_custom_call" | custom-call | tf_op jit(solution)/shard_map/pallas_call | solution.py:570
  27.5 2.9 %collective-permute-start.6 = (f32[5,4,1024]{2,1,0:T(4,128)S(1)}, f32[5,4,1024]{2,1,0:T(4,128)S(1)}, u32[]{:S(2)}, u32[]{:S(2)}) collective-permute-start(f32[5,4,1024]{2,1,0:T(4,128)S(1)} %get-tuple-element.48), channel_id=1, source_target_pairs={{4,8},{12,16},{20,24},{28,32},{36,40},{44,48},{52,56},{60,64},{68,... | collective-permute-start | bytes 245768 | tf_op jit(solution)/shard_map/ppermute | solution.py:524
  30.5 1.9 %collective-permute-start.7 = (f32[5,4,1024]{2,1,0:T(4,128)S(1)}, f32[5,4,1024]{2,1,0:T(4,128)S(1)}, u32[]{:S(2)}, u32[]{:S(2)}) collective-permute-start(f32[5,4,1024]{2,1,0:T(4,128)S(1)} %get-tuple-element.49), channel_id=1, source_target_pairs={{0,4},{4,0},{8,12},{12,8},{16,20},{20,16},{24,28},{28,24},{32,36},... | collective-permute-start | bytes 245768 | tf_op jit(solution)/shard_map/ppermute | solution.py:525
  32.4 0.2 shard_map.65.refs_10_.refs_9_
  32.6 0.7 collective-permute-done.6.refs_8_.refs_4_
  33.3 0.4 collective-permute-done.7.refs_9_.refs_5_
  33.6 0.8 shard_map.66
  34.5 3.8 %collective-permute-start.8 = (f32[3,4,1024]{2,1,0:T(4,128)S(1)}, f32[3,4,1024]{2,1,0:T(4,128)S(1)}, u32[]{:S(2)}, u32[]{:S(2)}) collective-permute-start(f32[3,4,1024]{2,1,0:T(4,128)S(1)} %get-tuple-element.52), channel_id=1, source_target_pairs={{4,8},{12,16},{20,24},{28,32},{36,40},{44,48},{52,56},{60,64},{68,... | collective-permute-start | bytes 147464 | tf_op jit(solution)/shard_map/ppermute | solution.py:524
  38.3 1.9 %collective-permute-start.9 = (f32[3,4,1024]{2,1,0:T(4,128)S(1)}, f32[3,4,1024]{2,1,0:T(4,128)S(1)}, u32[]{:S(2)}, u32[]{:S(2)}) collective-permute-start(f32[3,4,1024]{2,1,0:T(4,128)S(1)} %get-tuple-element.53), channel_id=1, source_target_pairs={{0,4},{4,0},{8,12},{12,8},{16,20},{20,16},{24,28},{28,24},{32,36},... | collective-permute-start | bytes 147464 | tf_op jit(solution)/shard_map/ppermute | solution.py:525
  40.2 1.3 %shard_map.67 = (f32[7,8,1024]{2,1,0:T(8,128)S(1)}, f32[7,8,1024]{2,1,0:T(8,128)S(1)}, f32[7,8,1024]{2,1,0:T(8,128)S(1)}, f32[1,128]{1,0:T(1,128)S(1)}) custom-call(f32[8,1024]{1,0:T(8,128)S(1)} %copy-done, f32[6,4,1024]{2,1,0:T(4,128)S(1)} %collective-permute-done.refs_3_.refs_1_, f32[6,4,1024]{2,1,0:T(4,128)S(1)} %collective-permute-done.1.refs_4_.refs_2_, ...), custom_call_target="tpu_custom_call" | custom-call | tf_op jit(solution)/shard_map/pallas_call | solution.py:575
  41.5 0.0 collective-permute-done.8.refs_5_
  41.5 0.0 collective-permute-done.9.refs_6_
  41.5 0.6 shard_map.68
  42.1 33.0 %all_to_all.23 = f32[128,1,128]{2,1,0:T(1,128)S(1)} all-to-all(f32[128,1,128]{2,1,0:T(1,128)S(1)} %bitcast.10), channel_id=1, replica_groups=mesh['blk'=128,'rhs'=4] {'blk'}, dimensions={0} | all-to-all | bytes 131072 | tf_op jit(solution)/shard_map/all_to_all | solution.py:585
  75.1 1.4 %shard_map.69 = (f32[4,128]{1,0:T(4,128)}, f32[7,8,128]{2,1,0:T(8,128)S(1)}) custom-call(f32[128,128]{1,0:T(8,128)S(1)} %bitcast.9), custom_call_target="tpu_custom_call" | custom-call | tf_op jit(solution)/shard_map/pallas_call | solution.py:586
  76.5 4.0 %all-to-all-start.1 = ((f32[4,1,128]{2,1,0:T(1,128)}), f32[4,1,128]{2,1,0:T(1,128)S(1)}, u32[]{:S(2)}, u32[]{:S(2)}) async-start(f32[4,1,128]{2,1,0:T(1,128)} %bitcast.4), calls=%async_computation.1 | async-start | bytes 4096 | tf_op jit(solution)/shard_map/all_to_all | solution.py:591
  80.5 0.8 shard_map.70
  81.3 3.2 %all-to-all-done.1 = f32[4,1,128]{2,1,0:T(1,128)S(1)} async-done(((f32[4,1,128]{2,1,0:T(1,128)}), f32[4,1,128]{2,1,0:T(1,128)S(1)}, u32[]{:S(2)}, u32[]{:S(2)}) %all-to-all-start.1) | async-done | bytes 2080 | tf_op jit(solution)/shard_map/all_to_all | solution.py:591
  84.5 0.6 reshape.11
Async XLA Ops:
  0.6 0.8 copy-start
  1.4 10.6 %copy-start.3 = (s32[8,1024]{1,0:T(8,128)S(1)}, s32[8,1024]{1,0:T(8,128)}, u32[]{:S(2)}) copy-start(s32[8,1024]{1,0:T(8,128)} %refs_1_.9) | copy-start | bytes 98308
  1.4 11.7 %copy-start.1 = (f32[4,8,1024]{2,1,0:T(8,128)S(1)}, f32[4,8,1024]{2,1,0:T(8,128)}, u32[]{:S(2)}) copy-start(f32[4,8,1024]{2,1,0:T(8,128)} %refs_1_.15) | copy-start | bytes 393220
  1.4 11.7 %copy-start.2 = (f32[4,8,1024]{2,1,0:T(8,128)S(1)}, f32[4,8,1024]{2,1,0:T(8,128)}, u32[]{:S(2)}) copy-start(f32[4,8,1024]{2,1,0:T(8,128)} %refs_0_.7) | copy-start | bytes 393220
  2.5 10.5 %collective-permute-start = (f32[6,4,1024]{2,1,0:T(4,128)S(1)}, f32[6,4,1024]{2,1,0:T(4,128)S(1)}, u32[]{:S(2)}, u32[]{:S(2)}) collective-permute-start(f32[6,4,1024]{2,1,0:T(4,128)S(1)} %get-tuple-element.32), channel_id=1, source_target_pairs={{4,8},{12,16},{20,24},{28,32},{36,40},{44,48},{52,56},{60,64},{68,... | collective-permute-start | bytes 294920 | tf_op jit(solution)/shard_map/ppermute | solution.py:524
  7.1 6.0 %collective-permute-start.1 = (f32[6,4,1024]{2,1,0:T(4,128)S(1)}, f32[6,4,1024]{2,1,0:T(4,128)S(1)}, u32[]{:S(2)}, u32[]{:S(2)}) collective-permute-start(f32[6,4,1024]{2,1,0:T(4,128)S(1)} %get-tuple-element.33), channel_id=1, source_target_pairs={{0,4},{4,0},{8,12},{12,8},{16,20},{20,16},{24,28},{28,24},{32,36},... | collective-permute-start | bytes 294920 | tf_op jit(solution)/shard_map/ppermute | solution.py:525
  14.1 5.2 %collective-permute-start.2 = (f32[8,1024]{1,0:T(8,128)S(1)}, f32[8,1024]{1,0:T(8,128)S(1)}, u32[]{:S(2)}, u32[]{:S(2)}) collective-permute-start(f32[8,1024]{1,0:T(8,128)S(1)} %get-tuple-element.41), channel_id=1, source_target_pairs={{4,8},{12,16},{20,24},{28,32},{36,40},{44,48},{52,56},{60,64},{68,... | collective-permute-start | bytes 98312 | tf_op jit(solution)/shard_map/ppermute | solution.py:524
  16.0 3.3 %collective-permute-start.3 = (f32[8,1024]{1,0:T(8,128)S(1)}, f32[8,1024]{1,0:T(8,128)S(1)}, u32[]{:S(2)}, u32[]{:S(2)}) collective-permute-start(f32[8,1024]{1,0:T(8,128)S(1)} %get-tuple-element.42), channel_id=1, source_target_pairs={{0,4},{4,0},{8,12},{12,8},{16,20},{20,16},{24,28},{28,24},{32,36},... | collective-permute-start | bytes 98312 | tf_op jit(solution)/shard_map/ppermute | solution.py:525
  20.2 6.3 %collective-permute-start.4 = (f32[4,1024]{1,0:T(4,128)S(1)}, f32[4,1024]{1,0:T(4,128)S(1)}, u32[]{:S(2)}, u32[]{:S(2)}) collective-permute-start(f32[4,1024]{1,0:T(4,128)S(1)} %get-tuple-element.44), channel_id=1, source_target_pairs={{4,8},{12,16},{20,24},{28,32},{36,40},{44,48},{52,56},{60,64},{68,... | collective-permute-start | bytes 49160 | tf_op jit(solution)/shard_map/ppermute | solution.py:524
  23.6 3.1 %collective-permute-start.5 = (f32[4,1024]{1,0:T(4,128)S(1)}, f32[4,1024]{1,0:T(4,128)S(1)}, u32[]{:S(2)}, u32[]{:S(2)}) collective-permute-start(f32[4,1024]{1,0:T(4,128)S(1)} %get-tuple-element.45), channel_id=1, source_target_pairs={{0,4},{4,0},{8,12},{12,8},{16,20},{20,16},{24,28},{28,24},{32,36},... | collective-permute-start | bytes 49160 | tf_op jit(solution)/shard_map/ppermute | solution.py:525
  27.5 5.8 %collective-permute-start.6 = (f32[5,4,1024]{2,1,0:T(4,128)S(1)}, f32[5,4,1024]{2,1,0:T(4,128)S(1)}, u32[]{:S(2)}, u32[]{:S(2)}) collective-permute-start(f32[5,4,1024]{2,1,0:T(4,128)S(1)} %get-tuple-element.48), channel_id=1, source_target_pairs={{4,8},{12,16},{20,24},{28,32},{36,40},{44,48},{52,56},{60,64},{68,... | collective-permute-start | bytes 245768 | tf_op jit(solution)/shard_map/ppermute | solution.py:524
  30.5 3.2 %collective-permute-start.7 = (f32[5,4,1024]{2,1,0:T(4,128)S(1)}, f32[5,4,1024]{2,1,0:T(4,128)S(1)}, u32[]{:S(2)}, u32[]{:S(2)}) collective-permute-start(f32[5,4,1024]{2,1,0:T(4,128)S(1)} %get-tuple-element.49), channel_id=1, source_target_pairs={{0,4},{4,0},{8,12},{12,8},{16,20},{20,16},{24,28},{28,24},{32,36},... | collective-permute-start | bytes 245768 | tf_op jit(solution)/shard_map/ppermute | solution.py:525
  34.5 7.0 %collective-permute-start.8 = (f32[3,4,1024]{2,1,0:T(4,128)S(1)}, f32[3,4,1024]{2,1,0:T(4,128)S(1)}, u32[]{:S(2)}, u32[]{:S(2)}) collective-permute-start(f32[3,4,1024]{2,1,0:T(4,128)S(1)} %get-tuple-element.52), channel_id=1, source_target_pairs={{4,8},{12,16},{20,24},{28,32},{36,40},{44,48},{52,56},{60,64},{68,... | collective-permute-start | bytes 147464 | tf_op jit(solution)/shard_map/ppermute | solution.py:524
  38.3 3.2 %collective-permute-start.9 = (f32[3,4,1024]{2,1,0:T(4,128)S(1)}, f32[3,4,1024]{2,1,0:T(4,128)S(1)}, u32[]{:S(2)}, u32[]{:S(2)}) collective-permute-start(f32[3,4,1024]{2,1,0:T(4,128)S(1)} %get-tuple-element.53), channel_id=1, source_target_pairs={{0,4},{4,0},{8,12},{12,8},{16,20},{20,16},{24,28},{28,24},{32,36},... | collective-permute-start | bytes 147464 | tf_op jit(solution)/shard_map/ppermute | solution.py:525
  76.5 8.0 %all-to-all-start.1 = ((f32[4,1,128]{2,1,0:T(1,128)}), f32[4,1,128]{2,1,0:T(1,128)S(1)}, u32[]{:S(2)}, u32[]{:S(2)}) async-start(f32[4,1,128]{2,1,0:T(1,128)} %bitcast.4), calls=%async_computation.1 | async-start | bytes 4096 | tf_op jit(solution)/shard_map/all_to_all | solution.py:591

commit v12 on v11

--- a/solution.py
+++ b/solution.py
@@ -233,7 +233,7 @@
     part = x[:, 0:128]
     for k in range(1, width // 128):
         part = part + x[:, k * 128 : (k + 1) * 128]
-    return jnp.sum(jnp.sum(part, axis=1, keepdims=True), axis=0, keepdims=True)
+    return jnp.sum(jnp.sum(part, axis=0, keepdims=True), axis=1, keepdims=True)
 
 
 def lane_row(values):

time: 85.6 us -> 85.6 us (level)
  no operation moved by 1% of the time
where the time goes in v12:
time: 85.6 us; the launch traced here: 85.1 us
  starting transfers between devices  33.2 us (39%)
  blocking collectives  33 us (39%)
  Pallas kernels  10.9 us (13%)
  waiting for transfers between devices  5.84 us (7%)
  local copies, waits for them, and re-layouts  1.35 us (2%)
    all_to_all x1, blocking collectives, local(): gathered = lax.all_to_all(mine, 'blk', 0, 0, tiled=True)  33 us
    ppermute x5, starting transfers between devices, exchange(): cross = lax.ppermute(cross, 'blk', cross_chip)  16.6 us
    ppermute x5, starting transfers between devices, exchange(): return (cross, lax.ppermute(chip, 'blk', on_chip))  12.5 us
    all_to_all x1, starting transfers between devices, local(): every = lax.all_to_all(ratio, 'rhs', 0, 0, tiled=True)  4.01 us
    all_to_all x1, waiting for transfers between devices, local(): every = lax.all_to_all(ratio, 'rhs', 0, 0, tiled=True)  3.2 us
    ppermute x5, waiting for transfers between devices, exchange(): cross = lax.ppermute(cross, 'blk', cross_chip)  2.06 us
  transfers between devices with their start and end apart: 11, of which 5 were waited for; matrix products, arithmetic and copies ran while one was open for 0% of the time, Pallas kernels for 5%

profile of v12, /device:TPU:1, one launch (start us, length us, event | category | flops | bytes accessed | tf_op | source)
XLA Modules:
  0.0 85.1 jit_solution(14481275700176113592)
XLA Ops:
  0.6 0.0 copy-start
  0.6 0.7 copy-done
  1.4 0.0 copy-start.3
  1.4 0.0 copy-start.1
  1.4 0.0 copy-start.2
  1.4 1.1 %shard_map.59 = (f32[6,4,1024]{2,1,0:T(4,128)S(1)}, f32[6,4,1024]{2,1,0:T(4,128)S(1)}) custom-call(f32[4,8,1024]{2,1,0:T(8,128)} %refs_0_.7, f32[4,8,1024]{2,1,0:T(8,128)} %refs_1_.15, f32[8,1024]{1,0:T(8,128)S(1)} %copy-done), custom_call_target="tpu_custom_call" | custom-call | tf_op jit(solution)/shard_map/pallas_call | solution.py:532
  2.5 4.6 %collective-permute-start = (f32[6,4,1024]{2,1,0:T(4,128)S(1)}, f32[6,4,1024]{2,1,0:T(4,128)S(1)}, u32[]{:S(2)}, u32[]{:S(2)}) collective-permute-start(f32[6,4,1024]{2,1,0:T(4,128)S(1)} %get-tuple-element.32), channel_id=1, source_target_pairs={{4,8},{12,16},{20,24},{28,32},{36,40},{44,48},{52,56},{60,64},{68,... | collective-permute-start | bytes 294920 | tf_op jit(solution)/shard_map/ppermute | solution.py:524
  7.1 4.9 %collective-permute-start.1 = (f32[6,4,1024]{2,1,0:T(4,128)S(1)}, f32[6,4,1024]{2,1,0:T(4,128)S(1)}, u32[]{:S(2)}, u32[]{:S(2)}) collective-permute-start(f32[6,4,1024]{2,1,0:T(4,128)S(1)} %get-tuple-element.33), channel_id=1, source_target_pairs={{0,4},{4,0},{8,12},{12,8},{16,20},{20,16},{24,28},{28,24},{32,36},... | collective-permute-start | bytes 294920 | tf_op jit(solution)/shard_map/ppermute | solution.py:525
  11.9 0.0 copy-done.3
  12.0 1.1 %shard_map.60 = (s32[14,8,1024]{2,1,0:T(8,128)S(1)}, f32[14,8,1024]{2,1,0:T(8,128)S(1)}, f32[7,8,1024]{2,1,0:T(8,128)S(1)}, f32[8,1024]{1,0:T(8,128)S(1)}, f32[3,8,1024]{2,1,0:T(8,128)S(1)}) custom-call(f32[8,1024]{1,0:T(8,128)S(1)} %copy-done, s32[8,1024]{1,0:T(8,128)S(1)} %copy-done.3), custom_call_target="tpu_custom_call" | custom-call | tf_op jit(solution)/shard_map/pallas_call | solution.py:546
  13.0 0.0 collective-permute-done.refs_3_.refs_1_
  13.0 0.0 collective-permute-done.1.refs_4_.refs_2_
  13.0 0.0 copy-done.1
  13.1 0.0 copy-done.2
  13.1 1.0 %shard_map.61 = (f32[4,8,1024]{2,1,0:T(8,128)S(1)}, f32[4,8,1024]{2,1,0:T(8,128)S(1)}, f32[4,8,1024]{2,1,0:T(8,128)S(1)}, f32[8,1024]{1,0:T(8,128)S(1)}, f32[8,1024]{1,0:T(8,128)S(1)}, /*index=5*/f32[1,128]{1,0:T(1,128)S(1)}) custom-call(f32[4,8,1024]{2,1,0:T(8,128)S(1)} %copy-done.2, f32[4,8,1024]{2,1,0:T(8,128)S(1)} %copy-done.1, f32[8,1024]{1,0:T(8,128)S(1)} %copy-done, ...), custom_call_target="tpu_custom_call" | custom-call | tf_op jit(solution)/shard_map/pallas_call | solution.py:558
  14.1 1.9 %collective-permute-start.2 = (f32[8,1024]{1,0:T(8,128)S(1)}, f32[8,1024]{1,0:T(8,128)S(1)}, u32[]{:S(2)}, u32[]{:S(2)}) collective-permute-start(f32[8,1024]{1,0:T(8,128)S(1)} %get-tuple-element.41), channel_id=1, source_target_pairs={{4,8},{12,16},{20,24},{28,32},{36,40},{44,48},{52,56},{60,64},{68,... | collective-permute-start | bytes 98312 | tf_op jit(solution)/shard_map/ppermute | solution.py:524
  16.0 1.9 %collective-permute-start.3 = (f32[8,1024]{1,0:T(8,128)S(1)}, f32[8,1024]{1,0:T(8,128)S(1)}, u32[]{:S(2)}, u32[]{:S(2)}) collective-permute-start(f32[8,1024]{1,0:T(8,128)S(1)} %get-tuple-element.42), channel_id=1, source_target_pairs={{0,4},{4,0},{8,12},{12,8},{16,20},{20,16},{24,28},{28,24},{32,36},... | collective-permute-start | bytes 98312 | tf_op jit(solution)/shard_map/ppermute | solution.py:525
  18.0 1.4 %collective-permute-done.2.refs_7_.refs_6_ = f32[8,1024]{1,0:T(8,128)S(1)} collective-permute-done((f32[8,1024]{1,0:T(8,128)S(1)}, f32[8,1024]{1,0:T(8,128)S(1)}, u32[]{:S(2)}, u32[]{:S(2)}) %collective-permute-start.2) | collective-permute-done | bytes 32800 | tf_op jit(solution)/shard_map/ppermute | solution.py:524
  19.3 0.0 collective-permute-done.3.refs_8_.refs_7_
  19.3 0.8 shard_map.62
  20.1 3.4 %collective-permute-start.4 = (f32[4,1024]{1,0:T(4,128)S(1)}, f32[4,1024]{1,0:T(4,128)S(1)}, u32[]{:S(2)}, u32[]{:S(2)}) collective-permute-start(f32[4,1024]{1,0:T(4,128)S(1)} %get-tuple-element.44), channel_id=1, source_target_pairs={{4,8},{12,16},{20,24},{28,32},{36,40},{44,48},{52,56},{60,64},{68,... | collective-permute-start | bytes 49160 | tf_op jit(solution)/shard_map/ppermute | solution.py:524
  23.6 1.9 %collective-permute-start.5 = (f32[4,1024]{1,0:T(4,128)S(1)}, f32[4,1024]{1,0:T(4,128)S(1)}, u32[]{:S(2)}, u32[]{:S(2)}) collective-permute-start(f32[4,1024]{1,0:T(4,128)S(1)} %get-tuple-element.45), channel_id=1, source_target_pairs={{0,4},{4,0},{8,12},{12,8},{16,20},{20,16},{24,28},{28,24},{32,36},... | collective-permute-start | bytes 49160 | tf_op jit(solution)/shard_map/ppermute | solution.py:525
  25.5 0.9 %shard_map.63.refs_7_.refs_3_ = f32[5,8,1024]{2,1,0:T(8,128)S(1)} custom-call(f32[8,1024]{1,0:T(8,128)S(1)} %copy-done, s32[14,8,1024]{2,1,0:T(8,128)S(1)} %get-tuple-element.34.refs_5_.refs_3_.refs_1_, f32[14,8,1024]{2,1,0:T(8,128)S(1)} %get-tuple-element.35.refs_6_.refs_4_.refs_2_, f32[7,8,1024]{2,1,0:T(8,128)S(1)} %get-tuple-element.36.refs_7_.refs_5_.refs_3_, ...), custom_call_target="tpu_custom_call" | custom-call | tf_op jit(solution)/shard_map/pallas_call | solution.py:566
  26.4 0.0 collective-permute-done.4.refs_8_
  26.4 0.2 collective-permute-done.5.refs_9_
  26.7 0.9 %shard_map.64 = (f32[4,8,1024]{2,1,0:T(8,128)S(1)}, f32[5,4,1024]{2,1,0:T(4,128)S(1)}, f32[5,4,1024]{2,1,0:T(4,128)S(1)}) custom-call(f32[4,8,1024]{2,1,0:T(8,128)S(1)} %get-tuple-element.43.refs_0_, f32[8,1024]{1,0:T(8,128)S(1)} %copy-done, f32[4,8,1024]{2,1,0:T(8,128)S(1)} %get-tuple-element.40.refs_2_, ...), custom_call_target="tpu_custom_call" | custom-call | tf_op jit(solution)/shard_map/pallas_call | solution.py:570
  27.5 2.9 %collective-permute-start.6 = (f32[5,4,1024]{2,1,0:T(4,128)S(1)}, f32[5,4,1024]{2,1,0:T(4,128)S(1)}, u32[]{:S(2)}, u32[]{:S(2)}) collective-permute-start(f32[5,4,1024]{2,1,0:T(4,128)S(1)} %get-tuple-element.48), channel_id=1, source_target_pairs={{4,8},{12,16},{20,24},{28,32},{36,40},{44,48},{52,56},{60,64},{68,... | collective-permute-start | bytes 245768 | tf_op jit(solution)/shard_map/ppermute | solution.py:524
  30.5 1.9 %collective-permute-start.7 = (f32[5,4,1024]{2,1,0:T(4,128)S(1)}, f32[5,4,1024]{2,1,0:T(4,128)S(1)}, u32[]{:S(2)}, u32[]{:S(2)}) collective-permute-start(f32[5,4,1024]{2,1,0:T(4,128)S(1)} %get-tuple-element.49), channel_id=1, source_target_pairs={{0,4},{4,0},{8,12},{12,8},{16,20},{20,16},{24,28},{28,24},{32,36},... | collective-permute-start | bytes 245768 | tf_op jit(solution)/shard_map/ppermute | solution.py:525
  32.4 0.2 shard_map.65.refs_10_.refs_9_
  32.6 0.7 collective-permute-done.6.refs_8_.refs_4_
  33.3 0.4 collective-permute-done.7.refs_9_.refs_5_
  33.6 0.8 shard_map.66
  34.5 3.8 %collective-permute-start.8 = (f32[3,4,1024]{2,1,0:T(4,128)S(1)}, f32[3,4,1024]{2,1,0:T(4,128)S(1)}, u32[]{:S(2)}, u32[]{:S(2)}) collective-permute-start(f32[3,4,1024]{2,1,0:T(4,128)S(1)} %get-tuple-element.52), channel_id=1, source_target_pairs={{4,8},{12,16},{20,24},{28,32},{36,40},{44,48},{52,56},{60,64},{68,... | collective-permute-start | bytes 147464 | tf_op jit(solution)/shard_map/ppermute | solution.py:524
  38.3 1.9 %collective-permute-start.9 = (f32[3,4,1024]{2,1,0:T(4,128)S(1)}, f32[3,4,1024]{2,1,0:T(4,128)S(1)}, u32[]{:S(2)}, u32[]{:S(2)}) collective-permute-start(f32[3,4,1024]{2,1,0:T(4,128)S(1)} %get-tuple-element.53), channel_id=1, source_target_pairs={{0,4},{4,0},{8,12},{12,8},{16,20},{20,16},{24,28},{28,24},{32,36},... | collective-permute-start | bytes 147464 | tf_op jit(solution)/shard_map/ppermute | solution.py:525
  40.2 1.3 %shard_map.67 = (f32[7,8,1024]{2,1,0:T(8,128)S(1)}, f32[7,8,1024]{2,1,0:T(8,128)S(1)}, f32[7,8,1024]{2,1,0:T(8,128)S(1)}, f32[1,128]{1,0:T(1,128)S(1)}) custom-call(f32[8,1024]{1,0:T(8,128)S(1)} %copy-done, f32[6,4,1024]{2,1,0:T(4,128)S(1)} %collective-permute-done.refs_3_.refs_1_, f32[6,4,1024]{2,1,0:T(4,128)S(1)} %collective-permute-done.1.refs_4_.refs_2_, ...), custom_call_target="tpu_custom_call" | custom-call | tf_op jit(solution)/shard_map/pallas_call | solution.py:575
  41.5 0.0 collective-permute-done.8.refs_5_
  41.5 0.0 collective-permute-done.9.refs_6_
  41.5 0.6 shard_map.68
  42.1 33.0 %all_to_all.23 = f32[128,1,128]{2,1,0:T(1,128)S(1)} all-to-all(f32[128,1,128]{2,1,0:T(1,128)S(1)} %bitcast.10), channel_id=1, replica_groups=mesh['blk'=128,'rhs'=4] {'blk'}, dimensions={0} | all-to-all | bytes 131072 | tf_op jit(solution)/shard_map/all_to_all | solution.py:585
  75.1 1.4 %shard_map.69 = (f32[4,128]{1,0:T(4,128)}, f32[7,8,128]{2,1,0:T(8,128)S(1)}) custom-call(f32[128,128]{1,0:T(8,128)S(1)} %bitcast.9), custom_call_target="tpu_custom_call" | custom-call | tf_op jit(solution)/shard_map/pallas_call | solution.py:586
  76.5 4.0 %all-to-all-start.1 = ((f32[4,1,128]{2,1,0:T(1,128)}), f32[4,1,128]{2,1,0:T(1,128)S(1)}, u32[]{:S(2)}, u32[]{:S(2)}) async-start(f32[4,1,128]{2,1,0:T(1,128)} %bitcast.4), calls=%async_computation.1 | async-start | bytes 4096 | tf_op jit(solution)/shard_map/all_to_all | solution.py:591
  80.5 0.8 shard_map.70
  81.3 3.2 %all-to-all-done.1 = f32[4,1,128]{2,1,0:T(1,128)S(1)} async-done(((f32[4,1,128]{2,1,0:T(1,128)}), f32[4,1,128]{2,1,0:T(1,128)S(1)}, u32[]{:S(2)}, u32[]{:S(2)}) %all-to-all-start.1) | async-done | bytes 2080 | tf_op jit(solution)/shard_map/all_to_all | solution.py:591
  84.5 0.6 reshape.11
Async XLA Ops:
  0.6 0.8 copy-start
  1.4 10.6 %copy-start.3 = (s32[8,1024]{1,0:T(8,128)S(1)}, s32[8,1024]{1,0:T(8,128)}, u32[]{:S(2)}) copy-start(s32[8,1024]{1,0:T(8,128)} %refs_1_.9) | copy-start | bytes 98308
  1.4 11.7 %copy-start.1 = (f32[4,8,1024]{2,1,0:T(8,128)S(1)}, f32[4,8,1024]{2,1,0:T(8,128)}, u32[]{:S(2)}) copy-start(f32[4,8,1024]{2,1,0:T(8,128)} %refs_1_.15) | copy-start | bytes 393220
  1.4 11.7 %copy-start.2 = (f32[4,8,1024]{2,1,0:T(8,128)S(1)}, f32[4,8,1024]{2,1,0:T(8,128)}, u32[]{:S(2)}) copy-start(f32[4,8,1024]{2,1,0:T(8,128)} %refs_0_.7) | copy-start | bytes 393220
  2.5 10.5 %collective-permute-start = (f32[6,4,1024]{2,1,0:T(4,128)S(1)}, f32[6,4,1024]{2,1,0:T(4,128)S(1)}, u32[]{:S(2)}, u32[]{:S(2)}) collective-permute-start(f32[6,4,1024]{2,1,0:T(4,128)S(1)} %get-tuple-element.32), channel_id=1, source_target_pairs={{4,8},{12,16},{20,24},{28,32},{36,40},{44,48},{52,56},{60,64},{68,... | collective-permute-start | bytes 294920 | tf_op jit(solution)/shard_map/ppermute | solution.py:524
  7.1 6.0 %collective-permute-start.1 = (f32[6,4,1024]{2,1,0:T(4,128)S(1)}, f32[6,4,1024]{2,1,0:T(4,128)S(1)}, u32[]{:S(2)}, u32[]{:S(2)}) collective-permute-start(f32[6,4,1024]{2,1,0:T(4,128)S(1)} %get-tuple-element.33), channel_id=1, source_target_pairs={{0,4},{4,0},{8,12},{12,8},{16,20},{20,16},{24,28},{28,24},{32,36},... | collective-permute-start | bytes 294920 | tf_op jit(solution)/shard_map/ppermute | solution.py:525
  14.1 5.2 %collective-permute-start.2 = (f32[8,1024]{1,0:T(8,128)S(1)}, f32[8,1024]{1,0:T(8,128)S(1)}, u32[]{:S(2)}, u32[]{:S(2)}) collective-permute-start(f32[8,1024]{1,0:T(8,128)S(1)} %get-tuple-element.41), channel_id=1, source_target_pairs={{4,8},{12,16},{20,24},{28,32},{36,40},{44,48},{52,56},{60,64},{68,... | collective-permute-start | bytes 98312 | tf_op jit(solution)/shard_map/ppermute | solution.py:524
  16.0 3.3 %collective-permute-start.3 = (f32[8,1024]{1,0:T(8,128)S(1)}, f32[8,1024]{1,0:T(8,128)S(1)}, u32[]{:S(2)}, u32[]{:S(2)}) collective-permute-start(f32[8,1024]{1,0:T(8,128)S(1)} %get-tuple-element.42), channel_id=1, source_target_pairs={{0,4},{4,0},{8,12},{12,8},{16,20},{20,16},{24,28},{28,24},{32,36},... | collective-permute-start | bytes 98312 | tf_op jit(solution)/shard_map/ppermute | solution.py:525
  20.1 6.3 %collective-permute-start.4 = (f32[4,1024]{1,0:T(4,128)S(1)}, f32[4,1024]{1,0:T(4,128)S(1)}, u32[]{:S(2)}, u32[]{:S(2)}) collective-permute-start(f32[4,1024]{1,0:T(4,128)S(1)} %get-tuple-element.44), channel_id=1, source_target_pairs={{4,8},{12,16},{20,24},{28,32},{36,40},{44,48},{52,56},{60,64},{68,... | collective-permute-start | bytes 49160 | tf_op jit(solution)/shard_map/ppermute | solution.py:524
  23.6 3.1 %collective-permute-start.5 = (f32[4,1024]{1,0:T(4,128)S(1)}, f32[4,1024]{1,0:T(4,128)S(1)}, u32[]{:S(2)}, u32[]{:S(2)}) collective-permute-start(f32[4,1024]{1,0:T(4,128)S(1)} %get-tuple-element.45), channel_id=1, source_target_pairs={{0,4},{4,0},{8,12},{12,8},{16,20},{20,16},{24,28},{28,24},{32,36},... | collective-permute-start | bytes 49160 | tf_op jit(solution)/shard_map/ppermute | solution.py:525
  27.5 5.8 %collective-permute-start.6 = (f32[5,4,1024]{2,1,0:T(4,128)S(1)}, f32[5,4,1024]{2,1,0:T(4,128)S(1)}, u32[]{:S(2)}, u32[]{:S(2)}) collective-permute-start(f32[5,4,1024]{2,1,0:T(4,128)S(1)} %get-tuple-element.48), channel_id=1, source_target_pairs={{4,8},{12,16},{20,24},{28,32},{36,40},{44,48},{52,56},{60,64},{68,... | collective-permute-start | bytes 245768 | tf_op jit(solution)/shard_map/ppermute | solution.py:524
  30.5 3.2 %collective-permute-start.7 = (f32[5,4,1024]{2,1,0:T(4,128)S(1)}, f32[5,4,1024]{2,1,0:T(4,128)S(1)}, u32[]{:S(2)}, u32[]{:S(2)}) collective-permute-start(f32[5,4,1024]{2,1,0:T(4,128)S(1)} %get-tuple-element.49), channel_id=1, source_target_pairs={{0,4},{4,0},{8,12},{12,8},{16,20},{20,16},{24,28},{28,24},{32,36},... | collective-permute-start | bytes 245768 | tf_op jit(solution)/shard_map/ppermute | solution.py:525
  34.5 7.0 %collective-permute-start.8 = (f32[3,4,1024]{2,1,0:T(4,128)S(1)}, f32[3,4,1024]{2,1,0:T(4,128)S(1)}, u32[]{:S(2)}, u32[]{:S(2)}) collective-permute-start(f32[3,4,1024]{2,1,0:T(4,128)S(1)} %get-tuple-element.52), channel_id=1, source_target_pairs={{4,8},{12,16},{20,24},{28,32},{36,40},{44,48},{52,56},{60,64},{68,... | collective-permute-start | bytes 147464 | tf_op jit(solution)/shard_map/ppermute | solution.py:524
  38.3 3.2 %collective-permute-start.9 = (f32[3,4,1024]{2,1,0:T(4,128)S(1)}, f32[3,4,1024]{2,1,0:T(4,128)S(1)}, u32[]{:S(2)}, u32[]{:S(2)}) collective-permute-start(f32[3,4,1024]{2,1,0:T(4,128)S(1)} %get-tuple-element.53), channel_id=1, source_target_pairs={{0,4},{4,0},{8,12},{12,8},{16,20},{20,16},{24,28},{28,24},{32,36},... | collective-permute-start | bytes 147464 | tf_op jit(solution)/shard_map/ppermute | solution.py:525
  76.5 8.0 %all-to-all-start.1 = ((f32[4,1,128]{2,1,0:T(1,128)}), f32[4,1,128]{2,1,0:T(1,128)S(1)}, u32[]{:S(2)}, u32[]{:S(2)}) async-start(f32[4,1,128]{2,1,0:T(1,128)} %bitcast.4), calls=%async_computation.1 | async-start | bytes 4096 | tf_op jit(solution)/shard_map/all_to_all | solution.py:591
